TPU v7x, 128 devices: a whole 4x4x4 slice. The times are simulated.
128 devices in a mesh: dom: 16 (over x, y), blk: 8 (over z, core).
Axes of the slice: x: 4, y: 4, z: 4, core: 2. Of those that a mesh axis runs over, the one named last changes fastest.
Arguments:
- node_features: bfloat16 [32768, 512], P(('dom', 'blk')), may hold values from -6 to 6
- norm_gain: float32 [512], replicated, may hold values from 0.25 to 1.75
- w_query: bfloat16 [512, 512], replicated, may hold values from -0.25 to 0.25
- w_key: bfloat16 [512, 512], replicated, may hold values from -0.25 to 0.25
- w_value: bfloat16 [512, 512], replicated, may hold values from -0.25 to 0.25
- w_out: bfloat16 [512, 512], replicated, may hold values from -1.5 to 1.5
- w_message: bfloat16 [512, 512], replicated, may hold values from -1 to 1
- node_cluster: int32 [32768], P(('dom', 'blk')), may hold values from 0 to 15
- block_pattern: int32 [128, 8], P(('dom', 'blk')), may hold values from 0 to 1, as said below
- send_rows: int32 [2048, 128], P(('dom', 'blk')), may hold values from 0 to 255
- send_counts: int32 [2048], P(('dom', 'blk')), may hold values from 32 to 128, as said below
- edge_src: int32 [524288], P(('dom', 'blk')), may hold values from 0 to 2047
- edge_dst: int32 [524288], P(('dom', 'blk')), may hold values from 0 to 255
- out_grad: bfloat16 [32768, 512], P(('dom', 'blk')), may hold values from -6 to 6
Outputs:
- layer_out: bfloat16 [32768, 512], P(('dom', 'blk'))
- feature_grad: bfloat16 [32768, 512], P(('dom', 'blk'))
- weight_grads: float32 [5, 512, 512], replicated
- gain_grad: float32 [512], replicated
Inputs may be any that keep to these rules, and one draw needn't show every extreme that they name: `block_pattern`: row g has a 1 at column (g mod 8); other entries are 0 or 1. `send_counts`: entry g * 16 + p is how many leading slots of device g's block to dom peer p are live; every device has one peer whose block has all 128 slots live.
All inputs are finite; a program needn't handle non-finite values.
Results may differ from a plain program's by a relative error of at most 0.013.
Values may be sent and summed in bfloat16 or wider, within the bound.
No kernel may reach another device: no remote copies, remote signals or barrier semaphores. Data moves between devices by JAX's collectives and lax.ppermute only.
A program may use at most 128 MiB of HBM per device.

v0:
```python
from functools import partial

import jax
import jax.numpy as jnp
from jax import lax
from jax.sharding import PartitionSpec as P

HEADS = 8
HEAD_DIM = 64


epsilon = 1e-06
score_shift = 8.0


def settle(array):
    return lax.optimization_barrier(array.astype(jnp.bfloat16)).astype(jnp.float32)


def rms_norm(features, norm_gain):
    scaling = lax.rsqrt(jnp.mean(features * features, axis=-1, keepdims=True) + epsilon)
    return features * scaling * norm_gain


def head_norm(projected):
    head_view = projected.reshape(projected.shape[0], HEADS, HEAD_DIM)
    scaling = lax.rsqrt(jnp.mean(head_view * head_view, axis=-1, keepdims=True) + epsilon)
    return (head_view * scaling).reshape(projected.shape)


def block_weights(query_heads, key_heads, allowed):
    scaling = score_shift / HEAD_DIM
    scores = (
        jnp.einsum("rhe,khe->hrk", query_heads, key_heads, preferred_element_type=jnp.float32)
        * scaling
    )
    return jnp.where(allowed[None], jnp.exp(scores - score_shift), 0.0)


def attend_piece(running, shard_piece, offset, query_heads, query_labels, pattern_row, skip_empty):
    key_rows, value_rows, key_labels = shard_piece
    row_count = query_heads.shape[0]
    piece_rows = key_rows.shape[0]
    part_count = max(piece_rows // row_count, 1)
    block_index = jnp.arange(pattern_row.shape[0], dtype=jnp.int32)
    for position in range(part_count):
        first_row = position * piece_rows // part_count
        last_row = (position + 1) * piece_rows // part_count
        part_rows = last_row - first_row
        key_part = key_rows[first_row:last_row].reshape(part_rows, HEADS, HEAD_DIM)
        value_part = value_rows[first_row:last_row].reshape(part_rows, HEADS, HEAD_DIM)
        label_part = key_labels[first_row:last_row]
        owners = (offset + first_row + jnp.arange(part_rows, dtype=jnp.int32)) // row_count
        block_flags = jnp.sum(
            jnp.where(owners[:, None] == block_index[None, :], pattern_row[None, :], 0), axis=1
        )
        allowed = (query_labels[:, None] == label_part[None, :]) & (block_flags[None, :] == 1)

        def accumulate(current, key_part=key_part, value_part=value_part, allowed=allowed):
            numer, denom = current
            weights = block_weights(query_heads, key_part, allowed)
            denom = denom + jnp.sum(weights, axis=2).T
            numer = numer + jnp.einsum(
                "hrk,khe->rhe",
                weights.astype(jnp.bfloat16),
                value_part,
                preferred_element_type=jnp.float32,
            )
            return (numer, denom)

        running = accumulate(running)
    return running


def pair_gradients(query_heads, grad_heads, correction, key_part, value_part, allowed):
    scaling = score_shift / HEAD_DIM
    weights = block_weights(query_heads, key_part, allowed)
    grad_dots = jnp.einsum(
        "rhe,khe->hrk", grad_heads, value_part, preferred_element_type=jnp.float32
    )
    slopes = (weights * (grad_dots - correction.T[:, :, None])).astype(jnp.bfloat16)
    dq_part = (
        jnp.einsum("hrk,khe->rhe", slopes, key_part, preferred_element_type=jnp.float32) * scaling
    )
    dk_part = (
        jnp.einsum("hrk,rhe->khe", slopes, query_heads, preferred_element_type=jnp.float32)
        * scaling
    )
    dv_part = jnp.einsum(
        "hrk,rhe->khe", weights.astype(jnp.bfloat16), grad_heads, preferred_element_type=jnp.float32
    )
    return (dq_part, dk_part, dv_part)


def key_block(
    query_heads, grad_heads, correction, query_labels, skip_empty, dq_total, block_inputs
):
    key_part, value_part, label_part, block_flag = block_inputs
    row_count = query_heads.shape[0]
    allowed = (query_labels[:, None] == label_part[None, :]) & (block_flag == 1)
    dq_part, dk_part, dv_part = pair_gradients(
        query_heads, grad_heads, correction, key_part, value_part, allowed
    )
    flat_terms = (dk_part.reshape(row_count, -1), dv_part.reshape(row_count, -1))
    return (dq_total + settle(dq_part), flat_terms)


def local(
    node_features,
    norm_gain,
    w_query,
    w_key,
    w_value,
    w_out,
    w_message,
    node_cluster,
    block_pattern,
    send_rows,
    send_counts,
    edge_src,
    edge_dst,
    out_grad,
):
    row_count = node_features.shape[0]
    feat_width = node_features.shape[1]
    peer_count = lax.axis_size("dom")
    block_count = lax.axis_size("blk")
    slot_count = send_rows.shape[1]
    features = node_features.astype(jnp.float32)
    normed_f, norm_pull = jax.vjp(rms_norm, features, norm_gain)
    normed = normed_f.astype(jnp.bfloat16)
    live_slots = jnp.arange(slot_count, dtype=jnp.int32)[None, :] < send_counts[:, None]
    outgoing = jnp.where(live_slots[:, :, None], normed[send_rows], jnp.zeros((), jnp.bfloat16))
    incoming = lax.all_to_all(outgoing, "dom", split_axis=0, concat_axis=0, tiled=True)
    query_f, query_pull = jax.vjp(
        head_norm, jnp.dot(normed, w_query, preferred_element_type=jnp.float32)
    )
    key_f, key_pull = jax.vjp(head_norm, jnp.dot(normed, w_key, preferred_element_type=jnp.float32))
    queries = query_f.astype(jnp.bfloat16)
    key_flat = key_f.astype(jnp.bfloat16)
    value_flat = jnp.dot(normed, w_value, preferred_element_type=jnp.float32).astype(jnp.bfloat16)
    query_heads = queries.reshape(row_count, HEADS, HEAD_DIM)
    pattern_row = block_pattern[0]
    start_state = (
        jnp.zeros((row_count, HEADS, HEAD_DIM), jnp.float32),
        jnp.zeros((row_count, HEADS), jnp.float32),
    )
    fold_step = partial(
        attend_piece,
        query_heads=query_heads,
        query_labels=node_cluster,
        pattern_row=pattern_row,
        skip_empty=False,
    )
    key_set = None
    key_set = (
        lax.all_gather(key_flat, "blk", axis=0, tiled=True),
        lax.all_gather(value_flat, "blk", axis=0, tiled=True),
        lax.all_gather(node_cluster, "blk", axis=0, tiled=True),
    )
    numer, denom = fold_step(start_state, key_set, 0)
    slot_table = incoming.reshape(peer_count * slot_count, feat_width)
    pair_index = edge_src * row_count + edge_dst
    edge_counts = jnp.zeros((peer_count * slot_count * row_count,), jnp.int32).at[pair_index].add(1)
    edge_counts = edge_counts.reshape(peer_count * slot_count, row_count).astype(jnp.bfloat16)
    degree = jnp.maximum(
        jax.ops.segment_sum(jnp.ones(edge_dst.shape, jnp.float32), edge_dst, row_count), 1.0
    )
    neighbour_sum = jnp.einsum(
        "sr,sd->rd", edge_counts, slot_table, preferred_element_type=jnp.float32
    )
    mean_rows = (neighbour_sum / degree[:, None]).astype(jnp.bfloat16)
    local_term = jnp.dot(mean_rows, w_message, preferred_element_type=jnp.float32)
    attn_heads = (numer / denom[..., None]).astype(jnp.bfloat16)
    attn_rows = attn_heads.reshape(row_count, feat_width)
    attn_proj = jnp.dot(attn_rows, w_out, preferred_element_type=jnp.float32)
    layer_out = (features + local_term + attn_proj).astype(jnp.bfloat16)
    grad_attn = jnp.einsum(
        "rd,ed->re", out_grad, w_out, preferred_element_type=jnp.float32
    ).reshape(row_count, HEADS, HEAD_DIM)
    grad_heads = (grad_attn / denom[..., None]).astype(jnp.bfloat16)
    correction = jnp.sum(grad_attn * attn_heads.astype(jnp.float32), axis=-1) / denom
    key_rows, value_rows, key_labels = key_set
    block_inputs = (
        key_rows.reshape(block_count, row_count, HEADS, HEAD_DIM),
        value_rows.reshape(block_count, row_count, HEADS, HEAD_DIM),
        key_labels.reshape(block_count, row_count),
        pattern_row,
    )
    block_step = partial(key_block, query_heads, grad_heads, correction, node_cluster, False)
    dq_heads, (key_terms, value_terms) = lax.scan(
        block_step, jnp.zeros((row_count, HEADS, HEAD_DIM), jnp.float32), block_inputs
    )
    key_grad, value_grad = (
        lax.psum_scatter(
            key_terms.reshape(block_count * row_count, feat_width).astype(jnp.bfloat16),
            "blk",
            scatter_dimension=0,
            tiled=True,
        ).astype(jnp.float32),
        lax.psum_scatter(
            value_terms.reshape(block_count * row_count, feat_width).astype(jnp.bfloat16),
            "blk",
            scatter_dimension=0,
            tiled=True,
        ).astype(jnp.float32),
    )
    dq_flat = dq_heads.reshape(row_count, feat_width)
    dquery = query_pull(dq_flat)[0].astype(jnp.bfloat16)
    dkey = key_pull(key_grad)[0].astype(jnp.bfloat16)
    dvalue = value_grad.astype(jnp.bfloat16)
    dmessage = (
        jnp.einsum("rd,ed->re", out_grad, w_message, preferred_element_type=jnp.float32)
        / degree[:, None]
    ).astype(jnp.bfloat16)
    slot_grads = jnp.dot(edge_counts, dmessage, preferred_element_type=jnp.float32).astype(
        jnp.bfloat16
    )
    returned = lax.all_to_all(
        slot_grads.reshape(peer_count, slot_count, feat_width),
        "dom",
        split_axis=0,
        concat_axis=0,
        tiled=True,
    )
    returned = jnp.where(live_slots[:, :, None], returned.astype(jnp.float32), 0.0)
    halo_grad = jax.ops.segment_sum(
        returned.reshape(peer_count * slot_count, feat_width), send_rows.reshape(-1), row_count
    )
    dnormed = jnp.einsum("rd,ed->re", dquery, w_query, preferred_element_type=jnp.float32)
    dnormed = dnormed + jnp.einsum("rd,ed->re", dkey, w_key, preferred_element_type=jnp.float32)
    dnormed = dnormed + jnp.einsum("rd,ed->re", dvalue, w_value, preferred_element_type=jnp.float32)
    dnormed = dnormed + halo_grad
    dfeatures, gain_term = norm_pull(dnormed)
    feature_grad = (out_grad.astype(jnp.float32) + dfeatures).astype(jnp.bfloat16)
    weight_terms = jnp.stack(
        [
            jnp.einsum("rd,re->de", normed, dquery, preferred_element_type=jnp.float32),
            jnp.einsum("rd,re->de", normed, dkey, preferred_element_type=jnp.float32),
            jnp.einsum("rd,re->de", normed, dvalue, preferred_element_type=jnp.float32),
            jnp.einsum("rd,re->de", attn_rows, out_grad, preferred_element_type=jnp.float32),
            jnp.einsum("rd,re->de", mean_rows, out_grad, preferred_element_type=jnp.float32),
        ]
    )
    weight_sums, gain_sum = lax.psum((weight_terms, gain_term), ("dom", "blk"))
    return (layer_out, feature_grad, weight_sums, gain_sum)


def solution(mesh):
    placed = (
        P(("dom", "blk"), None),
        P(),
        P(),
        P(),
        P(),
        P(),
        P(),
        P(("dom", "blk")),
        P(("dom", "blk"), None),
        P(("dom", "blk"), None),
        P(("dom", "blk")),
        P(("dom", "blk")),
        P(("dom", "blk")),
        P(("dom", "blk"), None),
    )
    return jax.shard_map(
        local,
        mesh=mesh,
        in_specs=placed,
        out_specs=(P(("dom", "blk"), None), P(("dom", "blk"), None), P(), P()),
        check_vma=False,
    )
```

profile of v0, /device:TPU:1, one launch (start us, length us, event | category | flops | bytes accessed | tf_op | source)
XLA Modules:
  0.0 467.6 jit_solution(4525256311109926087)
XLA Ops:
  15.0 2.1 copy.152
  18.3 13.1 %all-gather = s32[8,1,256]{2,1,0:T(1,128)S(1)} all-gather(s32[1,1,256]{2,1,0:T(1,128)S(1)} %bitcast.258), channel_id=1, replica_groups=mesh['dom'=16,'blk'=8] {'blk'}, dimensions={0}, use_global_device_ids=true | all-gather | bytes 9216 | tf_op jit(solution)/shard_map/all_gather | solution.py:159
  31.7 1.5 compare_and_fusion.1
  33.6 7.9 %all-gather.6.cloned.1.call-done = bf16[2048,512]{1,0:T(8,128)(2,1)} async-done(((bf16[256,512]{1,0:T(8,128)(2,1)}), bf16[2048,512]{1,0:T(8,128)(2,1)}) %all-gather.6.cloned.1.call-update) | async-done | bytes 2097168 | tf_op jit(solution)/shard_map/all_gather | solution.py:157
  41.5 2.5 fusion.54
  43.9 1.8 copy.156
  45.7 23.3 %all-gather.4.cloned.1.call-done = bf16[2048,512]{1,0:T(8,128)(2,1)} async-done(((bf16[256,512]{1,0:T(8,128)(2,1)}), bf16[2048,512]{1,0:T(8,128)(2,1)}) %all-gather.4.cloned.1.call-update) | async-done | bytes 2097168 | tf_op jit(solution)/shard_map/all_gather | solution.py:158
  69.0 2.8 fusion.55
  71.9 1.8 copy.150
  83.3 1.8 copy.174
  85.1 1.8 copy.173
  86.9 1.8 copy.177
  88.7 1.8 copy.176
  90.5 1.8 fusion.64
  101.9 6.1 %reshape.794 = bf16[8,256,8,64]{3,2,1,0:T(8,128)(2,1)} reshape(bf16[2048,512]{1,0:T(8,128)(2,1)} %all-gather.6.cloned.1.call-done) | data formatting | bytes 4194304 | tf_op jit(solution)/shard_map/reshape | solution.py:185
  108.0 5.1 %copy.182 = bf16[8,256,8,64]{1,3,2,0:T(8,128)(2,1)} copy(bf16[8,256,8,64]{3,2,1,0:T(8,128)(2,1)} %reshape.794) | data formatting | bytes 4194304
  113.1 6.1 %reshape.795 = bf16[8,256,8,64]{3,2,1,0:T(8,128)(2,1)} reshape(bf16[2048,512]{1,0:T(8,128)(2,1)} %all-gather.4.cloned.1.call-done) | data formatting | bytes 4194304 | tf_op jit(solution)/shard_map/reshape | solution.py:186
  119.3 5.1 %copy.183 = bf16[8,256,8,64]{1,3,2,0:T(8,128)(2,1)} copy(bf16[8,256,8,64]{3,2,1,0:T(8,128)(2,1)} %reshape.795) | data formatting | bytes 4194304
  124.4 67.0 %while.17 = (s32[]{:T(128)}, f32[256,8,64]{0,2,1:T(8,128)S(1)}, bf16[8,256,512]{1,2,0:T(8,128)(2,1)}, bf16[8,256,512]{2,1,0:T(8,128)(2,1)}, bf16[8,256,8,64]{1,3...) while((s32[]{:T(128)}, f32[256,8,64]{0,2,1:T(8,128)S(1)}, ...), condition=%wide.region_23.24_spmd.clone, body=%wide.region_22.23_spmd.clone.sunk | while | flops 340262912 | bytes 15088305 | solution.py:191
  125.8 1.6 bitcast_select_fusion.2
  134.1 1.6 bitcast_select_fusion.2
  142.5 1.6 bitcast_select_fusion.2
  150.9 1.6 bitcast_select_fusion.2
  159.2 1.6 bitcast_select_fusion.2
  167.6 1.6 bitcast_select_fusion.2
  176.0 1.6 bitcast_select_fusion.2
  184.4 1.6 bitcast_select_fusion.2
  191.4 4.0 copy.184
  196.1 7.5 %gather_fusion = bf16[2048,512]{1,0:T(8,128)(2,1)S(1)} fusion(bf16[256,512]{1,0:T(8,128)(2,1)S(1)} %fusion.38, s32[2048]{0:T(1024)S(1)} %fusion.48), kind=kCustom, calls=%fused_computation | custom fusion | bytes 4202496 | tf_op jit(solution)/shard_map/gather | solution.py:133
  203.7 1.5 broadcast_select_fusion
  205.2 6.6 %all-to-all-start = ((bf16[16,128,512]{2,1,0:T(8,128)(2,1)}), bf16[16,128,512]{2,1,0:T(8,128)(2,1)}, u32[]{:S(2)}, u32[]{:S(2)}) async-start(bf16[16,128,512]{2,1,0:T(8,128)(2,1)} %broadcast_select_fusion), calls=%async_computation | async-start | bytes 4194304 | tf_op jit(solution)/shard_map/all_to_all | solution.py:134
  212.6 22.4 %scatter_custom_fusion = s32[524288]{0:T(1024)S(1)} fusion(s32[4096]{0:T(1024)S(1)} %compare_select_fusion, s32[4096]{0:T(1024)S(1)} %broadcast.736, s32[]{:T(128)} %constant.148.clone.1), kind=kCustom, calls=%fused_computation.77 | custom fusion | flops 4096 | bytes 2097156 | tf_op jit(solution)/shard_map/scatter-add | solution.py:164
  236.1 1.5 convert_element_type.131
  237.6 28.8 %scatter_custom_fusion.1 = f32[256]{0:T(256)S(1)} fusion(s32[4096]{0:T(1024)S(1)} %copy-done.48, f32[4096]{0:T(1024)S(1)} %broadcast.737, f32[]{:T(128)} %constant.152.clone.1), kind=kCustom, calls=%fused_computation.188 | custom fusion | flops 4096 | bytes 1028 | tf_op jit(solution)/shard_map/scatter-add | solution.py:167
  266.4 2.4 convolution_convert_fusion
  268.8 6.6 %all-to-all-start.1 = ((bf16[16,128,512]{2,1,0:T(8,128)(2,1)}), bf16[16,128,512]{2,1,0:T(8,128)(2,1)S(1)}, u32[]{:S(2)}, u32[]{:S(2)}) async-start(bf16[16,128,512]{2,1,0:T(8,128)(2,1)} %bitcast.233), calls=%async_computation.3 | async-start | bytes 4194304 | tf_op jit(solution)/shard_map/all_to_all | solution.py:219
  275.4 3.4 fusion.21
  281.1 2.0 convert_multiply_fusion.4
  283.1 2.1 copy.186
  287.1 2.0 copy.187
  289.2 1.5 fusion.41
  292.7 2.3 fusion.16
  299.7 2.5 all-to-all-done.1
  302.2 2.5 convert_select_fusion
  306.9 13.5 %scatter_fusion = f32[256,512]{1,0:T(8,128)S(1)} fusion(f32[256,512]{1,0:T(8,128)S(1)} %convolution_add_fusion.7, s32[2048]{0:T(1024)S(1)} %bitcast.259, f32[2048,512]{1,0:T(8,128)} %bitcast.218), kind=kCustom, calls=%fused_computation.3 | custom fusion | flops 1048576 | bytes 12591104 | tf_op jit(solution)/shard_map/scatter-add | solution.py:227
  320.6 65.8 %psum.15 = f32[512]{0:T(512)} all-reduce(f32[512]{0:T(512)S(1)} %get-tuple-element.245), channel_id=1, replica_groups=mesh['dom'=16,'blk'=8] {'dom','blk'}, use_global_device_ids=true, to_apply=%region_32.33 | all-reduce | flops 512 | bytes 4096 | tf_op jit(solution)/shard_map/psum | solution.py:245
  387.3 67.9 %all-reduce.2.cloned.1.call-done = f32[5,512,512]{2,1,0:T(8,128)} async-done(((f32[5,512,512]{2,1,0:T(8,128)}), f32[5,512,512]{2,1,0:T(8,128)}) %all-reduce.2.cloned.1.call-update) | async-done | bytes 5242896 | tf_op jit(solution)/shard_map/psum | solution.py:245
  455.3 5.8 %copy.248 = f32[5,512,512]{2,1,0:T(8,128)} copy(f32[5,512,512]{2,1,0:T(8,128)} %all-reduce.2.cloned.1.call-done) | data formatting | bytes 10485760
  (293 shorter events, 93.4 us)
Async XLA Ops:
  7.2 259.2 %copy-start = (bf16[512,512]{1,0:T(8,128)(2,1)S(1)}, bf16[512,512]{1,0:T(8,128)(2,1)}, u32[]{:S(2)}) copy-start(bf16[512,512]{1,0:T(8,128)(2,1)} %param.22) | copy-start | bytes 1572868
  7.2 34.3 %all-gather.6.cloned.1.call-start = ((), (), s32[]{:S(2)}) async-start(), calls=%async_computation.5 | async-start | bytes 2359296 | tf_op jit(solution)/shard_map/all_gather | solution.py:157
  10.8 1.5 copy-start.1
  11.0 1.3 copy-start.19
  11.1 2.3 copy-start.21
  11.4 2.1 copy-start.6
  12.3 56.8 %all-gather.4.cloned.1.call-start = ((), (), s32[]{:S(2)}) async-start(), calls=%async_computation.4 | async-start | bytes 2359296 | tf_op jit(solution)/shard_map/all_gather | solution.py:158
  13.4 267.7 %reduce-scatter.3.cloned.1.call-start = ((), (), s32[]{:S(2)}) async-start(), calls=%async_computation.6 | async-start | bytes 2359296 | tf_op jit(solution)/shard_map/reduce_scatter | solution.py:195
  14.0 3.1 copy-start.3
  14.0 4.3 copy-start.44
  14.0 17.5 %copy-start.49 = (s32[1,8]{1,0:T(1,128)S(1)}, s32[1,8]{1,0:T(1,128)}, u32[]{:S(2)}) copy-start(s32[1,8]{1,0:T(1,128)} %param.24) | copy-start | bytes 100
  14.1 19.2 %copy-start.7 = (bf16[256,512]{1,0:T(8,128)(2,1)S(1)}, bf16[256,512]{1,0:T(8,128)(2,1)}, u32[]{:S(2)}) copy-start(bf16[256,512]{1,0:T(8,128)(2,1)} %param.29) | copy-start | bytes 786436
  14.1 19.2 %copy-start.17 = (bf16[512,512]{1,0:T(8,128)(2,1)S(1)}, bf16[512,512]{1,0:T(8,128)(2,1)}, u32[]{:S(2)}) copy-start(bf16[512,512]{1,0:T(8,128)(2,1)} %param.21) | copy-start | bytes 1572868
  90.5 1.8 copy-start.24
  90.5 2.1 copy-start.37
  90.5 2.1 copy-start.43
  93.4 1.0 copy-start.35
  93.4 1.0 copy-start.41
  94.3 1.0 copy-start.34
  94.3 1.0 copy-start.40
  95.1 1.0 copy-start.33
  95.2 1.0 copy-start.39
  96.0 1.0 copy-start.32
  96.9 1.0 copy-start.31
  99.8 1.0 copy-start.30
  196.1 7.5 %copy-start.50 = (s32[16]{0:T(128)S(1)}, s32[16]{0:T(128)}, u32[]{:S(2)}) copy-start(s32[16]{0:T(128)} %param.26) | copy-start | bytes 196
  205.2 63.5 %all-to-all-start = ((bf16[16,128,512]{2,1,0:T(8,128)(2,1)}), bf16[16,128,512]{2,1,0:T(8,128)(2,1)}, u32[]{:S(2)}, u32[]{:S(2)}) async-start(bf16[16,128,512]{2,1,0:T(8,128)(2,1)} %broadcast_select_fusion), calls=%async_computation | async-start | bytes 4194304 | tf_op jit(solution)/shard_map/all_to_all | solution.py:134
  211.8 80.8 %reduce-scatter.5.cloned.1.call-start = ((), (), s32[]{:S(2)}) async-start(), calls=%async_computation.7 | async-start | bytes 2359296 | tf_op jit(solution)/shard_map/reduce_scatter | solution.py:201
  236.1 30.3 %copy-start.8 = (bf16[256,512]{1,0:T(8,128)(2,1)S(1)}, bf16[256,512]{1,0:T(8,128)(2,1)}, u32[]{:S(2)}) copy-start(bf16[256,512]{1,0:T(8,128)(2,1)} %param.29) | copy-start | bytes 786436
  237.5 31.2 %copy-start.25 = (bf16[2048,256]{1,0:T(8,128)(2,1)}, bf16[2048,256]{1,0:T(8,128)(2,1)S(1)}, u32[]{:S(2)}) copy-start(bf16[2048,256]{1,0:T(8,128)(2,1)S(1)} %convert_element_type.131) | copy-start | bytes 3145732
  268.8 33.4 %all-to-all-start.1 = ((bf16[16,128,512]{2,1,0:T(8,128)(2,1)}), bf16[16,128,512]{2,1,0:T(8,128)(2,1)S(1)}, u32[]{:S(2)}, u32[]{:S(2)}) async-start(bf16[16,128,512]{2,1,0:T(8,128)(2,1)} %bitcast.233), calls=%async_computation.3 | async-start | bytes 4194304 | tf_op jit(solution)/shard_map/all_to_all | solution.py:219
  275.4 179.9 %all-reduce.2.cloned.1.call-start = ((), (), s32[]{:S(2)}) async-start(), calls=%async_computation.8 | async-start | bytes 10485760 | tf_op jit(solution)/shard_map/psum | solution.py:245
  275.4 3.4 copy-start.4
  281.1 8.1 %copy-start.2 = (f32[256,512]{1,0:T(8,128)S(1)}, f32[256,512]{1,0:T(8,128)}, u32[]{:S(2)}) copy-start(f32[256,512]{1,0:T(8,128)} %copy-done.1) | copy-start | bytes 1572868
  291.4 3.6 copy-start.9
  291.4 3.6 copy-start.27
  292.7 3.6 copy-start.28
  297.5 1.0 copy-start.29
  299.7 5.1 %copy-start.12 = (bf16[256,8,64]{0,2,1:T(8,128)(2,1)S(1)}, bf16[256,8,64]{0,2,1:T(8,128)(2,1)}, u32[]{:S(2)}) copy-start(bf16[256,8,64]{0,2,1:T(8,128)(2,1)} %copy-done.11) | copy-start | bytes 786436
  302.2 2.5 copy-start.22
  302.2 2.9 copy-start.16
  302.2 2.9 copy-start.18
  304.7 1.4 copy-start.14
  304.7 1.4 copy-start.15
  304.7 1.8 copy-start.20
  304.7 1.8 copy-start.26
  306.9 13.6 %copy-start.46 = (f32[512]{0:T(512)S(1)}, f32[512]{0:T(512)}, u32[]{:S(2)}) copy-start(f32[512]{0:T(512)} %param.17) | copy-start | bytes 6148
  306.9 79.6 %copy-start.10 = (bf16[256,512]{1,0:T(8,128)(2,1)S(1)}, bf16[256,512]{1,0:T(8,128)(2,1)}, u32[]{:S(2)}) copy-start(bf16[256,512]{1,0:T(8,128)(2,1)} %param.29) | copy-start | bytes 786436
  (10 other events, 8.3 us)
Sparse Core Ops, SparseCore 0:
  12.4 29.0 all-gather.5
  43.2 25.8 all-gather.3
  195.5 30.9 reduce-scatter.2
  228.8 32.8 reduce-scatter.4
  297.7 157.5 all-reduce.1
where the time goes:
time: 470 us; the launch traced here: 468 us
  waiting for transfers between devices  102 us (22%)
  local copies, waits for them, and re-layouts  97.6 us (21%)
  other arithmetic  84.2 us (18%)
  blocking collectives  78.9 us (17%)
  matrix products  70.8 us (15%)
  between operations  14.7 us (3%)
  starting transfers between devices  13.4 us (3%)
  loops' own time  5.81 us (1%)
    psum x1, waiting for transfers between devices, local(): weight_sums, gain_sum = lax.psum((weight_terms, gain_term), ('dom', 'blk'))  67.9 us
    psum x1, blocking collectives, local(): weight_sums, gain_sum = lax.psum((weight_terms, gain_term), ('dom', 'blk'))  65.8 us
    scatter-add x1, other arithmetic, local(): jax.ops.segment_sum(jnp.ones(edge_dst.shape, jnp.float32), edge_dst, row_...  28.8 us
    all_gather x1, waiting for transfers between devices, local(): lax.all_gather(value_flat, 'blk', axis=0, tiled=True)  23.3 us
    scatter-add x1, other arithmetic, local(): jnp.zeros((peer_count * slot_count * row_count,), jnp.int32).at[pair_index]  22.4 us
    unnamed x106, local copies, waits for them, and re-layouts  20.3 us
    dot_general x16, matrix products, block_weights(): jnp.einsum('rhe,khe->hrk', query_heads, key_heads, preferred_element_type...  19.7 us
    slice x9, local copies, waits for them, and re-layouts, attend_piece(): value_rows[first_row:last_row].reshape(part_rows, HEADS, HEAD_DIM)  13.6 us
  transfers between devices with their start and end apart: 7, of which 4 were waited for; matrix products, arithmetic and copies ran while one was open for 25% of the time, Pallas kernels for 0%

commit v1 on v0

v1 whole, which is shorter than its diff:
```python
import math

import jax
import jax.numpy as jnp
from jax import lax
from jax.experimental import pallas as pl
from jax.experimental.pallas import tpu as pltpu
from jax.sharding import PartitionSpec as P

F32 = jnp.float32
BF16 = jnp.bfloat16
EPS = 1e-06
D = 512
ROWS = 256
HEAD = 64
BLK = 8
DOM = 16
CAP = 128
SLOTS = DOM * CAP
EDGES = 4096
PAY = ROWS + 16
LOG2E = math.log2(math.e)
SCORE_MUL = LOG2E / 8.0
SCORE_SUB = (8.0 + 128.0) * LOG2E

NT = (((1,), (1,)), ((), ()))
NN = (((1,), (0,)), ((), ()))


def dot(a, b, dims=NN):
    return lax.dot_general(a, b, dims, preferred_element_type=F32)


def call(body, out_shape, scratch=(), smem=0, n_in=0):
    specs = [pl.BlockSpec(memory_space=pltpu.SMEM)] * smem + [pl.BlockSpec(memory_space=pltpu.VMEM)] * n_in
    return pl.pallas_call(
        body,
        out_shape=out_shape,
        in_specs=specs,
        out_specs=jax.tree.map(lambda _: pl.BlockSpec(memory_space=pltpu.VMEM), out_shape),
        scratch_shapes=list(scratch),
    )


def shape(dims, dtype):
    return jax.ShapeDtypeStruct(dims, dtype)


def norm_body(x_ref, gain_ref, label_ref, pattern_ref, out_ref):
    x = x_ref[...].astype(F32)
    scale = lax.rsqrt(jnp.mean(x * x, axis=-1, keepdims=True) + EPS)
    out_ref[0:ROWS, :] = (x * scale * gain_ref[...]).astype(BF16)
    row = lax.broadcasted_iota(jnp.int32, (16, ROWS), 0)
    labels = jnp.broadcast_to(label_ref[...].astype(F32), (16, ROWS))
    pattern = jnp.broadcast_to(pattern_ref[...].astype(F32), (16, ROWS))
    tail = jnp.where(row == 0, labels, jnp.where(row == 1, pattern, 0.0))
    out_ref[ROWS:PAY, 0:ROWS] = tail.astype(BF16)
    out_ref[ROWS:PAY, ROWS:D] = jnp.zeros((16, D - ROWS), BF16)


def outgoing_body(counts_ref, pay_ref, rows_ref, out_ref):
    normed = pay_ref[0:ROWS, :]
    columns = jnp.transpose(rows_ref[...].astype(F32))
    lane = lax.broadcasted_iota(jnp.int32, (CAP, ROWS), 1).astype(F32)
    slot = lax.broadcasted_iota(jnp.int32, (CAP, ROWS), 0)
    for p in range(DOM):
        hit = (lane == columns[:, p : p + 1]) & (slot < counts_ref[p])
        out_ref[p] = dot(jnp.where(hit, 1.0, 0.0).astype(BF16), normed).astype(BF16)


E_STEP = 512


def edges_body(src_ref, dst_ref, grad_ref, w_ref, counts_t_ref, degree_ref, slots_ref, acc_ref):
    low_row = lax.broadcasted_iota(jnp.int32, (512, E_STEP), 0)
    high_row = lax.broadcasted_iota(jnp.int32, (1024, E_STEP), 0)
    for step in range(EDGES // E_STEP):
        src = src_ref[step : step + 1, :]
        dst = dst_ref[step : step + 1, :]
        low = jnp.where(low_row == (src & 511), 1.0, 0.0).astype(BF16)
        high = jnp.where(high_row == ((src >> 9) * 256 + dst), 1.0, 0.0).astype(BF16)
        part = dot(low, high, NT)
        if step == 0:
            acc_ref[...] = part
        else:
            acc_ref[...] += part
    counts = acc_ref[...]
    per_row = jnp.sum(counts, axis=0, keepdims=True)
    per_row = per_row[:, 0:256] + per_row[:, 256:512] + per_row[:, 512:768] + per_row[:, 768:1024]
    degree = jnp.transpose(jnp.broadcast_to(jnp.maximum(per_row, 1.0), (128, ROWS)))
    degree_ref[...] = degree
    counts_t_ref[...] = jnp.transpose(counts).astype(BF16)
    counts = counts.astype(BF16)
    inverse = 1.0 / degree[:, 0:1]
    message = (dot(grad_ref[...], w_ref[...], NT) * inverse).astype(BF16)
    for high in range(4):
        part = dot(counts[:, high * 256 : (high + 1) * 256], message).astype(BF16)
        for k in range(4):
            slots_ref[high * 4 + k] = part[k * CAP : (k + 1) * CAP, :]


def mean_body(own_ref, counts_t_ref, degree_ref, table_ref, x_ref, w_ref, mine_ref, other_ref, base_ref, means_ref):
    total = jnp.zeros((ROWS, D), F32)
    for high in range(4):
        table = jnp.concatenate([table_ref[high * 4 + k] for k in range(4)], axis=0)
        total = total + dot(counts_t_ref[high * 256 : (high + 1) * 256, :], table)
    mean = total / degree_ref[:, 0:1]
    mean_rows = mean.astype(BF16)
    base_ref[...] = x_ref[...].astype(F32) + dot(mean_rows, w_ref[...])
    turned = jnp.transpose(mean_rows.astype(F32)).astype(BF16)
    for h in range(BLK):
        means_ref[h] = turned[h * HEAD : (h + 1) * HEAD, :]
    z, core = own_ref[0], own_ref[1]
    for dz in range(4):
        chip = ((z + dz) & 3) * 2
        mine_ref[dz] = means_ref[chip + core]
        other_ref[dz] = means_ref[chip + (1 - core)]


def attention_body(
    source_ref, na_ref, nb_ref, ga_ref, gb_ref, wqkv_ref, wo_ref,
    paya_ref, payb_ref, dw_ref,
    y_ref, s_ref, qaug_ref, kaug_ref, vaug_ref, kt_ref, vt_ref, w_ref, num_ref, dqt_ref, dq_ref, dk_ref, dv_ref, at_ref, gat_ref,
):
    lane = lax.broadcasted_iota(jnp.int32, (ROWS, 128), 1)
    left = lane < HEAD
    bits = []

    for r in range(BLK):
        n_ref, g_ref = (na_ref, ga_ref) if r < 4 else (nb_ref, gb_ref)
        part = n_ref[r % 4]
        normed = part[0:ROWS, :]
        tail = part[ROWS:PAY, :].astype(F32)
        projected = dot(normed, wqkv_ref[...])
        qk = projected[:, 0:128]
        square = qk * qk
        scale_q = lax.rsqrt(jnp.sum(jnp.where(left, square, 0.0), axis=-1, keepdims=True) * (1.0 / HEAD) + EPS)
        scale_k = lax.rsqrt(jnp.sum(jnp.where(left, 0.0, square), axis=-1, keepdims=True) * (1.0 / HEAD) + EPS)
        scale = jnp.where(left, scale_q, scale_k)
        y = qk * scale
        y_ref[r] = y
        s_ref[r] = scale
        label = jnp.transpose(jnp.broadcast_to(tail[0:1, 0:ROWS], (8, ROWS)))[:, 0:1]
        one_hot = jnp.where((lane - HEAD).astype(F32) == label, 32.0, 0.0)
        qaug_ref[r] = jnp.where(left, y, one_hot).astype(BF16)
        turned = pltpu.roll(y, HEAD, 1)
        kaug_ref[r] = jnp.where(left, turned, one_hot).astype(BF16)
        kt_ref[r] = jnp.transpose(turned)[0:HEAD, :].astype(BF16)
        value = jnp.where(left, projected[:, 128:256], jnp.where(lane < HEAD + 2, 1.0, 0.0))
        vaug_ref[r] = value.astype(BF16)
        vt_ref[r] = jnp.transpose(value).astype(BF16)
        gat_ref[r] = dot(wo_ref[...], g_ref[r % 4], NT)
        flags = jnp.where(tail[1:2, 0:128] == 1.0, 1 << jnp.minimum(lane[0:1, :], 8), 0)
        bits.append(jnp.sum(flags.astype(F32)).astype(jnp.int32))
        dk_ref[r] = jnp.zeros((ROWS, 128), F32)
        dv_ref[r] = jnp.zeros((ROWS, 128), F32)

    def query_block(i, bits_i):
        num_ref[...] = jnp.zeros((128, ROWS), F32)
        dqt_ref[...] = jnp.zeros((HEAD, ROWS), F32)

        def forward(j, carry):
            @pl.when(((bits_i >> source_ref[j]) & 1) == 1)
            def _():
                scores = dot(kaug_ref[j], qaug_ref[i], NT)
                weights = jnp.exp2(scores * SCORE_MUL - SCORE_SUB).astype(BF16)
                w_ref[j] = weights
                num_ref[...] += dot(vt_ref[j], weights)
            return carry

        lax.fori_loop(0, BLK, forward, 0)
        inverse = 1.0 / num_ref[HEAD : HEAD + 1, :]
        attn = (num_ref[0:HEAD, :] * inverse).astype(BF16)
        at_ref[i] = attn
        grad_attn = gat_ref[i]
        grad = grad_attn * inverse
        minus = jnp.sum(grad_attn * attn.astype(F32), axis=0, keepdims=True) * (-inverse)
        coarse = minus.astype(BF16).astype(F32)
        row = lax.broadcasted_iota(jnp.int32, (HEAD, ROWS), 0)
        extra = jnp.where(row == 0, coarse, jnp.where(row == 1, minus - coarse, 0.0))
        grad_aug = jnp.concatenate([grad, extra], axis=0)
        grad_rows = jnp.transpose(grad_aug).astype(BF16)
        grad_aug = grad_aug.astype(BF16)

        def backward(j, carry):
            @pl.when(((bits_i >> source_ref[j]) & 1) == 1)
            def _():
                weights = w_ref[j]
                slopes = (weights.astype(F32) * dot(vaug_ref[j], grad_aug)).astype(BF16)
                dqt_ref[...] += dot(kt_ref[j], slopes)
                dk_ref[j] += dot(slopes, qaug_ref[i])
                dv_ref[j] += dot(weights, grad_rows)
            return carry

        lax.fori_loop(0, BLK, backward, 0)
        dq_ref[i] = jnp.transpose(jnp.concatenate([dqt_ref[...], dqt_ref[...]], axis=0))

    for i in range(BLK):
        query_block(i, bits[i])

    dw = jnp.zeros((192, D), F32)
    dwo = jnp.zeros((HEAD, D), F32)
    for r in range(BLK):
        n_ref, g_ref = (na_ref, ga_ref) if r < 4 else (nb_ref, gb_ref)
        pay_ref = paya_ref if r < 4 else payb_ref
        y = y_ref[r]
        grad = jnp.where(left, dq_ref[r], pltpu.roll(dk_ref[r], HEAD, 1)) * (8.0 / HEAD)
        product = y * grad
        mean_q = jnp.sum(jnp.where(left, product, 0.0), axis=-1, keepdims=True) * (1.0 / HEAD)
        mean_k = jnp.sum(jnp.where(left, 0.0, product), axis=-1, keepdims=True) * (1.0 / HEAD)
        first = (s_ref[r] * (grad - y * jnp.where(left, mean_q, mean_k))).astype(BF16)
        attn = at_ref[r].astype(F32)
        attn = jnp.transpose(jnp.concatenate([attn, attn], axis=0))
        second = jnp.where(left, dv_ref[r], attn).astype(BF16)
        pay_ref[r % 4, :, 0:128] = first
        pay_ref[r % 4, :, 128:256] = second
        first_t = jnp.transpose(first.astype(F32)).astype(BF16)
        second_t = jnp.transpose(second.astype(F32)).astype(BF16)
        dw = dw + dot(jnp.concatenate([first_t, second_t[0:HEAD]], axis=0), n_ref[r % 4, 0:ROWS, :])
        dwo = dwo + dot(second_t[HEAD:128], g_ref[r % 4])
    dw_ref[0:192, :] = dw
    dw_ref[192:256, :] = dwo


def chunks_body(m0_ref, m1_ref, m2_ref, m3_ref, ga_ref, gb_ref, dw_ref, out_ref):
    total = jnp.zeros((HEAD, D), F32)
    for dz, m_ref in enumerate((m0_ref, m1_ref, m2_ref, m3_ref)):
        total = total + dot(m_ref[0], ga_ref[dz]) + dot(m_ref[1], gb_ref[dz])
    for a in range(4):
        for b in range(4):
            out_ref[a * 4 + b, 0:64, :] = dw_ref[a * 64 : (a + 1) * 64, b * 128 : (b + 1) * 128].astype(BF16)
            out_ref[a * 4 + b, 64:80, :] = total[a * 16 : (a + 1) * 16, b * 128 : (b + 1) * 128].astype(BF16)


def chunk_sum_body(in_ref, out_ref):
    total = in_ref[0].astype(F32)
    for p in range(1, DOM):
        total = total + in_ref[p].astype(F32)
    total = total.astype(BF16)
    for p in range(DOM):
        out_ref[p] = total


def rows_body(
    own_ref, counts_ref, r0_ref, r1_ref, r2_ref, r3_ref, back_ref, rows_ref, base_ref, x_ref, gain_ref, grad_ref,
    wq_ref, wk_ref, wv_ref, wo_ref, out_ref, feature_ref, gain_grad_ref, dq_ref, dk_ref, dv_ref, at_ref,
):
    left = lax.broadcasted_iota(jnp.int32, (ROWS, 128), 1) < HEAD
    z, core = own_ref[0], own_ref[1]
    even = core == 0
    for dz, r_ref in enumerate((r0_ref, r1_ref, r2_ref, r3_ref)):
        chip = (z + dz) & 3
        one, two = r_ref[0].astype(F32), r_ref[1].astype(F32)
        low, high = jnp.where(even, one, two), jnp.where(even, two, one)
        low0, low1 = low[:, 0:128], low[:, 128:256]
        high0, high1 = high[:, 0:128], high[:, 128:256]
        dq_ref[chip] = jnp.where(left, low0, pltpu.roll(high0, HEAD, 1)).astype(BF16)
        dk_ref[chip] = jnp.where(left, pltpu.roll(low0, HEAD, 1), high0).astype(BF16)
        dv_ref[chip] = jnp.where(left, low1, pltpu.roll(high1, HEAD, 1)).astype(BF16)
        at_ref[chip] = jnp.where(left, pltpu.roll(low1, HEAD, 1), high1).astype(BF16)

    def whole(ref):
        return jnp.concatenate([ref[m] for m in range(4)], axis=1)

    out_ref[...] = (base_ref[...] + dot(whole(at_ref), wo_ref[...])).astype(BF16)
    dnormed = dot(whole(dq_ref), wq_ref[...], NT) + dot(whole(dk_ref), wk_ref[...], NT)
    dnormed = dnormed + dot(whole(dv_ref), wv_ref[...], NT)
    row = lax.broadcasted_iota(jnp.int32, (ROWS, CAP), 0)
    slot = lax.broadcasted_iota(jnp.int32, (ROWS, CAP), 1)
    for k in range(4):
        hits = []
        for p in range(4 * k, 4 * k + 4):
            hit = (row == rows_ref[p : p + 1, :]) & (slot < counts_ref[p])
            hits.append(jnp.where(hit, 1.0, 0.0).astype(BF16))
        part = jnp.concatenate([back_ref[p] for p in range(4 * k, 4 * k + 4)], axis=0)
        dnormed = dnormed + dot(jnp.concatenate(hits, axis=1), part)
    x = x_ref[...].astype(F32)
    scale = lax.rsqrt(jnp.mean(x * x, axis=-1, keepdims=True) + EPS)
    gain_grad_ref[...] = jnp.sum(dnormed * (x * scale), axis=0, keepdims=True)
    scaled = dnormed * gain_ref[...]
    inner = jnp.mean(scaled * x, axis=-1, keepdims=True)
    dx = scale * scaled - x * (scale * scale * scale * inner)
    feature_ref[...] = (grad_ref[...].astype(F32) + dx).astype(BF16)


def weights_body(in_ref, out_ref):
    which = pl.program_id(0)
    for t in range(3):
        @pl.when(which == t)
        def _():
            for b in range(4):
                part = jnp.concatenate([in_ref[h, t * 4 + b, 0:64, :].astype(F32) for h in range(BLK)], axis=0)
                out_ref[0, b * 128 : (b + 1) * 128, :] = jnp.transpose(part)

    @pl.when(which == 3)
    def _():
        for h in range(BLK):
            for b in range(4):
                out_ref[0, h * 64 : (h + 1) * 64, b * 128 : (b + 1) * 128] = in_ref[h, 12 + b, 0:64, :].astype(F32)

    @pl.when(which == 4)
    def _():
        for h in range(BLK):
            for a in range(4):
                for b in range(4):
                    top = h * 64 + a * 16
                    out_ref[0, top : top + 16, b * 128 : (b + 1) * 128] = in_ref[h, a * 4 + b, 64:80, :].astype(F32)


def chip_shift(step, swap):
    return [(z * 2 + c, ((z + step) % 4) * 2 + (c ^ swap)) for z in range(4) for c in range(2)]


def along_chips(array, step):
    return lax.ppermute(array, "blk", chip_shift(step, 0))


def other_core(array):
    return lax.ppermute(array, "blk", chip_shift(0, 1))


def gather_blocks(block):
    mine = jnp.stack([block] + [along_chips(block, step) for step in (1, 2, 3)])
    return mine, other_core(mine)


def local(
    x, gain, wq, wk, wv, wo, wm, cluster, pattern, send_rows, send_counts, edge_src, edge_dst, out_grad
):
    me = lax.axis_index("blk").astype(jnp.int32)
    z, core = me // 2, me % 2
    own = jnp.stack([z, core])
    r = jnp.arange(BLK, dtype=jnp.int32)
    source = ((z - r % 4) % 4) * 2 + (core ^ (r // 4))
    gain_row = gain.reshape(1, D)

    ga, gb = gather_blocks(out_grad)

    pattern_row = jnp.pad(pattern, ((0, 0), (0, ROWS - BLK)))
    pay = call(norm_body, shape((PAY, D), BF16), n_in=4)(x, gain_row, cluster.reshape(1, ROWS), pattern_row)
    na, nb = gather_blocks(pay)
    outgoing = call(outgoing_body, shape((DOM, CAP, D), BF16), smem=1, n_in=2)(send_counts, pay, send_rows)
    incoming = lax.all_to_all(outgoing, "dom", split_axis=0, concat_axis=0, tiled=True)

    counts_t, degree, slot_grads = call(
        edges_body,
        (shape((1024, 512), BF16), shape((ROWS, 128), F32), shape((DOM, CAP, D), BF16)),
        scratch=[pltpu.VMEM((512, 1024), F32)],
        n_in=4,
    )(edge_src.reshape(EDGES // E_STEP, E_STEP), edge_dst.reshape(EDGES // E_STEP, E_STEP), out_grad, wm)

    mine, other, base = call(
        mean_body,
        (shape((4, HEAD, ROWS), BF16), shape((4, HEAD, ROWS), BF16), shape((ROWS, D), F32)),
        scratch=[pltpu.VMEM((BLK, HEAD, ROWS), BF16)],
        smem=1,
        n_in=5,
    )(own, counts_t, degree, incoming, x, wm)
    back = lax.all_to_all(slot_grads, "dom", split_axis=0, concat_axis=0, tiled=True)
    other = other_core(other)
    means = [jnp.stack([mine[dz], other[dz]]) for dz in range(4)]
    means = [means[0]] + [along_chips(means[dz], dz) for dz in (1, 2, 3)]

    def head_columns(w):
        return lax.dynamic_slice(w, (0, me * HEAD), (D, HEAD))

    wqkv = jnp.concatenate(
        [head_columns(wq), head_columns(wk), head_columns(wv), jnp.zeros((D, HEAD), BF16)], axis=1
    )
    wo_head = lax.dynamic_slice(wo, (me * HEAD, 0), (HEAD, D))
    pay_a, pay_b, dw = call(
        attention_body,
        (shape((4, ROWS, 256), BF16), shape((4, ROWS, 256), BF16), shape((256, D), F32)),
        scratch=[
            pltpu.VMEM((BLK, ROWS, 128), F32),
            pltpu.VMEM((BLK, ROWS, 128), F32),
            pltpu.VMEM((BLK, ROWS, 128), BF16),
            pltpu.VMEM((BLK, ROWS, 128), BF16),
            pltpu.VMEM((BLK, ROWS, 128), BF16),
            pltpu.VMEM((BLK, HEAD, ROWS), BF16),
            pltpu.VMEM((BLK, 128, ROWS), BF16),
            pltpu.VMEM((BLK, ROWS, ROWS), BF16),
            pltpu.VMEM((128, ROWS), F32),
            pltpu.VMEM((HEAD, ROWS), F32),
            pltpu.VMEM((BLK, ROWS, 128), F32),
            pltpu.VMEM((BLK, ROWS, 128), F32),
            pltpu.VMEM((BLK, ROWS, 128), F32),
            pltpu.VMEM((BLK, HEAD, ROWS), BF16),
            pltpu.VMEM((BLK, HEAD, ROWS), F32),
        ],
        smem=1,
        n_in=6,
    )(source, na, nb, ga, gb, wqkv, wo_head)

    chunks = call(chunks_body, shape((DOM, 80, 128), BF16), n_in=7)(*means, ga, gb, dw)
    chunks = lax.all_to_all(chunks, "dom", split_axis=0, concat_axis=0, tiled=True)
    chunks = call(chunk_sum_body, shape((DOM, 80, 128), BF16), n_in=1)(chunks)
    chunks = lax.all_to_all(chunks, "dom", split_axis=0, concat_axis=0, tiled=True)
    chunks = lax.all_gather(chunks.reshape(DOM * 80, 128), "blk", axis=0, tiled=True)
    weight_grads = pl.pallas_call(
        weights_body,
        grid=(5,),
        out_shape=shape((5, D, D), F32),
        in_specs=[pl.BlockSpec((BLK, DOM, 80, 128), lambda t: (0, 0, 0, 0))],
        out_specs=pl.BlockSpec((1, D, D), lambda t: (t, 0, 0)),
    )(chunks.reshape(BLK, DOM, 80, 128))

    pay_b = other_core(pay_b)
    results = [jnp.stack([pay_a[dz], pay_b[dz]]) for dz in range(4)]
    results = [results[0]] + [along_chips(results[dz], -dz) for dz in (1, 2, 3)]
    layer_out, feature_grad, gain_part = call(
        rows_body,
        (shape((ROWS, D), BF16), shape((ROWS, D), BF16), shape((1, D), F32)),
        scratch=[pltpu.VMEM((4, ROWS, 128), BF16)] * 4,
        smem=2,
        n_in=14,
    )(own, send_counts, *results, back, send_rows, base, x, gain_row, out_grad, wq, wk, wv, wo)
    gain_parts = jnp.broadcast_to(gain_part.reshape(1, 4, 128), (DOM * BLK, 4, 128))
    gain_parts = lax.all_to_all(gain_parts, ("dom", "blk"), split_axis=0, concat_axis=0, tiled=True)
    gain_grad = jnp.sum(gain_parts, axis=0).reshape(D)
    return layer_out, feature_grad, weight_grads, gain_grad


def solution(mesh):
    both = ("dom", "blk")
    placed = (
        P(both, None), P(), P(), P(), P(), P(), P(), P(both), P(both, None), P(both, None), P(both), P(both), P(both),
        P(both, None),
    )
    return jax.shard_map(
        local,
        mesh=mesh,
        in_specs=placed,
        out_specs=(P(both, None), P(both, None), P(), P()),
        check_vma=False,
    )
```

time: 470 us -> 234 us (0.50)
  local copies, waits for them, and re-layouts: 97.6 us -> 10.4 us
  other arithmetic: 84.2 us -> 6.17 us
  Pallas kernels: 0 us -> 74.3 us
  matrix products: 70.8 us -> 0 us
  waiting for transfers between devices: 102 us -> 41.1 us
  blocking collectives: 78.9 us -> 53.4 us
  starting transfers between devices: 13.4 us -> 35.3 us
  loops' own time: 5.81 us -> 0 us
    pallas_call x0 -> x9, Pallas kernels: none -> 74.3 us  [the longest x1 42.1 us: local(): call(attention_body, (shape((4, ROWS, 256), BF16), shape((4, ROWS, 256),...]
    dot_general x72 -> x0, matrix products: 70.8 us -> none  [the longest x16 19.7 us: block_weights(): jnp.einsum('rhe,khe->hrk', query_heads, key_heads, preferred_element_type...]
    psum x1 -> x0, waiting for transfers between devices: 67.9 us -> none  [local(): weight_sums, gain_sum = lax.psum((weight_terms, gain_term), ('dom', 'blk'))]
    psum x1 -> x0, blocking collectives: 65.8 us -> none  [local(): weight_sums, gain_sum = lax.psum((weight_terms, gain_term), ('dom', 'blk'))]
    scatter-add x3 -> x0, other arithmetic: 64.7 us -> none  [the longest x1 28.8 us: local(): jax.ops.segment_sum(jnp.ones(edge_dst.shape, jnp.float32), edge_dst, row_...]
    all_to_all x0 -> x3, blocking collectives: none -> 53.4 us  [the longest x2 32.3 us: local(): lax.all_to_all(chunks, 'dom', split_axis=0, concat_axis=0, tiled=True)]
    all_gather x2 -> x1, waiting for transfers between devices: 31.2 us -> 0.01 us  [local(): lax.all_gather(chunks.reshape(DOM * 80, 128), 'blk', axis=0, tiled=True)]
    ppermute x0 -> x16, waiting for transfers between devices: none -> 26.2 us  [the longest x12 24 us: along_chips(): return lax.ppermute(array, 'blk', chip_shift(step, 0))]
  transfers between devices with their start and end apart: 7 -> 19, of which waited for: 4 -> 10; matrix products, arithmetic and copies ran while one was open for 25% -> 5% of each run, Pallas kernels for 0% -> 24%
where the time goes in v1:
time: 234 us; the launch traced here: 235 us
  Pallas kernels  74.3 us (32%)
  blocking collectives  53.4 us (23%)
  waiting for transfers between devices  41.1 us (18%)
  starting transfers between devices  35.3 us (15%)
  between operations  14.2 us (6%)
  local copies, waits for them, and re-layouts  10.4 us (4%)
  other arithmetic  6.17 us (3%)
    pallas_call x1, Pallas kernels, local(): call(attention_body, (shape((4, ROWS, 256), BF16), shape((4, ROWS, 256),...  42.1 us
    all_to_all x2, blocking collectives, local(): lax.all_to_all(chunks, 'dom', split_axis=0, concat_axis=0, tiled=True)  32.3 us
    ppermute x12, waiting for transfers between devices, along_chips(): return lax.ppermute(array, 'blk', chip_shift(step, 0))  24 us
    all_to_all x1, blocking collectives, local(): lax.all_to_all(gain_parts, ('dom', 'blk'), split_axis=0, concat_axis=0, t...  21.1 us
    all_to_all x1, waiting for transfers between devices, local(): lax.all_to_all(slot_grads, 'dom', split_axis=0, concat_axis=0, tiled=True)  14.9 us
    ppermute x12, starting transfers between devices, along_chips(): return lax.ppermute(array, 'blk', chip_shift(step, 0))  14.4 us
    ppermute x4, starting transfers between devices, other_core(): return lax.ppermute(array, 'blk', chip_shift(0, 1))  9.27 us
    pallas_call x1, Pallas kernels, local(): call(edges_body, (shape((1024, 512), BF16), shape((ROWS, 128), F32), shap...  8.13 us
  transfers between devices with their start and end apart: 19, of which 10 were waited for; matrix products, arithmetic and copies ran while one was open for 5% of the time, Pallas kernels for 24%

profile of v1, /device:TPU:1, one launch (start us, length us, event | category | flops | bytes accessed | tf_op | source)
XLA Modules:
  0.0 234.9 jit_solution(4426853758452205035)
XLA Ops:
  7.2 1.2 pad.4.pattern_ref
  8.4 1.8 shard_map.165.pay_ref
  10.2 3.2 %shard_map.168 = bf16[16,128,512]{2,1,0:T(8,128)(2,1)} custom-call(s32[16]{0:T(128)} %counts_ref.3, bf16[272,512]{1,0:T(8,128)(2,1)} %shard_map.165.pay_ref, s32[16,128]{1,0:T(8,128)} %rows_ref.3), custom_call_target="tpu_custom_call" | custom-call | tf_op jit(solution)/shard_map/pallas_call | solution.py:342
  13.4 7.7 %all-to-all-start.1 = ((bf16[16,128,512]{2,1,0:T(8,128)(2,1)}), bf16[16,128,512]{2,1,0:T(8,128)(2,1)S(1)}, u32[]{:S(2)}, u32[]{:S(2)}) async-start(bf16[16,128,512]{2,1,0:T(8,128)(2,1)} %shard_map.168), calls=%async_computation.1 | async-start | bytes 4194304 | tf_op jit(solution)/shard_map/all_to_all | solution.py:343
  21.2 3.8 %collective-permute-start.2 = (bf16[272,512]{1,0:T(8,128)(2,1)S(1)}, bf16[272,512]{1,0:T(8,128)(2,1)S(1)}, u32[]{:S(2)}, u32[]{:S(2)}) collective-permute-start(bf16[272,512]{1,0:T(8,128)(2,1)S(1)} %copy-done.3), channel_id=1, source_target_pairs={{0,6},{1,7},{2,0},{3,1},{4,2},{5,3},{6,4},{7,5},{8,14},{9,15},{10,... | collective-permute-start | bytes 835592 | tf_op jit(solution)/shard_map/ppermute | solution.py:315
  25.0 0.7 collective-permute-start
  25.7 2.0 collective-permute-start.6
  27.7 1.8 collective-permute-start.5
  29.4 5.6 %collective-permute-done.2 = bf16[272,512]{1,0:T(8,128)(2,1)S(1)} collective-permute-done((bf16[272,512]{1,0:T(8,128)(2,1)S(1)}, bf16[272,512]{1,0:T(8,128)(2,1)S(1)}, u32[]{:S(2)}, u32[]{:S(2)}) %collective-permute-start.2) | collective-permute-done | bytes 278560 | tf_op jit(solution)/shard_map/ppermute | solution.py:315
  35.1 6.2 %collective-permute-done = bf16[272,512]{1,0:T(8,128)(2,1)S(1)} collective-permute-done((bf16[272,512]{1,0:T(8,128)(2,1)S(1)}, bf16[272,512]{1,0:T(8,128)(2,1)S(1)}, u32[]{:S(2)}, u32[]{:S(2)}) %collective-permute-start) | collective-permute-done | bytes 278560 | tf_op jit(solution)/shard_map/ppermute | solution.py:315
  41.3 1.1 pad_maximum_fusion.na_ref
  42.5 4.3 %collective-permute-start.3 = (bf16[4,272,512]{2,1,0:T(8,128)(2,1)}, bf16[4,272,512]{2,1,0:T(8,128)(2,1)}, u32[]{:S(2)}, u32[]{:S(2)}) collective-permute-start(bf16[4,272,512]{2,1,0:T(8,128)(2,1)} %pad_maximum_fusion.na_ref), channel_id=1, source_target_pairs={{0,1},{1,0},{2,3},{3,2},{4,5},{5,4},{6,7},{7,6},{8,9},{9,8},{10,11... | collective-permute-start | bytes 3342344 | tf_op jit(solution)/shard_map/ppermute | solution.py:319
  47.1 4.6 %collective-permute-done.4 = bf16[256,512]{1,0:T(8,128)(2,1)S(1)} collective-permute-done((bf16[256,512]{1,0:T(8,128)(2,1)S(1)}, bf16[256,512]{1,0:T(8,128)(2,1)S(1)}, u32[]{:S(2)}, u32[]{:S(2)}) %collective-permute-start.4) | collective-permute-done | bytes 262176 | tf_op jit(solution)/shard_map/ppermute | solution.py:315
  51.8 1.1 collective-permute-start.7
  52.9 0.6 reshape.33.src_ref
  54.2 8.1 %shard_map.167 = (bf16[1024,512]{1,0:T(8,128)(2,1)}, f32[256,128]{1,0:T(8,128)}, bf16[16,128,512]{2,1,0:T(8,128)(2,1)}) custom-call(s32[8,512]{1,0:T(8,128)} %reshape.33.src_ref, s32[8,512]{1,0:T(8,128)} %reshape.34.dst_ref, bf16[256,512]{1,0:T(8,128)(2,1)} %grad_ref.3, bf16[512,512]{1,0:T(8,128)(2,1)} %w_ref.3), custom_call_target="tpu_custom_call" | custom-call | tf_op jit(solution)/shard_map/pallas_call | solution.py:345
  62.9 0.6 pad_add_fusion.own_ref
  63.5 1.5 constant_dynamic-slice_fusion.wo_ref
  65.0 1.0 constant_dynamic-slice_fusion.3
  66.0 1.1 constant_dynamic-slice_fusion.1
  67.1 0.9 maximum_maximum_fusion.wqkv_ref
  68.0 42.1 %shard_map.166 = (bf16[4,256,256]{2,1,0:T(8,128)(2,1)}, bf16[4,256,256]{2,1,0:T(8,128)(2,1)}, f32[256,512]{1,0:T(8,128)}) custom-call(s32[8]{0:T(128)} %fusion.2.source_ref, bf16[4,272,512]{2,1,0:T(8,128)(2,1)} %pad_maximum_fusion.na_ref, bf16[4,272,512]{2,1,0:T(8,128)(2,1)} %collective-permute-done.3.nb_ref, bf16[4,256,512]{2,1,0:T(8,128)(2,1)} %copy-done, ...), custom_call_target="tpu_custom_call" | custom-call | tf_op jit(solution)/shard_map/pallas_call | solution.py:371
  110.0 1.4 copy-done.2
  111.4 3.9 %shard_map.169 = (bf16[4,64,256]{2,1,0:T(8,128)(2,1)}, bf16[4,64,256]{2,1,0:T(8,128)(2,1)}, f32[256,512]{1,0:T(8,128)}) custom-call(s32[2]{0:T(128)} %pad_add_fusion.own_ref, bf16[1024,512]{1,0:T(8,128)(2,1)} %get-tuple-element.19.counts_t_ref, f32[256,128]{1,0:T(8,128)} %get-tuple-element.20.degree_ref, bf16[16,128,512]{2,1,0:T(8,128)(2,1)} %copy-done.2, ...), custom_call_target="tpu_custom_call" | custom-call | tf_op jit(solution)/shard_map/pallas_call | solution.py:352
  115.3 0.8 fusion.7
  116.1 0.7 collective-permute-done.12
  116.9 1.9 collective-permute-start.14
  118.8 1.0 collective-permute-start.15
  119.8 0.6 pad_maximum_fusion.6.m0_ref
  120.4 2.8 %collective-permute-done.13.m1_ref = bf16[2,64,256]{2,1,0:T(8,128)(2,1)S(1)} collective-permute-done((bf16[2,64,256]{2,1,0:T(8,128)(2,1)S(1)}, bf16[2,64,256]{2,1,0:T(8,128)(2,1)S(1)}, u32[]{:S(2)}, u32[]{:S(2)}) %collective-permute-start.13) | collective-permute-done | bytes 65568 | tf_op jit(solution)/shard_map/ppermute | solution.py:315
  124.0 3.0 %shard_map.171 = bf16[16,80,128]{2,1,0:T(8,128)(2,1)} custom-call(bf16[2,64,256]{2,1,0:T(8,128)(2,1)} %pad_maximum_fusion.6.m0_ref, bf16[2,64,256]{2,1,0:T(8,128)(2,1)} %copy-done.9, bf16[2,64,256]{2,1,0:T(8,128)(2,1)} %copy-done.10, bf16[2,64,256]{2,1,0:T(8,128)(2,1)} %copy-done.11, bf16[4,256,512]{2,1,0:T(8,128)(2,1)} %copy-done, ...), custom_call_target="tpu_custom_call" | custom-call | tf_op jit(solution)/shard_map/pallas_call | solution.py:395
  127.1 20.3 %all_to_all.25.in_ref = bf16[16,80,128]{2,1,0:T(8,128)(2,1)} all-to-all(bf16[16,80,128]{2,1,0:T(8,128)(2,1)} %shard_map.171), channel_id=1, replica_groups=mesh['dom'=16,'blk'=8] {'dom'}, dimensions={0} | all-to-all | bytes 655360 | tf_op jit(solution)/shard_map/all_to_all | solution.py:396
  147.4 1.7 shard_map.172
  149.1 12.0 %all_to_all.26 = bf16[16,80,128]{2,1,0:T(8,128)(2,1)} all-to-all(bf16[16,80,128]{2,1,0:T(8,128)(2,1)} %shard_map.172), channel_id=1, replica_groups=mesh['dom'=16,'blk'=8] {'dom'}, dimensions={0} | all-to-all | bytes 655360 | tf_op jit(solution)/shard_map/all_to_all | solution.py:398
  161.2 3.9 %all-to-all-start = ((bf16[16,128,512]{2,1,0:T(8,128)(2,1)}), bf16[16,128,512]{2,1,0:T(8,128)(2,1)S(1)}, u32[]{:S(2)}, u32[]{:S(2)}) async-start(bf16[16,128,512]{2,1,0:T(8,128)(2,1)} %get-tuple-element.18), calls=%async_computation | async-start | bytes 4194304 | tf_op jit(solution)/shard_map/all_to_all | solution.py:359
  165.0 3.8 %collective-permute-start.8 = (bf16[4,256,256]{2,1,0:T(8,128)(2,1)S(1)}, bf16[4,256,256]{2,1,0:T(8,128)(2,1)S(1)}, u32[]{:S(2)}, u32[]{:S(2)}) collective-permute-start(bf16[4,256,256]{2,1,0:T(8,128)(2,1)S(1)} %copy-done.14), channel_id=1, source_target_pairs={{0,1},{1,0},{2,3},{3,2},{4,5},{5,4},{6,7},{7,6},{8,9},{9,8},{10,11... | collective-permute-start | bytes 1572872 | tf_op jit(solution)/shard_map/ppermute | solution.py:319
  168.9 1.5 collective-permute-done.8
  170.4 2.6 %collective-permute-start.9 = (bf16[2,256,256]{2,1,0:T(8,128)(2,1)S(1)}, bf16[2,256,256]{2,1,0:T(8,128)(2,1)S(1)}, u32[]{:S(2)}, u32[]{:S(2)}) collective-permute-start(bf16[2,256,256]{2,1,0:T(8,128)(2,1)S(1)} %pad_maximum_fusion.3), channel_id=1, source_target_pairs={{0,6},{1,7},{2,0},{3,1},{4,2},{5,3},{6,4},{7,5},{8,14},{9,15},{10,... | collective-permute-start | bytes 786440 | tf_op jit(solution)/shard_map/ppermute | solution.py:315
  173.1 0.7 pad_maximum_fusion.5
  174.4 0.7 pad_maximum_fusion.2.r0_ref
  175.2 14.9 %all-to-all-done.back_ref = bf16[16,128,512]{2,1,0:T(8,128)(2,1)S(1)} async-done(((bf16[16,128,512]{2,1,0:T(8,128)(2,1)}), bf16[16,128,512]{2,1,0:T(8,128)(2,1)S(1)}, u32[]{:S(2)}, u32[]{:S(2)}) %all-to-all-start) | async-done | bytes 2097184 | tf_op jit(solution)/shard_map/all_to_all | solution.py:359
  190.0 4.3 %collective-permute-done.11.r3_ref = bf16[2,256,256]{2,1,0:T(8,128)(2,1)S(1)} collective-permute-done((bf16[2,256,256]{2,1,0:T(8,128)(2,1)}, bf16[2,256,256]{2,1,0:T(8,128)(2,1)S(1)}, u32[]{:S(2)}, u32[]{:S(2)}) %collective-permute-start.11) | collective-permute-done | bytes 262176 | tf_op jit(solution)/shard_map/ppermute | solution.py:315
  194.4 0.7 copy-done.8
  195.1 5.3 %shard_map.170 = (bf16[256,512]{1,0:T(8,128)(2,1)}, bf16[256,512]{1,0:T(8,128)(2,1)}, f32[1,512]{1,0:T(1,128)}) custom-call(s32[2]{0:T(128)} %pad_add_fusion.own_ref, s32[16]{0:T(128)} %counts_ref.3, bf16[2,256,256]{2,1,0:T(8,128)(2,1)} %pad_maximum_fusion.2.r0_ref, bf16[2,256,256]{2,1,0:T(8,128)(2,1)} %copy-done.6, bf16[2,256,256]{2,1,0:T(8,128)(2,1)} %copy-done.7, ...), custom_call_target="tpu_custom_call" | custom-call | tf_op jit(solution)/shard_map/pallas_call | solution.py:411
  200.4 0.7 broadcast_in_dim.12
  201.1 21.1 %all_to_all.27 = f32[128,4,128]{2,1,0:T(4,128)S(1)} all-to-all(f32[128,4,128]{2,1,0:T(4,128)S(1)} %broadcast_in_dim.12), channel_id=1, replica_groups=mesh['dom'=16,'blk'=8] {'dom','blk'}, dimensions={0} | all-to-all | bytes 524288 | tf_op jit(solution)/shard_map/all_to_all | solution.py:419
  222.2 0.7 reduce_sum.9
  222.9 5.2 %shard_map.173 = f32[5,512,512]{2,1,0:T(8,128)} custom-call(bf16[8,16,80,128]{3,2,1,0:T(8,128)(2,1)} %bitcast.16), custom_call_target="tpu_custom_call" | custom-call | tf_op jit(solution)/shard_map/pallas_call | solution.py:400
  (60 shorter events, 3.5 us)
Async XLA Ops:
  13.4 7.8 %copy-start.3 = (bf16[272,512]{1,0:T(8,128)(2,1)S(1)}, bf16[272,512]{1,0:T(8,128)(2,1)}, u32[]{:S(2)}) copy-start(bf16[272,512]{1,0:T(8,128)(2,1)} %shard_map.165.pay_ref) | copy-start | bytes 835588
  13.4 12.3 %copy-start.4 = (bf16[256,512]{1,0:T(8,128)(2,1)S(1)}, bf16[256,512]{1,0:T(8,128)(2,1)}, u32[]{:S(2)}) copy-start(bf16[256,512]{1,0:T(8,128)(2,1)} %grad_ref.3) | copy-start | bytes 786436
  13.4 96.6 %all-to-all-start.1 = ((bf16[16,128,512]{2,1,0:T(8,128)(2,1)}), bf16[16,128,512]{2,1,0:T(8,128)(2,1)S(1)}, u32[]{:S(2)}, u32[]{:S(2)}) async-start(bf16[16,128,512]{2,1,0:T(8,128)(2,1)} %shard_map.168), calls=%async_computation.1 | async-start | bytes 4194304 | tf_op jit(solution)/shard_map/all_to_all | solution.py:343
  21.1 201.8 %all-gather.2.cloned.1.call-start = ((), (), s32[]{:S(2)}) async-start(), calls=%async_computation.5 | async-start | bytes 2949120 | tf_op jit(solution)/shard_map/all_gather | solution.py:399
  21.2 13.9 %collective-permute-start.2 = (bf16[272,512]{1,0:T(8,128)(2,1)S(1)}, bf16[272,512]{1,0:T(8,128)(2,1)S(1)}, u32[]{:S(2)}, u32[]{:S(2)}) collective-permute-start(bf16[272,512]{1,0:T(8,128)(2,1)S(1)} %copy-done.3), channel_id=1, source_target_pairs={{0,6},{1,7},{2,0},{3,1},{4,2},{5,3},{6,4},{7,5},{8,14},{9,15},{10,... | collective-permute-start | bytes 835592 | tf_op jit(solution)/shard_map/ppermute | solution.py:315
  25.0 10.1 %collective-permute-start.1 = (bf16[272,512]{1,0:T(8,128)(2,1)S(1)}, bf16[272,512]{1,0:T(8,128)(2,1)S(1)}, u32[]{:S(2)}, u32[]{:S(2)}) collective-permute-start(bf16[272,512]{1,0:T(8,128)(2,1)S(1)} %copy-done.3), channel_id=1, source_target_pairs={{0,4},{1,5},{2,6},{3,7},{4,0},{5,1},{6,2},{7,3},{8,12},{9,13},{10,... | collective-permute-start | bytes 835592 | tf_op jit(solution)/shard_map/ppermute | solution.py:315
  25.0 16.3 %collective-permute-start = (bf16[272,512]{1,0:T(8,128)(2,1)S(1)}, bf16[272,512]{1,0:T(8,128)(2,1)S(1)}, u32[]{:S(2)}, u32[]{:S(2)}) collective-permute-start(bf16[272,512]{1,0:T(8,128)(2,1)S(1)} %copy-done.3), channel_id=1, source_target_pairs={{0,2},{1,3},{2,4},{3,5},{4,6},{5,7},{6,0},{7,1},{8,10},{9,11},{10,... | collective-permute-start | bytes 835592 | tf_op jit(solution)/shard_map/ppermute | solution.py:315
  25.7 21.4 %collective-permute-start.6 = (bf16[256,512]{1,0:T(8,128)(2,1)S(1)}, bf16[256,512]{1,0:T(8,128)(2,1)S(1)}, u32[]{:S(2)}, u32[]{:S(2)}) collective-permute-start(bf16[256,512]{1,0:T(8,128)(2,1)S(1)} %copy-done.4), channel_id=1, source_target_pairs={{0,6},{1,7},{2,0},{3,1},{4,2},{5,3},{6,4},{7,5},{8,14},{9,15},{10,... | collective-permute-start | bytes 786440 | tf_op jit(solution)/shard_map/ppermute | solution.py:315
  27.7 19.4 %collective-permute-start.5 = (bf16[256,512]{1,0:T(8,128)(2,1)S(1)}, bf16[256,512]{1,0:T(8,128)(2,1)S(1)}, u32[]{:S(2)}, u32[]{:S(2)}) collective-permute-start(bf16[256,512]{1,0:T(8,128)(2,1)S(1)} %copy-done.4), channel_id=1, source_target_pairs={{0,4},{1,5},{2,6},{3,7},{4,0},{5,1},{6,2},{7,3},{8,12},{9,13},{10,... | collective-permute-start | bytes 786440 | tf_op jit(solution)/shard_map/ppermute | solution.py:315
  35.1 16.6 %collective-permute-start.4 = (bf16[256,512]{1,0:T(8,128)(2,1)S(1)}, bf16[256,512]{1,0:T(8,128)(2,1)S(1)}, u32[]{:S(2)}, u32[]{:S(2)}) collective-permute-start(bf16[256,512]{1,0:T(8,128)(2,1)S(1)} %copy-done.4), channel_id=1, source_target_pairs={{0,2},{1,3},{2,4},{3,5},{4,6},{5,7},{6,0},{7,1},{8,10},{9,11},{10,... | collective-permute-start | bytes 786440 | tf_op jit(solution)/shard_map/ppermute | solution.py:315
  42.5 10.4 %copy-start.12 = (s32[4096]{0:T(1024)S(1)}, s32[4096]{0:T(1024)}, u32[]{:S(2)}) copy-start(s32[4096]{0:T(1024)} %param.25) | copy-start | bytes 49156
  42.5 11.0 %copy-start.13 = (s32[4096]{0:T(1024)S(1)}, s32[4096]{0:T(1024)}, u32[]{:S(2)}) copy-start(s32[4096]{0:T(1024)} %param.26) | copy-start | bytes 49156
  42.5 25.5 %collective-permute-start.3 = (bf16[4,272,512]{2,1,0:T(8,128)(2,1)}, bf16[4,272,512]{2,1,0:T(8,128)(2,1)}, u32[]{:S(2)}, u32[]{:S(2)}) collective-permute-start(bf16[4,272,512]{2,1,0:T(8,128)(2,1)} %pad_maximum_fusion.na_ref), channel_id=1, source_target_pairs={{0,1},{1,0},{2,3},{3,2},{4,5},{5,4},{6,7},{7,6},{8,9},{9,8},{10,11... | collective-permute-start | bytes 3342344 | tf_op jit(solution)/shard_map/ppermute | solution.py:319
  51.8 16.2 %copy-start = (bf16[4,256,512]{2,1,0:T(8,128)(2,1)}, bf16[4,256,512]{2,1,0:T(8,128)(2,1)S(1)}, u32[]{:S(2)}) copy-start(bf16[4,256,512]{2,1,0:T(8,128)(2,1)S(1)} %pad_maximum_fusion.1.ga_ref) | copy-start | bytes 3145732
  51.8 16.2 %collective-permute-start.7 = (bf16[4,256,512]{2,1,0:T(8,128)(2,1)S(1)}, bf16[4,256,512]{2,1,0:T(8,128)(2,1)}, u32[]{:S(2)}, u32[]{:S(2)}) collective-permute-start(bf16[4,256,512]{2,1,0:T(8,128)(2,1)S(1)} %pad_maximum_fusion.1.ga_ref), channel_id=1, source_target_pairs={{0,1},{1,0},{2,3},{3,2},{4,5},{5,4},{6,7},{7,6},{8,9},{9,8},{10,11... | collective-permute-start | bytes 3145736 | tf_op jit(solution)/shard_map/ppermute | solution.py:319
  110.0 1.4 copy-start.2
  115.3 1.6 collective-permute-start.12
  116.8 6.3 %collective-permute-start.13 = (bf16[2,64,256]{2,1,0:T(8,128)(2,1)S(1)}, bf16[2,64,256]{2,1,0:T(8,128)(2,1)S(1)}, u32[]{:S(2)}, u32[]{:S(2)}) collective-permute-start(bf16[2,64,256]{2,1,0:T(8,128)(2,1)S(1)} %pad_maximum_fusion.7), channel_id=1, source_target_pairs={{0,2},{1,3},{2,4},{3,5},{4,6},{5,7},{6,0},{7,1},{8,10},{9,11},{10,... | collective-permute-start | bytes 196616 | tf_op jit(solution)/shard_map/ppermute | solution.py:315
  116.9 6.2 %collective-permute-start.14 = (bf16[2,64,256]{2,1,0:T(8,128)(2,1)S(1)}, bf16[2,64,256]{2,1,0:T(8,128)(2,1)S(1)}, u32[]{:S(2)}, u32[]{:S(2)}) collective-permute-start(bf16[2,64,256]{2,1,0:T(8,128)(2,1)S(1)} %pad_maximum_fusion.8), channel_id=1, source_target_pairs={{0,4},{1,5},{2,6},{3,7},{4,0},{5,1},{6,2},{7,3},{8,12},{9,13},{10,... | collective-permute-start | bytes 196616 | tf_op jit(solution)/shard_map/ppermute | solution.py:315
  118.8 4.6 %collective-permute-start.15 = (bf16[2,64,256]{2,1,0:T(8,128)(2,1)S(1)}, bf16[2,64,256]{2,1,0:T(8,128)(2,1)S(1)}, u32[]{:S(2)}, u32[]{:S(2)}) collective-permute-start(bf16[2,64,256]{2,1,0:T(8,128)(2,1)S(1)} %pad_maximum_fusion.9), channel_id=1, source_target_pairs={{0,6},{1,7},{2,0},{3,1},{4,2},{5,3},{6,4},{7,5},{8,14},{9,15},{10,... | collective-permute-start | bytes 196616 | tf_op jit(solution)/shard_map/ppermute | solution.py:315
  123.2 0.6 copy-start.9
  123.2 0.6 copy-start.10
  123.4 0.6 copy-start.11
  161.1 3.9 %copy-start.14 = (bf16[4,256,256]{2,1,0:T(8,128)(2,1)S(1)}, bf16[4,256,256]{2,1,0:T(8,128)(2,1)}, u32[]{:S(2)}) copy-start(bf16[4,256,256]{2,1,0:T(8,128)(2,1)} %get-tuple-element.17) | copy-start | bytes 1572868
  161.2 7.7 %copy-start.5 = (bf16[4,256,256]{2,1,0:T(8,128)(2,1)S(1)}, bf16[4,256,256]{2,1,0:T(8,128)(2,1)}, u32[]{:S(2)}) copy-start(bf16[4,256,256]{2,1,0:T(8,128)(2,1)} %get-tuple-element.16) | copy-start | bytes 1572868
  161.2 28.9 %all-to-all-start = ((bf16[16,128,512]{2,1,0:T(8,128)(2,1)}), bf16[16,128,512]{2,1,0:T(8,128)(2,1)S(1)}, u32[]{:S(2)}, u32[]{:S(2)}) async-start(bf16[16,128,512]{2,1,0:T(8,128)(2,1)} %get-tuple-element.18), calls=%async_computation | async-start | bytes 4194304 | tf_op jit(solution)/shard_map/all_to_all | solution.py:359
  165.0 5.3 %collective-permute-start.8 = (bf16[4,256,256]{2,1,0:T(8,128)(2,1)S(1)}, bf16[4,256,256]{2,1,0:T(8,128)(2,1)S(1)}, u32[]{:S(2)}, u32[]{:S(2)}) collective-permute-start(bf16[4,256,256]{2,1,0:T(8,128)(2,1)S(1)} %copy-done.14), channel_id=1, source_target_pairs={{0,1},{1,0},{2,3},{3,2},{4,5},{5,4},{6,7},{7,6},{8,9},{9,8},{10,11... | collective-permute-start | bytes 1572872 | tf_op jit(solution)/shard_map/ppermute | solution.py:319
  170.4 19.6 %collective-permute-start.9 = (bf16[2,256,256]{2,1,0:T(8,128)(2,1)S(1)}, bf16[2,256,256]{2,1,0:T(8,128)(2,1)S(1)}, u32[]{:S(2)}, u32[]{:S(2)}) collective-permute-start(bf16[2,256,256]{2,1,0:T(8,128)(2,1)S(1)} %pad_maximum_fusion.3), channel_id=1, source_target_pairs={{0,6},{1,7},{2,0},{3,1},{4,2},{5,3},{6,4},{7,5},{8,14},{9,15},{10,... | collective-permute-start | bytes 786440 | tf_op jit(solution)/shard_map/ppermute | solution.py:315
  173.0 17.0 %collective-permute-start.10 = (bf16[2,256,256]{2,1,0:T(8,128)(2,1)S(1)}, bf16[2,256,256]{2,1,0:T(8,128)(2,1)S(1)}, u32[]{:S(2)}, u32[]{:S(2)}) collective-permute-start(bf16[2,256,256]{2,1,0:T(8,128)(2,1)S(1)} %pad_maximum_fusion.4), channel_id=1, source_target_pairs={{0,4},{1,5},{2,6},{3,7},{4,0},{5,1},{6,2},{7,3},{8,12},{9,13},{10,... | collective-permute-start | bytes 786440 | tf_op jit(solution)/shard_map/ppermute | solution.py:315
  173.9 20.5 %collective-permute-start.11 = (bf16[2,256,256]{2,1,0:T(8,128)(2,1)}, bf16[2,256,256]{2,1,0:T(8,128)(2,1)S(1)}, u32[]{:S(2)}, u32[]{:S(2)}) collective-permute-start(bf16[2,256,256]{2,1,0:T(8,128)(2,1)} %pad_maximum_fusion.5), channel_id=1, source_target_pairs={{0,2},{1,3},{2,4},{3,5},{4,6},{5,7},{6,0},{7,1},{8,10},{9,11},{10,... | collective-permute-start | bytes 786440 | tf_op jit(solution)/shard_map/ppermute | solution.py:315
  190.0 4.3 %copy-start.1 = (bf16[16,128,512]{2,1,0:T(8,128)(2,1)}, bf16[16,128,512]{2,1,0:T(8,128)(2,1)S(1)}, u32[]{:S(2)}) copy-start(bf16[16,128,512]{2,1,0:T(8,128)(2,1)S(1)} %all-to-all-done.back_ref) | copy-start | bytes 6291460
  190.0 4.3 %copy-start.6 = (bf16[2,256,256]{2,1,0:T(8,128)(2,1)}, bf16[2,256,256]{2,1,0:T(8,128)(2,1)S(1)}, u32[]{:S(2)}) copy-start(bf16[2,256,256]{2,1,0:T(8,128)(2,1)S(1)} %collective-permute-done.9.r1_ref) | copy-start | bytes 786436
  190.0 4.3 %copy-start.7 = (bf16[2,256,256]{2,1,0:T(8,128)(2,1)}, bf16[2,256,256]{2,1,0:T(8,128)(2,1)S(1)}, u32[]{:S(2)}) copy-start(bf16[2,256,256]{2,1,0:T(8,128)(2,1)S(1)} %collective-permute-done.10.r2_ref) | copy-start | bytes 786436
  194.3 0.7 copy-start.8
Sparse Core Ops, SparseCore 0:
  161.3 38.2 all-gather.1

commit v2 on v1

v2 whole, which is shorter than its diff:
```python
import math

import jax
import jax.numpy as jnp
from jax import lax
from jax.experimental import pallas as pl
from jax.experimental.pallas import tpu as pltpu
from jax.sharding import PartitionSpec as P

F32 = jnp.float32
BF16 = jnp.bfloat16
EPS = 1e-06
D = 512
ROWS = 256
HEAD = 64
BLK = 8
DOM = 16
CAP = 128
EDGES = 4096
PAY = 2 * ROWS + 16
LOG2E = math.log2(math.e)
SCORE_MUL = LOG2E / 8.0
SCORE_SUB = (8.0 + 256.0) * LOG2E
CHUNK = 80
SPREAD = 4 * CHUNK + 16

NT = (((1,), (1,)), ((), ()))
NN = (((1,), (0,)), ((), ()))


def dot(a, b, dims=NN):
    return lax.dot_general(a, b, dims, preferred_element_type=F32)


def call(body, out_shape, operands, scratch=(), scalars=0, micros=2):
    specs = [pl.BlockSpec(memory_space=pltpu.SMEM)] * scalars
    specs += [pl.BlockSpec(memory_space=pltpu.VMEM)] * (len(operands) - scalars)
    return pl.pallas_call(
        body,
        out_shape=out_shape,
        in_specs=specs,
        out_specs=jax.tree.map(lambda _: pl.BlockSpec(memory_space=pltpu.VMEM), out_shape),
        scratch_shapes=list(scratch),
        cost_estimate=pl.CostEstimate(flops=int(micros * 1e9), transcendentals=0, bytes_accessed=1 << 20),
    )(*operands)


def shape(dims, dtype):
    return jax.ShapeDtypeStruct(dims, dtype)


def position():
    me = lax.axis_index("blk").astype(jnp.int32)
    return lax.shift_right_logical(me, 1), me & 1


def norm_body(pattern_ref, x_ref, gain_ref, label_ref, grad_ref, out_ref):
    x = x_ref[...].astype(F32)
    scale = lax.rsqrt(jnp.mean(x * x, axis=-1, keepdims=True) + EPS)
    out_ref[0:ROWS, :] = (x * scale * gain_ref[...]).astype(BF16)
    out_ref[ROWS : 2 * ROWS, :] = grad_ref[...]
    row = lax.broadcasted_iota(jnp.int32, (16, ROWS), 0)
    lane = lax.broadcasted_iota(jnp.int32, (16, ROWS), 1)
    tail = jnp.where(row == 0, label_ref[...].astype(F32), 0.0)
    for b in range(BLK):
        flag = jnp.where(pattern_ref[0, b] == 1, 1.0, 0.0)
        tail = jnp.where((row == 1 + b) & (lane >= 0), flag, tail)
    out_ref[2 * ROWS : PAY, 0:ROWS] = tail.astype(BF16)
    out_ref[2 * ROWS : PAY, ROWS:D] = jnp.zeros((16, D - ROWS), BF16)


def outgoing_body(counts_ref, pay_ref, rows_ref, out_ref):
    normed = pay_ref[0:ROWS, :]
    columns = jnp.transpose(rows_ref[...].astype(F32))
    lane = lax.broadcasted_iota(jnp.int32, (CAP, ROWS), 1).astype(F32)
    slot = lax.broadcasted_iota(jnp.int32, (CAP, ROWS), 0)
    for p in range(DOM):
        hit = (lane == columns[:, p : p + 1]) & (slot < counts_ref[p])
        out_ref[p] = dot(jnp.where(hit, 1.0, 0.0).astype(BF16), normed).astype(BF16)


E_ROWS = 4


def edges_body(
    src_ref, dst_ref, grad_ref, w_ref, wq_ref, wk_ref, wv_ref, wo_ref,
    counts_t_ref, degree_ref, slots_ref, wqkv_ref, wo_head_ref, acc_ref,
):
    z, core = position()
    for m in range(4):
        @pl.when(z == m)
        def _():
            for k, ref in enumerate((wq_ref, wk_ref, wv_ref)):
                pair = jnp.transpose(ref[:, m * 128 : (m + 1) * 128].astype(F32))
                picked = jnp.where(core == 0, pair[0:HEAD], pair[HEAD:128])
                wqkv_ref[k * HEAD : (k + 1) * HEAD, :] = picked.astype(BF16)
            for c in range(2):
                @pl.when(core == c)
                def _():
                    wo_head_ref[...] = wo_ref[m * 128 + c * HEAD : m * 128 + (c + 1) * HEAD, :]

    low_row = lax.broadcasted_iota(jnp.int32, (512, E_ROWS * 128), 0)
    high_row = lax.broadcasted_iota(jnp.int32, (1024, E_ROWS * 128), 0)
    for step in range(EDGES // (E_ROWS * 128)):
        rows = [step * E_ROWS + k for k in range(E_ROWS)]
        src = jnp.concatenate([src_ref[k : k + 1, :] for k in rows], axis=1)
        dst = jnp.concatenate([dst_ref[k : k + 1, :] for k in rows], axis=1)
        low = jnp.where(low_row == (src & 511), 1.0, 0.0).astype(BF16)
        high = jnp.where(high_row == ((src >> 9) * 256 + dst), 1.0, 0.0).astype(BF16)
        part = dot(low, high, NT)
        if step == 0:
            acc_ref[...] = part
        else:
            acc_ref[...] += part
    counts = acc_ref[...]
    per_row = jnp.sum(counts, axis=0, keepdims=True)
    per_row = per_row[:, 0:256] + per_row[:, 256:512] + per_row[:, 512:768] + per_row[:, 768:1024]
    degree = jnp.transpose(jnp.broadcast_to(jnp.maximum(per_row, 1.0), (128, ROWS)))
    degree_ref[...] = degree
    counts_t_ref[...] = jnp.transpose(counts).astype(BF16)
    counts = counts.astype(BF16)
    inverse = 1.0 / degree[:, 0:1]
    message = (dot(grad_ref[...], w_ref[...], NT) * inverse).astype(BF16)
    for high in range(4):
        part = dot(counts[:, high * 256 : (high + 1) * 256], message).astype(BF16)
        for k in range(4):
            slots_ref[high * 4 + k] = part[k * CAP : (k + 1) * CAP, :]


def mean_body(counts_t_ref, degree_ref, table_ref, x_ref, w_ref, mine_ref, other_ref, base_ref, means_ref):
    total = jnp.zeros((ROWS, D), F32)
    for high in range(4):
        table = jnp.concatenate([table_ref[high * 4 + k] for k in range(4)], axis=0)
        total = total + dot(counts_t_ref[high * 256 : (high + 1) * 256, :], table)
    mean_rows = (total / degree_ref[:, 0:1]).astype(BF16)
    base_ref[...] = x_ref[...].astype(F32) + dot(mean_rows, w_ref[...])
    turned = jnp.transpose(mean_rows.astype(F32)).astype(BF16)
    for h in range(BLK):
        means_ref[h] = turned[h * HEAD : (h + 1) * HEAD, :]
    z, core = position()
    for dz in range(4):
        chip = ((z + dz) & 3) * 2
        mine_ref[dz] = means_ref[chip + core]
        other_ref[dz] = means_ref[chip + (1 - core)]


def attention_body(
    p0_ref, p1_ref, p2_ref, p3_ref, p4_ref, p5_ref, p6_ref, p7_ref, wqkv_ref, wo_ref,
    r0_ref, r1_ref, r2_ref, r3_ref, dw_ref,
    y_ref, s_ref, qt_ref, kt_ref, k_ref, v_ref, vt_ref, w_ref, dq_ref, dk_ref, dv_ref, at_ref, ga_ref,
):
    pays = (p0_ref, p1_ref, p2_ref, p3_ref, p4_ref, p5_ref, p6_ref, p7_ref)
    outs = (r0_ref, r1_ref, r2_ref, r3_ref)
    z, core = position()
    row = lax.broadcasted_iota(jnp.int32, (HEAD, ROWS), 0)
    number = row.astype(F32)

    def head_scale(part):
        return lax.rsqrt(jnp.sum(part * part, axis=0, keepdims=True) * (1.0 / HEAD) + EPS)

    for r in range(BLK):
        pay = pays[r]
        projected = dot(wqkv_ref[...], pay[0:ROWS, :], NT)
        query, key, value = projected[0:HEAD], projected[HEAD:128], projected[128:192]
        scale_q, scale_k = head_scale(query), head_scale(key)
        query, key = query * scale_q, key * scale_k
        y_ref[r, 0:HEAD] = query
        y_ref[r, HEAD:128] = key
        s_ref[r, 0:1] = scale_q
        s_ref[r, 1:2] = scale_k
        tail = pay[2 * ROWS : PAY, 0:ROWS].astype(F32)
        same = jnp.where(number == tail[0:1], 32.0, 0.0)
        sender = ((z - (r & 3)) & 3) * 2 + (core ^ (r >> 2))
        wanted = jnp.concatenate([jnp.zeros((16, ROWS), F32), tail[1:9] * 32.0, jnp.zeros((40, ROWS), F32)], axis=0)
        owner = jnp.where(row == 16 + sender, 32.0, 0.0)
        qt_ref[r] = jnp.concatenate([query, same + wanted], axis=0).astype(BF16)
        key = jnp.concatenate([key, same + owner], axis=0)
        kt_ref[r] = key[0:HEAD].astype(BF16)
        k_ref[r] = jnp.transpose(key).astype(BF16)
        value = jnp.concatenate([value, jnp.where(row < 2, 1.0, 0.0)], axis=0)
        vt_ref[r] = value[0:80].astype(BF16)
        v_ref[r] = jnp.transpose(value).astype(BF16)
        ga_ref[r] = dot(wo_ref[...], pay[ROWS : 2 * ROWS, :], NT)
        dk_ref[r] = jnp.zeros((HEAD, ROWS), F32)
        dv_ref[r] = jnp.zeros((HEAD, ROWS), F32)

    keys_t = jnp.concatenate([kt_ref[j] for j in range(BLK)], axis=1)
    values_t = jnp.concatenate([vt_ref[j] for j in range(BLK)], axis=1)

    def query_block(i, carry):
        query = qt_ref[i]
        for j in range(BLK):
            scores = dot(k_ref[j], query)
            w_ref[j] = jnp.exp2(scores * SCORE_MUL - SCORE_SUB).astype(BF16)
        numer = dot(values_t, w_ref[...].reshape(BLK * ROWS, ROWS))
        inverse = 1.0 / numer[HEAD : HEAD + 1]
        attn = (numer[0:HEAD] * inverse).astype(BF16)
        at_ref[i] = attn
        grad_attn = ga_ref[i]
        minus = jnp.sum(grad_attn * attn.astype(F32), axis=0, keepdims=True) * (-inverse)
        coarse = minus.astype(BF16).astype(F32)
        extra = jnp.where(row == 0, coarse, jnp.where(row == 1, minus - coarse, 0.0))
        grad = jnp.concatenate([grad_attn * inverse, extra], axis=0).astype(BF16)
        dq = jnp.zeros((HEAD, ROWS), F32)
        for j in range(BLK):
            weights = w_ref[j]
            slopes = (weights.astype(F32) * dot(v_ref[j], grad)).astype(BF16)
            dq = dq + dot(kt_ref[j], slopes)
            dk_ref[j] += dot(query[0:HEAD], slopes, NT)
            dv_ref[j] += dot(grad[0:HEAD], weights, NT)
        dq_ref[i] = dq
        return carry

    lax.fori_loop(0, BLK, query_block, 0)

    dw = jnp.zeros((192, D), F32)
    dwo = jnp.zeros((HEAD, D), F32)
    for r in range(BLK):
        pay = pays[r]

        def pull(grad, y, scale):
            grad = grad * (8.0 / HEAD)
            return scale * (grad - y * (jnp.sum(y * grad, axis=0, keepdims=True) * (1.0 / HEAD)))

        dquery = pull(dq_ref[r], y_ref[r, 0:HEAD], s_ref[r, 0:1])
        dkey = pull(dk_ref[r], y_ref[r, HEAD:128], s_ref[r, 1:2])
        first = jnp.concatenate([dquery, dkey], axis=0)
        second = jnp.concatenate([dv_ref[r], at_ref[r].astype(F32)], axis=0)
        outs[r & 3][r >> 2, :, 0:128] = jnp.transpose(first).astype(BF16)
        outs[r & 3][r >> 2, :, 128:256] = jnp.transpose(second).astype(BF16)
        left = jnp.concatenate([first, second[0:HEAD]], axis=0).astype(BF16)
        dw = dw + dot(left, pay[0:ROWS, :])
        dwo = dwo + dot(at_ref[r], pay[ROWS : 2 * ROWS, :])
    dw_ref[0:192, :] = dw
    dw_ref[192:256, :] = dwo


def chunks_body(
    p0_ref, p1_ref, p2_ref, p3_ref, p4_ref, p5_ref, p6_ref, p7_ref, m0_ref, m1_ref, m2_ref, m3_ref, dw_ref, out_ref
):
    pays = (p0_ref, p1_ref, p2_ref, p3_ref, p4_ref, p5_ref, p6_ref, p7_ref)
    total = jnp.zeros((HEAD, D), F32)
    for dz, m_ref in enumerate((m0_ref, m1_ref, m2_ref, m3_ref)):
        for c in range(2):
            total = total + dot(m_ref[c], pays[4 * c + dz][ROWS : 2 * ROWS, :])
    for a in range(4):
        for b in range(4):
            out_ref[a * 4 + b, 0:64, :] = dw_ref[a * 64 : (a + 1) * 64, b * 128 : (b + 1) * 128].astype(BF16)
            out_ref[a * 4 + b, 64:80, :] = total[a * 16 : (a + 1) * 16, b * 128 : (b + 1) * 128].astype(BF16)


def chunk_sum_body(in_ref, out_ref):
    total = in_ref[0].astype(F32)
    for p in range(1, DOM):
        total = total + in_ref[p].astype(F32)
    out_ref[...] = total.astype(BF16)


def spread_body(c0_ref, c1_ref, c2_ref, c3_ref, g0_ref, g1_ref, g2_ref, g3_ref, out_ref, gains_ref):
    z, core = position()
    for dz, g_ref in enumerate((g0_ref, g1_ref, g2_ref, g3_ref)):
        gains_ref[dz] = g_ref[...]
    gain = jnp.zeros((8, 128), F32)
    for b in range(BLK):
        gain = gain + gains_ref[(z - (b >> 1)) & 3, core ^ (b & 1)]
    coarse = gain.astype(BF16).astype(F32)
    fine = (gain - coarse).astype(BF16).astype(F32)
    tail = jnp.concatenate([coarse, fine], axis=0).astype(BF16)
    for p in range(DOM):
        for dz, c_ref in enumerate((c0_ref, c1_ref, c2_ref, c3_ref)):
            out_ref[p, dz * CHUNK : (dz + 1) * CHUNK, :] = c_ref[...]
        out_ref[p, 4 * CHUNK : SPREAD, :] = tail


def rows_body(
    counts_ref, r0_ref, r1_ref, r2_ref, r3_ref, t0_ref, t1_ref, t2_ref, t3_ref, back_ref, rows_ref, base_ref, x_ref,
    gain_ref, grad_ref, wq_ref, wk_ref, wv_ref, wo_ref,
    out_ref, feature_ref, gain_grad_ref, dq_ref, dk_ref, dv_ref, at_ref,
):
    left = lax.broadcasted_iota(jnp.int32, (ROWS, 128), 1) < HEAD
    z, core = position()
    even = core == 0
    for dz, (r_ref, t_ref) in enumerate(zip((r0_ref, r1_ref, r2_ref, r3_ref), (t0_ref, t1_ref, t2_ref, t3_ref))):
        chip = (z + dz) & 3
        one, two = r_ref[0].astype(F32), t_ref[...].astype(F32)
        low, high = jnp.where(even, one, two), jnp.where(even, two, one)
        low0, low1 = low[:, 0:128], low[:, 128:256]
        high0, high1 = high[:, 0:128], high[:, 128:256]
        dq_ref[chip] = jnp.where(left, low0, pltpu.roll(high0, HEAD, 1)).astype(BF16)
        dk_ref[chip] = jnp.where(left, pltpu.roll(low0, HEAD, 1), high0).astype(BF16)
        dv_ref[chip] = jnp.where(left, low1, pltpu.roll(high1, HEAD, 1)).astype(BF16)
        at_ref[chip] = jnp.where(left, pltpu.roll(low1, HEAD, 1), high1).astype(BF16)

    def whole(ref):
        return jnp.concatenate([ref[m] for m in range(4)], axis=1)

    out_ref[...] = (base_ref[...] + dot(whole(at_ref), wo_ref[...])).astype(BF16)
    dnormed = dot(whole(dq_ref), wq_ref[...], NT) + dot(whole(dk_ref), wk_ref[...], NT)
    dnormed = dnormed + dot(whole(dv_ref), wv_ref[...], NT)
    row = lax.broadcasted_iota(jnp.int32, (ROWS, CAP), 0)
    slot = lax.broadcasted_iota(jnp.int32, (ROWS, CAP), 1)
    for k in range(4):
        hits = []
        for p in range(4 * k, 4 * k + 4):
            hit = (row == rows_ref[p : p + 1, :]) & (slot < counts_ref[p])
            hits.append(jnp.where(hit, 1.0, 0.0).astype(BF16))
        part = jnp.concatenate([back_ref[p] for p in range(4 * k, 4 * k + 4)], axis=0)
        dnormed = dnormed + dot(jnp.concatenate(hits, axis=1), part)
    x = x_ref[...].astype(F32)
    scale = lax.rsqrt(jnp.mean(x * x, axis=-1, keepdims=True) + EPS)
    gain_grad = jnp.sum(dnormed * (x * scale), axis=0, keepdims=True)
    gain_grad_ref[...] = jnp.zeros((8, 128), F32)
    for k in range(4):
        gain_grad_ref[k : k + 1, :] = gain_grad[:, k * 128 : (k + 1) * 128]
    scaled = dnormed * gain_ref[...]
    inner = jnp.mean(scaled * x, axis=-1, keepdims=True)
    dx = scale * scaled - x * (scale * scale * scale * inner)
    feature_ref[...] = (grad_ref[...].astype(F32) + dx).astype(BF16)


def weights_body(mine_ref, other_ref, out_ref, gain_ref):
    which = pl.program_id(0)
    z, core = position()

    @pl.when(which == 0)
    def _():
        gain = jnp.zeros((8, 128), F32)
        for p in range(DOM):
            tail = mine_ref[p, 4 * CHUNK : SPREAD, :].astype(F32)
            gain = gain + (tail[0:8] + tail[8:16])
        gain_ref[...] = gain

    for c in range(2):
        @pl.when(core == c)
        def _():
            def piece(h, p, top, size):
                start = ((z - (h >> 1)) & 3) * CHUNK + top
                ref = mine_ref if h & 1 == c else other_ref
                return ref[p, pl.ds(pl.multiple_of(start, 16), size), :].astype(F32)

            @pl.when(which < 3)
            def _():
                for b in range(4):
                    part = jnp.concatenate([piece(h, which * 4 + b, 0, 64) for h in range(BLK)], axis=0)
                    out_ref[0, b * 128 : (b + 1) * 128, :] = jnp.transpose(part)

            @pl.when(which == 3)
            def _():
                for h in range(BLK):
                    for b in range(4):
                        out_ref[0, h * 64 : (h + 1) * 64, b * 128 : (b + 1) * 128] = piece(h, 12 + b, 0, 64)

            @pl.when(which == 4)
            def _():
                for h in range(BLK):
                    for a in range(4):
                        for b in range(4):
                            top = h * 64 + a * 16
                            out_ref[0, top : top + 16, b * 128 : (b + 1) * 128] = piece(h, a * 4 + b, 64, 16)


def chip_shift(step, swap):
    return [(z * 2 + c, ((z + step) % 4) * 2 + (c ^ swap)) for z in range(4) for c in range(2)]


def along_chips(array, step):
    return lax.ppermute(array, "blk", chip_shift(step, 0))


def other_core(array):
    return lax.ppermute(array, "blk", chip_shift(0, 1))


def to_dom_peers(array):
    return lax.all_to_all(array, "dom", split_axis=0, concat_axis=0, tiled=True)


def local(
    x, gain, wq, wk, wv, wo, wm, cluster, pattern, send_rows, send_counts, edge_src, edge_dst, out_grad
):
    gain_row = gain.reshape(1, D)
    pay = call(norm_body, shape((PAY, D), BF16), (pattern, x, gain_row, cluster.reshape(1, ROWS), out_grad), scalars=1)
    pays = [pay] + [along_chips(pay, step) for step in (1, 2, 3)]
    pays = pays + [other_core(part) for part in pays]
    outgoing = call(outgoing_body, shape((DOM, CAP, D), BF16), (send_counts, pay, send_rows), scalars=1, micros=3)
    incoming = to_dom_peers(outgoing)

    counts_t, degree, slot_grads, wqkv, wo_head = call(
        edges_body,
        (
            shape((1024, 512), BF16), shape((ROWS, 128), F32), shape((DOM, CAP, D), BF16),
            shape((192, D), BF16), shape((HEAD, D), BF16),
        ),
        (edge_src.reshape(32, 128), edge_dst.reshape(32, 128), out_grad, wm, wq, wk, wv, wo),
        scratch=[pltpu.VMEM((512, 1024), F32)],
        micros=10,
    )
    incoming, slot_grads = lax.optimization_barrier((incoming, slot_grads))
    back = to_dom_peers(slot_grads)

    mine, other, base = call(
        mean_body,
        (shape((4, HEAD, ROWS), BF16), shape((4, HEAD, ROWS), BF16), shape((ROWS, D), F32)),
        (counts_t, degree, incoming, x, wm),
        scratch=[pltpu.VMEM((BLK, HEAD, ROWS), BF16)],
        micros=4,
    )
    other = other_core(other)
    means = [jnp.stack([mine[dz], other[dz]]) for dz in range(4)]
    means = [means[0]] + [along_chips(means[dz], dz) for dz in (1, 2, 3)]

    *results, dw = call(
        attention_body,
        (*[shape((2, ROWS, 256), BF16)] * 4, shape((256, D), F32)),
        (*pays, wqkv, wo_head),
        scratch=[
            pltpu.VMEM((BLK, 128, ROWS), F32),
            pltpu.VMEM((BLK, 8, ROWS), F32),
            pltpu.VMEM((BLK, 128, ROWS), BF16),
            pltpu.VMEM((BLK, HEAD, ROWS), BF16),
            pltpu.VMEM((BLK, ROWS, 128), BF16),
            pltpu.VMEM((BLK, ROWS, 128), BF16),
            pltpu.VMEM((BLK, 80, ROWS), BF16),
            pltpu.VMEM((BLK, ROWS, ROWS), BF16),
            pltpu.VMEM((BLK, HEAD, ROWS), F32),
            pltpu.VMEM((BLK, HEAD, ROWS), F32),
            pltpu.VMEM((BLK, HEAD, ROWS), F32),
            pltpu.VMEM((BLK, HEAD, ROWS), BF16),
            pltpu.VMEM((BLK, HEAD, ROWS), F32),
        ],
        micros=30,
    )

    chunks = call(chunks_body, shape((DOM, CHUNK, 128), BF16), (*pays, *means, dw), micros=3)
    chunks, back = lax.optimization_barrier((chunks, back))
    chunk = call(chunk_sum_body, shape((CHUNK, 128), BF16), (to_dom_peers(chunks),), micros=1)
    chunk_parts = [chunk] + [along_chips(chunk, step) for step in (1, 2, 3)]

    results = [results[0]] + [along_chips(results[dz], -dz) for dz in (1, 2, 3)]
    swapped = [other_core(part[1]) for part in results]
    layer_out, feature_grad, gain_part = call(
        rows_body,
        (shape((ROWS, D), BF16), shape((ROWS, D), BF16), shape((8, 128), F32)),
        (send_counts, *results, *swapped, back, send_rows, base, x, gain_row, out_grad, wq, wk, wv, wo),
        scratch=[pltpu.VMEM((4, ROWS, 128), BF16)] * 4,
        scalars=1,
        micros=5,
    )
    gain_part = jnp.stack([gain_part, other_core(gain_part)])
    gain_parts = [gain_part] + [along_chips(gain_part, step) for step in (1, 2, 3)]
    spread = call(
        spread_body,
        shape((DOM, SPREAD, 128), BF16),
        (*chunk_parts, *gain_parts),
        scratch=[pltpu.VMEM((4, 2, 8, 128), F32)],
    )
    gathered = to_dom_peers(spread)
    whole = pl.BlockSpec((DOM, SPREAD, 128), lambda t: (0, 0, 0))
    weight_grads, gain_grad = pl.pallas_call(
        weights_body,
        grid=(5,),
        out_shape=(shape((5, D, D), F32), shape((8, 128), F32)),
        in_specs=[whole, whole],
        out_specs=(pl.BlockSpec((1, D, D), lambda t: (t, 0, 0)), pl.BlockSpec((8, 128), lambda t: (0, 0))),
    )(gathered, other_core(gathered))
    return layer_out, feature_grad, weight_grads, gain_grad[0:4].reshape(D)


def solution(mesh):
    both = ("dom", "blk")
    placed = (
        P(both, None), P(), P(), P(), P(), P(), P(), P(both), P(both, None), P(both, None), P(both), P(both), P(both),
        P(both, None),
    )
    return jax.shard_map(
        local,
        mesh=mesh,
        in_specs=placed,
        out_specs=(P(both, None), P(both, None), P(), P()),
        check_vma=False,
    )
```

time: 234 us -> 187 us (0.80)
  blocking collectives: 53.4 us -> 24.6 us
  starting transfers between devices: 35.3 us -> 49.7 us
  between operations: 14.2 us -> 0.95 us
  Pallas kernels: 74.3 us -> 64.3 us
  other arithmetic: 6.17 us -> 0.66 us
  waiting for transfers between devices: 41.1 us -> 37.3 us
    all_to_all x3 -> x1, blocking collectives: 53.4 us -> 24.6 us  [to_dom_peers(): return lax.all_to_all(array, 'dom', split_axis=0, concat_axis=0, tiled=True)]
    pallas_call x9 -> x10, Pallas kernels: 74.3 us -> 64.3 us  [the longest x9 59.2 us: call(): pl.pallas_call(body, out_shape=out_shape, in_specs=specs, out_specs=jax.t...]
    all_to_all x2 -> x3, starting transfers between devices: 11.6 us -> 19.2 us  [to_dom_peers(): return lax.all_to_all(array, 'dom', split_axis=0, concat_axis=0, tiled=True)]
    ppermute x4 -> x11, starting transfers between devices: 9.27 us -> 14.3 us  [other_core(): return lax.ppermute(array, 'blk', chip_shift(0, 1))]
    dynamic_slice x3 -> x0, local copies, waits for them, and re-layouts: 3.58 us -> none  [the longest x2 2.12 us: head_columns(): return lax.dynamic_slice(w, (0, me * HEAD), (D, HEAD))]
    another operation x7 -> x1, other arithmetic: 3.38 us -> 0.01 us  [local(): gain_part = jnp.stack([gain_part, other_core(gain_part)])]
    all_to_all x2 -> x3, waiting for transfers between devices: 14.9 us -> 11.8 us  [to_dom_peers(): return lax.all_to_all(array, 'dom', split_axis=0, concat_axis=0, tiled=True)]
    unnamed x30 -> x50, local copies, waits for them, and re-layouts: 2.71 us -> 5.76 us
  transfers between devices with their start and end apart: 19 -> 29, of which waited for: 10 -> 9; matrix products, arithmetic and copies ran while one was open for 5% -> 1% of each run, Pallas kernels for 24% -> 30%
where the time goes in v2:
time: 187 us; the launch traced here: 186 us
  Pallas kernels  64.3 us (34%)
  starting transfers between devices  49.7 us (27%)
  waiting for transfers between devices  37.3 us (20%)
  blocking collectives  24.6 us (13%)
  local copies, waits for them, and re-layouts  8.78 us (5%)
    pallas_call x9, Pallas kernels, call(): pl.pallas_call(body, out_shape=out_shape, in_specs=specs, out_specs=jax.t...  59.2 us
    all_to_all x1, blocking collectives, to_dom_peers(): return lax.all_to_all(array, 'dom', split_axis=0, concat_axis=0, tiled=True)  24.6 us
    ppermute x15, waiting for transfers between devices, along_chips(): return lax.ppermute(array, 'blk', chip_shift(step, 0))  22.3 us
    all_to_all x3, starting transfers between devices, to_dom_peers(): return lax.all_to_all(array, 'dom', split_axis=0, concat_axis=0, tiled=True)  19.2 us
    ppermute x15, starting transfers between devices, along_chips(): return lax.ppermute(array, 'blk', chip_shift(step, 0))  16.2 us
    ppermute x11, starting transfers between devices, other_core(): return lax.ppermute(array, 'blk', chip_shift(0, 1))  14.3 us
    all_to_all x3, waiting for transfers between devices, to_dom_peers(): return lax.all_to_all(array, 'dom', split_axis=0, concat_axis=0, tiled=True)  11.8 us
    unnamed x50, local copies, waits for them, and re-layouts  5.76 us
  transfers between devices with their start and end apart: 29, of which 9 were waited for; matrix products, arithmetic and copies ran while one was open for 1% of the time, Pallas kernels for 30%

profile of v2, /device:TPU:1, one launch (start us, length us, event | category | flops | bytes accessed | tf_op | source)
XLA Modules:
  0.0 186.4 jit_solution(7843814709882937324)
XLA Ops:
  0.6 2.0 %shard_map.165.p0_ref.pay_ref = bf16[528,512]{1,0:T(8,128)(2,1)} custom-call(s32[1,8]{1,0:T(1,128)} %pattern_ref.1, bf16[256,512]{1,0:T(8,128)(2,1)} %x_ref.5, f32[1,512]{1,0:T(1,128)} %bitcast.20, s32[1,256]{1,0:T(1,128)} %bitcast.22, bf16[256,512]{1,0:T(8,128)(2,1)} %grad_ref.5), custom_call_target="tpu_custom_call" | custom-call | flops 2000000000 | bytes 1048576 | tf_op jit(solution)/shard_map/pallas_call | solution.py:38
  2.6 4.6 %collective-permute-start.2 = (bf16[528,512]{1,0:T(8,128)(2,1)}, bf16[528,512]{1,0:T(8,128)(2,1)S(1)}, u32[]{:S(2)}, u32[]{:S(2)}) collective-permute-start(bf16[528,512]{1,0:T(8,128)(2,1)} %shard_map.165.p0_ref.pay_ref), channel_id=1, source_target_pairs={{0,6},{1,7},{2,0},{3,1},{4,2},{5,3},{6,4},{7,5},{8,14},{9,15},{10,... | collective-permute-start | bytes 1622024 | tf_op jit(solution)/shard_map/ppermute | solution.py:367
  7.2 0.7 collective-permute-start
  7.9 1.5 collective-permute-start.3
  9.4 3.2 %shard_map.168 = bf16[16,128,512]{2,1,0:T(8,128)(2,1)} custom-call(s32[16]{0:T(128)} %counts_ref.3, bf16[528,512]{1,0:T(8,128)(2,1)} %shard_map.165.p0_ref.pay_ref, s32[16,128]{1,0:T(8,128)} %rows_ref.3), custom_call_target="tpu_custom_call" | custom-call | flops 3000000000 | bytes 1048576 | tf_op jit(solution)/shard_map/pallas_call | solution.py:38
  12.7 6.8 %all-to-all-start = ((bf16[16,128,512]{2,1,0:T(8,128)(2,1)}), bf16[16,128,512]{2,1,0:T(8,128)(2,1)S(1)}, u32[]{:S(2)}, u32[]{:S(2)}) async-start(bf16[16,128,512]{2,1,0:T(8,128)(2,1)} %shard_map.168), calls=%async_computation | async-start | bytes 4194304 | tf_op jit(solution)/shard_map/all_to_all | solution.py:375
  19.5 10.5 %collective-permute-done.2.p3_ref = bf16[528,512]{1,0:T(8,128)(2,1)S(1)} collective-permute-done((bf16[528,512]{1,0:T(8,128)(2,1)}, bf16[528,512]{1,0:T(8,128)(2,1)S(1)}, u32[]{:S(2)}, u32[]{:S(2)}) %collective-permute-start.2) | collective-permute-done | bytes 540704 | tf_op jit(solution)/shard_map/ppermute | solution.py:367
  29.9 1.7 collective-permute-start.6
  31.7 2.5 %collective-permute-done.p1_ref = bf16[528,512]{1,0:T(8,128)(2,1)} collective-permute-done((bf16[528,512]{1,0:T(8,128)(2,1)}, bf16[528,512]{1,0:T(8,128)(2,1)}, u32[]{:S(2)}, u32[]{:S(2)}) %collective-permute-start) | collective-permute-done | bytes 540704 | tf_op jit(solution)/shard_map/ppermute | solution.py:367
  34.2 0.8 collective-permute-start.4
  35.0 9.1 %shard_map.166 = (bf16[1024,512]{1,0:T(8,128)(2,1)}, f32[256,128]{1,0:T(8,128)}, bf16[16,128,512]{2,1,0:T(8,128)(2,1)}, bf16[192,512]{1,0:T(8,128)(2,1)}, bf16[64,512]{1,0:T(8,128)(2,1)}) custom-call(s32[32,128]{1,0:T(8,128)} %bitcast.18, s32[32,128]{1,0:T(8,128)} %bitcast.19, bf16[256,512]{1,0:T(8,128)(2,1)} %grad_ref.5, bf16[512,512]{1,0:T(8,128)(2,1)} %w_ref.3, ...), custom_call_target="tpu_custom_call" | custom-call | flops 10000000000 | bytes 1048576 | tf_op jit(solution)/shard_map/pallas_call | solution.py:38
  44.2 27.9 %shard_map.167 = (bf16[2,256,256]{2,1,0:T(8,128)(2,1)}, bf16[2,256,256]{2,1,0:T(8,128)(2,1)}, bf16[2,256,256]{2,1,0:T(8,128)(2,1)}, bf16[2,256,256]{2,1,0:T(8,128)(2,1)}, f32[256,512]{1,0:T(8,128)}) custom-call(bf16[528,512]{1,0:T(8,128)(2,1)} %shard_map.165.p0_ref.pay_ref, bf16[528,512]{1,0:T(8,128)(2,1)} %collective-permute-done.p1_ref, ...), custom_call_target="tpu_custom_call" | custom-call | flops 30000001024 | bytes 1048576 | tf_op jit(solution)/shard_map/pallas_call | solution.py:38
  72.1 0.6 collective-permute-start.7
  72.8 0.9 slice_bitcast_fusion.3
  73.7 0.6 collective-permute-start.10
  74.9 5.4 %collective-permute-done.7.r1_ref = bf16[2,256,256]{2,1,0:T(8,128)(2,1)S(1)} collective-permute-done((bf16[2,256,256]{2,1,0:T(8,128)(2,1)}, bf16[2,256,256]{2,1,0:T(8,128)(2,1)S(1)}, u32[]{:S(2)}, u32[]{:S(2)}) %collective-permute-start.7) | collective-permute-done | bytes 262176 | tf_op jit(solution)/shard_map/ppermute | solution.py:367
  80.3 1.3 collective-permute-start.11
  81.5 1.4 copy-done.2
  82.9 6.8 %all-to-all-start.1 = ((bf16[16,128,512]{2,1,0:T(8,128)(2,1)}), bf16[16,128,512]{2,1,0:T(8,128)(2,1)S(1)}, u32[]{:S(2)}, u32[]{:S(2)}) async-start(bf16[16,128,512]{2,1,0:T(8,128)(2,1)} %get-tuple-element.39), calls=%async_computation.1 | async-start | bytes 4194304 | tf_op jit(solution)/shard_map/all_to_all | solution.py:375
  89.7 4.1 %shard_map.169 = (bf16[4,64,256]{2,1,0:T(8,128)(2,1)}, bf16[4,64,256]{2,1,0:T(8,128)(2,1)}, f32[256,512]{1,0:T(8,128)}) custom-call(bf16[1024,512]{1,0:T(8,128)(2,1)} %get-tuple-element.32.counts_t_ref, f32[256,128]{1,0:T(8,128)} %get-tuple-element.33.degree_ref, bf16[16,128,512]{2,1,0:T(8,128)(2,1)} %copy-done.2, bf16[256,512]{1,0:T(8,128)(2,1)} %x_ref.5, ...), custom_call_target="tpu_custom_call" | custom-call | flops 4000000000 | bytes 1048576 | tf_op jit(solution)/shard_map/pallas_call | solution.py:38
  94.1 0.8 fusion
  95.5 2.7 %collective-permute-start.16 = (bf16[2,64,256]{2,1,0:T(8,128)(2,1)S(1)}, bf16[2,64,256]{2,1,0:T(8,128)(2,1)S(1)}, u32[]{:S(2)}, u32[]{:S(2)}) collective-permute-start(bf16[2,64,256]{2,1,0:T(8,128)(2,1)S(1)} %pad_maximum_fusion.2), channel_id=1, source_target_pairs={{0,4},{1,5},{2,6},{3,7},{4,0},{5,1},{6,2},{7,3},{8,12},{9,13},{10,... | collective-permute-start | bytes 196616 | tf_op jit(solution)/shard_map/ppermute | solution.py:367
  98.5 0.6 pad_maximum_fusion.m0_ref
  99.2 0.9 collective-permute-done.15.m1_ref
  100.1 2.5 %collective-permute-start.12 = (bf16[256,256]{1,0:T(8,128)(2,1)S(1)}, bf16[256,256]{1,0:T(8,128)(2,1)S(1)}, u32[]{:S(2)}, u32[]{:S(2)}) collective-permute-start(bf16[256,256]{1,0:T(8,128)(2,1)S(1)} %slice_bitcast_fusion.1), channel_id=1, source_target_pairs={{0,1},{1,0},{2,3},{3,2},{4,5},{5,4},{6,7},{7,6},{8,9},{9,8},{10,11... | collective-permute-start | bytes 393224 | tf_op jit(solution)/shard_map/ppermute | solution.py:371
  103.3 3.6 %shard_map.170 = bf16[16,80,128]{2,1,0:T(8,128)(2,1)} custom-call(bf16[528,512]{1,0:T(8,128)(2,1)} %shard_map.165.p0_ref.pay_ref, bf16[528,512]{1,0:T(8,128)(2,1)} %collective-permute-done.p1_ref, bf16[528,512]{1,0:T(8,128)(2,1)} %copy-done.11, bf16[528,512]{1,0:T(8,128)(2,1)} %copy-done.10, bf16[528,512]{1,0:T(8,128)(2,1)} %collective-permute-done.3.p4_ref, ...), custom_call_target="tpu_custom_call" | custom-call | flops 3000000000 | bytes 1048576 | tf_op jit(solution)/shard_map/pallas_call | solution.py:38
  107.0 11.8 %all-to-all-done.1.back_ref = bf16[16,128,512]{2,1,0:T(8,128)(2,1)S(1)} async-done(((bf16[16,128,512]{2,1,0:T(8,128)(2,1)}), bf16[16,128,512]{2,1,0:T(8,128)(2,1)S(1)}, u32[]{:S(2)}, u32[]{:S(2)}) %all-to-all-start.1) | async-done | bytes 2097184 | tf_op jit(solution)/shard_map/all_to_all | solution.py:375
  118.7 5.7 %all-to-all-start.2 = ((bf16[16,80,128]{2,1,0:T(8,128)(2,1)}), bf16[16,80,128]{2,1,0:T(8,128)(2,1)S(1)}, u32[]{:S(2)}, u32[]{:S(2)}) async-start(bf16[16,80,128]{2,1,0:T(8,128)(2,1)} %shard_map.170), calls=%async_computation.2 | async-start | bytes 655360 | tf_op jit(solution)/shard_map/all_to_all | solution.py:375
  124.5 0.6 copy-done.12
  125.3 5.5 %shard_map.171 = (bf16[256,512]{1,0:T(8,128)(2,1)}, bf16[256,512]{1,0:T(8,128)(2,1)}, f32[8,128]{1,0:T(8,128)}) custom-call(s32[16]{0:T(128)} %counts_ref.3, bf16[2,256,256]{2,1,0:T(8,128)(2,1)} %get-tuple-element.28.r0_ref, bf16[2,256,256]{2,1,0:T(8,128)(2,1)} %copy-done.5, bf16[2,256,256]{2,1,0:T(8,128)(2,1)} %copy-done.6, bf16[2,256,256]{2,1,0:T(8,128)(2,1)} %copy-done.7, ...), custom_call_target="tpu_custom_call" | custom-call | flops 5000000000 | bytes 1048576 | tf_op jit(solution)/shard_map/pallas_call | solution.py:38
  130.8 1.5 collective-permute-start.21
  132.3 0.7 copy-done.4
  133.1 1.6 shard_map.172.c0_ref
  134.7 1.4 collective-permute-start.20
  136.1 0.6 collective-permute-start.18
  136.7 2.2 %collective-permute-start.24 = (f32[2,8,128]{2,1,0:T(8,128)S(1)}, f32[2,8,128]{2,1,0:T(8,128)S(1)}, u32[]{:S(2)}, u32[]{:S(2)}) collective-permute-start(f32[2,8,128]{2,1,0:T(8,128)S(1)} %pad_maximum_fusion.4.g0_ref), channel_id=1, source_target_pairs={{0,6},{1,7},{2,0},{3,1},{4,2},{5,3},{6,4},{7,5},{8,14},{9,15},{10,... | collective-permute-start | bytes 24584 | tf_op jit(solution)/shard_map/ppermute | solution.py:367
  138.9 1.8 collective-permute-start.23
  140.6 0.7 collective-permute-start.22
  141.4 1.5 collective-permute-done.23.g2_ref
  142.9 1.5 collective-permute-done.22.g1_ref
  145.0 0.6 copy-done.21
  145.6 2.1 %shard_map.173 = bf16[16,336,128]{2,1,0:T(8,128)(2,1)} custom-call(bf16[80,128]{1,0:T(8,128)(2,1)} %shard_map.172.c0_ref, bf16[80,128]{1,0:T(8,128)(2,1)} %copy-done.21, bf16[80,128]{1,0:T(8,128)(2,1)} %copy-done.20, bf16[80,128]{1,0:T(8,128)(2,1)} %copy-done.19, f32[2,8,128]{2,1,0:T(8,128)} %copy-done.8, f32[2,8,128]{2,1,0:T(8,128)} %copy-done.24, ...), custom_call_target="tpu_custom_call" | custom-call | flops 2000000000 | bytes 1048576 | tf_op jit(solution)/shard_map/pallas_call | solution.py:38
  147.7 24.6 %all_to_all.20.mine_ref = bf16[16,336,128]{2,1,0:T(8,128)(2,1)S(1)} all-to-all(bf16[16,336,128]{2,1,0:T(8,128)(2,1)} %shard_map.173), channel_id=1, replica_groups=mesh['dom'=16,'blk'=8] {'dom'}, dimensions={0} | all-to-all | bytes 2752512 | tf_op jit(solution)/shard_map/all_to_all | solution.py:375
  172.3 3.8 %collective-permute-start.25 = (bf16[16,336,128]{2,1,0:T(8,128)(2,1)S(1)}, bf16[16,336,128]{2,1,0:T(8,128)(2,1)S(1)}, u32[]{:S(2)}, u32[]{:S(2)}) collective-permute-start(bf16[16,336,128]{2,1,0:T(8,128)(2,1)S(1)} %all_to_all.20.mine_ref), channel_id=1, source_target_pairs={{0,1},{1,0},{2,3},{3,2},{4,5},{5,4},{6,7},{7,6},{8,9},{9,8},{10,11... | collective-permute-start | bytes 4128776 | tf_op jit(solution)/shard_map/ppermute | solution.py:371
  176.1 2.8 %collective-permute-done.25.other_ref = bf16[16,336,128]{2,1,0:T(8,128)(2,1)S(1)} collective-permute-done((bf16[16,336,128]{2,1,0:T(8,128)(2,1)S(1)}, bf16[16,336,128]{2,1,0:T(8,128)(2,1)S(1)}, u32[]{:S(2)}, u32[]{:S(2)}) %collective-permute-start.25) | collective-permute-done | bytes 1376288 | tf_op jit(solution)/shard_map/ppermute | solution.py:371
  178.9 1.1 copy-done.3
  179.9 5.2 %shard_map.174 = (f32[5,512,512]{2,1,0:T(8,128)}, f32[8,128]{1,0:T(8,128)}) custom-call(bf16[16,336,128]{2,1,0:T(8,128)(2,1)} %copy-done, bf16[16,336,128]{2,1,0:T(8,128)(2,1)} %copy-done.3), custom_call_target="tpu_custom_call" | custom-call | tf_op jit(solution)/shard_map/pallas_call | solution.py:459
  185.1 1.3 slice_bitcast_fusion.4
  (83 shorter events, 3.5 us)
Async XLA Ops:
  2.6 27.3 %collective-permute-start.2 = (bf16[528,512]{1,0:T(8,128)(2,1)}, bf16[528,512]{1,0:T(8,128)(2,1)S(1)}, u32[]{:S(2)}, u32[]{:S(2)}) collective-permute-start(bf16[528,512]{1,0:T(8,128)(2,1)} %shard_map.165.p0_ref.pay_ref), channel_id=1, source_target_pairs={{0,6},{1,7},{2,0},{3,1},{4,2},{5,3},{6,4},{7,5},{8,14},{9,15},{10,... | collective-permute-start | bytes 1622024 | tf_op jit(solution)/shard_map/ppermute | solution.py:367
  7.2 24.4 %collective-permute-start.1 = (bf16[528,512]{1,0:T(8,128)(2,1)}, bf16[528,512]{1,0:T(8,128)(2,1)S(1)}, u32[]{:S(2)}, u32[]{:S(2)}) collective-permute-start(bf16[528,512]{1,0:T(8,128)(2,1)} %shard_map.165.p0_ref.pay_ref), channel_id=1, source_target_pairs={{0,4},{1,5},{2,6},{3,7},{4,0},{5,1},{6,2},{7,3},{8,12},{9,13},{10,... | collective-permute-start | bytes 1622024 | tf_op jit(solution)/shard_map/ppermute | solution.py:367
  7.2 27.0 %collective-permute-start = (bf16[528,512]{1,0:T(8,128)(2,1)}, bf16[528,512]{1,0:T(8,128)(2,1)}, u32[]{:S(2)}, u32[]{:S(2)}) collective-permute-start(bf16[528,512]{1,0:T(8,128)(2,1)} %shard_map.165.p0_ref.pay_ref), channel_id=1, source_target_pairs={{0,2},{1,3},{2,4},{3,5},{4,6},{5,7},{6,0},{7,1},{8,10},{9,11},{10,... | collective-permute-start | bytes 1622024 | tf_op jit(solution)/shard_map/ppermute | solution.py:367
  7.9 36.3 %collective-permute-start.3 = (bf16[528,512]{1,0:T(8,128)(2,1)}, bf16[528,512]{1,0:T(8,128)(2,1)}, u32[]{:S(2)}, u32[]{:S(2)}) collective-permute-start(bf16[528,512]{1,0:T(8,128)(2,1)} %shard_map.165.p0_ref.pay_ref), channel_id=1, source_target_pairs={{0,1},{1,0},{2,3},{3,2},{4,5},{5,4},{6,7},{7,6},{8,9},{9,8},{10,11... | collective-permute-start | bytes 1622024 | tf_op jit(solution)/shard_map/ppermute | solution.py:371
  12.7 68.8 %all-to-all-start = ((bf16[16,128,512]{2,1,0:T(8,128)(2,1)}), bf16[16,128,512]{2,1,0:T(8,128)(2,1)S(1)}, u32[]{:S(2)}, u32[]{:S(2)}) async-start(bf16[16,128,512]{2,1,0:T(8,128)(2,1)} %shard_map.168), calls=%async_computation | async-start | bytes 4194304 | tf_op jit(solution)/shard_map/all_to_all | solution.py:375
  29.9 14.2 %copy-start.10 = (bf16[528,512]{1,0:T(8,128)(2,1)}, bf16[528,512]{1,0:T(8,128)(2,1)S(1)}, u32[]{:S(2)}) copy-start(bf16[528,512]{1,0:T(8,128)(2,1)S(1)} %collective-permute-done.2.p3_ref) | copy-start | bytes 1622020
  29.9 14.3 %collective-permute-start.6 = (bf16[528,512]{1,0:T(8,128)(2,1)S(1)}, bf16[528,512]{1,0:T(8,128)(2,1)}, u32[]{:S(2)}, u32[]{:S(2)}) collective-permute-start(bf16[528,512]{1,0:T(8,128)(2,1)S(1)} %collective-permute-done.2.p3_ref), channel_id=1, source_target_pairs={{0,1},{1,0},{2,3},{3,2},{4,5},{5,4},{6,7},{7,6},{8,9},{9,8},{10,11... | collective-permute-start | bytes 1622024 | tf_op jit(solution)/shard_map/ppermute | solution.py:371
  31.6 12.6 %copy-start.11 = (bf16[528,512]{1,0:T(8,128)(2,1)}, bf16[528,512]{1,0:T(8,128)(2,1)S(1)}, u32[]{:S(2)}) copy-start(bf16[528,512]{1,0:T(8,128)(2,1)S(1)} %collective-permute-done.1.p2_ref) | copy-start | bytes 1622020
  31.6 12.6 %collective-permute-start.5 = (bf16[528,512]{1,0:T(8,128)(2,1)S(1)}, bf16[528,512]{1,0:T(8,128)(2,1)}, u32[]{:S(2)}, u32[]{:S(2)}) collective-permute-start(bf16[528,512]{1,0:T(8,128)(2,1)S(1)} %collective-permute-done.1.p2_ref), channel_id=1, source_target_pairs={{0,1},{1,0},{2,3},{3,2},{4,5},{5,4},{6,7},{7,6},{8,9},{9,8},{10,11... | collective-permute-start | bytes 1622024 | tf_op jit(solution)/shard_map/ppermute | solution.py:371
  34.2 10.0 %collective-permute-start.4 = (bf16[528,512]{1,0:T(8,128)(2,1)}, bf16[528,512]{1,0:T(8,128)(2,1)}, u32[]{:S(2)}, u32[]{:S(2)}) collective-permute-start(bf16[528,512]{1,0:T(8,128)(2,1)} %collective-permute-done.p1_ref), channel_id=1, source_target_pairs={{0,1},{1,0},{2,3},{3,2},{4,5},{5,4},{6,7},{7,6},{8,9},{9,8},{10,11... | collective-permute-start | bytes 1622024 | tf_op jit(solution)/shard_map/ppermute | solution.py:371
  72.1 8.1 %collective-permute-start.7 = (bf16[2,256,256]{2,1,0:T(8,128)(2,1)}, bf16[2,256,256]{2,1,0:T(8,128)(2,1)S(1)}, u32[]{:S(2)}, u32[]{:S(2)}) collective-permute-start(bf16[2,256,256]{2,1,0:T(8,128)(2,1)} %get-tuple-element.29), channel_id=1, source_target_pairs={{0,6},{1,7},{2,0},{3,1},{4,2},{5,3},{6,4},{7,5},{8,14},{9,15},{10,... | collective-permute-start | bytes 786440 | tf_op jit(solution)/shard_map/ppermute | solution.py:367
  72.7 16.9 %collective-permute-start.8 = (bf16[2,256,256]{2,1,0:T(8,128)(2,1)}, bf16[2,256,256]{2,1,0:T(8,128)(2,1)S(1)}, u32[]{:S(2)}, u32[]{:S(2)}) collective-permute-start(bf16[2,256,256]{2,1,0:T(8,128)(2,1)} %get-tuple-element.30), channel_id=1, source_target_pairs={{0,4},{1,5},{2,6},{3,7},{4,0},{5,1},{6,2},{7,3},{8,12},{9,13},{10,... | collective-permute-start | bytes 786440 | tf_op jit(solution)/shard_map/ppermute | solution.py:367
  73.7 50.8 %collective-permute-start.10 = (bf16[256,256]{1,0:T(8,128)(2,1)S(1)}, bf16[256,256]{1,0:T(8,128)(2,1)S(1)}, u32[]{:S(2)}, u32[]{:S(2)}) collective-permute-start(bf16[256,256]{1,0:T(8,128)(2,1)S(1)} %slice_bitcast_fusion.3), channel_id=1, source_target_pairs={{0,1},{1,0},{2,3},{3,2},{4,5},{5,4},{6,7},{7,6},{8,9},{9,8},{10,11... | collective-permute-start | bytes 393224 | tf_op jit(solution)/shard_map/ppermute | solution.py:371
  74.3 15.4 %collective-permute-start.9 = (bf16[2,256,256]{2,1,0:T(8,128)(2,1)}, bf16[2,256,256]{2,1,0:T(8,128)(2,1)S(1)}, u32[]{:S(2)}, u32[]{:S(2)}) collective-permute-start(bf16[2,256,256]{2,1,0:T(8,128)(2,1)} %get-tuple-element.31), channel_id=1, source_target_pairs={{0,2},{1,3},{2,4},{3,5},{4,6},{5,7},{6,0},{7,1},{8,10},{9,11},{10,... | collective-permute-start | bytes 786440 | tf_op jit(solution)/shard_map/ppermute | solution.py:367
  80.3 2.6 %copy-start.5 = (bf16[2,256,256]{2,1,0:T(8,128)(2,1)}, bf16[2,256,256]{2,1,0:T(8,128)(2,1)S(1)}, u32[]{:S(2)}) copy-start(bf16[2,256,256]{2,1,0:T(8,128)(2,1)S(1)} %collective-permute-done.7.r1_ref) | copy-start | bytes 786436
  80.3 44.2 %collective-permute-start.11 = (bf16[256,256]{1,0:T(8,128)(2,1)S(1)}, bf16[256,256]{1,0:T(8,128)(2,1)S(1)}, u32[]{:S(2)}, u32[]{:S(2)}) collective-permute-start(bf16[256,256]{1,0:T(8,128)(2,1)S(1)} %slice_bitcast_fusion.2), channel_id=1, source_target_pairs={{0,1},{1,0},{2,3},{3,2},{4,5},{5,4},{6,7},{7,6},{8,9},{9,8},{10,11... | collective-permute-start | bytes 393224 | tf_op jit(solution)/shard_map/ppermute | solution.py:371
  81.5 1.4 copy-start.2
  82.9 35.9 %all-to-all-start.1 = ((bf16[16,128,512]{2,1,0:T(8,128)(2,1)}), bf16[16,128,512]{2,1,0:T(8,128)(2,1)S(1)}, u32[]{:S(2)}, u32[]{:S(2)}) async-start(bf16[16,128,512]{2,1,0:T(8,128)(2,1)} %get-tuple-element.39), calls=%async_computation.1 | async-start | bytes 4194304 | tf_op jit(solution)/shard_map/all_to_all | solution.py:375
  89.7 4.1 %copy-start.6 = (bf16[2,256,256]{2,1,0:T(8,128)(2,1)}, bf16[2,256,256]{2,1,0:T(8,128)(2,1)S(1)}, u32[]{:S(2)}) copy-start(bf16[2,256,256]{2,1,0:T(8,128)(2,1)S(1)} %collective-permute-done.8.r2_ref) | copy-start | bytes 786436
  89.7 4.1 %copy-start.7 = (bf16[2,256,256]{2,1,0:T(8,128)(2,1)}, bf16[2,256,256]{2,1,0:T(8,128)(2,1)S(1)}, u32[]{:S(2)}) copy-start(bf16[2,256,256]{2,1,0:T(8,128)(2,1)S(1)} %collective-permute-done.9.r3_ref) | copy-start | bytes 786436
  93.8 1.6 collective-permute-start.14
  95.4 4.7 %collective-permute-start.15 = (bf16[2,64,256]{2,1,0:T(8,128)(2,1)S(1)}, bf16[2,64,256]{2,1,0:T(8,128)(2,1)S(1)}, u32[]{:S(2)}, u32[]{:S(2)}) collective-permute-start(bf16[2,64,256]{2,1,0:T(8,128)(2,1)S(1)} %pad_maximum_fusion.1), channel_id=1, source_target_pairs={{0,2},{1,3},{2,4},{3,5},{4,6},{5,7},{6,0},{7,1},{8,10},{9,11},{10,... | collective-permute-start | bytes 196616 | tf_op jit(solution)/shard_map/ppermute | solution.py:367
  95.5 7.1 %collective-permute-start.16 = (bf16[2,64,256]{2,1,0:T(8,128)(2,1)S(1)}, bf16[2,64,256]{2,1,0:T(8,128)(2,1)S(1)}, u32[]{:S(2)}, u32[]{:S(2)}) collective-permute-start(bf16[2,64,256]{2,1,0:T(8,128)(2,1)S(1)} %pad_maximum_fusion.2), channel_id=1, source_target_pairs={{0,4},{1,5},{2,6},{3,7},{4,0},{5,1},{6,2},{7,3},{8,12},{9,13},{10,... | collective-permute-start | bytes 196616 | tf_op jit(solution)/shard_map/ppermute | solution.py:367
  98.2 4.5 %collective-permute-start.17 = (bf16[2,64,256]{2,1,0:T(8,128)(2,1)S(1)}, bf16[2,64,256]{2,1,0:T(8,128)(2,1)S(1)}, u32[]{:S(2)}, u32[]{:S(2)}) collective-permute-start(bf16[2,64,256]{2,1,0:T(8,128)(2,1)S(1)} %pad_maximum_fusion.3), channel_id=1, source_target_pairs={{0,6},{1,7},{2,0},{3,1},{4,2},{5,3},{6,4},{7,5},{8,14},{9,15},{10,... | collective-permute-start | bytes 196616 | tf_op jit(solution)/shard_map/ppermute | solution.py:367
  100.1 2.6 %copy-start.16 = (bf16[2,64,256]{2,1,0:T(8,128)(2,1)}, bf16[2,64,256]{2,1,0:T(8,128)(2,1)S(1)}, u32[]{:S(2)}) copy-start(bf16[2,64,256]{2,1,0:T(8,128)(2,1)S(1)} %collective-permute-done.15.m1_ref) | copy-start | bytes 196612
  100.1 24.4 %collective-permute-start.12 = (bf16[256,256]{1,0:T(8,128)(2,1)S(1)}, bf16[256,256]{1,0:T(8,128)(2,1)S(1)}, u32[]{:S(2)}, u32[]{:S(2)}) collective-permute-start(bf16[256,256]{1,0:T(8,128)(2,1)S(1)} %slice_bitcast_fusion.1), channel_id=1, source_target_pairs={{0,1},{1,0},{2,3},{3,2},{4,5},{5,4},{6,7},{7,6},{8,9},{9,8},{10,11... | collective-permute-start | bytes 393224 | tf_op jit(solution)/shard_map/ppermute | solution.py:371
  102.6 21.9 %collective-permute-start.13 = (bf16[256,256]{1,0:T(8,128)(2,1)S(1)}, bf16[256,256]{1,0:T(8,128)(2,1)S(1)}, u32[]{:S(2)}, u32[]{:S(2)}) collective-permute-start(bf16[256,256]{1,0:T(8,128)(2,1)S(1)} %slice_bitcast_fusion), channel_id=1, source_target_pairs={{0,1},{1,0},{2,3},{3,2},{4,5},{5,4},{6,7},{7,6},{8,9},{9,8},{10,11... | collective-permute-start | bytes 393224 | tf_op jit(solution)/shard_map/ppermute | solution.py:371
  118.7 5.8 %copy-start.1 = (bf16[16,128,512]{2,1,0:T(8,128)(2,1)}, bf16[16,128,512]{2,1,0:T(8,128)(2,1)S(1)}, u32[]{:S(2)}) copy-start(bf16[16,128,512]{2,1,0:T(8,128)(2,1)S(1)} %all-to-all-done.1.back_ref) | copy-start | bytes 6291460
  118.7 13.6 %all-to-all-start.2 = ((bf16[16,80,128]{2,1,0:T(8,128)(2,1)}), bf16[16,80,128]{2,1,0:T(8,128)(2,1)S(1)}, u32[]{:S(2)}, u32[]{:S(2)}) async-start(bf16[16,80,128]{2,1,0:T(8,128)(2,1)} %shard_map.170), calls=%async_computation.2 | async-start | bytes 655360 | tf_op jit(solution)/shard_map/all_to_all | solution.py:375
  124.5 0.7 copy-start.12
  124.5 0.7 copy-start.13
  124.5 0.8 copy-start.14
  124.5 0.8 copy-start.15
  130.8 5.9 %copy-start.9 = (f32[8,128]{1,0:T(8,128)S(1)}, f32[8,128]{1,0:T(8,128)}, u32[]{:S(2)}) copy-start(f32[8,128]{1,0:T(8,128)} %get-tuple-element.45) | copy-start | bytes 12292
  130.8 5.9 %collective-permute-start.21 = (f32[8,128]{1,0:T(8,128)}, f32[8,128]{1,0:T(8,128)S(1)}, u32[]{:S(2)}, u32[]{:S(2)}) collective-permute-start(f32[8,128]{1,0:T(8,128)} %get-tuple-element.45), channel_id=1, source_target_pairs={{0,1},{1,0},{2,3},{3,2},{4,5},{5,4},{6,7},{7,6},{8,9},{9,8},{10,11... | collective-permute-start | bytes 12296 | tf_op jit(solution)/shard_map/ppermute | solution.py:371
  132.3 0.7 copy-start.4
  134.7 9.7 %collective-permute-start.20 = (bf16[80,128]{1,0:T(8,128)(2,1)}, bf16[80,128]{1,0:T(8,128)(2,1)S(1)}, u32[]{:S(2)}, u32[]{:S(2)}) collective-permute-start(bf16[80,128]{1,0:T(8,128)(2,1)} %shard_map.172.c0_ref), channel_id=1, source_target_pairs={{0,6},{1,7},{2,0},{3,1},{4,2},{5,3},{6,4},{7,5},{8,14},{9,15},{10,... | collective-permute-start | bytes 61448 | tf_op jit(solution)/shard_map/ppermute | solution.py:367
  136.1 8.3 %collective-permute-start.19 = (bf16[80,128]{1,0:T(8,128)(2,1)}, bf16[80,128]{1,0:T(8,128)(2,1)S(1)}, u32[]{:S(2)}, u32[]{:S(2)}) collective-permute-start(bf16[80,128]{1,0:T(8,128)(2,1)} %shard_map.172.c0_ref), channel_id=1, source_target_pairs={{0,4},{1,5},{2,6},{3,7},{4,0},{5,1},{6,2},{7,3},{8,12},{9,13},{10,... | collective-permute-start | bytes 61448 | tf_op jit(solution)/shard_map/ppermute | solution.py:367
  136.1 8.3 %collective-permute-start.18 = (bf16[80,128]{1,0:T(8,128)(2,1)}, bf16[80,128]{1,0:T(8,128)(2,1)S(1)}, u32[]{:S(2)}, u32[]{:S(2)}) collective-permute-start(bf16[80,128]{1,0:T(8,128)(2,1)} %shard_map.172.c0_ref), channel_id=1, source_target_pairs={{0,2},{1,3},{2,4},{3,5},{4,6},{5,7},{6,0},{7,1},{8,10},{9,11},{10,... | collective-permute-start | bytes 61448 | tf_op jit(solution)/shard_map/ppermute | solution.py:367
  136.7 7.7 %copy-start.8 = (f32[2,8,128]{2,1,0:T(8,128)}, f32[2,8,128]{2,1,0:T(8,128)S(1)}, u32[]{:S(2)}) copy-start(f32[2,8,128]{2,1,0:T(8,128)S(1)} %pad_maximum_fusion.4.g0_ref) | copy-start | bytes 24580
  136.7 3.9 %collective-permute-start.24 = (f32[2,8,128]{2,1,0:T(8,128)S(1)}, f32[2,8,128]{2,1,0:T(8,128)S(1)}, u32[]{:S(2)}, u32[]{:S(2)}) collective-permute-start(f32[2,8,128]{2,1,0:T(8,128)S(1)} %pad_maximum_fusion.4.g0_ref), channel_id=1, source_target_pairs={{0,6},{1,7},{2,0},{3,1},{4,2},{5,3},{6,4},{7,5},{8,14},{9,15},{10,... | collective-permute-start | bytes 24584 | tf_op jit(solution)/shard_map/ppermute | solution.py:367
  138.9 4.0 %collective-permute-start.23 = (f32[2,8,128]{2,1,0:T(8,128)S(1)}, f32[2,8,128]{2,1,0:T(8,128)S(1)}, u32[]{:S(2)}, u32[]{:S(2)}) collective-permute-start(f32[2,8,128]{2,1,0:T(8,128)S(1)} %pad_maximum_fusion.4.g0_ref), channel_id=1, source_target_pairs={{0,4},{1,5},{2,6},{3,7},{4,0},{5,1},{6,2},{7,3},{8,12},{9,13},{10,... | collective-permute-start | bytes 24584 | tf_op jit(solution)/shard_map/ppermute | solution.py:367
  140.6 3.8 %copy-start.22 = (f32[2,8,128]{2,1,0:T(8,128)}, f32[2,8,128]{2,1,0:T(8,128)S(1)}, u32[]{:S(2)}) copy-start(f32[2,8,128]{2,1,0:T(8,128)S(1)} %collective-permute-done.24.g3_ref) | copy-start | bytes 24580
  140.6 3.7 %collective-permute-start.22 = (f32[2,8,128]{2,1,0:T(8,128)S(1)}, f32[2,8,128]{2,1,0:T(8,128)S(1)}, u32[]{:S(2)}, u32[]{:S(2)}) collective-permute-start(f32[2,8,128]{2,1,0:T(8,128)S(1)} %pad_maximum_fusion.4.g0_ref), channel_id=1, source_target_pairs={{0,2},{1,3},{2,4},{3,5},{4,6},{5,7},{6,0},{7,1},{8,10},{9,11},{10,... | collective-permute-start | bytes 24584 | tf_op jit(solution)/shard_map/ppermute | solution.py:367
  142.9 1.5 copy-start.23
  172.3 6.6 %copy-start = (bf16[16,336,128]{2,1,0:T(8,128)(2,1)}, bf16[16,336,128]{2,1,0:T(8,128)(2,1)S(1)}, u32[]{:S(2)}) copy-start(bf16[16,336,128]{2,1,0:T(8,128)(2,1)S(1)} %all_to_all.20.mine_ref) | copy-start | bytes 4128772
  172.3 6.6 %collective-permute-start.25 = (bf16[16,336,128]{2,1,0:T(8,128)(2,1)S(1)}, bf16[16,336,128]{2,1,0:T(8,128)(2,1)S(1)}, u32[]{:S(2)}, u32[]{:S(2)}) collective-permute-start(bf16[16,336,128]{2,1,0:T(8,128)(2,1)S(1)} %all_to_all.20.mine_ref), channel_id=1, source_target_pairs={{0,1},{1,0},{2,3},{3,2},{4,5},{5,4},{6,7},{7,6},{8,9},{9,8},{10,11... | collective-permute-start | bytes 4128776 | tf_op jit(solution)/shard_map/ppermute | solution.py:371
  178.9 1.1 copy-start.3
  (6 other events, 3.7 us)

commit v3 on v2

--- a/solution.py
+++ b/solution.py
@@ -54,10 +54,11 @@
     return lax.shift_right_logical(me, 1), me & 1
 
 
-def norm_body(pattern_ref, x_ref, gain_ref, label_ref, grad_ref, out_ref):
+def norm_body(pattern_ref, counts_ref, x_ref, gain_ref, label_ref, grad_ref, rows_ref, out_ref, slots_ref):
     x = x_ref[...].astype(F32)
     scale = lax.rsqrt(jnp.mean(x * x, axis=-1, keepdims=True) + EPS)
-    out_ref[0:ROWS, :] = (x * scale * gain_ref[...]).astype(BF16)
+    normed = (x * scale * gain_ref[...]).astype(BF16)
+    out_ref[0:ROWS, :] = normed
     out_ref[ROWS : 2 * ROWS, :] = grad_ref[...]
     row = lax.broadcasted_iota(jnp.int32, (16, ROWS), 0)
     lane = lax.broadcasted_iota(jnp.int32, (16, ROWS), 1)
@@ -67,16 +68,12 @@
         tail = jnp.where((row == 1 + b) & (lane >= 0), flag, tail)
     out_ref[2 * ROWS : PAY, 0:ROWS] = tail.astype(BF16)
     out_ref[2 * ROWS : PAY, ROWS:D] = jnp.zeros((16, D - ROWS), BF16)
-
-
-def outgoing_body(counts_ref, pay_ref, rows_ref, out_ref):
-    normed = pay_ref[0:ROWS, :]
     columns = jnp.transpose(rows_ref[...].astype(F32))
     lane = lax.broadcasted_iota(jnp.int32, (CAP, ROWS), 1).astype(F32)
     slot = lax.broadcasted_iota(jnp.int32, (CAP, ROWS), 0)
     for p in range(DOM):
         hit = (lane == columns[:, p : p + 1]) & (slot < counts_ref[p])
-        out_ref[p] = dot(jnp.where(hit, 1.0, 0.0).astype(BF16), normed).astype(BF16)
+        slots_ref[p] = dot(jnp.where(hit, 1.0, 0.0).astype(BF16), normed).astype(BF16)
 
 
 E_ROWS = 4
@@ -147,7 +144,7 @@
 def attention_body(
     p0_ref, p1_ref, p2_ref, p3_ref, p4_ref, p5_ref, p6_ref, p7_ref, wqkv_ref, wo_ref,
     r0_ref, r1_ref, r2_ref, r3_ref, dw_ref,
-    y_ref, s_ref, qt_ref, kt_ref, k_ref, v_ref, vt_ref, w_ref, dq_ref, dk_ref, dv_ref, at_ref, ga_ref,
+    y_ref, s_ref, qt_ref, kt_ref, k_ref, v_ref, vt_ref, w_ref, dq_ref, dk_ref, dv_ref, at_ref, ga_ref, sl_ref, qr_ref, gr_ref,
 ):
     pays = (p0_ref, p1_ref, p2_ref, p3_ref, p4_ref, p5_ref, p6_ref, p7_ref)
     outs = (r0_ref, r1_ref, r2_ref, r3_ref)
@@ -181,8 +178,7 @@
         vt_ref[r] = value[0:80].astype(BF16)
         v_ref[r] = jnp.transpose(value).astype(BF16)
         ga_ref[r] = dot(wo_ref[...], pay[ROWS : 2 * ROWS, :], NT)
-        dk_ref[r] = jnp.zeros((HEAD, ROWS), F32)
-        dv_ref[r] = jnp.zeros((HEAD, ROWS), F32)
+        qr_ref[r] = jnp.transpose(qt_ref[r].astype(F32)).astype(BF16)
 
     keys_t = jnp.concatenate([kt_ref[j] for j in range(BLK)], axis=1)
     values_t = jnp.concatenate([vt_ref[j] for j in range(BLK)], axis=1)
@@ -191,8 +187,8 @@
         query = qt_ref[i]
         for j in range(BLK):
             scores = dot(k_ref[j], query)
-            w_ref[j] = jnp.exp2(scores * SCORE_MUL - SCORE_SUB).astype(BF16)
-        numer = dot(values_t, w_ref[...].reshape(BLK * ROWS, ROWS))
+            w_ref[i, j] = jnp.exp2(scores * SCORE_MUL - SCORE_SUB).astype(BF16)
+        numer = dot(values_t, w_ref[i].reshape(BLK * ROWS, ROWS))
         inverse = 1.0 / numer[HEAD : HEAD + 1]
         attn = (numer[0:HEAD] * inverse).astype(BF16)
         at_ref[i] = attn
@@ -201,17 +197,25 @@
         coarse = minus.astype(BF16).astype(F32)
         extra = jnp.where(row == 0, coarse, jnp.where(row == 1, minus - coarse, 0.0))
         grad = jnp.concatenate([grad_attn * inverse, extra], axis=0).astype(BF16)
-        dq = jnp.zeros((HEAD, ROWS), F32)
+        gr_ref[i] = jnp.transpose(grad.astype(F32)).astype(BF16)
         for j in range(BLK):
-            weights = w_ref[j]
-            slopes = (weights.astype(F32) * dot(v_ref[j], grad)).astype(BF16)
-            dq = dq + dot(kt_ref[j], slopes)
-            dk_ref[j] += dot(query[0:HEAD], slopes, NT)
-            dv_ref[j] += dot(grad[0:HEAD], weights, NT)
-        dq_ref[i] = dq
+            sl_ref[i, j] = (w_ref[i, j].astype(F32) * dot(v_ref[j], grad)).astype(BF16)
+        dq_ref[i] = dot(keys_t, sl_ref[i].reshape(BLK * ROWS, ROWS))
         return carry
 
     lax.fori_loop(0, BLK, query_block, 0)
+
+    queries = jnp.concatenate([qr_ref[i] for i in range(BLK)], axis=0)
+    grads = jnp.concatenate([gr_ref[i] for i in range(BLK)], axis=0)
+
+    def key_block(j, carry):
+        slopes = jnp.concatenate([sl_ref[i, j] for i in range(BLK)], axis=1)
+        dk_ref[j] = jnp.transpose(dot(slopes, queries))[0:HEAD]
+        weights = jnp.concatenate([w_ref[i, j] for i in range(BLK)], axis=1)
+        dv_ref[j] = jnp.transpose(dot(weights, grads))[0:HEAD]
+        return carry
+
+    lax.fori_loop(0, BLK, key_block, 0)
 
     dw = jnp.zeros((192, D), F32)
     dwo = jnp.zeros((HEAD, D), F32)
@@ -249,26 +253,33 @@
             out_ref[a * 4 + b, 64:80, :] = total[a * 16 : (a + 1) * 16, b * 128 : (b + 1) * 128].astype(BF16)
 
 
-def chunk_sum_body(in_ref, out_ref):
+def chunk_sum_body(in_ref, g0_ref, g1_ref, out_ref):
     total = in_ref[0].astype(F32)
     for p in range(1, DOM):
         total = total + in_ref[p].astype(F32)
-    out_ref[...] = total.astype(BF16)
-
-
-def spread_body(c0_ref, c1_ref, c2_ref, c3_ref, g0_ref, g1_ref, g2_ref, g3_ref, out_ref, gains_ref):
-    z, core = position()
-    for dz, g_ref in enumerate((g0_ref, g1_ref, g2_ref, g3_ref)):
-        gains_ref[dz] = g_ref[...]
+    out_ref[0:CHUNK, :] = total.astype(BF16)
+    z, core = position()
+    one, two = g0_ref[...], g1_ref[...]
+    gain = jnp.where(core == 0, one, two) + jnp.where(core == 0, two, one)
+    coarse = gain.astype(BF16).astype(F32)
+    fine = gain - coarse
+    out_ref[CHUNK : CHUNK + 16, :] = jnp.concatenate([coarse, fine], axis=0).astype(BF16)
+
+
+def spread_body(c0_ref, c1_ref, c2_ref, c3_ref, out_ref, gains_ref):
+    z, core = position()
+    for dz, c_ref in enumerate((c0_ref, c1_ref, c2_ref, c3_ref)):
+        tail = c_ref[CHUNK : CHUNK + 16, :].astype(F32)
+        gains_ref[dz] = tail[0:8] + tail[8:16]
     gain = jnp.zeros((8, 128), F32)
-    for b in range(BLK):
-        gain = gain + gains_ref[(z - (b >> 1)) & 3, core ^ (b & 1)]
+    for chip in range(4):
+        gain = gain + gains_ref[(z - chip) & 3]
     coarse = gain.astype(BF16).astype(F32)
     fine = (gain - coarse).astype(BF16).astype(F32)
     tail = jnp.concatenate([coarse, fine], axis=0).astype(BF16)
     for p in range(DOM):
         for dz, c_ref in enumerate((c0_ref, c1_ref, c2_ref, c3_ref)):
-            out_ref[p, dz * CHUNK : (dz + 1) * CHUNK, :] = c_ref[...]
+            out_ref[p, dz * CHUNK : (dz + 1) * CHUNK, :] = c_ref[0:CHUNK, :]
         out_ref[p, 4 * CHUNK : SPREAD, :] = tail
 
 
@@ -328,7 +339,8 @@
         for p in range(DOM):
             tail = mine_ref[p, 4 * CHUNK : SPREAD, :].astype(F32)
             gain = gain + (tail[0:8] + tail[8:16])
-        gain_ref[...] = gain
+        for k in range(4):
+            gain_ref[:, k * 128 : (k + 1) * 128] = gain[k : k + 1, :]
 
     for c in range(2):
         @pl.when(core == c)
@@ -379,11 +391,15 @@
     x, gain, wq, wk, wv, wo, wm, cluster, pattern, send_rows, send_counts, edge_src, edge_dst, out_grad
 ):
     gain_row = gain.reshape(1, D)
-    pay = call(norm_body, shape((PAY, D), BF16), (pattern, x, gain_row, cluster.reshape(1, ROWS), out_grad), scalars=1)
+    pay, outgoing = call(
+        norm_body,
+        (shape((PAY, D), BF16), shape((DOM, CAP, D), BF16)),
+        (pattern, send_counts, x, gain_row, cluster.reshape(1, ROWS), out_grad, send_rows),
+        scalars=2,
+        micros=4,
+    )
+    incoming = to_dom_peers(outgoing)
     pays = [pay] + [along_chips(pay, step) for step in (1, 2, 3)]
-    pays = pays + [other_core(part) for part in pays]
-    outgoing = call(outgoing_body, shape((DOM, CAP, D), BF16), (send_counts, pay, send_rows), scalars=1, micros=3)
-    incoming = to_dom_peers(outgoing)
 
     counts_t, degree, slot_grads, wqkv, wo_head = call(
         edges_body,
@@ -395,6 +411,8 @@
         scratch=[pltpu.VMEM((512, 1024), F32)],
         micros=10,
     )
+    *pays, degree = lax.optimization_barrier((*pays, degree))
+    pays = pays + [other_core(part) for part in pays]
     incoming, slot_grads = lax.optimization_barrier((incoming, slot_grads))
     back = to_dom_peers(slot_grads)
 
@@ -409,6 +427,7 @@
     means = [jnp.stack([mine[dz], other[dz]]) for dz in range(4)]
     means = [means[0]] + [along_chips(means[dz], dz) for dz in (1, 2, 3)]
 
+    *pays, base = lax.optimization_barrier((*pays, base))
     *results, dw = call(
         attention_body,
         (*[shape((2, ROWS, 256), BF16)] * 4, shape((256, D), F32)),
@@ -421,20 +440,22 @@
             pltpu.VMEM((BLK, ROWS, 128), BF16),
             pltpu.VMEM((BLK, ROWS, 128), BF16),
             pltpu.VMEM((BLK, 80, ROWS), BF16),
-            pltpu.VMEM((BLK, ROWS, ROWS), BF16),
+            pltpu.VMEM((BLK, BLK, ROWS, ROWS), BF16),
             pltpu.VMEM((BLK, HEAD, ROWS), F32),
             pltpu.VMEM((BLK, HEAD, ROWS), F32),
             pltpu.VMEM((BLK, HEAD, ROWS), F32),
             pltpu.VMEM((BLK, HEAD, ROWS), BF16),
             pltpu.VMEM((BLK, HEAD, ROWS), F32),
+            pltpu.VMEM((BLK, BLK, ROWS, ROWS), BF16),
+            pltpu.VMEM((BLK, ROWS, 128), BF16),
+            pltpu.VMEM((BLK, ROWS, 128), BF16),
         ],
         micros=30,
     )
 
     chunks = call(chunks_body, shape((DOM, CHUNK, 128), BF16), (*pays, *means, dw), micros=3)
     chunks, back = lax.optimization_barrier((chunks, back))
-    chunk = call(chunk_sum_body, shape((CHUNK, 128), BF16), (to_dom_peers(chunks),), micros=1)
-    chunk_parts = [chunk] + [along_chips(chunk, step) for step in (1, 2, 3)]
+    chunks = to_dom_peers(chunks)
 
     results = [results[0]] + [along_chips(results[dz], -dz) for dz in (1, 2, 3)]
     swapped = [other_core(part[1]) for part in results]
@@ -446,24 +467,21 @@
         scalars=1,
         micros=5,
     )
-    gain_part = jnp.stack([gain_part, other_core(gain_part)])
-    gain_parts = [gain_part] + [along_chips(gain_part, step) for step in (1, 2, 3)]
-    spread = call(
-        spread_body,
-        shape((DOM, SPREAD, 128), BF16),
-        (*chunk_parts, *gain_parts),
-        scratch=[pltpu.VMEM((4, 2, 8, 128), F32)],
-    )
+    chunk = call(
+        chunk_sum_body, shape((CHUNK + 16, 128), BF16), (chunks, gain_part, other_core(gain_part)), micros=1
+    )
+    chunk_parts = [chunk] + [along_chips(chunk, step) for step in (1, 2, 3)]
+    spread = call(spread_body, shape((DOM, SPREAD, 128), BF16), chunk_parts, scratch=[pltpu.VMEM((4, 8, 128), F32)])
     gathered = to_dom_peers(spread)
     whole = pl.BlockSpec((DOM, SPREAD, 128), lambda t: (0, 0, 0))
     weight_grads, gain_grad = pl.pallas_call(
         weights_body,
         grid=(5,),
-        out_shape=(shape((5, D, D), F32), shape((8, 128), F32)),
+        out_shape=(shape((5, D, D), F32), shape((1, D), F32)),
         in_specs=[whole, whole],
-        out_specs=(pl.BlockSpec((1, D, D), lambda t: (t, 0, 0)), pl.BlockSpec((8, 128), lambda t: (0, 0))),
+        out_specs=(pl.BlockSpec((1, D, D), lambda t: (t, 0, 0)), pl.BlockSpec((1, D), lambda t: (0, 0))),
     )(gathered, other_core(gathered))
-    return layer_out, feature_grad, weight_grads, gain_grad[0:4].reshape(D)
+    return layer_out, feature_grad, weight_grads, gain_grad.reshape(D)
 
 
 def solution(mesh):

time: 187 us -> 171 us (0.914)
  Pallas kernels: 64.3 us -> 57.5 us
  waiting for transfers between devices: 37.3 us -> 30.8 us
  local copies, waits for them, and re-layouts: 8.78 us -> 6.05 us
    all_to_all x3, waiting for transfers between devices: 11.8 us -> 0.48 us  [to_dom_peers(): return lax.all_to_all(array, 'dom', split_axis=0, concat_axis=0, tiled=True)]
    pallas_call x9 -> x8, Pallas kernels: 59.2 us -> 52.4 us  [call(): pl.pallas_call(body, out_shape=out_shape, in_specs=specs, out_specs=jax.t...]
    ppermute x11, starting transfers between devices: 14.3 us -> 9.9 us  [other_core(): return lax.ppermute(array, 'blk', chip_shift(0, 1))]
    ppermute x15 -> x12, waiting for transfers between devices: 22.3 us -> 26.5 us  [along_chips(): return lax.ppermute(array, 'blk', chip_shift(step, 0))]
    ppermute x15 -> x12, starting transfers between devices: 16.2 us -> 18.4 us  [along_chips(): return lax.ppermute(array, 'blk', chip_shift(step, 0))]
    all_to_all x3, starting transfers between devices: 19.2 us -> 21.3 us  [to_dom_peers(): return lax.all_to_all(array, 'dom', split_axis=0, concat_axis=0, tiled=True)]
    unnamed x50 -> x36, local copies, waits for them, and re-layouts: 5.76 us -> 5.09 us
  transfers between devices with their start and end apart: 29 -> 26, of which waited for: 9 -> 11; matrix products, arithmetic and copies ran while one was open for 1% -> 1% of each run, Pallas kernels for 30% -> 27%
where the time goes in v3:
time: 171 us; the launch traced here: 170 us
  Pallas kernels  57.5 us (34%)
  starting transfers between devices  49.6 us (29%)
  waiting for transfers between devices  30.8 us (18%)
  blocking collectives  24.6 us (14%)
  local copies, waits for them, and re-layouts  6.05 us (4%)
    pallas_call x8, Pallas kernels, call(): pl.pallas_call(body, out_shape=out_shape, in_specs=specs, out_specs=jax.t...  52.4 us
    ppermute x12, waiting for transfers between devices, along_chips(): return lax.ppermute(array, 'blk', chip_shift(step, 0))  26.5 us
    all_to_all x1, blocking collectives, to_dom_peers(): return lax.all_to_all(array, 'dom', split_axis=0, concat_axis=0, tiled=True)  24.6 us
    all_to_all x3, starting transfers between devices, to_dom_peers(): return lax.all_to_all(array, 'dom', split_axis=0, concat_axis=0, tiled=True)  21.3 us
    ppermute x12, starting transfers between devices, along_chips(): return lax.ppermute(array, 'blk', chip_shift(step, 0))  18.4 us
    ppermute x11, starting transfers between devices, other_core(): return lax.ppermute(array, 'blk', chip_shift(0, 1))  9.9 us
    pallas_call x1, Pallas kernels, local(): pl.pallas_call(weights_body, grid=(5,), out_shape=(shape((5, D, D), F32),...  5.19 us
    unnamed x36, local copies, waits for them, and re-layouts  5.09 us
  transfers between devices with their start and end apart: 26, of which 11 were waited for; matrix products, arithmetic and copies ran while one was open for 1% of the time, Pallas kernels for 27%

profile of v3, /device:TPU:1, one launch (start us, length us, event | category | flops | bytes accessed | tf_op | source)
XLA Modules:
  0.0 170.1 jit_solution(5304654755482648598)
XLA Ops:
  0.6 3.4 %shard_map.165 = (bf16[528,512]{1,0:T(8,128)(2,1)}, bf16[16,128,512]{2,1,0:T(8,128)(2,1)}) custom-call(s32[1,8]{1,0:T(1,128)} %pattern_ref.1, s32[16]{0:T(128)} %counts_ref.3, bf16[256,512]{1,0:T(8,128)(2,1)} %x_ref.5, f32[1,512]{1,0:T(1,128)} %bitcast.15, s32[1,256]{1,0:T(1,128)} %bitcast.18, bf16[256,512]{1,0:T(8,128)(2,1)} %grad_ref.5, s32[16,128]{1,0:T(8,128)} %rows_ref.3), custom_call_target="tpu_custom_call" | custom-call | flops 4000000000 | bytes 1048576 | tf_op jit(solution)/shard_map/pallas_call | solution.py:38
  4.1 7.7 %all-to-all-start = ((bf16[16,128,512]{2,1,0:T(8,128)(2,1)}), bf16[16,128,512]{2,1,0:T(8,128)(2,1)S(1)}, u32[]{:S(2)}, u32[]{:S(2)}) async-start(bf16[16,128,512]{2,1,0:T(8,128)(2,1)} %get-tuple-element.50), calls=%async_computation | async-start | bytes 4194304 | tf_op jit(solution)/shard_map/all_to_all | solution.py:387
  11.8 3.8 %collective-permute-start.2 = (bf16[528,512]{1,0:T(8,128)(2,1)S(1)}, bf16[528,512]{1,0:T(8,128)(2,1)S(1)}, u32[]{:S(2)}, u32[]{:S(2)}) collective-permute-start(bf16[528,512]{1,0:T(8,128)(2,1)S(1)} %copy-done.9), channel_id=1, source_target_pairs={{0,6},{1,7},{2,0},{3,1},{4,2},{5,3},{6,4},{7,5},{8,14},{9,15},{10,... | collective-permute-start | bytes 1622024 | tf_op jit(solution)/shard_map/ppermute | solution.py:379
  15.6 0.7 collective-permute-start
  16.3 9.0 %shard_map.166 = (bf16[1024,512]{1,0:T(8,128)(2,1)}, f32[256,128]{1,0:T(8,128)}, bf16[16,128,512]{2,1,0:T(8,128)(2,1)}, bf16[192,512]{1,0:T(8,128)(2,1)}, bf16[64,512]{1,0:T(8,128)(2,1)}) custom-call(s32[32,128]{1,0:T(8,128)} %bitcast.13, s32[32,128]{1,0:T(8,128)} %bitcast.14, bf16[256,512]{1,0:T(8,128)(2,1)} %grad_ref.5, bf16[512,512]{1,0:T(8,128)(2,1)} %w_ref.3, ...), custom_call_target="tpu_custom_call" | custom-call | flops 10000000000 | bytes 1048576 | tf_op jit(solution)/shard_map/pallas_call | solution.py:38
  25.3 12.4 %collective-permute-done.2.p3_ref = bf16[528,512]{1,0:T(8,128)(2,1)S(1)} collective-permute-done((bf16[528,512]{1,0:T(8,128)(2,1)S(1)}, bf16[528,512]{1,0:T(8,128)(2,1)S(1)}, u32[]{:S(2)}, u32[]{:S(2)}) %collective-permute-start.2) | collective-permute-done | bytes 540704 | tf_op jit(solution)/shard_map/ppermute | solution.py:379
  37.7 4.7 %collective-permute-done.p1_ref = bf16[528,512]{1,0:T(8,128)(2,1)} collective-permute-done((bf16[528,512]{1,0:T(8,128)(2,1)S(1)}, bf16[528,512]{1,0:T(8,128)(2,1)}, u32[]{:S(2)}, u32[]{:S(2)}) %collective-permute-start) | collective-permute-done | bytes 540704 | tf_op jit(solution)/shard_map/ppermute | solution.py:379
  42.4 0.8 collective-permute-start.3
  43.2 0.5 collective-permute-start.5
  43.7 1.3 copy-done.2
  45.1 6.7 %all-to-all-start.1 = ((bf16[16,128,512]{2,1,0:T(8,128)(2,1)}), bf16[16,128,512]{2,1,0:T(8,128)(2,1)S(1)}, u32[]{:S(2)}, u32[]{:S(2)}) async-start(bf16[16,128,512]{2,1,0:T(8,128)(2,1)} %get-tuple-element.71), calls=%async_computation.1 | async-start | bytes 4194304 | tf_op jit(solution)/shard_map/all_to_all | solution.py:387
  51.7 3.9 %shard_map.167 = (bf16[4,64,256]{2,1,0:T(8,128)(2,1)}, bf16[4,64,256]{2,1,0:T(8,128)(2,1)}, f32[256,512]{1,0:T(8,128)}) custom-call(bf16[1024,512]{1,0:T(8,128)(2,1)} %get-tuple-element.48.counts_t_ref, f32[256,128]{1,0:T(8,128)} %get-tuple-element.49.degree_ref, bf16[16,128,512]{2,1,0:T(8,128)(2,1)} %copy-done.2, bf16[256,512]{1,0:T(8,128)(2,1)} %x_ref.5, ...), custom_call_target="tpu_custom_call" | custom-call | flops 4000000000 | bytes 1048576 | tf_op jit(solution)/shard_map/pallas_call | solution.py:38
  55.7 0.8 collective-permute-start.14
  56.5 23.2 %shard_map.168 = (bf16[2,256,256]{2,1,0:T(8,128)(2,1)}, bf16[2,256,256]{2,1,0:T(8,128)(2,1)}, bf16[2,256,256]{2,1,0:T(8,128)(2,1)}, bf16[2,256,256]{2,1,0:T(8,128)(2,1)}, f32[256,512]{1,0:T(8,128)}) custom-call(bf16[528,512]{1,0:T(8,128)(2,1)} %get-tuple-element.54.p0_ref, bf16[528,512]{1,0:T(8,128)(2,1)} %collective-permute-done.p1_ref, ...), custom_call_target="tpu_custom_call" | custom-call | flops 30000001024 | bytes 1048576 | tf_op jit(solution)/shard_map/pallas_call | solution.py:38
  79.7 0.9 slice_bitcast_fusion.3
  80.7 0.7 collective-permute-start.7
  81.4 0.9 collective-permute-start.9
  82.3 1.9 %collective-permute-start.15 = (bf16[2,64,256]{2,1,0:T(8,128)(2,1)S(1)}, bf16[2,64,256]{2,1,0:T(8,128)(2,1)S(1)}, u32[]{:S(2)}, u32[]{:S(2)}) collective-permute-start(bf16[2,64,256]{2,1,0:T(8,128)(2,1)S(1)} %pad_maximum_fusion.1), channel_id=1, source_target_pairs={{0,2},{1,3},{2,4},{3,5},{4,6},{5,7},{6,0},{7,1},{8,10},{9,11},{10,... | collective-permute-start | bytes 196616 | tf_op jit(solution)/shard_map/ppermute | solution.py:379
  84.2 0.6 pad_maximum_fusion.m0_ref
  84.8 3.6 %collective-permute-done.7.r1_ref = bf16[2,256,256]{2,1,0:T(8,128)(2,1)S(1)} collective-permute-done((bf16[2,256,256]{2,1,0:T(8,128)(2,1)}, bf16[2,256,256]{2,1,0:T(8,128)(2,1)S(1)}, u32[]{:S(2)}, u32[]{:S(2)}) %collective-permute-start.7) | collective-permute-done | bytes 262176 | tf_op jit(solution)/shard_map/ppermute | solution.py:379
  88.4 0.4 collective-permute-start.16
  88.8 1.4 collective-permute-done.8.r2_ref
  90.2 6.2 %collective-permute-start.17 = (bf16[2,64,256]{2,1,0:T(8,128)(2,1)S(1)}, bf16[2,64,256]{2,1,0:T(8,128)(2,1)S(1)}, u32[]{:S(2)}, u32[]{:S(2)}) collective-permute-start(bf16[2,64,256]{2,1,0:T(8,128)(2,1)S(1)} %pad_maximum_fusion.3), channel_id=1, source_target_pairs={{0,6},{1,7},{2,0},{3,1},{4,2},{5,3},{6,4},{7,5},{8,14},{9,15},{10,... | collective-permute-start | bytes 196616 | tf_op jit(solution)/shard_map/ppermute | solution.py:379
  96.4 0.5 collective-permute-done.9.r3_ref
  96.9 2.0 %collective-permute-start.11 = (bf16[256,256]{1,0:T(8,128)(2,1)S(1)}, bf16[256,256]{1,0:T(8,128)(2,1)}, u32[]{:S(2)}, u32[]{:S(2)}) collective-permute-start(bf16[256,256]{1,0:T(8,128)(2,1)S(1)} %slice_bitcast_fusion.2), channel_id=1, source_target_pairs={{0,1},{1,0},{2,3},{3,2},{4,5},{5,4},{6,7},{7,6},{8,9},{9,8},{10,11... | collective-permute-start | bytes 393224 | tf_op jit(solution)/shard_map/ppermute | solution.py:383
  99.0 0.5 collective-permute-start.12
  99.5 0.7 collective-permute-start.13
  100.3 0.6 copy-done.13
  100.9 3.6 %shard_map.169 = bf16[16,80,128]{2,1,0:T(8,128)(2,1)} custom-call(bf16[528,512]{1,0:T(8,128)(2,1)} %get-tuple-element.54.p0_ref, bf16[528,512]{1,0:T(8,128)(2,1)} %collective-permute-done.p1_ref, bf16[528,512]{1,0:T(8,128)(2,1)} %collective-permute-done.1.p2_ref, bf16[528,512]{1,0:T(8,128)(2,1)} %copy-done.10, ...), custom_call_target="tpu_custom_call" | custom-call | flops 3000000000 | bytes 1048576 | tf_op jit(solution)/shard_map/pallas_call | solution.py:38
  104.6 7.0 %all-to-all-start.2 = ((bf16[16,80,128]{2,1,0:T(8,128)(2,1)}), bf16[16,80,128]{2,1,0:T(8,128)(2,1)S(1)}, u32[]{:S(2)}, u32[]{:S(2)}) async-start(bf16[16,80,128]{2,1,0:T(8,128)(2,1)} %shard_map.169), calls=%async_computation.2 | async-start | bytes 655360 | tf_op jit(solution)/shard_map/all_to_all | solution.py:387
  111.6 5.5 %shard_map.170 = (bf16[256,512]{1,0:T(8,128)(2,1)}, bf16[256,512]{1,0:T(8,128)(2,1)}, f32[8,128]{1,0:T(8,128)}) custom-call(s32[16]{0:T(128)} %counts_ref.3, bf16[2,256,256]{2,1,0:T(8,128)(2,1)} %get-tuple-element.64.r0_ref, bf16[2,256,256]{2,1,0:T(8,128)(2,1)} %copy-done.6, bf16[2,256,256]{2,1,0:T(8,128)(2,1)} %copy-done.7, bf16[2,256,256]{2,1,0:T(8,128)(2,1)} %copy-done.8, ...), custom_call_target="tpu_custom_call" | custom-call | flops 5000000000 | bytes 1048576 | tf_op jit(solution)/shard_map/pallas_call | solution.py:38
  117.1 0.7 collective-permute-start.18
  117.8 1.0 collective-permute-done.18.g1_ref
  118.9 0.5 all-to-all-done.2.in_ref
  119.5 0.7 copy-done.4
  120.2 1.6 shard_map.171.c0_ref
  121.8 3.3 %collective-permute-start.21 = (bf16[96,128]{1,0:T(8,128)(2,1)}, bf16[96,128]{1,0:T(8,128)(2,1)S(1)}, u32[]{:S(2)}, u32[]{:S(2)}) collective-permute-start(bf16[96,128]{1,0:T(8,128)(2,1)} %shard_map.171.c0_ref), channel_id=1, source_target_pairs={{0,6},{1,7},{2,0},{3,1},{4,2},{5,3},{6,4},{7,5},{8,14},{9,15},{10,... | collective-permute-start | bytes 73736 | tf_op jit(solution)/shard_map/ppermute | solution.py:379
  125.1 0.6 collective-permute-start.19
  125.7 0.6 collective-permute-done.21.c3_ref
  126.3 3.2 %collective-permute-done.20.c2_ref = bf16[96,128]{1,0:T(8,128)(2,1)S(1)} collective-permute-done((bf16[96,128]{1,0:T(8,128)(2,1)}, bf16[96,128]{1,0:T(8,128)(2,1)S(1)}, u32[]{:S(2)}, u32[]{:S(2)}) %collective-permute-start.20) | collective-permute-done | bytes 24608 | tf_op jit(solution)/shard_map/ppermute | solution.py:379
  129.5 0.6 copy-done.15
  130.1 0.6 copy-done.16
  130.7 2.0 %shard_map.172 = bf16[16,336,128]{2,1,0:T(8,128)(2,1)} custom-call(bf16[96,128]{1,0:T(8,128)(2,1)} %shard_map.171.c0_ref, bf16[96,128]{1,0:T(8,128)(2,1)} %copy-done.16, bf16[96,128]{1,0:T(8,128)(2,1)} %copy-done.15, bf16[96,128]{1,0:T(8,128)(2,1)} %copy-done.14), custom_call_target="tpu_custom_call" | custom-call | flops 2000000000 | bytes 1048576 | tf_op jit(solution)/shard_map/pallas_call | solution.py:38
  132.8 24.6 %all_to_all.20.mine_ref = bf16[16,336,128]{2,1,0:T(8,128)(2,1)S(1)} all-to-all(bf16[16,336,128]{2,1,0:T(8,128)(2,1)} %shard_map.172), channel_id=1, replica_groups=mesh['dom'=16,'blk'=8] {'dom'}, dimensions={0} | all-to-all | bytes 2752512 | tf_op jit(solution)/shard_map/all_to_all | solution.py:387
  157.4 3.6 %collective-permute-start.22 = (bf16[16,336,128]{2,1,0:T(8,128)(2,1)S(1)}, bf16[16,336,128]{2,1,0:T(8,128)(2,1)S(1)}, u32[]{:S(2)}, u32[]{:S(2)}) collective-permute-start(bf16[16,336,128]{2,1,0:T(8,128)(2,1)S(1)} %all_to_all.20.mine_ref), channel_id=1, source_target_pairs={{0,1},{1,0},{2,3},{3,2},{4,5},{5,4},{6,7},{7,6},{8,9},{9,8},{10,11... | collective-permute-start | bytes 4128776 | tf_op jit(solution)/shard_map/ppermute | solution.py:383
  161.1 2.8 %collective-permute-done.22.other_ref = bf16[16,336,128]{2,1,0:T(8,128)(2,1)S(1)} collective-permute-done((bf16[16,336,128]{2,1,0:T(8,128)(2,1)S(1)}, bf16[16,336,128]{2,1,0:T(8,128)(2,1)S(1)}, u32[]{:S(2)}, u32[]{:S(2)}) %collective-permute-start.22) | collective-permute-done | bytes 1376288 | tf_op jit(solution)/shard_map/ppermute | solution.py:383
  163.8 1.1 copy-done.3
  164.9 5.2 %shard_map.173 = (f32[5,512,512]{2,1,0:T(8,128)}, f32[1,512]{1,0:T(1,128)}) custom-call(bf16[16,336,128]{2,1,0:T(8,128)(2,1)} %copy-done, bf16[16,336,128]{2,1,0:T(8,128)(2,1)} %copy-done.3), custom_call_target="tpu_custom_call" | custom-call | tf_op jit(solution)/shard_map/pallas_call | solution.py:477
  (60 shorter events, 0.5 us)
Async XLA Ops:
  4.1 7.7 %copy-start.9 = (bf16[528,512]{1,0:T(8,128)(2,1)S(1)}, bf16[528,512]{1,0:T(8,128)(2,1)}, u32[]{:S(2)}) copy-start(bf16[528,512]{1,0:T(8,128)(2,1)} %get-tuple-element.54.p0_ref) | copy-start | bytes 1622020
  4.1 39.7 %all-to-all-start = ((bf16[16,128,512]{2,1,0:T(8,128)(2,1)}), bf16[16,128,512]{2,1,0:T(8,128)(2,1)S(1)}, u32[]{:S(2)}, u32[]{:S(2)}) async-start(bf16[16,128,512]{2,1,0:T(8,128)(2,1)} %get-tuple-element.50), calls=%async_computation | async-start | bytes 4194304 | tf_op jit(solution)/shard_map/all_to_all | solution.py:387
  11.8 25.9 %collective-permute-start.2 = (bf16[528,512]{1,0:T(8,128)(2,1)S(1)}, bf16[528,512]{1,0:T(8,128)(2,1)S(1)}, u32[]{:S(2)}, u32[]{:S(2)}) collective-permute-start(bf16[528,512]{1,0:T(8,128)(2,1)S(1)} %copy-done.9), channel_id=1, source_target_pairs={{0,6},{1,7},{2,0},{3,1},{4,2},{5,3},{6,4},{7,5},{8,14},{9,15},{10,... | collective-permute-start | bytes 1622024 | tf_op jit(solution)/shard_map/ppermute | solution.py:379
  15.6 22.1 %collective-permute-start.1 = (bf16[528,512]{1,0:T(8,128)(2,1)S(1)}, bf16[528,512]{1,0:T(8,128)(2,1)}, u32[]{:S(2)}, u32[]{:S(2)}) collective-permute-start(bf16[528,512]{1,0:T(8,128)(2,1)S(1)} %copy-done.9), channel_id=1, source_target_pairs={{0,4},{1,5},{2,6},{3,7},{4,0},{5,1},{6,2},{7,3},{8,12},{9,13},{10,... | collective-permute-start | bytes 1622024 | tf_op jit(solution)/shard_map/ppermute | solution.py:379
  15.6 26.7 %collective-permute-start = (bf16[528,512]{1,0:T(8,128)(2,1)S(1)}, bf16[528,512]{1,0:T(8,128)(2,1)}, u32[]{:S(2)}, u32[]{:S(2)}) collective-permute-start(bf16[528,512]{1,0:T(8,128)(2,1)S(1)} %copy-done.9), channel_id=1, source_target_pairs={{0,2},{1,3},{2,4},{3,5},{4,6},{5,7},{6,0},{7,1},{8,10},{9,11},{10,... | collective-permute-start | bytes 1622024 | tf_op jit(solution)/shard_map/ppermute | solution.py:379
  37.7 18.0 %copy-start.10 = (bf16[528,512]{1,0:T(8,128)(2,1)}, bf16[528,512]{1,0:T(8,128)(2,1)S(1)}, u32[]{:S(2)}) copy-start(bf16[528,512]{1,0:T(8,128)(2,1)S(1)} %collective-permute-done.2.p3_ref) | copy-start | bytes 1622020
  42.4 14.1 %collective-permute-start.3 = (bf16[528,512]{1,0:T(8,128)(2,1)S(1)}, bf16[528,512]{1,0:T(8,128)(2,1)}, u32[]{:S(2)}, u32[]{:S(2)}) collective-permute-start(bf16[528,512]{1,0:T(8,128)(2,1)S(1)} %copy-done.9), channel_id=1, source_target_pairs={{0,1},{1,0},{2,3},{3,2},{4,5},{5,4},{6,7},{7,6},{8,9},{9,8},{10,11... | collective-permute-start | bytes 1622024 | tf_op jit(solution)/shard_map/ppermute | solution.py:383
  43.2 13.2 %collective-permute-start.4 = (bf16[528,512]{1,0:T(8,128)(2,1)}, bf16[528,512]{1,0:T(8,128)(2,1)}, u32[]{:S(2)}, u32[]{:S(2)}) collective-permute-start(bf16[528,512]{1,0:T(8,128)(2,1)} %collective-permute-done.p1_ref), channel_id=1, source_target_pairs={{0,1},{1,0},{2,3},{3,2},{4,5},{5,4},{6,7},{7,6},{8,9},{9,8},{10,11... | collective-permute-start | bytes 1622024 | tf_op jit(solution)/shard_map/ppermute | solution.py:383
  43.2 13.2 %collective-permute-start.5 = (bf16[528,512]{1,0:T(8,128)(2,1)}, bf16[528,512]{1,0:T(8,128)(2,1)}, u32[]{:S(2)}, u32[]{:S(2)}) collective-permute-start(bf16[528,512]{1,0:T(8,128)(2,1)} %collective-permute-done.1.p2_ref), channel_id=1, source_target_pairs={{0,1},{1,0},{2,3},{3,2},{4,5},{5,4},{6,7},{7,6},{8,9},{9,8},{10,11... | collective-permute-start | bytes 1622024 | tf_op jit(solution)/shard_map/ppermute | solution.py:383
  43.7 12.7 %collective-permute-start.6 = (bf16[528,512]{1,0:T(8,128)(2,1)S(1)}, bf16[528,512]{1,0:T(8,128)(2,1)}, u32[]{:S(2)}, u32[]{:S(2)}) collective-permute-start(bf16[528,512]{1,0:T(8,128)(2,1)S(1)} %collective-permute-done.2.p3_ref), channel_id=1, source_target_pairs={{0,1},{1,0},{2,3},{3,2},{4,5},{5,4},{6,7},{7,6},{8,9},{9,8},{10,11... | collective-permute-start | bytes 1622024 | tf_op jit(solution)/shard_map/ppermute | solution.py:383
  43.7 1.3 copy-start.2
  45.1 59.5 %all-to-all-start.1 = ((bf16[16,128,512]{2,1,0:T(8,128)(2,1)}), bf16[16,128,512]{2,1,0:T(8,128)(2,1)S(1)}, u32[]{:S(2)}, u32[]{:S(2)}) async-start(bf16[16,128,512]{2,1,0:T(8,128)(2,1)} %get-tuple-element.71), calls=%async_computation.1 | async-start | bytes 4194304 | tf_op jit(solution)/shard_map/all_to_all | solution.py:387
  55.7 26.6 %collective-permute-start.14 = (bf16[4,64,256]{2,1,0:T(8,128)(2,1)}, bf16[4,64,256]{2,1,0:T(8,128)(2,1)S(1)}, u32[]{:S(2)}, u32[]{:S(2)}) collective-permute-start(bf16[4,64,256]{2,1,0:T(8,128)(2,1)} %get-tuple-element.69), channel_id=1, source_target_pairs={{0,1},{1,0},{2,3},{3,2},{4,5},{5,4},{6,7},{7,6},{8,9},{9,8},{10,11... | collective-permute-start | bytes 393224 | tf_op jit(solution)/shard_map/ppermute | solution.py:383
  56.5 25.7 %copy-start.5 = (bf16[4,64,256]{2,1,0:T(8,128)(2,1)S(1)}, bf16[4,64,256]{2,1,0:T(8,128)(2,1)}, u32[]{:S(2)}) copy-start(bf16[4,64,256]{2,1,0:T(8,128)(2,1)} %get-tuple-element.68) | copy-start | bytes 393220
  80.6 30.9 %collective-permute-start.10 = (bf16[256,256]{1,0:T(8,128)(2,1)S(1)}, bf16[256,256]{1,0:T(8,128)(2,1)}, u32[]{:S(2)}, u32[]{:S(2)}) collective-permute-start(bf16[256,256]{1,0:T(8,128)(2,1)S(1)} %slice_bitcast_fusion.3), channel_id=1, source_target_pairs={{0,1},{1,0},{2,3},{3,2},{4,5},{5,4},{6,7},{7,6},{8,9},{9,8},{10,11... | collective-permute-start | bytes 393224 | tf_op jit(solution)/shard_map/ppermute | solution.py:383
  80.7 7.7 %collective-permute-start.7 = (bf16[2,256,256]{2,1,0:T(8,128)(2,1)}, bf16[2,256,256]{2,1,0:T(8,128)(2,1)S(1)}, u32[]{:S(2)}, u32[]{:S(2)}) collective-permute-start(bf16[2,256,256]{2,1,0:T(8,128)(2,1)} %get-tuple-element.65), channel_id=1, source_target_pairs={{0,6},{1,7},{2,0},{3,1},{4,2},{5,3},{6,4},{7,5},{8,14},{9,15},{10,... | collective-permute-start | bytes 786440 | tf_op jit(solution)/shard_map/ppermute | solution.py:379
  81.4 8.9 %collective-permute-start.8 = (bf16[2,256,256]{2,1,0:T(8,128)(2,1)}, bf16[2,256,256]{2,1,0:T(8,128)(2,1)S(1)}, u32[]{:S(2)}, u32[]{:S(2)}) collective-permute-start(bf16[2,256,256]{2,1,0:T(8,128)(2,1)} %get-tuple-element.66), channel_id=1, source_target_pairs={{0,4},{1,5},{2,6},{3,7},{4,0},{5,1},{6,2},{7,3},{8,12},{9,13},{10,... | collective-permute-start | bytes 786440 | tf_op jit(solution)/shard_map/ppermute | solution.py:379
  81.4 15.6 %collective-permute-start.9 = (bf16[2,256,256]{2,1,0:T(8,128)(2,1)}, bf16[2,256,256]{2,1,0:T(8,128)(2,1)S(1)}, u32[]{:S(2)}, u32[]{:S(2)}) collective-permute-start(bf16[2,256,256]{2,1,0:T(8,128)(2,1)} %get-tuple-element.67), channel_id=1, source_target_pairs={{0,2},{1,3},{2,4},{3,5},{4,6},{5,7},{6,0},{7,1},{8,10},{9,11},{10,... | collective-permute-start | bytes 786440 | tf_op jit(solution)/shard_map/ppermute | solution.py:379
  82.3 16.7 %collective-permute-start.15 = (bf16[2,64,256]{2,1,0:T(8,128)(2,1)S(1)}, bf16[2,64,256]{2,1,0:T(8,128)(2,1)S(1)}, u32[]{:S(2)}, u32[]{:S(2)}) collective-permute-start(bf16[2,64,256]{2,1,0:T(8,128)(2,1)S(1)} %pad_maximum_fusion.1), channel_id=1, source_target_pairs={{0,2},{1,3},{2,4},{3,5},{4,6},{5,7},{6,0},{7,1},{8,10},{9,11},{10,... | collective-permute-start | bytes 196616 | tf_op jit(solution)/shard_map/ppermute | solution.py:379
  88.4 16.1 %copy-start.6 = (bf16[2,256,256]{2,1,0:T(8,128)(2,1)}, bf16[2,256,256]{2,1,0:T(8,128)(2,1)S(1)}, u32[]{:S(2)}) copy-start(bf16[2,256,256]{2,1,0:T(8,128)(2,1)S(1)} %collective-permute-done.7.r1_ref) | copy-start | bytes 786436
  88.4 11.1 %collective-permute-start.16 = (bf16[2,64,256]{2,1,0:T(8,128)(2,1)S(1)}, bf16[2,64,256]{2,1,0:T(8,128)(2,1)S(1)}, u32[]{:S(2)}, u32[]{:S(2)}) collective-permute-start(bf16[2,64,256]{2,1,0:T(8,128)(2,1)S(1)} %pad_maximum_fusion.2), channel_id=1, source_target_pairs={{0,4},{1,5},{2,6},{3,7},{4,0},{5,1},{6,2},{7,3},{8,12},{9,13},{10,... | collective-permute-start | bytes 196616 | tf_op jit(solution)/shard_map/ppermute | solution.py:379
  90.2 14.3 %copy-start.7 = (bf16[2,256,256]{2,1,0:T(8,128)(2,1)}, bf16[2,256,256]{2,1,0:T(8,128)(2,1)S(1)}, u32[]{:S(2)}) copy-start(bf16[2,256,256]{2,1,0:T(8,128)(2,1)S(1)} %collective-permute-done.8.r2_ref) | copy-start | bytes 786436
  90.2 10.0 %collective-permute-start.17 = (bf16[2,64,256]{2,1,0:T(8,128)(2,1)S(1)}, bf16[2,64,256]{2,1,0:T(8,128)(2,1)S(1)}, u32[]{:S(2)}, u32[]{:S(2)}) collective-permute-start(bf16[2,64,256]{2,1,0:T(8,128)(2,1)S(1)} %pad_maximum_fusion.3), channel_id=1, source_target_pairs={{0,6},{1,7},{2,0},{3,1},{4,2},{5,3},{6,4},{7,5},{8,14},{9,15},{10,... | collective-permute-start | bytes 196616 | tf_op jit(solution)/shard_map/ppermute | solution.py:379
  96.9 3.4 %copy-start.8 = (bf16[2,256,256]{2,1,0:T(8,128)(2,1)}, bf16[2,256,256]{2,1,0:T(8,128)(2,1)S(1)}, u32[]{:S(2)}) copy-start(bf16[2,256,256]{2,1,0:T(8,128)(2,1)S(1)} %collective-permute-done.9.r3_ref) | copy-start | bytes 786436
  96.9 14.6 %collective-permute-start.11 = (bf16[256,256]{1,0:T(8,128)(2,1)S(1)}, bf16[256,256]{1,0:T(8,128)(2,1)}, u32[]{:S(2)}, u32[]{:S(2)}) collective-permute-start(bf16[256,256]{1,0:T(8,128)(2,1)S(1)} %slice_bitcast_fusion.2), channel_id=1, source_target_pairs={{0,1},{1,0},{2,3},{3,2},{4,5},{5,4},{6,7},{7,6},{8,9},{9,8},{10,11... | collective-permute-start | bytes 393224 | tf_op jit(solution)/shard_map/ppermute | solution.py:383
  99.0 1.3 copy-start.11
  99.0 12.5 %collective-permute-start.12 = (bf16[256,256]{1,0:T(8,128)(2,1)S(1)}, bf16[256,256]{1,0:T(8,128)(2,1)}, u32[]{:S(2)}, u32[]{:S(2)}) collective-permute-start(bf16[256,256]{1,0:T(8,128)(2,1)S(1)} %slice_bitcast_fusion.1), channel_id=1, source_target_pairs={{0,1},{1,0},{2,3},{3,2},{4,5},{5,4},{6,7},{7,6},{8,9},{9,8},{10,11... | collective-permute-start | bytes 393224 | tf_op jit(solution)/shard_map/ppermute | solution.py:383
  99.5 0.8 copy-start.12
  99.5 12.0 %collective-permute-start.13 = (bf16[256,256]{1,0:T(8,128)(2,1)S(1)}, bf16[256,256]{1,0:T(8,128)(2,1)}, u32[]{:S(2)}, u32[]{:S(2)}) collective-permute-start(bf16[256,256]{1,0:T(8,128)(2,1)S(1)} %slice_bitcast_fusion), channel_id=1, source_target_pairs={{0,1},{1,0},{2,3},{3,2},{4,5},{5,4},{6,7},{7,6},{8,9},{9,8},{10,11... | collective-permute-start | bytes 393224 | tf_op jit(solution)/shard_map/ppermute | solution.py:383
  100.3 0.6 copy-start.13
  104.6 7.0 %copy-start.1 = (bf16[16,128,512]{2,1,0:T(8,128)(2,1)}, bf16[16,128,512]{2,1,0:T(8,128)(2,1)S(1)}, u32[]{:S(2)}) copy-start(bf16[16,128,512]{2,1,0:T(8,128)(2,1)S(1)} %all-to-all-done.1.back_ref) | copy-start | bytes 6291460
  104.6 14.8 %all-to-all-start.2 = ((bf16[16,80,128]{2,1,0:T(8,128)(2,1)}), bf16[16,80,128]{2,1,0:T(8,128)(2,1)S(1)}, u32[]{:S(2)}, u32[]{:S(2)}) async-start(bf16[16,80,128]{2,1,0:T(8,128)(2,1)} %shard_map.169), calls=%async_computation.2 | async-start | bytes 655360 | tf_op jit(solution)/shard_map/all_to_all | solution.py:387
  117.1 1.8 %collective-permute-start.18 = (f32[8,128]{1,0:T(8,128)}, f32[8,128]{1,0:T(8,128)S(1)}, u32[]{:S(2)}, u32[]{:S(2)}) collective-permute-start(f32[8,128]{1,0:T(8,128)} %get-tuple-element.77.g0_ref), channel_id=1, source_target_pairs={{0,1},{1,0},{2,3},{3,2},{4,5},{5,4},{6,7},{7,6},{8,9},{9,8},{10,11... | collective-permute-start | bytes 12296 | tf_op jit(solution)/shard_map/ppermute | solution.py:383
  118.9 0.6 copy-start.17
  119.5 0.7 copy-start.4
  121.8 4.4 %collective-permute-start.21 = (bf16[96,128]{1,0:T(8,128)(2,1)}, bf16[96,128]{1,0:T(8,128)(2,1)S(1)}, u32[]{:S(2)}, u32[]{:S(2)}) collective-permute-start(bf16[96,128]{1,0:T(8,128)(2,1)} %shard_map.171.c0_ref), channel_id=1, source_target_pairs={{0,6},{1,7},{2,0},{3,1},{4,2},{5,3},{6,4},{7,5},{8,14},{9,15},{10,... | collective-permute-start | bytes 73736 | tf_op jit(solution)/shard_map/ppermute | solution.py:379
  125.1 4.4 %collective-permute-start.20 = (bf16[96,128]{1,0:T(8,128)(2,1)}, bf16[96,128]{1,0:T(8,128)(2,1)S(1)}, u32[]{:S(2)}, u32[]{:S(2)}) collective-permute-start(bf16[96,128]{1,0:T(8,128)(2,1)} %shard_map.171.c0_ref), channel_id=1, source_target_pairs={{0,4},{1,5},{2,6},{3,7},{4,0},{5,1},{6,2},{7,3},{8,12},{9,13},{10,... | collective-permute-start | bytes 73736 | tf_op jit(solution)/shard_map/ppermute | solution.py:379
  125.1 4.4 %collective-permute-start.19 = (bf16[96,128]{1,0:T(8,128)(2,1)}, bf16[96,128]{1,0:T(8,128)(2,1)S(1)}, u32[]{:S(2)}, u32[]{:S(2)}) collective-permute-start(bf16[96,128]{1,0:T(8,128)(2,1)} %shard_map.171.c0_ref), channel_id=1, source_target_pairs={{0,2},{1,3},{2,4},{3,5},{4,6},{5,7},{6,0},{7,1},{8,10},{9,11},{10,... | collective-permute-start | bytes 73736 | tf_op jit(solution)/shard_map/ppermute | solution.py:379
  126.3 3.2 %copy-start.14 = (bf16[96,128]{1,0:T(8,128)(2,1)}, bf16[96,128]{1,0:T(8,128)(2,1)S(1)}, u32[]{:S(2)}) copy-start(bf16[96,128]{1,0:T(8,128)(2,1)S(1)} %collective-permute-done.21.c3_ref) | copy-start | bytes 73732
  129.5 0.6 copy-start.15
  130.1 0.6 copy-start.16
  157.4 6.4 %copy-start = (bf16[16,336,128]{2,1,0:T(8,128)(2,1)}, bf16[16,336,128]{2,1,0:T(8,128)(2,1)S(1)}, u32[]{:S(2)}) copy-start(bf16[16,336,128]{2,1,0:T(8,128)(2,1)S(1)} %all_to_all.20.mine_ref) | copy-start | bytes 4128772
  157.4 6.4 %collective-permute-start.22 = (bf16[16,336,128]{2,1,0:T(8,128)(2,1)S(1)}, bf16[16,336,128]{2,1,0:T(8,128)(2,1)S(1)}, u32[]{:S(2)}, u32[]{:S(2)}) collective-permute-start(bf16[16,336,128]{2,1,0:T(8,128)(2,1)S(1)} %all_to_all.20.mine_ref), channel_id=1, source_target_pairs={{0,1},{1,0},{2,3},{3,2},{4,5},{5,4},{6,7},{7,6},{8,9},{9,8},{10,11... | collective-permute-start | bytes 4128776 | tf_op jit(solution)/shard_map/ppermute | solution.py:383
  163.8 1.1 copy-start.3

commit v4 on v3

--- a/solution.py
+++ b/solution.py
@@ -21,8 +21,8 @@
 LOG2E = math.log2(math.e)
 SCORE_MUL = LOG2E / 8.0
 SCORE_SUB = (8.0 + 256.0) * LOG2E
-CHUNK = 80
-SPREAD = 4 * CHUNK + 16
+CHUNK = 64 + 64 + 16
+SPREAD = 4 * 64 + 64 + 16
 
 NT = (((1,), (1,)), ((), ()))
 NN = (((1,), (0,)), ((), ()))
@@ -124,29 +124,47 @@
             slots_ref[high * 4 + k] = part[k * CAP : (k + 1) * CAP, :]
 
 
-def mean_body(counts_t_ref, degree_ref, table_ref, x_ref, w_ref, mine_ref, other_ref, base_ref, means_ref):
+def mean_body(counts_t_ref, degree_ref, table_ref, x_ref, grad_ref, w_ref, base_ref, mine_ref, other_ref):
     total = jnp.zeros((ROWS, D), F32)
     for high in range(4):
         table = jnp.concatenate([table_ref[high * 4 + k] for k in range(4)], axis=0)
         total = total + dot(counts_t_ref[high * 256 : (high + 1) * 256, :], table)
     mean_rows = (total / degree_ref[:, 0:1]).astype(BF16)
     base_ref[...] = x_ref[...].astype(F32) + dot(mean_rows, w_ref[...])
-    turned = jnp.transpose(mean_rows.astype(F32)).astype(BF16)
-    for h in range(BLK):
-        means_ref[h] = turned[h * HEAD : (h + 1) * HEAD, :]
-    z, core = position()
-    for dz in range(4):
-        chip = ((z + dz) & 3) * 2
-        mine_ref[dz] = means_ref[chip + core]
-        other_ref[dz] = means_ref[chip + (1 - core)]
+    dw = dot(jnp.transpose(mean_rows.astype(F32)).astype(BF16), grad_ref[...]).astype(BF16)
+    z, core = position()
+    for half in range(2):
+        def fill(ref):
+            for p in range(DOM):
+                top = half * 256 + p * 16
+                for b in range(4):
+                    ref[p, b * 16 : (b + 1) * 16, :] = dw[top : top + 16, b * 128 : (b + 1) * 128]
+
+        @pl.when(core == half)
+        def _():
+            fill(mine_ref)
+
+        @pl.when(core != half)
+        def _():
+            fill(other_ref)
 
 
 def attention_body(
-    p0_ref, p1_ref, p2_ref, p3_ref, p4_ref, p5_ref, p6_ref, p7_ref, wqkv_ref, wo_ref,
-    r0_ref, r1_ref, r2_ref, r3_ref, dw_ref,
+    p0_ref, p1_ref, t2_ref, b2_ref, p3_ref, p4_ref, p5_ref, t6_ref, b6_ref, p7_ref, wqkv_ref, wo_ref, mine_ref, other_ref,
+    r0_ref, r1_ref, r2_ref, r3_ref, chunks_ref,
     y_ref, s_ref, qt_ref, kt_ref, k_ref, v_ref, vt_ref, w_ref, dq_ref, dk_ref, dv_ref, at_ref, ga_ref, sl_ref, qr_ref, gr_ref,
 ):
-    pays = (p0_ref, p1_ref, p2_ref, p3_ref, p4_ref, p5_ref, p6_ref, p7_ref)
+    pays = (p0_ref, p1_ref, (t2_ref, b2_ref), p3_ref, p4_ref, p5_ref, (t6_ref, b6_ref), p7_ref)
+
+    def normed_of(pay):
+        return pay[0][...] if isinstance(pay, tuple) else pay[0:ROWS, :]
+
+    def grads_of(pay):
+        return pay[1][0:ROWS, :] if isinstance(pay, tuple) else pay[ROWS : 2 * ROWS, :]
+
+    def tail_of(pay):
+        return pay[1][ROWS : PAY - ROWS, 0:ROWS] if isinstance(pay, tuple) else pay[2 * ROWS : PAY, 0:ROWS]
+
     outs = (r0_ref, r1_ref, r2_ref, r3_ref)
     z, core = position()
     row = lax.broadcasted_iota(jnp.int32, (HEAD, ROWS), 0)
@@ -157,7 +175,7 @@
 
     for r in range(BLK):
         pay = pays[r]
-        projected = dot(wqkv_ref[...], pay[0:ROWS, :], NT)
+        projected = dot(wqkv_ref[...], normed_of(pay), NT)
         query, key, value = projected[0:HEAD], projected[HEAD:128], projected[128:192]
         scale_q, scale_k = head_scale(query), head_scale(key)
         query, key = query * scale_q, key * scale_k
@@ -165,7 +183,7 @@
         y_ref[r, HEAD:128] = key
         s_ref[r, 0:1] = scale_q
         s_ref[r, 1:2] = scale_k
-        tail = pay[2 * ROWS : PAY, 0:ROWS].astype(F32)
+        tail = tail_of(pay).astype(F32)
         same = jnp.where(number == tail[0:1], 32.0, 0.0)
         sender = ((z - (r & 3)) & 3) * 2 + (core ^ (r >> 2))
         wanted = jnp.concatenate([jnp.zeros((16, ROWS), F32), tail[1:9] * 32.0, jnp.zeros((40, ROWS), F32)], axis=0)
@@ -177,7 +195,7 @@
         value = jnp.concatenate([value, jnp.where(row < 2, 1.0, 0.0)], axis=0)
         vt_ref[r] = value[0:80].astype(BF16)
         v_ref[r] = jnp.transpose(value).astype(BF16)
-        ga_ref[r] = dot(wo_ref[...], pay[ROWS : 2 * ROWS, :], NT)
+        ga_ref[r] = dot(wo_ref[...], grads_of(pay), NT)
         qr_ref[r] = jnp.transpose(qt_ref[r].astype(F32)).astype(BF16)
 
     keys_t = jnp.concatenate([kt_ref[j] for j in range(BLK)], axis=1)
@@ -233,54 +251,43 @@
         outs[r & 3][r >> 2, :, 0:128] = jnp.transpose(first).astype(BF16)
         outs[r & 3][r >> 2, :, 128:256] = jnp.transpose(second).astype(BF16)
         left = jnp.concatenate([first, second[0:HEAD]], axis=0).astype(BF16)
-        dw = dw + dot(left, pay[0:ROWS, :])
-        dwo = dwo + dot(at_ref[r], pay[ROWS : 2 * ROWS, :])
-    dw_ref[0:192, :] = dw
-    dw_ref[192:256, :] = dwo
-
-
-def chunks_body(
-    p0_ref, p1_ref, p2_ref, p3_ref, p4_ref, p5_ref, p6_ref, p7_ref, m0_ref, m1_ref, m2_ref, m3_ref, dw_ref, out_ref
-):
-    pays = (p0_ref, p1_ref, p2_ref, p3_ref, p4_ref, p5_ref, p6_ref, p7_ref)
-    total = jnp.zeros((HEAD, D), F32)
-    for dz, m_ref in enumerate((m0_ref, m1_ref, m2_ref, m3_ref)):
-        for c in range(2):
-            total = total + dot(m_ref[c], pays[4 * c + dz][ROWS : 2 * ROWS, :])
+        dw = dw + dot(left, normed_of(pay))
+        dwo = dwo + dot(at_ref[r], grads_of(pay))
+    dw = jnp.concatenate([dw, dwo], axis=0).astype(BF16)
     for a in range(4):
         for b in range(4):
-            out_ref[a * 4 + b, 0:64, :] = dw_ref[a * 64 : (a + 1) * 64, b * 128 : (b + 1) * 128].astype(BF16)
-            out_ref[a * 4 + b, 64:80, :] = total[a * 16 : (a + 1) * 16, b * 128 : (b + 1) * 128].astype(BF16)
+            p = a * 4 + b
+            chunks_ref[p, 0:64, :] = dw[a * 64 : (a + 1) * 64, b * 128 : (b + 1) * 128]
+            chunks_ref[p, 64:128, :] = (mine_ref[p].astype(F32) + other_ref[p].astype(F32)).astype(BF16)
 
 
 def chunk_sum_body(in_ref, g0_ref, g1_ref, out_ref):
     total = in_ref[0].astype(F32)
     for p in range(1, DOM):
         total = total + in_ref[p].astype(F32)
-    out_ref[0:CHUNK, :] = total.astype(BF16)
+    out_ref[0:128, :] = total.astype(BF16)
     z, core = position()
     one, two = g0_ref[...], g1_ref[...]
     gain = jnp.where(core == 0, one, two) + jnp.where(core == 0, two, one)
     coarse = gain.astype(BF16).astype(F32)
     fine = gain - coarse
-    out_ref[CHUNK : CHUNK + 16, :] = jnp.concatenate([coarse, fine], axis=0).astype(BF16)
-
-
-def spread_body(c0_ref, c1_ref, c2_ref, c3_ref, out_ref, gains_ref):
+    out_ref[128:CHUNK, :] = jnp.concatenate([coarse, fine], axis=0).astype(BF16)
+
+
+def spread_body(c0_ref, c1_ref, c2_ref, c3_ref, out_ref, parts_ref):
     z, core = position()
     for dz, c_ref in enumerate((c0_ref, c1_ref, c2_ref, c3_ref)):
-        tail = c_ref[CHUNK : CHUNK + 16, :].astype(F32)
-        gains_ref[dz] = tail[0:8] + tail[8:16]
-    gain = jnp.zeros((8, 128), F32)
+        parts_ref[dz] = c_ref[64:CHUNK, :].astype(F32)
+    total = jnp.zeros((80, 128), F32)
     for chip in range(4):
-        gain = gain + gains_ref[(z - chip) & 3]
+        total = total + parts_ref[(z - chip) & 3]
+    gain = total[64:72] + total[72:80]
     coarse = gain.astype(BF16).astype(F32)
-    fine = (gain - coarse).astype(BF16).astype(F32)
-    tail = jnp.concatenate([coarse, fine], axis=0).astype(BF16)
+    tail = jnp.concatenate([total[0:64], coarse, gain - coarse], axis=0).astype(BF16)
     for p in range(DOM):
         for dz, c_ref in enumerate((c0_ref, c1_ref, c2_ref, c3_ref)):
-            out_ref[p, dz * CHUNK : (dz + 1) * CHUNK, :] = c_ref[0:CHUNK, :]
-        out_ref[p, 4 * CHUNK : SPREAD, :] = tail
+            out_ref[p, dz * 64 : (dz + 1) * 64, :] = c_ref[0:64, :]
+        out_ref[p, 256:SPREAD, :] = tail
 
 
 def rows_body(
@@ -337,7 +344,7 @@
     def _():
         gain = jnp.zeros((8, 128), F32)
         for p in range(DOM):
-            tail = mine_ref[p, 4 * CHUNK : SPREAD, :].astype(F32)
+            tail = mine_ref[p, 320:SPREAD, :].astype(F32)
             gain = gain + (tail[0:8] + tail[8:16])
         for k in range(4):
             gain_ref[:, k * 128 : (k + 1) * 128] = gain[k : k + 1, :]
@@ -345,30 +352,32 @@
     for c in range(2):
         @pl.when(core == c)
         def _():
-            def piece(h, p, top, size):
-                start = ((z - (h >> 1)) & 3) * CHUNK + top
+            def piece(h, p):
+                start = ((z - (h >> 1)) & 3) * 64
                 ref = mine_ref if h & 1 == c else other_ref
-                return ref[p, pl.ds(pl.multiple_of(start, 16), size), :].astype(F32)
+                return ref[p, pl.ds(pl.multiple_of(start, 64), 64), :].astype(F32)
 
             @pl.when(which < 3)
             def _():
                 for b in range(4):
-                    part = jnp.concatenate([piece(h, which * 4 + b, 0, 64) for h in range(BLK)], axis=0)
+                    part = jnp.concatenate([piece(h, which * 4 + b) for h in range(BLK)], axis=0)
                     out_ref[0, b * 128 : (b + 1) * 128, :] = jnp.transpose(part)
 
             @pl.when(which == 3)
             def _():
                 for h in range(BLK):
                     for b in range(4):
-                        out_ref[0, h * 64 : (h + 1) * 64, b * 128 : (b + 1) * 128] = piece(h, 12 + b, 0, 64)
+                        out_ref[0, h * 64 : (h + 1) * 64, b * 128 : (b + 1) * 128] = piece(h, 12 + b)
 
             @pl.when(which == 4)
             def _():
-                for h in range(BLK):
-                    for a in range(4):
+                for half in range(2):
+                    ref = mine_ref if half == c else other_ref
+                    for p in range(DOM):
+                        top = half * 256 + p * 16
                         for b in range(4):
-                            top = h * 64 + a * 16
-                            out_ref[0, top : top + 16, b * 128 : (b + 1) * 128] = piece(h, a * 4 + b, 64, 16)
+                            part = ref[p, 256 + b * 16 : 272 + b * 16, :]
+                            out_ref[0, top : top + 16, b * 128 : (b + 1) * 128] = part.astype(F32)
 
 
 def chip_shift(step, swap):
@@ -399,7 +408,7 @@
         micros=4,
     )
     incoming = to_dom_peers(outgoing)
-    pays = [pay] + [along_chips(pay, step) for step in (1, 2, 3)]
+    near, far = along_chips(pay, 1), along_chips(pay, 3)
 
     counts_t, degree, slot_grads, wqkv, wo_head = call(
         edges_body,
@@ -411,27 +420,23 @@
         scratch=[pltpu.VMEM((512, 1024), F32)],
         micros=10,
     )
-    *pays, degree = lax.optimization_barrier((*pays, degree))
+    near, far, degree = lax.optimization_barrier((near, far, degree))
+    pays = [pay, near, along_chips(near[0:ROWS], 1), along_chips(far[ROWS:PAY], 3), far]
     pays = pays + [other_core(part) for part in pays]
     incoming, slot_grads = lax.optimization_barrier((incoming, slot_grads))
     back = to_dom_peers(slot_grads)
 
-    mine, other, base = call(
+    base, mine, other = call(
         mean_body,
-        (shape((4, HEAD, ROWS), BF16), shape((4, HEAD, ROWS), BF16), shape((ROWS, D), F32)),
-        (counts_t, degree, incoming, x, wm),
-        scratch=[pltpu.VMEM((BLK, HEAD, ROWS), BF16)],
+        (shape((ROWS, D), F32), shape((DOM, 64, 128), BF16), shape((DOM, 64, 128), BF16)),
+        (counts_t, degree, incoming, x, out_grad, wm),
         micros=4,
     )
-    other = other_core(other)
-    means = [jnp.stack([mine[dz], other[dz]]) for dz in range(4)]
-    means = [means[0]] + [along_chips(means[dz], dz) for dz in (1, 2, 3)]
-
-    *pays, base = lax.optimization_barrier((*pays, base))
-    *results, dw = call(
+
+    *results, chunks = call(
         attention_body,
-        (*[shape((2, ROWS, 256), BF16)] * 4, shape((256, D), F32)),
-        (*pays, wqkv, wo_head),
+        (*[shape((2, ROWS, 256), BF16)] * 4, shape((DOM, 128, 128), BF16)),
+        (*pays, wqkv, wo_head, mine, other_core(other)),
         scratch=[
             pltpu.VMEM((BLK, 128, ROWS), F32),
             pltpu.VMEM((BLK, 8, ROWS), F32),
@@ -450,14 +455,13 @@
             pltpu.VMEM((BLK, ROWS, 128), BF16),
             pltpu.VMEM((BLK, ROWS, 128), BF16),
         ],
-        micros=30,
-    )
-
-    chunks = call(chunks_body, shape((DOM, CHUNK, 128), BF16), (*pays, *means, dw), micros=3)
+        micros=12,
+    )
     chunks, back = lax.optimization_barrier((chunks, back))
     chunks = to_dom_peers(chunks)
 
     results = [results[0]] + [along_chips(results[dz], -dz) for dz in (1, 2, 3)]
+    *results, back = lax.optimization_barrier((*results, back))
     swapped = [other_core(part[1]) for part in results]
     layer_out, feature_grad, gain_part = call(
         rows_body,
@@ -465,13 +469,13 @@
         (send_counts, *results, *swapped, back, send_rows, base, x, gain_row, out_grad, wq, wk, wv, wo),
         scratch=[pltpu.VMEM((4, ROWS, 128), BF16)] * 4,
         scalars=1,
-        micros=5,
+        micros=0.001,
     )
     chunk = call(
-        chunk_sum_body, shape((CHUNK + 16, 128), BF16), (chunks, gain_part, other_core(gain_part)), micros=1
+        chunk_sum_body, shape((CHUNK, 128), BF16), (chunks, gain_part, other_core(gain_part)), micros=1
     )
     chunk_parts = [chunk] + [along_chips(chunk, step) for step in (1, 2, 3)]
-    spread = call(spread_body, shape((DOM, SPREAD, 128), BF16), chunk_parts, scratch=[pltpu.VMEM((4, 8, 128), F32)])
+    spread = call(spread_body, shape((DOM, SPREAD, 128), BF16), chunk_parts, scratch=[pltpu.VMEM((4, 80, 128), F32)])
     gathered = to_dom_peers(spread)
     whole = pl.BlockSpec((DOM, SPREAD, 128), lambda t: (0, 0, 0))
     weight_grads, gain_grad = pl.pallas_call(

time: 171 us -> 156 us (0.912)
  starting transfers between devices: 49.6 us -> 44.4 us
  waiting for transfers between devices: 30.8 us -> 25.8 us
  Pallas kernels: 57.5 us -> 54.5 us
    ppermute x12 -> x10, waiting for transfers between devices: 26.5 us -> 19 us  [along_chips(): return lax.ppermute(array, 'blk', chip_shift(step, 0))]
    ppermute x12 -> x10, starting transfers between devices: 18.4 us -> 10.9 us  [along_chips(): return lax.ppermute(array, 'blk', chip_shift(step, 0))]
    pallas_call x8 -> x7, Pallas kernels: 52.4 us -> 49.3 us  [call(): pl.pallas_call(body, out_shape=out_shape, in_specs=specs, out_specs=jax.t...]
    ppermute x11 -> x12, waiting for transfers between devices: 3.81 us -> 6.82 us  [other_core(): return lax.ppermute(array, 'blk', chip_shift(0, 1))]
    ppermute x11 -> x12, starting transfers between devices: 9.9 us -> 12.7 us  [other_core(): return lax.ppermute(array, 'blk', chip_shift(0, 1))]
    unnamed x36 -> x32, local copies, waits for them, and re-layouts: 5.09 us -> 4.66 us
  transfers between devices with their start and end apart: 26 -> 25, of which waited for: 11 -> 15; matrix products, arithmetic and copies ran while one was open for 1% -> 1% of each run, Pallas kernels for 27% -> 27%
where the time goes in v4:
time: 156 us
  Pallas kernels  54.5 us (35%)
  starting transfers between devices  44.4 us (28%)
  waiting for transfers between devices  25.8 us (17%)
  blocking collectives  24.6 us (16%)
  local copies, waits for them, and re-layouts  5.73 us (4%)
    pallas_call x7, Pallas kernels, call(): pl.pallas_call(body, out_shape=out_shape, in_specs=specs, out_specs=jax.t...  49.3 us
    all_to_all x1, blocking collectives, to_dom_peers(): return lax.all_to_all(array, 'dom', split_axis=0, concat_axis=0, tiled=True)  24.6 us
    all_to_all x3, starting transfers between devices, to_dom_peers(): return lax.all_to_all(array, 'dom', split_axis=0, concat_axis=0, tiled=True)  20.8 us
    ppermute x10, waiting for transfers between devices, along_chips(): return lax.ppermute(array, 'blk', chip_shift(step, 0))  19 us
    ppermute x12, starting transfers between devices, other_core(): return lax.ppermute(array, 'blk', chip_shift(0, 1))  12.7 us
    ppermute x10, starting transfers between devices, along_chips(): return lax.ppermute(array, 'blk', chip_shift(step, 0))  10.9 us
    ppermute x12, waiting for transfers between devices, other_core(): return lax.ppermute(array, 'blk', chip_shift(0, 1))  6.82 us
    pallas_call x1, Pallas kernels, local(): pl.pallas_call(weights_body, grid=(5,), out_shape=(shape((5, D, D), F32),...  5.19 us
  transfers between devices with their start and end apart: 25, of which 15 were waited for; matrix products, arithmetic and copies ran while one was open for 1% of the time, Pallas kernels for 27%

profile of v4, /device:TPU:1, one launch (start us, length us, event | category | flops | bytes accessed | tf_op | source)
XLA Modules:
  0.0 155.8 jit_solution(4485098675514665816)
XLA Ops:
  0.6 3.4 %shard_map.165 = (bf16[528,512]{1,0:T(8,128)(2,1)}, bf16[16,128,512]{2,1,0:T(8,128)(2,1)}) custom-call(s32[1,8]{1,0:T(1,128)} %pattern_ref.1, s32[16]{0:T(128)} %counts_ref.3, bf16[256,512]{1,0:T(8,128)(2,1)} %x_ref.5, f32[1,512]{1,0:T(1,128)} %bitcast.13, s32[1,256]{1,0:T(1,128)} %bitcast.18, bf16[256,512]{1,0:T(8,128)(2,1)} %grad_ref.7, s32[16,128]{1,0:T(8,128)} %rows_ref.3), custom_call_target="tpu_custom_call" | custom-call | flops 4000000000 | bytes 1048576 | tf_op jit(solution)/shard_map/pallas_call | solution.py:38
  4.1 7.6 %all-to-all-start = ((bf16[16,128,512]{2,1,0:T(8,128)(2,1)}), bf16[16,128,512]{2,1,0:T(8,128)(2,1)S(1)}, u32[]{:S(2)}, u32[]{:S(2)}) async-start(bf16[16,128,512]{2,1,0:T(8,128)(2,1)} %get-tuple-element.44), calls=%async_computation | async-start | bytes 4194304 | tf_op jit(solution)/shard_map/all_to_all | solution.py:396
  11.7 3.8 %collective-permute-start.1 = (bf16[528,512]{1,0:T(8,128)(2,1)}, bf16[528,512]{1,0:T(8,128)(2,1)S(1)}, u32[]{:S(2)}, u32[]{:S(2)}) collective-permute-start(bf16[528,512]{1,0:T(8,128)(2,1)} %get-tuple-element.36.p0_ref), channel_id=1, source_target_pairs={{0,6},{1,7},{2,0},{3,1},{4,2},{5,3},{6,4},{7,5},{8,14},{9,15},{10,... | collective-permute-start | bytes 1622024 | tf_op jit(solution)/shard_map/ppermute | solution.py:388
  15.5 8.9 %shard_map.166 = (bf16[1024,512]{1,0:T(8,128)(2,1)}, f32[256,128]{1,0:T(8,128)}, bf16[16,128,512]{2,1,0:T(8,128)(2,1)}, bf16[192,512]{1,0:T(8,128)(2,1)}, bf16[64,512]{1,0:T(8,128)(2,1)}) custom-call(s32[32,128]{1,0:T(8,128)} %bitcast.15, s32[32,128]{1,0:T(8,128)} %bitcast.16, bf16[256,512]{1,0:T(8,128)(2,1)} %grad_ref.7, bf16[512,512]{1,0:T(8,128)(2,1)} %w_ref.3, ...), custom_call_target="tpu_custom_call" | custom-call | flops 10000000000 | bytes 1048576 | tf_op jit(solution)/shard_map/pallas_call | solution.py:38
  24.4 2.0 %collective-permute-done.1.p3_ref = bf16[528,512]{1,0:T(8,128)(2,1)S(1)} collective-permute-done((bf16[528,512]{1,0:T(8,128)(2,1)}, bf16[528,512]{1,0:T(8,128)(2,1)S(1)}, u32[]{:S(2)}, u32[]{:S(2)}) %collective-permute-start.1) | collective-permute-done | bytes 540704 | tf_op jit(solution)/shard_map/ppermute | solution.py:388
  26.4 3.0 %collective-permute-done.p1_ref = bf16[528,512]{1,0:T(8,128)(2,1)S(1)} collective-permute-done((bf16[528,512]{1,0:T(8,128)(2,1)}, bf16[528,512]{1,0:T(8,128)(2,1)S(1)}, u32[]{:S(2)}, u32[]{:S(2)}) %collective-permute-start) | collective-permute-done | bytes 540704 | tf_op jit(solution)/shard_map/ppermute | solution.py:388
  29.5 0.4 collective-permute-start.3
  29.8 1.2 collective-permute-start.2
  31.1 2.7 %collective-permute-start.4 = (bf16[528,512]{1,0:T(8,128)(2,1)}, bf16[528,512]{1,0:T(8,128)(2,1)}, u32[]{:S(2)}, u32[]{:S(2)}) collective-permute-start(bf16[528,512]{1,0:T(8,128)(2,1)} %get-tuple-element.36.p0_ref), channel_id=1, source_target_pairs={{0,1},{1,0},{2,3},{3,2},{4,5},{5,4},{6,7},{7,6},{8,9},{9,8},{10,11... | collective-permute-start | bytes 1622024 | tf_op jit(solution)/shard_map/ppermute | solution.py:392
  33.8 0.5 collective-permute-start.8
  34.3 2.6 %collective-permute-done.2.t2_ref = bf16[256,512]{1,0:T(8,128)(2,1)} collective-permute-done((bf16[256,512]{1,0:T(8,128)(2,1)S(1)}, bf16[256,512]{1,0:T(8,128)(2,1)}, u32[]{:S(2)}, u32[]{:S(2)}) %collective-permute-start.2) | collective-permute-done | bytes 262176 | tf_op jit(solution)/shard_map/ppermute | solution.py:388
  36.9 3.1 %collective-permute-start.6 = (bf16[256,512]{1,0:T(8,128)(2,1)}, bf16[256,512]{1,0:T(8,128)(2,1)}, u32[]{:S(2)}, u32[]{:S(2)}) collective-permute-start(bf16[256,512]{1,0:T(8,128)(2,1)} %collective-permute-done.2.t2_ref), channel_id=1, source_target_pairs={{0,1},{1,0},{2,3},{3,2},{4,5},{5,4},{6,7},{7,6},{8,9},{9,8},{10,11... | collective-permute-start | bytes 786440 | tf_op jit(solution)/shard_map/ppermute | solution.py:392
  40.1 1.3 copy-done.2
  41.4 6.4 %all-to-all-start.1 = ((bf16[16,128,512]{2,1,0:T(8,128)(2,1)}), bf16[16,128,512]{2,1,0:T(8,128)(2,1)S(1)}, u32[]{:S(2)}, u32[]{:S(2)}) async-start(bf16[16,128,512]{2,1,0:T(8,128)(2,1)} %get-tuple-element.54), calls=%async_computation.1 | async-start | bytes 4194304 | tf_op jit(solution)/shard_map/all_to_all | solution.py:396
  47.8 4.3 %shard_map.167 = (f32[256,512]{1,0:T(8,128)}, bf16[16,64,128]{2,1,0:T(8,128)(2,1)}, bf16[16,64,128]{2,1,0:T(8,128)(2,1)}) custom-call(bf16[1024,512]{1,0:T(8,128)(2,1)} %get-tuple-element.42.counts_t_ref, f32[256,128]{1,0:T(8,128)} %get-tuple-element.43.degree_ref, bf16[16,128,512]{2,1,0:T(8,128)(2,1)} %copy-done.2, bf16[256,512]{1,0:T(8,128)(2,1)} %x_ref.5, ...), custom_call_target="tpu_custom_call" | custom-call | flops 4000000000 | bytes 1048576 | tf_op jit(solution)/shard_map/pallas_call | solution.py:38
  52.1 1.0 collective-permute-start.9
  53.1 1.5 collective-permute-done.9.other_ref
  54.6 23.3 %shard_map.168 = (bf16[2,256,256]{2,1,0:T(8,128)(2,1)}, bf16[2,256,256]{2,1,0:T(8,128)(2,1)}, bf16[2,256,256]{2,1,0:T(8,128)(2,1)}, bf16[2,256,256]{2,1,0:T(8,128)(2,1)}, bf16[16,128,128]{2,1,0:T(8,128)(2,1)}) custom-call(bf16[528,512]{1,0:T(8,128)(2,1)} %get-tuple-element.36.p0_ref, bf16[528,512]{1,0:T(8,128)(2,1)} %copy-done.10, ...), custom_call_target="tpu_custom_call" | custom-call | flops 12000000000 | bytes 1048576 | tf_op jit(solution)/shard_map/pallas_call | solution.py:38
  77.9 3.3 %collective-permute-start.10 = (bf16[2,256,256]{2,1,0:T(8,128)(2,1)}, bf16[2,256,256]{2,1,0:T(8,128)(2,1)S(1)}, u32[]{:S(2)}, u32[]{:S(2)}) collective-permute-start(bf16[2,256,256]{2,1,0:T(8,128)(2,1)} %get-tuple-element.50), channel_id=1, source_target_pairs={{0,6},{1,7},{2,0},{3,1},{4,2},{5,3},{6,4},{7,5},{8,14},{9,15},{10,... | collective-permute-start | bytes 786440 | tf_op jit(solution)/shard_map/ppermute | solution.py:388
  81.2 0.7 collective-permute-start.12
  81.9 6.9 %all-to-all-start.2 = ((bf16[16,128,128]{2,1,0:T(8,128)(2,1)}), bf16[16,128,128]{2,1,0:T(8,128)(2,1)S(1)}, u32[]{:S(2)}, u32[]{:S(2)}) async-start(bf16[16,128,128]{2,1,0:T(8,128)(2,1)} %get-tuple-element.64), calls=%async_computation.2 | async-start | bytes 1048576 | tf_op jit(solution)/shard_map/all_to_all | solution.py:396
  88.8 3.5 %collective-permute-done.10.r1_ref = bf16[2,256,256]{2,1,0:T(8,128)(2,1)S(1)} collective-permute-done((bf16[2,256,256]{2,1,0:T(8,128)(2,1)}, bf16[2,256,256]{2,1,0:T(8,128)(2,1)S(1)}, u32[]{:S(2)}, u32[]{:S(2)}) %collective-permute-start.10) | collective-permute-done | bytes 262176 | tf_op jit(solution)/shard_map/ppermute | solution.py:388
  92.3 3.9 %collective-permute-done.12.r3_ref = bf16[2,256,256]{2,1,0:T(8,128)(2,1)S(1)} collective-permute-done((bf16[2,256,256]{2,1,0:T(8,128)(2,1)}, bf16[2,256,256]{2,1,0:T(8,128)(2,1)S(1)}, u32[]{:S(2)}, u32[]{:S(2)}) %collective-permute-start.12) | collective-permute-done | bytes 262176 | tf_op jit(solution)/shard_map/ppermute | solution.py:388
  96.2 1.0 slice_bitcast_fusion.3
  97.2 0.9 collective-permute-start.16
  98.2 0.4 collective-permute-start.14
  98.7 0.4 collective-permute-done.16.t3_ref
  99.1 0.5 collective-permute-done.15.t2_ref
  99.6 0.2 collective-permute-done.14.t1_ref
  99.8 0.3 collective-permute-done.13.t0_ref
  100.1 5.5 %shard_map.169 = (bf16[256,512]{1,0:T(8,128)(2,1)}, bf16[256,512]{1,0:T(8,128)(2,1)}, f32[8,128]{1,0:T(8,128)}) custom-call(s32[16]{0:T(128)} %counts_ref.3, bf16[2,256,256]{2,1,0:T(8,128)(2,1)} %get-tuple-element.56.r0_ref, bf16[2,256,256]{2,1,0:T(8,128)(2,1)} %copy-done.4, bf16[2,256,256]{2,1,0:T(8,128)(2,1)} %copy-done.5, bf16[2,256,256]{2,1,0:T(8,128)(2,1)} %copy-done.6, ...), custom_call_target="tpu_custom_call" | custom-call | flops 1000000 | bytes 1048576 | tf_op jit(solution)/shard_map/pallas_call | solution.py:38
  105.8 1.2 collective-permute-done.17.g1_ref
  107.0 0.6 copy-done.15
  107.6 0.8 copy-done.7
  108.4 1.7 %shard_map.170.c0_ref = bf16[144,128]{1,0:T(8,128)(2,1)} custom-call(bf16[16,128,128]{2,1,0:T(8,128)(2,1)} %copy-done.7, f32[8,128]{1,0:T(8,128)} %get-tuple-element.65.g0_ref, f32[8,128]{1,0:T(8,128)} %copy-done.15), custom_call_target="tpu_custom_call" | custom-call | flops 1000000000 | bytes 1048576 | tf_op jit(solution)/shard_map/pallas_call | solution.py:38
  110.2 0.6 collective-permute-start.20
  110.8 0.8 collective-permute-start.18
  111.6 1.5 collective-permute-done.20.c3_ref
  113.2 2.1 %collective-permute-done.19.c2_ref = bf16[144,128]{1,0:T(8,128)(2,1)S(1)} collective-permute-done((bf16[144,128]{1,0:T(8,128)(2,1)}, bf16[144,128]{1,0:T(8,128)(2,1)S(1)}, u32[]{:S(2)}, u32[]{:S(2)}) %collective-permute-start.19) | collective-permute-done | bytes 36896 | tf_op jit(solution)/shard_map/ppermute | solution.py:388
  115.3 0.4 collective-permute-done.18.c1_ref
  115.7 0.2 copy-done.13
  115.9 0.6 copy-done.14
  116.5 2.1 %shard_map.171 = bf16[16,336,128]{2,1,0:T(8,128)(2,1)} custom-call(bf16[144,128]{1,0:T(8,128)(2,1)} %shard_map.170.c0_ref, bf16[144,128]{1,0:T(8,128)(2,1)} %copy-done.14, bf16[144,128]{1,0:T(8,128)(2,1)} %copy-done.13, bf16[144,128]{1,0:T(8,128)(2,1)} %copy-done.12), custom_call_target="tpu_custom_call" | custom-call | flops 2000000000 | bytes 1048576 | tf_op jit(solution)/shard_map/pallas_call | solution.py:38
  118.6 24.6 %all_to_all.20.mine_ref = bf16[16,336,128]{2,1,0:T(8,128)(2,1)S(1)} all-to-all(bf16[16,336,128]{2,1,0:T(8,128)(2,1)} %shard_map.171), channel_id=1, replica_groups=mesh['dom'=16,'blk'=8] {'dom'}, dimensions={0} | all-to-all | bytes 2752512 | tf_op jit(solution)/shard_map/all_to_all | solution.py:396
  143.2 3.6 %collective-permute-start.21 = (bf16[16,336,128]{2,1,0:T(8,128)(2,1)S(1)}, bf16[16,336,128]{2,1,0:T(8,128)(2,1)S(1)}, u32[]{:S(2)}, u32[]{:S(2)}) collective-permute-start(bf16[16,336,128]{2,1,0:T(8,128)(2,1)S(1)} %all_to_all.20.mine_ref), channel_id=1, source_target_pairs={{0,1},{1,0},{2,3},{3,2},{4,5},{5,4},{6,7},{7,6},{8,9},{9,8},{10,11... | collective-permute-start | bytes 4128776 | tf_op jit(solution)/shard_map/ppermute | solution.py:392
  146.8 2.8 %collective-permute-done.21.other_ref = bf16[16,336,128]{2,1,0:T(8,128)(2,1)S(1)} collective-permute-done((bf16[16,336,128]{2,1,0:T(8,128)(2,1)S(1)}, bf16[16,336,128]{2,1,0:T(8,128)(2,1)S(1)}, u32[]{:S(2)}, u32[]{:S(2)}) %collective-permute-start.21) | collective-permute-done | bytes 1376288 | tf_op jit(solution)/shard_map/ppermute | solution.py:392
  149.6 1.1 copy-done.3
  150.7 5.2 %shard_map.172 = (f32[5,512,512]{2,1,0:T(8,128)}, f32[1,512]{1,0:T(1,128)}) custom-call(bf16[16,336,128]{2,1,0:T(8,128)(2,1)} %copy-done.1, bf16[16,336,128]{2,1,0:T(8,128)(2,1)} %copy-done.3), custom_call_target="tpu_custom_call" | custom-call | tf_op jit(solution)/shard_map/pallas_call | solution.py:481
  (49 shorter events, 0.6 us)
Async XLA Ops:
  4.1 36.0 %all-to-all-start = ((bf16[16,128,512]{2,1,0:T(8,128)(2,1)}), bf16[16,128,512]{2,1,0:T(8,128)(2,1)S(1)}, u32[]{:S(2)}, u32[]{:S(2)}) async-start(bf16[16,128,512]{2,1,0:T(8,128)(2,1)} %get-tuple-element.44), calls=%async_computation | async-start | bytes 4194304 | tf_op jit(solution)/shard_map/all_to_all | solution.py:396
  11.7 14.8 %collective-permute-start.1 = (bf16[528,512]{1,0:T(8,128)(2,1)}, bf16[528,512]{1,0:T(8,128)(2,1)S(1)}, u32[]{:S(2)}, u32[]{:S(2)}) collective-permute-start(bf16[528,512]{1,0:T(8,128)(2,1)} %get-tuple-element.36.p0_ref), channel_id=1, source_target_pairs={{0,6},{1,7},{2,0},{3,1},{4,2},{5,3},{6,4},{7,5},{8,14},{9,15},{10,... | collective-permute-start | bytes 1622024 | tf_op jit(solution)/shard_map/ppermute | solution.py:388
  15.5 13.9 %collective-permute-start = (bf16[528,512]{1,0:T(8,128)(2,1)}, bf16[528,512]{1,0:T(8,128)(2,1)S(1)}, u32[]{:S(2)}, u32[]{:S(2)}) collective-permute-start(bf16[528,512]{1,0:T(8,128)(2,1)} %get-tuple-element.36.p0_ref), channel_id=1, source_target_pairs={{0,2},{1,3},{2,4},{3,5},{4,6},{5,7},{6,0},{7,1},{8,10},{9,11},{10,... | collective-permute-start | bytes 1622024 | tf_op jit(solution)/shard_map/ppermute | solution.py:388
  26.4 15.0 %copy-start.8 = (bf16[528,512]{1,0:T(8,128)(2,1)}, bf16[528,512]{1,0:T(8,128)(2,1)S(1)}, u32[]{:S(2)}) copy-start(bf16[528,512]{1,0:T(8,128)(2,1)S(1)} %collective-permute-done.1.p3_ref) | copy-start | bytes 1622020
  29.4 11.9 %copy-start.10 = (bf16[528,512]{1,0:T(8,128)(2,1)}, bf16[528,512]{1,0:T(8,128)(2,1)S(1)}, u32[]{:S(2)}) copy-start(bf16[528,512]{1,0:T(8,128)(2,1)S(1)} %collective-permute-done.p1_ref) | copy-start | bytes 1622020
  29.5 10.5 %collective-permute-start.3 = (bf16[272,512]{1,0:T(8,128)(2,1)S(1)}, bf16[272,512]{1,0:T(8,128)(2,1)S(1)}, u32[]{:S(2)}, u32[]{:S(2)}) collective-permute-start(bf16[272,512]{1,0:T(8,128)(2,1)S(1)} %slice.19), channel_id=1, source_target_pairs={{0,6},{1,7},{2,0},{3,1},{4,2},{5,3},{6,4},{7,5},{8,14},{9,15},{10,... | collective-permute-start | bytes 835592 | tf_op jit(solution)/shard_map/ppermute | solution.py:388
  29.8 7.0 %collective-permute-start.2 = (bf16[256,512]{1,0:T(8,128)(2,1)S(1)}, bf16[256,512]{1,0:T(8,128)(2,1)}, u32[]{:S(2)}, u32[]{:S(2)}) collective-permute-start(bf16[256,512]{1,0:T(8,128)(2,1)S(1)} %slice.18), channel_id=1, source_target_pairs={{0,2},{1,3},{2,4},{3,5},{4,6},{5,7},{6,0},{7,1},{8,10},{9,11},{10,... | collective-permute-start | bytes 786440 | tf_op jit(solution)/shard_map/ppermute | solution.py:388
  31.1 21.0 %collective-permute-start.4 = (bf16[528,512]{1,0:T(8,128)(2,1)}, bf16[528,512]{1,0:T(8,128)(2,1)}, u32[]{:S(2)}, u32[]{:S(2)}) collective-permute-start(bf16[528,512]{1,0:T(8,128)(2,1)} %get-tuple-element.36.p0_ref), channel_id=1, source_target_pairs={{0,1},{1,0},{2,3},{3,2},{4,5},{5,4},{6,7},{7,6},{8,9},{9,8},{10,11... | collective-permute-start | bytes 1622024 | tf_op jit(solution)/shard_map/ppermute | solution.py:392
  33.8 19.3 %collective-permute-start.5 = (bf16[528,512]{1,0:T(8,128)(2,1)S(1)}, bf16[528,512]{1,0:T(8,128)(2,1)}, u32[]{:S(2)}, u32[]{:S(2)}) collective-permute-start(bf16[528,512]{1,0:T(8,128)(2,1)S(1)} %collective-permute-done.p1_ref), channel_id=1, source_target_pairs={{0,1},{1,0},{2,3},{3,2},{4,5},{5,4},{6,7},{7,6},{8,9},{9,8},{10,11... | collective-permute-start | bytes 1622024 | tf_op jit(solution)/shard_map/ppermute | solution.py:392
  33.8 19.3 %collective-permute-start.8 = (bf16[528,512]{1,0:T(8,128)(2,1)S(1)}, bf16[528,512]{1,0:T(8,128)(2,1)}, u32[]{:S(2)}, u32[]{:S(2)}) collective-permute-start(bf16[528,512]{1,0:T(8,128)(2,1)S(1)} %collective-permute-done.1.p3_ref), channel_id=1, source_target_pairs={{0,1},{1,0},{2,3},{3,2},{4,5},{5,4},{6,7},{7,6},{8,9},{9,8},{10,11... | collective-permute-start | bytes 1622024 | tf_op jit(solution)/shard_map/ppermute | solution.py:392
  36.9 16.2 %collective-permute-start.6 = (bf16[256,512]{1,0:T(8,128)(2,1)}, bf16[256,512]{1,0:T(8,128)(2,1)}, u32[]{:S(2)}, u32[]{:S(2)}) collective-permute-start(bf16[256,512]{1,0:T(8,128)(2,1)} %collective-permute-done.2.t2_ref), channel_id=1, source_target_pairs={{0,1},{1,0},{2,3},{3,2},{4,5},{5,4},{6,7},{7,6},{8,9},{9,8},{10,11... | collective-permute-start | bytes 786440 | tf_op jit(solution)/shard_map/ppermute | solution.py:392
  40.0 12.1 %copy-start.11 = (bf16[272,512]{1,0:T(8,128)(2,1)}, bf16[272,512]{1,0:T(8,128)(2,1)S(1)}, u32[]{:S(2)}) copy-start(bf16[272,512]{1,0:T(8,128)(2,1)S(1)} %collective-permute-done.3.b2_ref) | copy-start | bytes 835588
  40.0 13.1 %collective-permute-start.7 = (bf16[272,512]{1,0:T(8,128)(2,1)S(1)}, bf16[272,512]{1,0:T(8,128)(2,1)}, u32[]{:S(2)}, u32[]{:S(2)}) collective-permute-start(bf16[272,512]{1,0:T(8,128)(2,1)S(1)} %collective-permute-done.3.b2_ref), channel_id=1, source_target_pairs={{0,1},{1,0},{2,3},{3,2},{4,5},{5,4},{6,7},{7,6},{8,9},{9,8},{10,11... | collective-permute-start | bytes 835592 | tf_op jit(solution)/shard_map/ppermute | solution.py:392
  40.1 1.3 copy-start.2
  41.4 40.5 %all-to-all-start.1 = ((bf16[16,128,512]{2,1,0:T(8,128)(2,1)}), bf16[16,128,512]{2,1,0:T(8,128)(2,1)S(1)}, u32[]{:S(2)}, u32[]{:S(2)}) async-start(bf16[16,128,512]{2,1,0:T(8,128)(2,1)} %get-tuple-element.54), calls=%async_computation.1 | async-start | bytes 4194304 | tf_op jit(solution)/shard_map/all_to_all | solution.py:396
  52.1 2.5 %collective-permute-start.9 = (bf16[16,64,128]{2,1,0:T(8,128)(2,1)}, bf16[16,64,128]{2,1,0:T(8,128)(2,1)}, u32[]{:S(2)}, u32[]{:S(2)}) collective-permute-start(bf16[16,64,128]{2,1,0:T(8,128)(2,1)} %get-tuple-element.48), channel_id=1, source_target_pairs={{0,1},{1,0},{2,3},{3,2},{4,5},{5,4},{6,7},{7,6},{8,9},{9,8},{10,11... | collective-permute-start | bytes 786440 | tf_op jit(solution)/shard_map/ppermute | solution.py:392
  77.9 14.4 %collective-permute-start.10 = (bf16[2,256,256]{2,1,0:T(8,128)(2,1)}, bf16[2,256,256]{2,1,0:T(8,128)(2,1)S(1)}, u32[]{:S(2)}, u32[]{:S(2)}) collective-permute-start(bf16[2,256,256]{2,1,0:T(8,128)(2,1)} %get-tuple-element.50), channel_id=1, source_target_pairs={{0,6},{1,7},{2,0},{3,1},{4,2},{5,3},{6,4},{7,5},{8,14},{9,15},{10,... | collective-permute-start | bytes 786440 | tf_op jit(solution)/shard_map/ppermute | solution.py:388
  81.2 11.1 %collective-permute-start.11 = (bf16[2,256,256]{2,1,0:T(8,128)(2,1)}, bf16[2,256,256]{2,1,0:T(8,128)(2,1)S(1)}, u32[]{:S(2)}, u32[]{:S(2)}) collective-permute-start(bf16[2,256,256]{2,1,0:T(8,128)(2,1)} %get-tuple-element.51), channel_id=1, source_target_pairs={{0,4},{1,5},{2,6},{3,7},{4,0},{5,1},{6,2},{7,3},{8,12},{9,13},{10,... | collective-permute-start | bytes 786440 | tf_op jit(solution)/shard_map/ppermute | solution.py:388
  81.2 15.0 %collective-permute-start.12 = (bf16[2,256,256]{2,1,0:T(8,128)(2,1)}, bf16[2,256,256]{2,1,0:T(8,128)(2,1)S(1)}, u32[]{:S(2)}, u32[]{:S(2)}) collective-permute-start(bf16[2,256,256]{2,1,0:T(8,128)(2,1)} %get-tuple-element.52), channel_id=1, source_target_pairs={{0,2},{1,3},{2,4},{3,5},{4,6},{5,7},{6,0},{7,1},{8,10},{9,11},{10,... | collective-permute-start | bytes 786440 | tf_op jit(solution)/shard_map/ppermute | solution.py:388
  81.9 18.2 %copy-start = (bf16[16,128,512]{2,1,0:T(8,128)(2,1)}, bf16[16,128,512]{2,1,0:T(8,128)(2,1)S(1)}, u32[]{:S(2)}) copy-start(bf16[16,128,512]{2,1,0:T(8,128)(2,1)S(1)} %all-to-all-done.1.back_ref) | copy-start | bytes 6291460
  81.9 25.1 %all-to-all-start.2 = ((bf16[16,128,128]{2,1,0:T(8,128)(2,1)}), bf16[16,128,128]{2,1,0:T(8,128)(2,1)S(1)}, u32[]{:S(2)}, u32[]{:S(2)}) async-start(bf16[16,128,128]{2,1,0:T(8,128)(2,1)} %get-tuple-element.64), calls=%async_computation.2 | async-start | bytes 1048576 | tf_op jit(solution)/shard_map/all_to_all | solution.py:396
  92.3 7.8 %copy-start.4 = (bf16[2,256,256]{2,1,0:T(8,128)(2,1)}, bf16[2,256,256]{2,1,0:T(8,128)(2,1)S(1)}, u32[]{:S(2)}) copy-start(bf16[2,256,256]{2,1,0:T(8,128)(2,1)S(1)} %collective-permute-done.10.r1_ref) | copy-start | bytes 786436
  92.3 7.8 %copy-start.5 = (bf16[2,256,256]{2,1,0:T(8,128)(2,1)}, bf16[2,256,256]{2,1,0:T(8,128)(2,1)S(1)}, u32[]{:S(2)}) copy-start(bf16[2,256,256]{2,1,0:T(8,128)(2,1)S(1)} %collective-permute-done.11.r2_ref) | copy-start | bytes 786436
  96.2 3.9 %copy-start.6 = (bf16[2,256,256]{2,1,0:T(8,128)(2,1)}, bf16[2,256,256]{2,1,0:T(8,128)(2,1)S(1)}, u32[]{:S(2)}) copy-start(bf16[2,256,256]{2,1,0:T(8,128)(2,1)S(1)} %collective-permute-done.12.r3_ref) | copy-start | bytes 786436
  97.2 1.9 %collective-permute-start.16 = (bf16[256,256]{1,0:T(8,128)(2,1)S(1)}, bf16[256,256]{1,0:T(8,128)(2,1)S(1)}, u32[]{:S(2)}, u32[]{:S(2)}) collective-permute-start(bf16[256,256]{1,0:T(8,128)(2,1)S(1)} %slice_bitcast_fusion), channel_id=1, source_target_pairs={{0,1},{1,0},{2,3},{3,2},{4,5},{5,4},{6,7},{7,6},{8,9},{9,8},{10,11... | collective-permute-start | bytes 393224 | tf_op jit(solution)/shard_map/ppermute | solution.py:392
  98.1 1.5 collective-permute-start.15
  98.2 1.6 %collective-permute-start.14 = (bf16[256,256]{1,0:T(8,128)(2,1)S(1)}, bf16[256,256]{1,0:T(8,128)(2,1)}, u32[]{:S(2)}, u32[]{:S(2)}) collective-permute-start(bf16[256,256]{1,0:T(8,128)(2,1)S(1)} %slice_bitcast_fusion.2), channel_id=1, source_target_pairs={{0,1},{1,0},{2,3},{3,2},{4,5},{5,4},{6,7},{7,6},{8,9},{9,8},{10,11... | collective-permute-start | bytes 393224 | tf_op jit(solution)/shard_map/ppermute | solution.py:392
  98.6 1.5 collective-permute-start.13
  99.1 1.0 copy-start.9
  105.7 1.4 collective-permute-start.17
  107.0 0.6 copy-start.15
  107.6 0.8 copy-start.7
  110.2 3.0 %collective-permute-start.20 = (bf16[144,128]{1,0:T(8,128)(2,1)}, bf16[144,128]{1,0:T(8,128)(2,1)S(1)}, u32[]{:S(2)}, u32[]{:S(2)}) collective-permute-start(bf16[144,128]{1,0:T(8,128)(2,1)} %shard_map.170.c0_ref), channel_id=1, source_target_pairs={{0,6},{1,7},{2,0},{3,1},{4,2},{5,3},{6,4},{7,5},{8,14},{9,15},{10,... | collective-permute-start | bytes 110600 | tf_op jit(solution)/shard_map/ppermute | solution.py:388
  110.8 4.5 %collective-permute-start.19 = (bf16[144,128]{1,0:T(8,128)(2,1)}, bf16[144,128]{1,0:T(8,128)(2,1)S(1)}, u32[]{:S(2)}, u32[]{:S(2)}) collective-permute-start(bf16[144,128]{1,0:T(8,128)(2,1)} %shard_map.170.c0_ref), channel_id=1, source_target_pairs={{0,4},{1,5},{2,6},{3,7},{4,0},{5,1},{6,2},{7,3},{8,12},{9,13},{10,... | collective-permute-start | bytes 110600 | tf_op jit(solution)/shard_map/ppermute | solution.py:388
  110.8 4.9 %collective-permute-start.18 = (bf16[144,128]{1,0:T(8,128)(2,1)}, bf16[144,128]{1,0:T(8,128)(2,1)S(1)}, u32[]{:S(2)}, u32[]{:S(2)}) collective-permute-start(bf16[144,128]{1,0:T(8,128)(2,1)} %shard_map.170.c0_ref), channel_id=1, source_target_pairs={{0,2},{1,3},{2,4},{3,5},{4,6},{5,7},{6,0},{7,1},{8,10},{9,11},{10,... | collective-permute-start | bytes 110600 | tf_op jit(solution)/shard_map/ppermute | solution.py:388
  113.2 2.5 %copy-start.12 = (bf16[144,128]{1,0:T(8,128)(2,1)}, bf16[144,128]{1,0:T(8,128)(2,1)S(1)}, u32[]{:S(2)}) copy-start(bf16[144,128]{1,0:T(8,128)(2,1)S(1)} %collective-permute-done.20.c3_ref) | copy-start | bytes 110596
  115.3 0.6 copy-start.13
  115.9 0.6 copy-start.14
  143.2 6.4 %copy-start.1 = (bf16[16,336,128]{2,1,0:T(8,128)(2,1)}, bf16[16,336,128]{2,1,0:T(8,128)(2,1)S(1)}, u32[]{:S(2)}) copy-start(bf16[16,336,128]{2,1,0:T(8,128)(2,1)S(1)} %all_to_all.20.mine_ref) | copy-start | bytes 4128772
  143.2 6.4 %collective-permute-start.21 = (bf16[16,336,128]{2,1,0:T(8,128)(2,1)S(1)}, bf16[16,336,128]{2,1,0:T(8,128)(2,1)S(1)}, u32[]{:S(2)}, u32[]{:S(2)}) collective-permute-start(bf16[16,336,128]{2,1,0:T(8,128)(2,1)S(1)} %all_to_all.20.mine_ref), channel_id=1, source_target_pairs={{0,1},{1,0},{2,3},{3,2},{4,5},{5,4},{6,7},{7,6},{8,9},{9,8},{10,11... | collective-permute-start | bytes 4128776 | tf_op jit(solution)/shard_map/ppermute | solution.py:392
  149.6 1.1 copy-start.3

commit v5 on v4

--- a/solution.py
+++ b/solution.py
@@ -23,6 +23,7 @@
 SCORE_SUB = (8.0 + 256.0) * LOG2E
 CHUNK = 64 + 64 + 16
 SPREAD = 4 * 64 + 64 + 16
+PART = 160
 
 NT = (((1,), (1,)), ((), ()))
 NN = (((1,), (0,)), ((), ()))
@@ -47,6 +48,11 @@
 
 def shape(dims, dtype):
     return jax.ShapeDtypeStruct(dims, dtype)
+
+
+def dom_position():
+    me = lax.axis_index("dom").astype(jnp.int32)
+    return lax.shift_right_logical(me, 2), me & 3
 
 
 def position():
@@ -261,20 +267,27 @@
             chunks_ref[p, 64:128, :] = (mine_ref[p].astype(F32) + other_ref[p].astype(F32)).astype(BF16)
 
 
-def chunk_sum_body(in_ref, g0_ref, g1_ref, out_ref):
+def chunk_sum_body(in_ref, g0_ref, g1_ref, wqkv_ref, out_ref, extra_ref):
     total = in_ref[0].astype(F32)
     for p in range(1, DOM):
         total = total + in_ref[p].astype(F32)
     out_ref[0:128, :] = total.astype(BF16)
     z, core = position()
+    kind, lanes = dom_position()
     one, two = g0_ref[...], g1_ref[...]
-    gain = jnp.where(core == 0, one, two) + jnp.where(core == 0, two, one)
-    coarse = gain.astype(BF16).astype(F32)
-    fine = gain - coarse
-    out_ref[128:CHUNK, :] = jnp.concatenate([coarse, fine], axis=0).astype(BF16)
-
-
-def spread_body(c0_ref, c1_ref, c2_ref, c3_ref, out_ref, parts_ref):
+    extra_ref[...] = jnp.where(core == 0, one, two) + jnp.where(core == 0, two, one)
+    for b in range(4):
+        @pl.when((kind < 3) & (lanes == b))
+        def _():
+            start = pl.multiple_of(jnp.minimum(kind, 2) * HEAD, HEAD)
+            weights = wqkv_ref[pl.ds(start, HEAD), b * 128 : (b + 1) * 128].astype(F32)
+            extra_ref[4:5, :] = jnp.sum(weights * total[0:HEAD], axis=0, keepdims=True)
+    extra = extra_ref[...]
+    coarse = extra.astype(BF16).astype(F32)
+    out_ref[128:CHUNK, :] = jnp.concatenate([coarse, extra - coarse], axis=0).astype(BF16)
+
+
+def spread_body(c0_ref, c1_ref, c2_ref, c3_ref, first_ref, second_ref, parts_ref):
     z, core = position()
     for dz, c_ref in enumerate((c0_ref, c1_ref, c2_ref, c3_ref)):
         parts_ref[dz] = c_ref[64:CHUNK, :].astype(F32)
@@ -284,16 +297,35 @@
     gain = total[64:72] + total[72:80]
     coarse = gain.astype(BF16).astype(F32)
     tail = jnp.concatenate([total[0:64], coarse, gain - coarse], axis=0).astype(BF16)
-    for p in range(DOM):
-        for dz, c_ref in enumerate((c0_ref, c1_ref, c2_ref, c3_ref)):
-            out_ref[p, dz * 64 : (dz + 1) * 64, :] = c_ref[0:64, :]
-        out_ref[p, 256:SPREAD, :] = tail
+    whole = jnp.concatenate([c_ref[0:64, :] for c_ref in (c0_ref, c1_ref, c2_ref, c3_ref)] + [tail], axis=0)
+    first_ref[...] = whole[0:PART]
+    second_ref[...] = whole[PART:SPREAD]
+
+
+def halo_body(counts_ref, back_ref, rows_ref, x_ref, out_ref, gain_grad_ref):
+    row = lax.broadcasted_iota(jnp.int32, (ROWS, CAP), 0)
+    slot = lax.broadcasted_iota(jnp.int32, (ROWS, CAP), 1)
+    total = jnp.zeros((ROWS, D), F32)
+    for k in range(4):
+        hits = []
+        for p in range(4 * k, 4 * k + 4):
+            hit = (row == rows_ref[p : p + 1, :]) & (slot < counts_ref[p])
+            hits.append(jnp.where(hit, 1.0, 0.0).astype(BF16))
+        part = jnp.concatenate([back_ref[p] for p in range(4 * k, 4 * k + 4)], axis=0)
+        total = total + dot(jnp.concatenate(hits, axis=1), part)
+    out_ref[...] = total
+    x = x_ref[...].astype(F32)
+    scale = lax.rsqrt(jnp.mean(x * x, axis=-1, keepdims=True) + EPS)
+    gain_grad = jnp.sum(total * (x * scale), axis=0, keepdims=True)
+    gain_grad_ref[...] = jnp.zeros((8, 128), F32)
+    for k in range(4):
+        gain_grad_ref[k : k + 1, :] = gain_grad[:, k * 128 : (k + 1) * 128]
 
 
 def rows_body(
-    counts_ref, r0_ref, r1_ref, r2_ref, r3_ref, t0_ref, t1_ref, t2_ref, t3_ref, back_ref, rows_ref, base_ref, x_ref,
+    r0_ref, r1_ref, r2_ref, r3_ref, t0_ref, t1_ref, t2_ref, t3_ref, halo_ref, base_ref, x_ref,
     gain_ref, grad_ref, wq_ref, wk_ref, wv_ref, wo_ref,
-    out_ref, feature_ref, gain_grad_ref, dq_ref, dk_ref, dv_ref, at_ref,
+    out_ref, feature_ref, dq_ref, dk_ref, dv_ref, at_ref,
 ):
     left = lax.broadcasted_iota(jnp.int32, (ROWS, 128), 1) < HEAD
     z, core = position()
@@ -314,70 +346,67 @@
 
     out_ref[...] = (base_ref[...] + dot(whole(at_ref), wo_ref[...])).astype(BF16)
     dnormed = dot(whole(dq_ref), wq_ref[...], NT) + dot(whole(dk_ref), wk_ref[...], NT)
-    dnormed = dnormed + dot(whole(dv_ref), wv_ref[...], NT)
-    row = lax.broadcasted_iota(jnp.int32, (ROWS, CAP), 0)
-    slot = lax.broadcasted_iota(jnp.int32, (ROWS, CAP), 1)
-    for k in range(4):
-        hits = []
-        for p in range(4 * k, 4 * k + 4):
-            hit = (row == rows_ref[p : p + 1, :]) & (slot < counts_ref[p])
-            hits.append(jnp.where(hit, 1.0, 0.0).astype(BF16))
-        part = jnp.concatenate([back_ref[p] for p in range(4 * k, 4 * k + 4)], axis=0)
-        dnormed = dnormed + dot(jnp.concatenate(hits, axis=1), part)
+    dnormed = dnormed + dot(whole(dv_ref), wv_ref[...], NT) + halo_ref[...]
     x = x_ref[...].astype(F32)
     scale = lax.rsqrt(jnp.mean(x * x, axis=-1, keepdims=True) + EPS)
-    gain_grad = jnp.sum(dnormed * (x * scale), axis=0, keepdims=True)
-    gain_grad_ref[...] = jnp.zeros((8, 128), F32)
-    for k in range(4):
-        gain_grad_ref[k : k + 1, :] = gain_grad[:, k * 128 : (k + 1) * 128]
     scaled = dnormed * gain_ref[...]
     inner = jnp.mean(scaled * x, axis=-1, keepdims=True)
     dx = scale * scaled - x * (scale * scale * scale * inner)
     feature_ref[...] = (grad_ref[...].astype(F32) + dx).astype(BF16)
 
 
-def weights_body(mine_ref, other_ref, out_ref, gain_ref):
+def weights_body(*refs):
+    gain_in_ref, out_ref, gain_ref, all_ref = refs[16:20]
     which = pl.program_id(0)
-    z, core = position()
 
     @pl.when(which == 0)
     def _():
+        z, core = position()
+        x, y = dom_position()
+        for c in range(2):
+            owner = core ^ c
+            for dx in range(4):
+                for dy in range(4):
+                    p = ((x - dx) & 3) * 4 + ((y - dy) & 3)
+                    all_ref[owner, p, 0:PART, :] = refs[c * 8 + dx][dy]
+                    all_ref[owner, p, PART:SPREAD, :] = refs[c * 8 + 4 + dy][dx]
         gain = jnp.zeros((8, 128), F32)
+        through = []
         for p in range(DOM):
-            tail = mine_ref[p, 320:SPREAD, :].astype(F32)
-            gain = gain + (tail[0:8] + tail[8:16])
-        for k in range(4):
-            gain_ref[:, k * 128 : (k + 1) * 128] = gain[k : k + 1, :]
-
-    for c in range(2):
-        @pl.when(core == c)
-        def _():
-            def piece(h, p):
-                start = ((z - (h >> 1)) & 3) * 64
-                ref = mine_ref if h & 1 == c else other_ref
-                return ref[p, pl.ds(pl.multiple_of(start, 64), 64), :].astype(F32)
-
-            @pl.when(which < 3)
-            def _():
+            tails = [all_ref[c, p, 320:SPREAD, :].astype(F32) for c in range(2)]
+            tails = [tail[0:8] + tail[8:16] for tail in tails]
+            gain = gain + jnp.where(core == 0, tails[0], tails[1])
+            through.append(tails[0] + tails[1])
+        for b in range(4):
+            part = (through[b] + through[4 + b] + through[8 + b])[4:5]
+            lanes = slice(b * 128, (b + 1) * 128)
+            gain_ref[:, lanes] = gain[b : b + 1] + part / gain_in_ref[:, lanes]
+
+    def piece(h, p):
+        z, core = position()
+        start = pl.multiple_of(((z - (h >> 1)) & 3) * 64, 64)
+        return all_ref[h & 1, p, pl.ds(start, 64), :].astype(F32)
+
+    @pl.when(which < 3)
+    def _():
+        for b in range(4):
+            part = jnp.concatenate([piece(h, which * 4 + b) for h in range(BLK)], axis=0)
+            out_ref[0, b * 128 : (b + 1) * 128, :] = jnp.transpose(part)
+
+    @pl.when(which == 3)
+    def _():
+        for h in range(BLK):
+            for b in range(4):
+                out_ref[0, h * 64 : (h + 1) * 64, b * 128 : (b + 1) * 128] = piece(h, 12 + b)
+
+    @pl.when(which == 4)
+    def _():
+        for half in range(2):
+            for p in range(DOM):
+                top = half * 256 + p * 16
                 for b in range(4):
-                    part = jnp.concatenate([piece(h, which * 4 + b) for h in range(BLK)], axis=0)
-                    out_ref[0, b * 128 : (b + 1) * 128, :] = jnp.transpose(part)
-
-            @pl.when(which == 3)
-            def _():
-                for h in range(BLK):
-                    for b in range(4):
-                        out_ref[0, h * 64 : (h + 1) * 64, b * 128 : (b + 1) * 128] = piece(h, 12 + b)
-
-            @pl.when(which == 4)
-            def _():
-                for half in range(2):
-                    ref = mine_ref if half == c else other_ref
-                    for p in range(DOM):
-                        top = half * 256 + p * 16
-                        for b in range(4):
-                            part = ref[p, 256 + b * 16 : 272 + b * 16, :]
-                            out_ref[0, top : top + 16, b * 128 : (b + 1) * 128] = part.astype(F32)
+                    part = all_ref[half, p, 256 + b * 16 : 272 + b * 16, :]
+                    out_ref[0, top : top + 16, b * 128 : (b + 1) * 128] = part.astype(F32)
 
 
 def chip_shift(step, swap):
@@ -390,6 +419,11 @@
 
 def other_core(array):
     return lax.ppermute(array, "blk", chip_shift(0, 1))
+
+
+def along_dom(array, x_step, y_step):
+    pairs = [(x * 4 + y, (x + x_step) % 4 * 4 + (y + y_step) % 4) for x in range(4) for y in range(4)]
+    return lax.ppermute(array, "dom", pairs)
 
 
 def to_dom_peers(array):
@@ -457,34 +491,54 @@
         ],
         micros=12,
     )
-    chunks, back = lax.optimization_barrier((chunks, back))
+    chunks, back, *results = lax.optimization_barrier((chunks, back, *results))
     chunks = to_dom_peers(chunks)
-
+    halo, gain_part = call(
+        halo_body,
+        (shape((ROWS, D), F32), shape((8, 128), F32)),
+        (send_counts, back, send_rows, x),
+        scalars=1,
+        micros=3,
+    )
     results = [results[0]] + [along_chips(results[dz], -dz) for dz in (1, 2, 3)]
-    *results, back = lax.optimization_barrier((*results, back))
     swapped = [other_core(part[1]) for part in results]
-    layer_out, feature_grad, gain_part = call(
-        rows_body,
-        (shape((ROWS, D), BF16), shape((ROWS, D), BF16), shape((8, 128), F32)),
-        (send_counts, *results, *swapped, back, send_rows, base, x, gain_row, out_grad, wq, wk, wv, wo),
-        scratch=[pltpu.VMEM((4, ROWS, 128), BF16)] * 4,
-        scalars=1,
-        micros=0.001,
-    )
+    chunks, *swapped = lax.optimization_barrier((chunks, *swapped))
     chunk = call(
-        chunk_sum_body, shape((CHUNK, 128), BF16), (chunks, gain_part, other_core(gain_part)), micros=1
+        chunk_sum_body,
+        shape((CHUNK, 128), BF16),
+        (chunks, gain_part, other_core(gain_part), wqkv),
+        scratch=[pltpu.VMEM((8, 128), F32)],
+        micros=1,
     )
     chunk_parts = [chunk] + [along_chips(chunk, step) for step in (1, 2, 3)]
-    spread = call(spread_body, shape((DOM, SPREAD, 128), BF16), chunk_parts, scratch=[pltpu.VMEM((4, 80, 128), F32)])
-    gathered = to_dom_peers(spread)
-    whole = pl.BlockSpec((DOM, SPREAD, 128), lambda t: (0, 0, 0))
+    first, second = call(
+        spread_body,
+        (shape((PART, 128), BF16), shape((SPREAD - PART, 128), BF16)),
+        chunk_parts,
+        scratch=[pltpu.VMEM((4, 80, 128), F32)],
+        micros=1,
+    )
+    first = jnp.stack([first] + [along_dom(first, 0, step) for step in (1, 2, 3)])
+    second = jnp.stack([second] + [along_dom(second, step, 0) for step in (1, 2, 3)])
+    parts = [first] + [along_dom(first, step, 0) for step in (1, 2, 3)]
+    parts = parts + [second] + [along_dom(second, 0, step) for step in (1, 2, 3)]
+    parts = parts + [other_core(part) for part in parts]
     weight_grads, gain_grad = pl.pallas_call(
         weights_body,
         grid=(5,),
         out_shape=(shape((5, D, D), F32), shape((1, D), F32)),
-        in_specs=[whole, whole],
+        in_specs=[pl.BlockSpec(part.shape, lambda t: (0, 0, 0)) for part in parts] + [pl.BlockSpec((1, D), lambda t: (0, 0))],
         out_specs=(pl.BlockSpec((1, D, D), lambda t: (t, 0, 0)), pl.BlockSpec((1, D), lambda t: (0, 0))),
-    )(gathered, other_core(gathered))
+        scratch_shapes=[pltpu.VMEM((2, DOM, SPREAD, 128), BF16)],
+    )(*parts, gain_row)
+
+    layer_out, feature_grad = call(
+        rows_body,
+        (shape((ROWS, D), BF16), shape((ROWS, D), BF16)),
+        (*results, *swapped, halo, base, x, gain_row, out_grad, wq, wk, wv, wo),
+        scratch=[pltpu.VMEM((4, ROWS, 128), BF16)] * 4,
+        micros=5,
+    )
     return layer_out, feature_grad, weight_grads, gain_grad.reshape(D)
 
 

time: 156 us -> 170 us (1.090)
  blocking collectives: 24.6 us -> 0 us
  starting transfers between devices: 44.4 us -> 62 us
  waiting for transfers between devices: 25.8 us -> 41 us
  Pallas kernels: 54.5 us -> 56.5 us
  local copies, waits for them, and re-layouts: 5.73 us -> 7.5 us
    all_to_all x1 -> x0, blocking collectives: 24.6 us -> none  [to_dom_peers(): return lax.all_to_all(array, 'dom', split_axis=0, concat_axis=0, tiled=True)]
    ppermute x0 -> x12, starting transfers between devices: none -> 13.7 us  [along_dom(): return lax.ppermute(array, 'dom', pairs)]
    ppermute x0 -> x12, waiting for transfers between devices: none -> 12.4 us  [along_dom(): return lax.ppermute(array, 'dom', pairs)]
    all_to_all x3, waiting for transfers between devices: 0.01 us -> 6.66 us  [to_dom_peers(): return lax.all_to_all(array, 'dom', split_axis=0, concat_axis=0, tiled=True)]
    ppermute x12 -> x19, starting transfers between devices: 12.7 us -> 18.1 us  [other_core(): return lax.ppermute(array, 'blk', chip_shift(0, 1))]
    ppermute x12 -> x19, waiting for transfers between devices: 6.82 us -> 3.02 us  [other_core(): return lax.ppermute(array, 'blk', chip_shift(0, 1))]
    all_to_all x3, starting transfers between devices: 20.8 us -> 18.3 us  [to_dom_peers(): return lax.all_to_all(array, 'dom', split_axis=0, concat_axis=0, tiled=True)]
    pallas_call x7 -> x8, Pallas kernels: 49.3 us -> 51 us  [call(): pl.pallas_call(body, out_shape=out_shape, in_specs=specs, out_specs=jax.t...]
  transfers between devices with their start and end apart: 25 -> 44, of which waited for: 15 -> 15; matrix products, arithmetic and copies ran while one was open for 1% -> 2% of each run, Pallas kernels for 27% -> 26%
where the time goes in v5:
time: 170 us
  starting transfers between devices  62 us (36%)
  Pallas kernels  56.5 us (33%)
  waiting for transfers between devices  41 us (24%)
  local copies, waits for them, and re-layouts  7.5 us (4%)
    pallas_call x8, Pallas kernels, call(): pl.pallas_call(body, out_shape=out_shape, in_specs=specs, out_specs=jax.t...  51 us
    ppermute x10, waiting for transfers between devices, along_chips(): return lax.ppermute(array, 'blk', chip_shift(step, 0))  18.9 us
    all_to_all x3, starting transfers between devices, to_dom_peers(): return lax.all_to_all(array, 'dom', split_axis=0, concat_axis=0, tiled=True)  18.3 us
    ppermute x19, starting transfers between devices, other_core(): return lax.ppermute(array, 'blk', chip_shift(0, 1))  18.1 us
    ppermute x12, starting transfers between devices, along_dom(): return lax.ppermute(array, 'dom', pairs)  13.7 us
    ppermute x12, waiting for transfers between devices, along_dom(): return lax.ppermute(array, 'dom', pairs)  12.4 us
    ppermute x10, starting transfers between devices, along_chips(): return lax.ppermute(array, 'blk', chip_shift(step, 0))  11.8 us
    all_to_all x3, waiting for transfers between devices, to_dom_peers(): return lax.all_to_all(array, 'dom', split_axis=0, concat_axis=0, tiled=True)  6.66 us
  transfers between devices with their start and end apart: 44, of which 15 were waited for; matrix products, arithmetic and copies ran while one was open for 2% of the time, Pallas kernels for 26%

profile of v5, /device:TPU:1, one launch (start us, length us, event | category | flops | bytes accessed | tf_op | source)
XLA Modules:
  0.0 169.6 jit_solution(9187454197758553046)
XLA Ops:
  0.6 3.4 %shard_map.165 = (bf16[528,512]{1,0:T(8,128)(2,1)}, bf16[16,128,512]{2,1,0:T(8,128)(2,1)}) custom-call(s32[1,8]{1,0:T(1,128)} %pattern_ref.1, s32[16]{0:T(128)} %counts_ref.3, bf16[256,512]{1,0:T(8,128)(2,1)} %x_ref.7, f32[1,512]{1,0:T(1,128)} %bitcast.29, s32[1,256]{1,0:T(1,128)} %bitcast.35, bf16[256,512]{1,0:T(8,128)(2,1)} %grad_ref.7, s32[16,128]{1,0:T(8,128)} %rows_ref.3), custom_call_target="tpu_custom_call" | custom-call | flops 4000000000 | bytes 1048576 | tf_op jit(solution)/shard_map/pallas_call | solution.py:39
  4.1 7.6 %all-to-all-start = ((bf16[16,128,512]{2,1,0:T(8,128)(2,1)}), bf16[16,128,512]{2,1,0:T(8,128)(2,1)S(1)}, u32[]{:S(2)}, u32[]{:S(2)}) async-start(bf16[16,128,512]{2,1,0:T(8,128)(2,1)} %get-tuple-element.51), calls=%async_computation | async-start | bytes 4194304 | tf_op jit(solution)/shard_map/all_to_all | solution.py:430
  11.7 3.8 %collective-permute-start.1 = (bf16[528,512]{1,0:T(8,128)(2,1)}, bf16[528,512]{1,0:T(8,128)(2,1)S(1)}, u32[]{:S(2)}, u32[]{:S(2)}) collective-permute-start(bf16[528,512]{1,0:T(8,128)(2,1)} %get-tuple-element.43.p0_ref), channel_id=1, source_target_pairs={{0,6},{1,7},{2,0},{3,1},{4,2},{5,3},{6,4},{7,5},{8,14},{9,15},{10,... | collective-permute-start | bytes 1622024 | tf_op jit(solution)/shard_map/ppermute | solution.py:417
  15.5 8.9 %shard_map.166 = (bf16[1024,512]{1,0:T(8,128)(2,1)}, f32[256,128]{1,0:T(8,128)}, bf16[16,128,512]{2,1,0:T(8,128)(2,1)}, bf16[192,512]{1,0:T(8,128)(2,1)}, bf16[64,512]{1,0:T(8,128)(2,1)}) custom-call(s32[32,128]{1,0:T(8,128)} %bitcast.32, s32[32,128]{1,0:T(8,128)} %bitcast.33, bf16[256,512]{1,0:T(8,128)(2,1)} %grad_ref.7, bf16[512,512]{1,0:T(8,128)(2,1)} %w_ref.3, ...), custom_call_target="tpu_custom_call" | custom-call | flops 10000000000 | bytes 1048576 | tf_op jit(solution)/shard_map/pallas_call | solution.py:39
  24.4 2.0 %collective-permute-done.1.p3_ref = bf16[528,512]{1,0:T(8,128)(2,1)S(1)} collective-permute-done((bf16[528,512]{1,0:T(8,128)(2,1)}, bf16[528,512]{1,0:T(8,128)(2,1)S(1)}, u32[]{:S(2)}, u32[]{:S(2)}) %collective-permute-start.1) | collective-permute-done | bytes 540704 | tf_op jit(solution)/shard_map/ppermute | solution.py:417
  26.4 3.0 %collective-permute-done.p1_ref = bf16[528,512]{1,0:T(8,128)(2,1)S(1)} collective-permute-done((bf16[528,512]{1,0:T(8,128)(2,1)}, bf16[528,512]{1,0:T(8,128)(2,1)S(1)}, u32[]{:S(2)}, u32[]{:S(2)}) %collective-permute-start) | collective-permute-done | bytes 540704 | tf_op jit(solution)/shard_map/ppermute | solution.py:417
  29.4 0.8 copy-done.20
  30.7 1.0 slice.18
  31.6 1.2 collective-permute-start.2
  32.8 6.7 %all-to-all-done.table_ref = bf16[16,128,512]{2,1,0:T(8,128)(2,1)S(1)} async-done(((bf16[16,128,512]{2,1,0:T(8,128)(2,1)}), bf16[16,128,512]{2,1,0:T(8,128)(2,1)S(1)}, u32[]{:S(2)}, u32[]{:S(2)}) %all-to-all-start) | async-done | bytes 2097184 | tf_op jit(solution)/shard_map/all_to_all | solution.py:430
  39.5 1.3 copy-done.1
  40.8 3.9 %all-to-all-start.1 = ((bf16[16,128,512]{2,1,0:T(8,128)(2,1)}), bf16[16,128,512]{2,1,0:T(8,128)(2,1)S(1)}, u32[]{:S(2)}, u32[]{:S(2)}) async-start(bf16[16,128,512]{2,1,0:T(8,128)(2,1)} %get-tuple-element.57), calls=%async_computation.1 | async-start | bytes 4194304 | tf_op jit(solution)/shard_map/all_to_all | solution.py:430
  44.8 3.3 %collective-permute-start.4 = (bf16[528,512]{1,0:T(8,128)(2,1)}, bf16[528,512]{1,0:T(8,128)(2,1)}, u32[]{:S(2)}, u32[]{:S(2)}) collective-permute-start(bf16[528,512]{1,0:T(8,128)(2,1)} %get-tuple-element.43.p0_ref), channel_id=1, source_target_pairs={{0,1},{1,0},{2,3},{3,2},{4,5},{5,4},{6,7},{7,6},{8,9},{9,8},{10,11... | collective-permute-start | bytes 1622024 | tf_op jit(solution)/shard_map/ppermute | solution.py:421
  49.2 4.3 %shard_map.167 = (f32[256,512]{1,0:T(8,128)}, bf16[16,64,128]{2,1,0:T(8,128)(2,1)}, bf16[16,64,128]{2,1,0:T(8,128)(2,1)}) custom-call(bf16[1024,512]{1,0:T(8,128)(2,1)} %get-tuple-element.49.counts_t_ref, f32[256,128]{1,0:T(8,128)} %get-tuple-element.50.degree_ref, bf16[16,128,512]{2,1,0:T(8,128)(2,1)} %copy-done.1, bf16[256,512]{1,0:T(8,128)(2,1)} %x_ref.7, ...), custom_call_target="tpu_custom_call" | custom-call | flops 4000000000 | bytes 1048576 | tf_op jit(solution)/shard_map/pallas_call | solution.py:39
  53.9 1.7 %collective-permute-done.9.other_ref = bf16[16,64,128]{2,1,0:T(8,128)(2,1)} collective-permute-done((bf16[16,64,128]{2,1,0:T(8,128)(2,1)}, bf16[16,64,128]{2,1,0:T(8,128)(2,1)}, u32[]{:S(2)}, u32[]{:S(2)}) %collective-permute-start.9) | collective-permute-done | bytes 262176 | tf_op jit(solution)/shard_map/ppermute | solution.py:421
  55.6 23.4 %shard_map.168 = (bf16[2,256,256]{2,1,0:T(8,128)(2,1)}, bf16[2,256,256]{2,1,0:T(8,128)(2,1)}, bf16[2,256,256]{2,1,0:T(8,128)(2,1)}, bf16[2,256,256]{2,1,0:T(8,128)(2,1)}, bf16[16,128,128]{2,1,0:T(8,128)(2,1)}) custom-call(bf16[528,512]{1,0:T(8,128)(2,1)} %get-tuple-element.43.p0_ref, bf16[528,512]{1,0:T(8,128)(2,1)} %copy-done.20, ...), custom_call_target="tpu_custom_call" | custom-call | flops 12000000000 | bytes 1048576 | tf_op jit(solution)/shard_map/pallas_call | solution.py:39
  79.0 3.8 %collective-permute-start.10 = (bf16[2,256,256]{2,1,0:T(8,128)(2,1)}, bf16[2,256,256]{2,1,0:T(8,128)(2,1)S(1)}, u32[]{:S(2)}, u32[]{:S(2)}) collective-permute-start(bf16[2,256,256]{2,1,0:T(8,128)(2,1)} %get-tuple-element.63), channel_id=1, source_target_pairs={{0,6},{1,7},{2,0},{3,1},{4,2},{5,3},{6,4},{7,5},{8,14},{9,15},{10,... | collective-permute-start | bytes 786440 | tf_op jit(solution)/shard_map/ppermute | solution.py:417
  82.9 6.8 %all-to-all-start.2 = ((bf16[16,128,128]{2,1,0:T(8,128)(2,1)}), bf16[16,128,128]{2,1,0:T(8,128)(2,1)S(1)}, u32[]{:S(2)}, u32[]{:S(2)}) async-start(bf16[16,128,128]{2,1,0:T(8,128)(2,1)} %get-tuple-element.66), calls=%async_computation.2 | async-start | bytes 1048576 | tf_op jit(solution)/shard_map/all_to_all | solution.py:430
  89.8 0.9 slice_bitcast_fusion.3
  91.5 1.0 collective-permute-start.12
  92.9 5.7 %collective-permute-done.11.r2_ref = bf16[2,256,256]{2,1,0:T(8,128)(2,1)S(1)} collective-permute-done((bf16[2,256,256]{2,1,0:T(8,128)(2,1)}, bf16[2,256,256]{2,1,0:T(8,128)(2,1)S(1)}, u32[]{:S(2)}, u32[]{:S(2)}) %collective-permute-start.11) | collective-permute-done | bytes 262176 | tf_op jit(solution)/shard_map/ppermute | solution.py:417
  98.7 2.9 %collective-permute-start.15 = (bf16[256,256]{1,0:T(8,128)(2,1)S(1)}, bf16[256,256]{1,0:T(8,128)(2,1)}, u32[]{:S(2)}, u32[]{:S(2)}) collective-permute-start(bf16[256,256]{1,0:T(8,128)(2,1)S(1)} %slice_bitcast_fusion.1), channel_id=1, source_target_pairs={{0,1},{1,0},{2,3},{3,2},{4,5},{5,4},{6,7},{7,6},{8,9},{9,8},{10,11... | collective-permute-start | bytes 393224 | tf_op jit(solution)/shard_map/ppermute | solution.py:421
  101.5 3.8 %collective-permute-done.12.r3_ref = bf16[2,256,256]{2,1,0:T(8,128)(2,1)S(1)} collective-permute-done((bf16[2,256,256]{2,1,0:T(8,128)(2,1)}, bf16[2,256,256]{2,1,0:T(8,128)(2,1)S(1)}, u32[]{:S(2)}, u32[]{:S(2)}) %collective-permute-start.12) | collective-permute-done | bytes 262176 | tf_op jit(solution)/shard_map/ppermute | solution.py:417
  106.5 3.1 %shard_map.169 = (f32[256,512]{1,0:T(8,128)}, f32[8,128]{1,0:T(8,128)}) custom-call(s32[16]{0:T(128)} %counts_ref.3, bf16[16,128,512]{2,1,0:T(8,128)(2,1)} %copy-done, s32[16,128]{1,0:T(8,128)} %rows_ref.3, bf16[256,512]{1,0:T(8,128)(2,1)} %x_ref.7), custom_call_target="tpu_custom_call" | custom-call | flops 3000000000 | bytes 1048576 | tf_op jit(solution)/shard_map/pallas_call | solution.py:39
  109.8 1.3 collective-permute-done.17.g1_ref
  111.6 1.8 %shard_map.171.c0_ref = bf16[144,128]{1,0:T(8,128)(2,1)} custom-call(bf16[16,128,128]{2,1,0:T(8,128)(2,1)} %copy-done.4, f32[8,128]{1,0:T(8,128)} %get-tuple-element.77.g0_ref, f32[8,128]{1,0:T(8,128)} %copy-done.31, bf16[192,512]{1,0:T(8,128)(2,1)} %get-tuple-element.47.wqkv_ref), custom_call_target="tpu_custom_call" | custom-call | flops 1000000000 | bytes 1048576 | tf_op jit(solution)/shard_map/pallas_call | solution.py:39
  113.8 1.1 collective-permute-start.18
  114.9 1.5 collective-permute-done.20.c3_ref
  116.5 1.8 %collective-permute-done.19.c2_ref = bf16[144,128]{1,0:T(8,128)(2,1)S(1)} collective-permute-done((bf16[144,128]{1,0:T(8,128)(2,1)}, bf16[144,128]{1,0:T(8,128)(2,1)S(1)}, u32[]{:S(2)}, u32[]{:S(2)}) %collective-permute-start.19) | collective-permute-done | bytes 36896 | tf_op jit(solution)/shard_map/ppermute | solution.py:417
  118.3 0.9 collective-permute-done.18.c1_ref
  119.8 1.5 shard_map.172
  121.3 2.5 %collective-permute-start.23 = (bf16[160,128]{1,0:T(8,128)(2,1)}, bf16[160,128]{1,0:T(8,128)(2,1)S(1)}, u32[]{:S(2)}, u32[]{:S(2)}) collective-permute-start(bf16[160,128]{1,0:T(8,128)(2,1)} %get-tuple-element.78), channel_id=1, source_target_pairs={{0,24},{8,0},{16,8},{24,16},{32,56},{40,32},{48,40},{56,48},{64,88... | collective-permute-start | bytes 122888 | tf_op jit(solution)/shard_map/ppermute | solution.py:426
  125.0 2.4 %collective-permute-start.29 = (bf16[176,128]{1,0:T(8,128)(2,1)}, bf16[176,128]{1,0:T(8,128)(2,1)S(1)}, u32[]{:S(2)}, u32[]{:S(2)}) collective-permute-start(bf16[176,128]{1,0:T(8,128)(2,1)} %get-tuple-element.79), channel_id=1, source_target_pairs={{0,96},{8,104},{16,112},{24,120},{32,0},{40,8},{48,16},{56,24},{64... | collective-permute-start | bytes 135176 | tf_op jit(solution)/shard_map/ppermute | solution.py:426
  128.8 0.8 pad_maximum_fusion.1.refs_0_
  129.6 3.0 %collective-permute-start.33 = (bf16[4,160,128]{2,1,0:T(8,128)(2,1)S(1)}, bf16[4,160,128]{2,1,0:T(8,128)(2,1)S(1)}, u32[]{:S(2)}, u32[]{:S(2)}) collective-permute-start(bf16[4,160,128]{2,1,0:T(8,128)(2,1)S(1)} %pad_maximum_fusion.1.refs_0_), channel_id=1, source_target_pairs={{0,1},{1,0},{2,3},{3,2},{4,5},{5,4},{6,7},{7,6},{8,9},{9,8},{10,11... | collective-permute-start | bytes 491528 | tf_op jit(solution)/shard_map/ppermute | solution.py:421
  132.7 2.4 %collective-permute-start.26 = (bf16[4,160,128]{2,1,0:T(8,128)(2,1)S(1)}, bf16[4,160,128]{2,1,0:T(8,128)(2,1)S(1)}, u32[]{:S(2)}, u32[]{:S(2)}) collective-permute-start(bf16[4,160,128]{2,1,0:T(8,128)(2,1)S(1)} %pad_maximum_fusion.1.refs_0_), channel_id=1, source_target_pairs={{0,96},{8,104},{16,112},{24,120},{32,0},{40,8},{48,16},{56,24},{64... | collective-permute-start | bytes 491528 | tf_op jit(solution)/shard_map/ppermute | solution.py:426
  136.2 1.5 collective-permute-start.24
  137.7 5.9 %collective-permute-done.27 = bf16[176,128]{1,0:T(8,128)(2,1)S(1)} collective-permute-done((bf16[176,128]{1,0:T(8,128)(2,1)}, bf16[176,128]{1,0:T(8,128)(2,1)S(1)}, u32[]{:S(2)}, u32[]{:S(2)}) %collective-permute-start.27) | collective-permute-done | bytes 45088 | tf_op jit(solution)/shard_map/ppermute | solution.py:426
  143.7 0.8 pad_maximum_fusion.refs_4_
  144.5 0.9 collective-permute-start.37
  145.6 1.1 collective-permute-start.31
  147.5 0.9 collective-permute-start.36
  148.5 3.0 %collective-permute-done.32.refs_7_ = bf16[4,176,128]{2,1,0:T(8,128)(2,1)S(1)} collective-permute-done((bf16[4,176,128]{2,1,0:T(8,128)(2,1)S(1)}, bf16[4,176,128]{2,1,0:T(8,128)(2,1)S(1)}, u32[]{:S(2)}, u32[]{:S(2)}) %collective-permute-start.32) | collective-permute-done | bytes 180256 | tf_op jit(solution)/shard_map/ppermute | solution.py:426
  151.5 1.3 collective-permute-start.34
  152.9 2.0 %collective-permute-start.40 = (bf16[4,176,128]{2,1,0:T(8,128)(2,1)S(1)}, bf16[4,176,128]{2,1,0:T(8,128)(2,1)S(1)}, u32[]{:S(2)}, u32[]{:S(2)}) collective-permute-start(bf16[4,176,128]{2,1,0:T(8,128)(2,1)S(1)} %collective-permute-done.32.refs_7_), channel_id=1, source_target_pairs={{0,1},{1,0},{2,3},{3,2},{4,5},{5,4},{6,7},{7,6},{8,9},{9,8},{10,11... | collective-permute-start | bytes 540680 | tf_op jit(solution)/shard_map/ppermute | solution.py:421
  154.9 2.5 %collective-permute-done.30.refs_5_ = bf16[4,176,128]{2,1,0:T(8,128)(2,1)S(1)} collective-permute-done((bf16[4,176,128]{2,1,0:T(8,128)(2,1)S(1)}, bf16[4,176,128]{2,1,0:T(8,128)(2,1)S(1)}, u32[]{:S(2)}, u32[]{:S(2)}) %collective-permute-start.30) | collective-permute-done | bytes 180256 | tf_op jit(solution)/shard_map/ppermute | solution.py:426
  158.0 4.5 %shard_map.170 = (bf16[256,512]{1,0:T(8,128)(2,1)}, bf16[256,512]{1,0:T(8,128)(2,1)}) custom-call(bf16[2,256,256]{2,1,0:T(8,128)(2,1)} %get-tuple-element.62.r0_ref, bf16[2,256,256]{2,1,0:T(8,128)(2,1)} %copy-done.21, bf16[2,256,256]{2,1,0:T(8,128)(2,1)} %copy-done.22, bf16[2,256,256]{2,1,0:T(8,128)(2,1)} %copy-done.23, bf16[256,256]{1,0:T(8,128)(2,1)} %copy-done.27, ...), custom_call_target="tpu_custom_call" | custom-call | flops 5000000000 | bytes 1048576 | tf_op jit(solution)/shard_map/pallas_call | solution.py:39
  164.1 5.5 %shard_map.173 = (f32[5,512,512]{2,1,0:T(8,128)}, f32[1,512]{1,0:T(1,128)}) custom-call(bf16[4,160,128]{2,1,0:T(8,128)(2,1)} %copy-done.3, bf16[4,160,128]{2,1,0:T(8,128)(2,1)} %copy-done.15, bf16[4,160,128]{2,1,0:T(8,128)(2,1)} %copy-done.14, bf16[4,160,128]{2,1,0:T(8,128)(2,1)} %copy-done.13, bf16[4,176,128]{2,1,0:T(8,128)(2,1)} %copy-done.2, ...), custom_call_target="tpu_custom_call" | custom-call | tf_op jit(solution)/shard_map/pallas_call | solution.py:526
  (121 shorter events, 13.0 us)
Async XLA Ops:
  4.1 35.4 %all-to-all-start = ((bf16[16,128,512]{2,1,0:T(8,128)(2,1)}), bf16[16,128,512]{2,1,0:T(8,128)(2,1)S(1)}, u32[]{:S(2)}, u32[]{:S(2)}) async-start(bf16[16,128,512]{2,1,0:T(8,128)(2,1)} %get-tuple-element.51), calls=%async_computation | async-start | bytes 4194304 | tf_op jit(solution)/shard_map/all_to_all | solution.py:430
  11.7 14.8 %collective-permute-start.1 = (bf16[528,512]{1,0:T(8,128)(2,1)}, bf16[528,512]{1,0:T(8,128)(2,1)S(1)}, u32[]{:S(2)}, u32[]{:S(2)}) collective-permute-start(bf16[528,512]{1,0:T(8,128)(2,1)} %get-tuple-element.43.p0_ref), channel_id=1, source_target_pairs={{0,6},{1,7},{2,0},{3,1},{4,2},{5,3},{6,4},{7,5},{8,14},{9,15},{10,... | collective-permute-start | bytes 1622024 | tf_op jit(solution)/shard_map/ppermute | solution.py:417
  15.5 13.9 %collective-permute-start = (bf16[528,512]{1,0:T(8,128)(2,1)}, bf16[528,512]{1,0:T(8,128)(2,1)S(1)}, u32[]{:S(2)}, u32[]{:S(2)}) collective-permute-start(bf16[528,512]{1,0:T(8,128)(2,1)} %get-tuple-element.43.p0_ref), channel_id=1, source_target_pairs={{0,2},{1,3},{2,4},{3,5},{4,6},{5,7},{6,0},{7,1},{8,10},{9,11},{10,... | collective-permute-start | bytes 1622024 | tf_op jit(solution)/shard_map/ppermute | solution.py:417
  26.4 21.8 %copy-start.19 = (bf16[528,512]{1,0:T(8,128)(2,1)}, bf16[528,512]{1,0:T(8,128)(2,1)S(1)}, u32[]{:S(2)}) copy-start(bf16[528,512]{1,0:T(8,128)(2,1)S(1)} %collective-permute-done.1.p3_ref) | copy-start | bytes 1622020
  30.3 18.5 %collective-permute-start.3 = (bf16[272,512]{1,0:T(8,128)(2,1)S(1)}, bf16[272,512]{1,0:T(8,128)(2,1)S(1)}, u32[]{:S(2)}, u32[]{:S(2)}) collective-permute-start(bf16[272,512]{1,0:T(8,128)(2,1)S(1)} %slice.19), channel_id=1, source_target_pairs={{0,6},{1,7},{2,0},{3,1},{4,2},{5,3},{6,4},{7,5},{8,14},{9,15},{10,... | collective-permute-start | bytes 835592 | tf_op jit(solution)/shard_map/ppermute | solution.py:417
  31.6 17.0 %collective-permute-start.2 = (bf16[256,512]{1,0:T(8,128)(2,1)S(1)}, bf16[256,512]{1,0:T(8,128)(2,1)}, u32[]{:S(2)}, u32[]{:S(2)}) collective-permute-start(bf16[256,512]{1,0:T(8,128)(2,1)S(1)} %slice.18), channel_id=1, source_target_pairs={{0,2},{1,3},{2,4},{3,5},{4,6},{5,7},{6,0},{7,1},{8,10},{9,11},{10,... | collective-permute-start | bytes 786440 | tf_op jit(solution)/shard_map/ppermute | solution.py:417
  40.8 38.2 %all-to-all-start.1 = ((bf16[16,128,512]{2,1,0:T(8,128)(2,1)}), bf16[16,128,512]{2,1,0:T(8,128)(2,1)S(1)}, u32[]{:S(2)}, u32[]{:S(2)}) async-start(bf16[16,128,512]{2,1,0:T(8,128)(2,1)} %get-tuple-element.57), calls=%async_computation.1 | async-start | bytes 4194304 | tf_op jit(solution)/shard_map/all_to_all | solution.py:430
  44.8 8.7 %collective-permute-start.4 = (bf16[528,512]{1,0:T(8,128)(2,1)}, bf16[528,512]{1,0:T(8,128)(2,1)}, u32[]{:S(2)}, u32[]{:S(2)}) collective-permute-start(bf16[528,512]{1,0:T(8,128)(2,1)} %get-tuple-element.43.p0_ref), channel_id=1, source_target_pairs={{0,1},{1,0},{2,3},{3,2},{4,5},{5,4},{6,7},{7,6},{8,9},{9,8},{10,11... | collective-permute-start | bytes 1622024 | tf_op jit(solution)/shard_map/ppermute | solution.py:421
  48.1 5.7 %collective-permute-start.5 = (bf16[528,512]{1,0:T(8,128)(2,1)}, bf16[528,512]{1,0:T(8,128)(2,1)}, u32[]{:S(2)}, u32[]{:S(2)}) collective-permute-start(bf16[528,512]{1,0:T(8,128)(2,1)} %copy-done.20), channel_id=1, source_target_pairs={{0,1},{1,0},{2,3},{3,2},{4,5},{5,4},{6,7},{7,6},{8,9},{9,8},{10,11... | collective-permute-start | bytes 1622024 | tf_op jit(solution)/shard_map/ppermute | solution.py:421
  48.2 5.7 %collective-permute-start.8 = (bf16[528,512]{1,0:T(8,128)(2,1)S(1)}, bf16[528,512]{1,0:T(8,128)(2,1)}, u32[]{:S(2)}, u32[]{:S(2)}) collective-permute-start(bf16[528,512]{1,0:T(8,128)(2,1)S(1)} %collective-permute-done.1.p3_ref), channel_id=1, source_target_pairs={{0,1},{1,0},{2,3},{3,2},{4,5},{5,4},{6,7},{7,6},{8,9},{9,8},{10,11... | collective-permute-start | bytes 1622024 | tf_op jit(solution)/shard_map/ppermute | solution.py:421
  48.6 5.2 %collective-permute-start.6 = (bf16[256,512]{1,0:T(8,128)(2,1)}, bf16[256,512]{1,0:T(8,128)(2,1)S(1)}, u32[]{:S(2)}, u32[]{:S(2)}) collective-permute-start(bf16[256,512]{1,0:T(8,128)(2,1)} %collective-permute-done.2.t2_ref), channel_id=1, source_target_pairs={{0,1},{1,0},{2,3},{3,2},{4,5},{5,4},{6,7},{7,6},{8,9},{9,8},{10,11... | collective-permute-start | bytes 786440 | tf_op jit(solution)/shard_map/ppermute | solution.py:421
  48.7 5.1 %collective-permute-start.7 = (bf16[272,512]{1,0:T(8,128)(2,1)S(1)}, bf16[272,512]{1,0:T(8,128)(2,1)S(1)}, u32[]{:S(2)}, u32[]{:S(2)}) collective-permute-start(bf16[272,512]{1,0:T(8,128)(2,1)S(1)} %collective-permute-done.3.b2_ref), channel_id=1, source_target_pairs={{0,1},{1,0},{2,3},{3,2},{4,5},{5,4},{6,7},{7,6},{8,9},{9,8},{10,11... | collective-permute-start | bytes 835592 | tf_op jit(solution)/shard_map/ppermute | solution.py:421
  53.5 2.1 %collective-permute-start.9 = (bf16[16,64,128]{2,1,0:T(8,128)(2,1)}, bf16[16,64,128]{2,1,0:T(8,128)(2,1)}, u32[]{:S(2)}, u32[]{:S(2)}) collective-permute-start(bf16[16,64,128]{2,1,0:T(8,128)(2,1)} %get-tuple-element.55), channel_id=1, source_target_pairs={{0,1},{1,0},{2,3},{3,2},{4,5},{5,4},{6,7},{7,6},{8,9},{9,8},{10,11... | collective-permute-start | bytes 786440 | tf_op jit(solution)/shard_map/ppermute | solution.py:421
  79.0 27.5 %copy-start = (bf16[16,128,512]{2,1,0:T(8,128)(2,1)}, bf16[16,128,512]{2,1,0:T(8,128)(2,1)S(1)}, u32[]{:S(2)}) copy-start(bf16[16,128,512]{2,1,0:T(8,128)(2,1)S(1)} %all-to-all-done.1.back_ref) | copy-start | bytes 6291460
  79.0 13.4 %collective-permute-start.10 = (bf16[2,256,256]{2,1,0:T(8,128)(2,1)}, bf16[2,256,256]{2,1,0:T(8,128)(2,1)S(1)}, u32[]{:S(2)}, u32[]{:S(2)}) collective-permute-start(bf16[2,256,256]{2,1,0:T(8,128)(2,1)} %get-tuple-element.63), channel_id=1, source_target_pairs={{0,6},{1,7},{2,0},{3,1},{4,2},{5,3},{6,4},{7,5},{8,14},{9,15},{10,... | collective-permute-start | bytes 786440 | tf_op jit(solution)/shard_map/ppermute | solution.py:417
  82.9 26.9 %all-to-all-start.2 = ((bf16[16,128,128]{2,1,0:T(8,128)(2,1)}), bf16[16,128,128]{2,1,0:T(8,128)(2,1)S(1)}, u32[]{:S(2)}, u32[]{:S(2)}) async-start(bf16[16,128,128]{2,1,0:T(8,128)(2,1)} %get-tuple-element.66), calls=%async_computation.2 | async-start | bytes 1048576 | tf_op jit(solution)/shard_map/all_to_all | solution.py:430
  89.7 9.0 %collective-permute-start.11 = (bf16[2,256,256]{2,1,0:T(8,128)(2,1)}, bf16[2,256,256]{2,1,0:T(8,128)(2,1)S(1)}, u32[]{:S(2)}, u32[]{:S(2)}) collective-permute-start(bf16[2,256,256]{2,1,0:T(8,128)(2,1)} %get-tuple-element.64), channel_id=1, source_target_pairs={{0,4},{1,5},{2,6},{3,7},{4,0},{5,1},{6,2},{7,3},{8,12},{9,13},{10,... | collective-permute-start | bytes 786440 | tf_op jit(solution)/shard_map/ppermute | solution.py:417
  90.7 19.0 %collective-permute-start.13 = (bf16[256,256]{1,0:T(8,128)(2,1)S(1)}, bf16[256,256]{1,0:T(8,128)(2,1)S(1)}, u32[]{:S(2)}, u32[]{:S(2)}) collective-permute-start(bf16[256,256]{1,0:T(8,128)(2,1)S(1)} %slice_bitcast_fusion.3), channel_id=1, source_target_pairs={{0,1},{1,0},{2,3},{3,2},{4,5},{5,4},{6,7},{7,6},{8,9},{9,8},{10,11... | collective-permute-start | bytes 393224 | tf_op jit(solution)/shard_map/ppermute | solution.py:421
  91.5 13.9 %collective-permute-start.12 = (bf16[2,256,256]{2,1,0:T(8,128)(2,1)}, bf16[2,256,256]{2,1,0:T(8,128)(2,1)S(1)}, u32[]{:S(2)}, u32[]{:S(2)}) collective-permute-start(bf16[2,256,256]{2,1,0:T(8,128)(2,1)} %get-tuple-element.65), channel_id=1, source_target_pairs={{0,2},{1,3},{2,4},{3,5},{4,6},{5,7},{6,0},{7,1},{8,10},{9,11},{10,... | collective-permute-start | bytes 786440 | tf_op jit(solution)/shard_map/ppermute | solution.py:417
  92.5 17.2 %collective-permute-start.14 = (bf16[256,256]{1,0:T(8,128)(2,1)S(1)}, bf16[256,256]{1,0:T(8,128)(2,1)}, u32[]{:S(2)}, u32[]{:S(2)}) collective-permute-start(bf16[256,256]{1,0:T(8,128)(2,1)S(1)} %slice_bitcast_fusion.2), channel_id=1, source_target_pairs={{0,1},{1,0},{2,3},{3,2},{4,5},{5,4},{6,7},{7,6},{8,9},{9,8},{10,11... | collective-permute-start | bytes 393224 | tf_op jit(solution)/shard_map/ppermute | solution.py:421
  98.7 11.1 %collective-permute-start.15 = (bf16[256,256]{1,0:T(8,128)(2,1)S(1)}, bf16[256,256]{1,0:T(8,128)(2,1)}, u32[]{:S(2)}, u32[]{:S(2)}) collective-permute-start(bf16[256,256]{1,0:T(8,128)(2,1)S(1)} %slice_bitcast_fusion.1), channel_id=1, source_target_pairs={{0,1},{1,0},{2,3},{3,2},{4,5},{5,4},{6,7},{7,6},{8,9},{9,8},{10,11... | collective-permute-start | bytes 393224 | tf_op jit(solution)/shard_map/ppermute | solution.py:421
  106.1 3.7 %collective-permute-start.16 = (bf16[256,256]{1,0:T(8,128)(2,1)S(1)}, bf16[256,256]{1,0:T(8,128)(2,1)}, u32[]{:S(2)}, u32[]{:S(2)}) collective-permute-start(bf16[256,256]{1,0:T(8,128)(2,1)S(1)} %slice_bitcast_fusion), channel_id=1, source_target_pairs={{0,1},{1,0},{2,3},{3,2},{4,5},{5,4},{6,7},{7,6},{8,9},{9,8},{10,11... | collective-permute-start | bytes 393224 | tf_op jit(solution)/shard_map/ppermute | solution.py:421
  109.6 1.4 collective-permute-start.17
  109.7 48.3 %copy-start.27 = (bf16[256,256]{1,0:T(8,128)(2,1)}, bf16[256,256]{1,0:T(8,128)(2,1)S(1)}, u32[]{:S(2)}) copy-start(bf16[256,256]{1,0:T(8,128)(2,1)S(1)} %collective-permute-done.13.t0_ref) | copy-start | bytes 393220
  113.5 3.0 %collective-permute-start.20 = (bf16[144,128]{1,0:T(8,128)(2,1)}, bf16[144,128]{1,0:T(8,128)(2,1)S(1)}, u32[]{:S(2)}, u32[]{:S(2)}) collective-permute-start(bf16[144,128]{1,0:T(8,128)(2,1)} %shard_map.171.c0_ref), channel_id=1, source_target_pairs={{0,6},{1,7},{2,0},{3,1},{4,2},{5,3},{6,4},{7,5},{8,14},{9,15},{10,... | collective-permute-start | bytes 110600 | tf_op jit(solution)/shard_map/ppermute | solution.py:417
  113.8 4.5 %collective-permute-start.19 = (bf16[144,128]{1,0:T(8,128)(2,1)}, bf16[144,128]{1,0:T(8,128)(2,1)S(1)}, u32[]{:S(2)}, u32[]{:S(2)}) collective-permute-start(bf16[144,128]{1,0:T(8,128)(2,1)} %shard_map.171.c0_ref), channel_id=1, source_target_pairs={{0,4},{1,5},{2,6},{3,7},{4,0},{5,1},{6,2},{7,3},{8,12},{9,13},{10,... | collective-permute-start | bytes 110600 | tf_op jit(solution)/shard_map/ppermute | solution.py:417
  113.8 5.4 %collective-permute-start.18 = (bf16[144,128]{1,0:T(8,128)(2,1)}, bf16[144,128]{1,0:T(8,128)(2,1)S(1)}, u32[]{:S(2)}, u32[]{:S(2)}) collective-permute-start(bf16[144,128]{1,0:T(8,128)(2,1)} %shard_map.171.c0_ref), channel_id=1, source_target_pairs={{0,2},{1,3},{2,4},{3,5},{4,6},{5,7},{6,0},{7,1},{8,10},{9,11},{10,... | collective-permute-start | bytes 110600 | tf_op jit(solution)/shard_map/ppermute | solution.py:417
  121.3 6.6 %collective-permute-start.23 = (bf16[160,128]{1,0:T(8,128)(2,1)}, bf16[160,128]{1,0:T(8,128)(2,1)S(1)}, u32[]{:S(2)}, u32[]{:S(2)}) collective-permute-start(bf16[160,128]{1,0:T(8,128)(2,1)} %get-tuple-element.78), channel_id=1, source_target_pairs={{0,24},{8,0},{16,8},{24,16},{32,56},{40,32},{48,40},{56,48},{64,88... | collective-permute-start | bytes 122888 | tf_op jit(solution)/shard_map/ppermute | solution.py:426
  123.8 4.6 %collective-permute-start.22 = (bf16[160,128]{1,0:T(8,128)(2,1)}, bf16[160,128]{1,0:T(8,128)(2,1)S(1)}, u32[]{:S(2)}, u32[]{:S(2)}) collective-permute-start(bf16[160,128]{1,0:T(8,128)(2,1)} %get-tuple-element.78), channel_id=1, source_target_pairs={{0,16},{8,24},{16,0},{24,8},{32,48},{40,56},{48,32},{56,40},{64,80... | collective-permute-start | bytes 122888 | tf_op jit(solution)/shard_map/ppermute | solution.py:426
  124.4 4.4 %collective-permute-start.21 = (bf16[160,128]{1,0:T(8,128)(2,1)}, bf16[160,128]{1,0:T(8,128)(2,1)S(1)}, u32[]{:S(2)}, u32[]{:S(2)}) collective-permute-start(bf16[160,128]{1,0:T(8,128)(2,1)} %get-tuple-element.78), channel_id=1, source_target_pairs={{0,8},{8,16},{16,24},{24,0},{32,40},{40,48},{48,56},{56,32},{64,72... | collective-permute-start | bytes 122888 | tf_op jit(solution)/shard_map/ppermute | solution.py:426
  125.0 10.7 %collective-permute-start.29 = (bf16[176,128]{1,0:T(8,128)(2,1)}, bf16[176,128]{1,0:T(8,128)(2,1)S(1)}, u32[]{:S(2)}, u32[]{:S(2)}) collective-permute-start(bf16[176,128]{1,0:T(8,128)(2,1)} %get-tuple-element.79), channel_id=1, source_target_pairs={{0,96},{8,104},{16,112},{24,120},{32,0},{40,8},{48,16},{56,24},{64... | collective-permute-start | bytes 135176 | tf_op jit(solution)/shard_map/ppermute | solution.py:426
  127.4 8.9 %collective-permute-start.28 = (bf16[176,128]{1,0:T(8,128)(2,1)}, bf16[176,128]{1,0:T(8,128)(2,1)S(1)}, u32[]{:S(2)}, u32[]{:S(2)}) collective-permute-start(bf16[176,128]{1,0:T(8,128)(2,1)} %get-tuple-element.79), channel_id=1, source_target_pairs={{0,64},{8,72},{16,80},{24,88},{32,96},{40,104},{48,112},{56,120},{... | collective-permute-start | bytes 135176 | tf_op jit(solution)/shard_map/ppermute | solution.py:426
  129.6 32.8 %copy-start.3 = (bf16[4,160,128]{2,1,0:T(8,128)(2,1)}, bf16[4,160,128]{2,1,0:T(8,128)(2,1)S(1)}, u32[]{:S(2)}) copy-start(bf16[4,160,128]{2,1,0:T(8,128)(2,1)S(1)} %pad_maximum_fusion.1.refs_0_) | copy-start | bytes 491524
  129.6 15.7 %collective-permute-start.33 = (bf16[4,160,128]{2,1,0:T(8,128)(2,1)S(1)}, bf16[4,160,128]{2,1,0:T(8,128)(2,1)S(1)}, u32[]{:S(2)}, u32[]{:S(2)}) collective-permute-start(bf16[4,160,128]{2,1,0:T(8,128)(2,1)S(1)} %pad_maximum_fusion.1.refs_0_), channel_id=1, source_target_pairs={{0,1},{1,0},{2,3},{3,2},{4,5},{5,4},{6,7},{7,6},{8,9},{9,8},{10,11... | collective-permute-start | bytes 491528 | tf_op jit(solution)/shard_map/ppermute | solution.py:421
  132.7 12.9 %collective-permute-start.26 = (bf16[4,160,128]{2,1,0:T(8,128)(2,1)S(1)}, bf16[4,160,128]{2,1,0:T(8,128)(2,1)S(1)}, u32[]{:S(2)}, u32[]{:S(2)}) collective-permute-start(bf16[4,160,128]{2,1,0:T(8,128)(2,1)S(1)} %pad_maximum_fusion.1.refs_0_), channel_id=1, source_target_pairs={{0,96},{8,104},{16,112},{24,120},{32,0},{40,8},{48,16},{56,24},{64... | collective-permute-start | bytes 491528 | tf_op jit(solution)/shard_map/ppermute | solution.py:426
  135.1 11.6 %collective-permute-start.25 = (bf16[4,160,128]{2,1,0:T(8,128)(2,1)S(1)}, bf16[4,160,128]{2,1,0:T(8,128)(2,1)S(1)}, u32[]{:S(2)}, u32[]{:S(2)}) collective-permute-start(bf16[4,160,128]{2,1,0:T(8,128)(2,1)S(1)} %pad_maximum_fusion.1.refs_0_), channel_id=1, source_target_pairs={{0,64},{8,72},{16,80},{24,88},{32,96},{40,104},{48,112},{56,120},{... | collective-permute-start | bytes 491528 | tf_op jit(solution)/shard_map/ppermute | solution.py:426
  135.7 8.0 %collective-permute-start.27 = (bf16[176,128]{1,0:T(8,128)(2,1)}, bf16[176,128]{1,0:T(8,128)(2,1)S(1)}, u32[]{:S(2)}, u32[]{:S(2)}) collective-permute-start(bf16[176,128]{1,0:T(8,128)(2,1)} %get-tuple-element.79), channel_id=1, source_target_pairs={{0,32},{8,40},{16,48},{24,56},{32,64},{40,72},{48,80},{56,88},{64,... | collective-permute-start | bytes 135176 | tf_op jit(solution)/shard_map/ppermute | solution.py:426
  136.2 11.2 %collective-permute-start.24 = (bf16[4,160,128]{2,1,0:T(8,128)(2,1)S(1)}, bf16[4,160,128]{2,1,0:T(8,128)(2,1)S(1)}, u32[]{:S(2)}, u32[]{:S(2)}) collective-permute-start(bf16[4,160,128]{2,1,0:T(8,128)(2,1)S(1)} %pad_maximum_fusion.1.refs_0_), channel_id=1, source_target_pairs={{0,32},{8,40},{16,48},{24,56},{32,64},{40,72},{48,80},{56,88},{64,... | collective-permute-start | bytes 491528 | tf_op jit(solution)/shard_map/ppermute | solution.py:426
  144.5 3.9 %collective-permute-start.37 = (bf16[4,176,128]{2,1,0:T(8,128)(2,1)S(1)}, bf16[4,176,128]{2,1,0:T(8,128)(2,1)S(1)}, u32[]{:S(2)}, u32[]{:S(2)}) collective-permute-start(bf16[4,176,128]{2,1,0:T(8,128)(2,1)S(1)} %pad_maximum_fusion.refs_4_), channel_id=1, source_target_pairs={{0,1},{1,0},{2,3},{3,2},{4,5},{5,4},{6,7},{7,6},{8,9},{9,8},{10,11... | collective-permute-start | bytes 540680 | tf_op jit(solution)/shard_map/ppermute | solution.py:421
  145.4 6.1 %collective-permute-start.32 = (bf16[4,176,128]{2,1,0:T(8,128)(2,1)S(1)}, bf16[4,176,128]{2,1,0:T(8,128)(2,1)S(1)}, u32[]{:S(2)}, u32[]{:S(2)}) collective-permute-start(bf16[4,176,128]{2,1,0:T(8,128)(2,1)S(1)} %pad_maximum_fusion.refs_4_), channel_id=1, source_target_pairs={{0,24},{8,0},{16,8},{24,16},{32,56},{40,32},{48,40},{56,48},{64,88... | collective-permute-start | bytes 540680 | tf_op jit(solution)/shard_map/ppermute | solution.py:426
  145.6 7.3 %collective-permute-start.31 = (bf16[4,176,128]{2,1,0:T(8,128)(2,1)S(1)}, bf16[4,176,128]{2,1,0:T(8,128)(2,1)S(1)}, u32[]{:S(2)}, u32[]{:S(2)}) collective-permute-start(bf16[4,176,128]{2,1,0:T(8,128)(2,1)S(1)} %pad_maximum_fusion.refs_4_), channel_id=1, source_target_pairs={{0,16},{8,24},{16,0},{24,8},{32,48},{40,56},{48,32},{56,40},{64,80... | collective-permute-start | bytes 540680 | tf_op jit(solution)/shard_map/ppermute | solution.py:426
  146.7 10.7 %collective-permute-start.30 = (bf16[4,176,128]{2,1,0:T(8,128)(2,1)S(1)}, bf16[4,176,128]{2,1,0:T(8,128)(2,1)S(1)}, u32[]{:S(2)}, u32[]{:S(2)}) collective-permute-start(bf16[4,176,128]{2,1,0:T(8,128)(2,1)S(1)} %pad_maximum_fusion.refs_4_), channel_id=1, source_target_pairs={{0,8},{8,16},{16,24},{24,0},{32,40},{40,48},{48,56},{56,32},{64,72... | collective-permute-start | bytes 540680 | tf_op jit(solution)/shard_map/ppermute | solution.py:426
  147.5 10.4 %collective-permute-start.36 = (bf16[4,160,128]{2,1,0:T(8,128)(2,1)S(1)}, bf16[4,160,128]{2,1,0:T(8,128)(2,1)S(1)}, u32[]{:S(2)}, u32[]{:S(2)}) collective-permute-start(bf16[4,160,128]{2,1,0:T(8,128)(2,1)S(1)} %collective-permute-done.26.refs_3_), channel_id=1, source_target_pairs={{0,1},{1,0},{2,3},{3,2},{4,5},{5,4},{6,7},{7,6},{8,9},{9,8},{10,11... | collective-permute-start | bytes 491528 | tf_op jit(solution)/shard_map/ppermute | solution.py:421
  148.4 14.2 %collective-permute-start.35 = (bf16[4,160,128]{2,1,0:T(8,128)(2,1)S(1)}, bf16[4,160,128]{2,1,0:T(8,128)(2,1)S(1)}, u32[]{:S(2)}, u32[]{:S(2)}) collective-permute-start(bf16[4,160,128]{2,1,0:T(8,128)(2,1)S(1)} %collective-permute-done.25.refs_2_), channel_id=1, source_target_pairs={{0,1},{1,0},{2,3},{3,2},{4,5},{5,4},{6,7},{7,6},{8,9},{9,8},{10,11... | collective-permute-start | bytes 491528 | tf_op jit(solution)/shard_map/ppermute | solution.py:421
  151.5 11.1 %collective-permute-start.34 = (bf16[4,160,128]{2,1,0:T(8,128)(2,1)S(1)}, bf16[4,160,128]{2,1,0:T(8,128)(2,1)S(1)}, u32[]{:S(2)}, u32[]{:S(2)}) collective-permute-start(bf16[4,160,128]{2,1,0:T(8,128)(2,1)S(1)} %collective-permute-done.24.refs_1_), channel_id=1, source_target_pairs={{0,1},{1,0},{2,3},{3,2},{4,5},{5,4},{6,7},{7,6},{8,9},{9,8},{10,11... | collective-permute-start | bytes 491528 | tf_op jit(solution)/shard_map/ppermute | solution.py:421
  152.9 9.7 %collective-permute-start.40 = (bf16[4,176,128]{2,1,0:T(8,128)(2,1)S(1)}, bf16[4,176,128]{2,1,0:T(8,128)(2,1)S(1)}, u32[]{:S(2)}, u32[]{:S(2)}) collective-permute-start(bf16[4,176,128]{2,1,0:T(8,128)(2,1)S(1)} %collective-permute-done.32.refs_7_), channel_id=1, source_target_pairs={{0,1},{1,0},{2,3},{3,2},{4,5},{5,4},{6,7},{7,6},{8,9},{9,8},{10,11... | collective-permute-start | bytes 540680 | tf_op jit(solution)/shard_map/ppermute | solution.py:421
  157.4 5.2 %collective-permute-start.39 = (bf16[4,176,128]{2,1,0:T(8,128)(2,1)S(1)}, bf16[4,176,128]{2,1,0:T(8,128)(2,1)S(1)}, u32[]{:S(2)}, u32[]{:S(2)}) collective-permute-start(bf16[4,176,128]{2,1,0:T(8,128)(2,1)S(1)} %collective-permute-done.31.refs_6_), channel_id=1, source_target_pairs={{0,1},{1,0},{2,3},{3,2},{4,5},{5,4},{6,7},{7,6},{8,9},{9,8},{10,11... | collective-permute-start | bytes 540680 | tf_op jit(solution)/shard_map/ppermute | solution.py:421
  157.9 4.7 %collective-permute-start.38 = (bf16[4,176,128]{2,1,0:T(8,128)(2,1)S(1)}, bf16[4,176,128]{2,1,0:T(8,128)(2,1)S(1)}, u32[]{:S(2)}, u32[]{:S(2)}) collective-permute-start(bf16[4,176,128]{2,1,0:T(8,128)(2,1)S(1)} %collective-permute-done.30.refs_5_), channel_id=1, source_target_pairs={{0,1},{1,0},{2,3},{3,2},{4,5},{5,4},{6,7},{7,6},{8,9},{9,8},{10,11... | collective-permute-start | bytes 540680 | tf_op jit(solution)/shard_map/ppermute | solution.py:421
  (28 other events, 172.1 us)

commit v6 on v5

--- a/solution.py
+++ b/solution.py
@@ -23,7 +23,6 @@
 SCORE_SUB = (8.0 + 256.0) * LOG2E
 CHUNK = 64 + 64 + 16
 SPREAD = 4 * 64 + 64 + 16
-PART = 160
 
 NT = (((1,), (1,)), ((), ()))
 NN = (((1,), (0,)), ((), ()))
@@ -287,7 +286,7 @@
     out_ref[128:CHUNK, :] = jnp.concatenate([coarse, extra - coarse], axis=0).astype(BF16)
 
 
-def spread_body(c0_ref, c1_ref, c2_ref, c3_ref, first_ref, second_ref, parts_ref):
+def spread_body(c0_ref, c1_ref, c2_ref, c3_ref, out_ref, parts_ref):
     z, core = position()
     for dz, c_ref in enumerate((c0_ref, c1_ref, c2_ref, c3_ref)):
         parts_ref[dz] = c_ref[64:CHUNK, :].astype(F32)
@@ -298,8 +297,8 @@
     coarse = gain.astype(BF16).astype(F32)
     tail = jnp.concatenate([total[0:64], coarse, gain - coarse], axis=0).astype(BF16)
     whole = jnp.concatenate([c_ref[0:64, :] for c_ref in (c0_ref, c1_ref, c2_ref, c3_ref)] + [tail], axis=0)
-    first_ref[...] = whole[0:PART]
-    second_ref[...] = whole[PART:SPREAD]
+    for p in range(DOM):
+        out_ref[p] = whole
 
 
 def halo_body(counts_ref, back_ref, rows_ref, x_ref, out_ref, gain_grad_ref):
@@ -355,27 +354,20 @@
     feature_ref[...] = (grad_ref[...].astype(F32) + dx).astype(BF16)
 
 
-def weights_body(*refs):
-    gain_in_ref, out_ref, gain_ref, all_ref = refs[16:20]
+def weights_body(mine_ref, other_ref, gain_in_ref, out_ref, gain_ref, all_ref):
     which = pl.program_id(0)
 
     @pl.when(which == 0)
     def _():
         z, core = position()
-        x, y = dom_position()
-        for c in range(2):
-            owner = core ^ c
-            for dx in range(4):
-                for dy in range(4):
-                    p = ((x - dx) & 3) * 4 + ((y - dy) & 3)
-                    all_ref[owner, p, 0:PART, :] = refs[c * 8 + dx][dy]
-                    all_ref[owner, p, PART:SPREAD, :] = refs[c * 8 + 4 + dy][dx]
+        all_ref[core] = mine_ref[...]
+        all_ref[1 - core] = other_ref[...]
         gain = jnp.zeros((8, 128), F32)
         through = []
         for p in range(DOM):
-            tails = [all_ref[c, p, 320:SPREAD, :].astype(F32) for c in range(2)]
+            tails = [ref[p, 320:SPREAD, :].astype(F32) for ref in (mine_ref, other_ref)]
             tails = [tail[0:8] + tail[8:16] for tail in tails]
-            gain = gain + jnp.where(core == 0, tails[0], tails[1])
+            gain = gain + tails[0]
             through.append(tails[0] + tails[1])
         for b in range(4):
             part = (through[b] + through[4 + b] + through[8 + b])[4:5]
@@ -419,11 +411,6 @@
 
 def other_core(array):
     return lax.ppermute(array, "blk", chip_shift(0, 1))
-
-
-def along_dom(array, x_step, y_step):
-    pairs = [(x * 4 + y, (x + x_step) % 4 * 4 + (y + y_step) % 4) for x in range(4) for y in range(4)]
-    return lax.ppermute(array, "dom", pairs)
 
 
 def to_dom_peers(array):
@@ -491,7 +478,7 @@
         ],
         micros=12,
     )
-    chunks, back, *results = lax.optimization_barrier((chunks, back, *results))
+    chunks, back = lax.optimization_barrier((chunks, back))
     chunks = to_dom_peers(chunks)
     halo, gain_part = call(
         halo_body,
@@ -500,9 +487,6 @@
         scalars=1,
         micros=3,
     )
-    results = [results[0]] + [along_chips(results[dz], -dz) for dz in (1, 2, 3)]
-    swapped = [other_core(part[1]) for part in results]
-    chunks, *swapped = lax.optimization_barrier((chunks, *swapped))
     chunk = call(
         chunk_sum_body,
         shape((CHUNK, 128), BF16),
@@ -511,34 +495,31 @@
         micros=1,
     )
     chunk_parts = [chunk] + [along_chips(chunk, step) for step in (1, 2, 3)]
-    first, second = call(
-        spread_body,
-        (shape((PART, 128), BF16), shape((SPREAD - PART, 128), BF16)),
-        chunk_parts,
-        scratch=[pltpu.VMEM((4, 80, 128), F32)],
-        micros=1,
-    )
-    first = jnp.stack([first] + [along_dom(first, 0, step) for step in (1, 2, 3)])
-    second = jnp.stack([second] + [along_dom(second, step, 0) for step in (1, 2, 3)])
-    parts = [first] + [along_dom(first, step, 0) for step in (1, 2, 3)]
-    parts = parts + [second] + [along_dom(second, 0, step) for step in (1, 2, 3)]
-    parts = parts + [other_core(part) for part in parts]
-    weight_grads, gain_grad = pl.pallas_call(
-        weights_body,
-        grid=(5,),
-        out_shape=(shape((5, D, D), F32), shape((1, D), F32)),
-        in_specs=[pl.BlockSpec(part.shape, lambda t: (0, 0, 0)) for part in parts] + [pl.BlockSpec((1, D), lambda t: (0, 0))],
-        out_specs=(pl.BlockSpec((1, D, D), lambda t: (t, 0, 0)), pl.BlockSpec((1, D), lambda t: (0, 0))),
-        scratch_shapes=[pltpu.VMEM((2, DOM, SPREAD, 128), BF16)],
-    )(*parts, gain_row)
-
+    spread = call(
+        spread_body, shape((DOM, SPREAD, 128), BF16), chunk_parts, scratch=[pltpu.VMEM((4, 80, 128), F32)], micros=1
+    )
+    spread, *results = lax.optimization_barrier((spread, *results))
+    gathered = to_dom_peers(spread)
+    results = [results[0]] + [along_chips(results[dz], -dz) for dz in (1, 2, 3)]
+    swapped = [other_core(part[1]) for part in results]
     layer_out, feature_grad = call(
         rows_body,
         (shape((ROWS, D), BF16), shape((ROWS, D), BF16)),
         (*results, *swapped, halo, base, x, gain_row, out_grad, wq, wk, wv, wo),
         scratch=[pltpu.VMEM((4, ROWS, 128), BF16)] * 4,
-        micros=5,
-    )
+        micros=2,
+    )
+    gathered, layer_out, feature_grad = lax.optimization_barrier((gathered, layer_out, feature_grad))
+    whole = pl.BlockSpec((DOM, SPREAD, 128), lambda t: (0, 0, 0))
+    row = pl.BlockSpec((1, D), lambda t: (0, 0))
+    weight_grads, gain_grad = pl.pallas_call(
+        weights_body,
+        grid=(5,),
+        out_shape=(shape((5, D, D), F32), shape((1, D), F32)),
+        in_specs=[whole, whole, row],
+        out_specs=(pl.BlockSpec((1, D, D), lambda t: (t, 0, 0)), row),
+        scratch_shapes=[pltpu.VMEM((2, DOM, SPREAD, 128), BF16)],
+    )(gathered, other_core(gathered), gain_row)
     return layer_out, feature_grad, weight_grads, gain_grad.reshape(D)
 
 

time: 170 us -> 148 us (0.87)
  starting transfers between devices: 62 us -> 50.9 us
  waiting for transfers between devices: 41 us -> 31.9 us
    ppermute x12 -> x0, starting transfers between devices: 13.7 us -> none  [along_dom(): return lax.ppermute(array, 'dom', pairs)]
    ppermute x12 -> x0, waiting for transfers between devices: 12.4 us -> none  [along_dom(): return lax.ppermute(array, 'dom', pairs)]
    ppermute x10, waiting for transfers between devices: 18.9 us -> 13.2 us  [along_chips(): return lax.ppermute(array, 'blk', chip_shift(step, 0))]
    all_to_all x3 -> x4, waiting for transfers between devices: 6.66 us -> 12.2 us  [to_dom_peers(): return lax.all_to_all(array, 'dom', split_axis=0, concat_axis=0, tiled=True)]
    all_to_all x3 -> x4, starting transfers between devices: 18.3 us -> 22.6 us  [to_dom_peers(): return lax.all_to_all(array, 'dom', split_axis=0, concat_axis=0, tiled=True)]
    ppermute x19 -> x12, waiting for transfers between devices: 3.02 us -> 6.48 us  [other_core(): return lax.ppermute(array, 'blk', chip_shift(0, 1))]
    ppermute x19 -> x12, starting transfers between devices: 18.1 us -> 16.1 us  [other_core(): return lax.ppermute(array, 'blk', chip_shift(0, 1))]
    unnamed x64 -> x50, local copies, waits for them, and re-layouts: 5.57 us -> 5.93 us
  transfers between devices with their start and end apart: 44 -> 26, of which waited for: 15 -> 11; matrix products, arithmetic and copies ran while one was open for 2% -> 1% of each run, Pallas kernels for 26% -> 30%
where the time goes in v6:
time: 148 us
  Pallas kernels  57 us (39%)
  starting transfers between devices  50.9 us (34%)
  waiting for transfers between devices  31.9 us (22%)
  local copies, waits for them, and re-layouts  6.95 us (5%)
    pallas_call x8, Pallas kernels, call(): pl.pallas_call(body, out_shape=out_shape, in_specs=specs, out_specs=jax.t...  51.6 us
    all_to_all x4, starting transfers between devices, to_dom_peers(): return lax.all_to_all(array, 'dom', split_axis=0, concat_axis=0, tiled=True)  22.6 us
    ppermute x12, starting transfers between devices, other_core(): return lax.ppermute(array, 'blk', chip_shift(0, 1))  16.1 us
    ppermute x10, waiting for transfers between devices, along_chips(): return lax.ppermute(array, 'blk', chip_shift(step, 0))  13.2 us
    all_to_all x4, waiting for transfers between devices, to_dom_peers(): return lax.all_to_all(array, 'dom', split_axis=0, concat_axis=0, tiled=True)  12.2 us
    ppermute x10, starting transfers between devices, along_chips(): return lax.ppermute(array, 'blk', chip_shift(step, 0))  12.2 us
    ppermute x12, waiting for transfers between devices, other_core(): return lax.ppermute(array, 'blk', chip_shift(0, 1))  6.48 us
    unnamed x50, local copies, waits for them, and re-layouts  5.93 us
  transfers between devices with their start and end apart: 26, of which 11 were waited for; matrix products, arithmetic and copies ran while one was open for 1% of the time, Pallas kernels for 30%

profile of v6, /device:TPU:1, one launch (start us, length us, event | category | flops | bytes accessed | tf_op | source)
XLA Modules:
  0.0 147.6 jit_solution(6036344318510204515)
XLA Ops:
  0.6 3.4 %shard_map.165 = (bf16[528,512]{1,0:T(8,128)(2,1)}, bf16[16,128,512]{2,1,0:T(8,128)(2,1)}) custom-call(s32[1,8]{1,0:T(1,128)} %pattern_ref.1, s32[16]{0:T(128)} %counts_ref.3, bf16[256,512]{1,0:T(8,128)(2,1)} %x_ref.7, f32[1,512]{1,0:T(1,128)} %bitcast.13, s32[1,256]{1,0:T(1,128)} %bitcast.19, bf16[256,512]{1,0:T(8,128)(2,1)} %grad_ref.7, s32[16,128]{1,0:T(8,128)} %rows_ref.3), custom_call_target="tpu_custom_call" | custom-call | flops 4000000000 | bytes 1048576 | tf_op jit(solution)/shard_map/pallas_call | solution.py:38
  4.1 7.6 %all-to-all-start = ((bf16[16,128,512]{2,1,0:T(8,128)(2,1)}), bf16[16,128,512]{2,1,0:T(8,128)(2,1)S(1)}, u32[]{:S(2)}, u32[]{:S(2)}) async-start(bf16[16,128,512]{2,1,0:T(8,128)(2,1)} %get-tuple-element.48), calls=%async_computation | async-start | bytes 4194304 | tf_op jit(solution)/shard_map/all_to_all | solution.py:417
  11.7 3.8 %collective-permute-start.1 = (bf16[528,512]{1,0:T(8,128)(2,1)}, bf16[528,512]{1,0:T(8,128)(2,1)S(1)}, u32[]{:S(2)}, u32[]{:S(2)}) collective-permute-start(bf16[528,512]{1,0:T(8,128)(2,1)} %get-tuple-element.40.p0_ref), channel_id=1, source_target_pairs={{0,6},{1,7},{2,0},{3,1},{4,2},{5,3},{6,4},{7,5},{8,14},{9,15},{10,... | collective-permute-start | bytes 1622024 | tf_op jit(solution)/shard_map/ppermute | solution.py:409
  15.5 9.0 %shard_map.166 = (bf16[1024,512]{1,0:T(8,128)(2,1)}, f32[256,128]{1,0:T(8,128)}, bf16[16,128,512]{2,1,0:T(8,128)(2,1)}, bf16[192,512]{1,0:T(8,128)(2,1)}, bf16[64,512]{1,0:T(8,128)(2,1)}) custom-call(s32[32,128]{1,0:T(8,128)} %bitcast.16, s32[32,128]{1,0:T(8,128)} %bitcast.17, bf16[256,512]{1,0:T(8,128)(2,1)} %grad_ref.7, bf16[512,512]{1,0:T(8,128)(2,1)} %w_ref.3, ...), custom_call_target="tpu_custom_call" | custom-call | flops 10000000000 | bytes 1048576 | tf_op jit(solution)/shard_map/pallas_call | solution.py:38
  24.5 1.9 %collective-permute-done.1.p3_ref = bf16[528,512]{1,0:T(8,128)(2,1)S(1)} collective-permute-done((bf16[528,512]{1,0:T(8,128)(2,1)}, bf16[528,512]{1,0:T(8,128)(2,1)S(1)}, u32[]{:S(2)}, u32[]{:S(2)}) %collective-permute-start.1) | collective-permute-done | bytes 540704 | tf_op jit(solution)/shard_map/ppermute | solution.py:409
  26.4 3.0 %collective-permute-done.p1_ref = bf16[528,512]{1,0:T(8,128)(2,1)S(1)} collective-permute-done((bf16[528,512]{1,0:T(8,128)(2,1)}, bf16[528,512]{1,0:T(8,128)(2,1)S(1)}, u32[]{:S(2)}, u32[]{:S(2)}) %collective-permute-start) | collective-permute-done | bytes 540704 | tf_op jit(solution)/shard_map/ppermute | solution.py:409
  29.4 0.8 copy-done.6
  30.3 0.4 collective-permute-start.3
  30.7 1.0 slice.18
  31.7 1.2 collective-permute-start.2
  32.9 6.6 %all-to-all-done.table_ref = bf16[16,128,512]{2,1,0:T(8,128)(2,1)S(1)} async-done(((bf16[16,128,512]{2,1,0:T(8,128)(2,1)}), bf16[16,128,512]{2,1,0:T(8,128)(2,1)S(1)}, u32[]{:S(2)}, u32[]{:S(2)}) %all-to-all-start) | async-done | bytes 2097184 | tf_op jit(solution)/shard_map/all_to_all | solution.py:417
  39.5 1.3 copy-done.2
  40.8 3.9 %all-to-all-start.1 = ((bf16[16,128,512]{2,1,0:T(8,128)(2,1)}), bf16[16,128,512]{2,1,0:T(8,128)(2,1)S(1)}, u32[]{:S(2)}, u32[]{:S(2)}) async-start(bf16[16,128,512]{2,1,0:T(8,128)(2,1)} %get-tuple-element.54), calls=%async_computation.1 | async-start | bytes 4194304 | tf_op jit(solution)/shard_map/all_to_all | solution.py:417
  44.8 3.3 %collective-permute-start.4 = (bf16[528,512]{1,0:T(8,128)(2,1)}, bf16[528,512]{1,0:T(8,128)(2,1)}, u32[]{:S(2)}, u32[]{:S(2)}) collective-permute-start(bf16[528,512]{1,0:T(8,128)(2,1)} %get-tuple-element.40.p0_ref), channel_id=1, source_target_pairs={{0,1},{1,0},{2,3},{3,2},{4,5},{5,4},{6,7},{7,6},{8,9},{9,8},{10,11... | collective-permute-start | bytes 1622024 | tf_op jit(solution)/shard_map/ppermute | solution.py:413
  48.2 0.4 collective-permute-start.8
  48.7 0.4 collective-permute-start.7
  49.2 4.3 %shard_map.167 = (f32[256,512]{1,0:T(8,128)}, bf16[16,64,128]{2,1,0:T(8,128)(2,1)}, bf16[16,64,128]{2,1,0:T(8,128)(2,1)}) custom-call(bf16[1024,512]{1,0:T(8,128)(2,1)} %get-tuple-element.46.counts_t_ref, f32[256,128]{1,0:T(8,128)} %get-tuple-element.47.degree_ref, bf16[16,128,512]{2,1,0:T(8,128)(2,1)} %copy-done.2, bf16[256,512]{1,0:T(8,128)(2,1)} %x_ref.7, ...), custom_call_target="tpu_custom_call" | custom-call | flops 4000000000 | bytes 1048576 | tf_op jit(solution)/shard_map/pallas_call | solution.py:38
  53.9 1.7 %collective-permute-done.9.other_ref = bf16[16,64,128]{2,1,0:T(8,128)(2,1)} collective-permute-done((bf16[16,64,128]{2,1,0:T(8,128)(2,1)}, bf16[16,64,128]{2,1,0:T(8,128)(2,1)}, u32[]{:S(2)}, u32[]{:S(2)}) %collective-permute-start.9) | collective-permute-done | bytes 262176 | tf_op jit(solution)/shard_map/ppermute | solution.py:413
  55.6 23.3 %shard_map.168 = (bf16[2,256,256]{2,1,0:T(8,128)(2,1)}, bf16[2,256,256]{2,1,0:T(8,128)(2,1)}, bf16[2,256,256]{2,1,0:T(8,128)(2,1)}, bf16[2,256,256]{2,1,0:T(8,128)(2,1)}, bf16[16,128,128]{2,1,0:T(8,128)(2,1)}) custom-call(bf16[528,512]{1,0:T(8,128)(2,1)} %get-tuple-element.40.p0_ref, bf16[528,512]{1,0:T(8,128)(2,1)} %copy-done.6, ...), custom_call_target="tpu_custom_call" | custom-call | flops 12000000000 | bytes 1048576 | tf_op jit(solution)/shard_map/pallas_call | solution.py:38
  79.0 6.8 %all-to-all-start.2 = ((bf16[16,128,128]{2,1,0:T(8,128)(2,1)}), bf16[16,128,128]{2,1,0:T(8,128)(2,1)S(1)}, u32[]{:S(2)}, u32[]{:S(2)}) async-start(bf16[16,128,128]{2,1,0:T(8,128)(2,1)} %get-tuple-element.55), calls=%async_computation.2 | async-start | bytes 1048576 | tf_op jit(solution)/shard_map/all_to_all | solution.py:417
  85.8 3.1 %shard_map.169 = (f32[256,512]{1,0:T(8,128)}, f32[8,128]{1,0:T(8,128)}) custom-call(s32[16]{0:T(128)} %counts_ref.3, bf16[16,128,512]{2,1,0:T(8,128)(2,1)} %copy-done.1, s32[16,128]{1,0:T(8,128)} %rows_ref.3, bf16[256,512]{1,0:T(8,128)(2,1)} %x_ref.7), custom_call_target="tpu_custom_call" | custom-call | flops 3000000000 | bytes 1048576 | tf_op jit(solution)/shard_map/pallas_call | solution.py:38
  89.0 0.4 collective-permute-start.10
  89.4 1.0 collective-permute-done.10.g1_ref
  90.4 5.5 %all-to-all-done.2.in_ref = bf16[16,128,128]{2,1,0:T(8,128)(2,1)S(1)} async-done(((bf16[16,128,128]{2,1,0:T(8,128)(2,1)}), bf16[16,128,128]{2,1,0:T(8,128)(2,1)S(1)}, u32[]{:S(2)}, u32[]{:S(2)}) %all-to-all-start.2) | async-done | bytes 524320 | tf_op jit(solution)/shard_map/all_to_all | solution.py:417
  96.0 0.8 copy-done.4
  96.8 1.8 %shard_map.170.c0_ref = bf16[144,128]{1,0:T(8,128)(2,1)} custom-call(bf16[16,128,128]{2,1,0:T(8,128)(2,1)} %copy-done.4, f32[8,128]{1,0:T(8,128)} %get-tuple-element.57.g0_ref, f32[8,128]{1,0:T(8,128)} %copy-done.24, bf16[192,512]{1,0:T(8,128)(2,1)} %get-tuple-element.44.wqkv_ref), custom_call_target="tpu_custom_call" | custom-call | flops 1000000000 | bytes 1048576 | tf_op jit(solution)/shard_map/pallas_call | solution.py:38
  98.6 3.8 %collective-permute-start.13 = (bf16[144,128]{1,0:T(8,128)(2,1)}, bf16[144,128]{1,0:T(8,128)(2,1)S(1)}, u32[]{:S(2)}, u32[]{:S(2)}) collective-permute-start(bf16[144,128]{1,0:T(8,128)(2,1)} %shard_map.170.c0_ref), channel_id=1, source_target_pairs={{0,6},{1,7},{2,0},{3,1},{4,2},{5,3},{6,4},{7,5},{8,14},{9,15},{10,... | collective-permute-start | bytes 110600 | tf_op jit(solution)/shard_map/ppermute | solution.py:409
  102.4 0.7 collective-permute-start.11
  103.1 0.7 collective-permute-done.13.c3_ref
  103.7 3.2 %collective-permute-done.12.c2_ref = bf16[144,128]{1,0:T(8,128)(2,1)S(1)} collective-permute-done((bf16[144,128]{1,0:T(8,128)(2,1)}, bf16[144,128]{1,0:T(8,128)(2,1)S(1)}, u32[]{:S(2)}, u32[]{:S(2)}) %collective-permute-start.12) | collective-permute-done | bytes 36896 | tf_op jit(solution)/shard_map/ppermute | solution.py:409
  107.0 0.6 copy-done.22
  107.6 0.6 copy-done.23
  108.2 2.1 %shard_map.171 = bf16[16,336,128]{2,1,0:T(8,128)(2,1)} custom-call(bf16[144,128]{1,0:T(8,128)(2,1)} %shard_map.170.c0_ref, bf16[144,128]{1,0:T(8,128)(2,1)} %copy-done.23, bf16[144,128]{1,0:T(8,128)(2,1)} %copy-done.22, bf16[144,128]{1,0:T(8,128)(2,1)} %copy-done.21), custom_call_target="tpu_custom_call" | custom-call | flops 1000000000 | bytes 1048576 | tf_op jit(solution)/shard_map/pallas_call | solution.py:38
  110.3 4.3 %all-to-all-start.3 = ((bf16[16,336,128]{2,1,0:T(8,128)(2,1)}), bf16[16,336,128]{2,1,0:T(8,128)(2,1)S(1)}, u32[]{:S(2)}, u32[]{:S(2)}) async-start(bf16[16,336,128]{2,1,0:T(8,128)(2,1)} %shard_map.171), calls=%async_computation.3 | async-start | bytes 2752512 | tf_op jit(solution)/shard_map/all_to_all | solution.py:417
  114.7 1.1 collective-permute-start.15
  115.9 3.6 %collective-permute-start.17 = (bf16[256,256]{1,0:T(8,128)(2,1)S(1)}, bf16[256,256]{1,0:T(8,128)(2,1)S(1)}, u32[]{:S(2)}, u32[]{:S(2)}) collective-permute-start(bf16[256,256]{1,0:T(8,128)(2,1)S(1)} %slice_bitcast_fusion.3), channel_id=1, source_target_pairs={{0,1},{1,0},{2,3},{3,2},{4,5},{5,4},{6,7},{7,6},{8,9},{9,8},{10,11... | collective-permute-start | bytes 393224 | tf_op jit(solution)/shard_map/ppermute | solution.py:413
  119.5 1.1 collective-permute-start.16
  120.5 5.8 %collective-permute-start.18 = (bf16[256,256]{1,0:T(8,128)(2,1)S(1)}, bf16[256,256]{1,0:T(8,128)(2,1)S(1)}, u32[]{:S(2)}, u32[]{:S(2)}) collective-permute-start(bf16[256,256]{1,0:T(8,128)(2,1)S(1)} %slice_bitcast_fusion.2), channel_id=1, source_target_pairs={{0,1},{1,0},{2,3},{3,2},{4,5},{5,4},{6,7},{7,6},{8,9},{9,8},{10,11... | collective-permute-start | bytes 393224 | tf_op jit(solution)/shard_map/ppermute | solution.py:413
  126.4 0.6 collective-permute-start.19
  127.0 4.3 %collective-permute-done.16.r3_ref = bf16[2,256,256]{2,1,0:T(8,128)(2,1)S(1)} collective-permute-done((bf16[2,256,256]{2,1,0:T(8,128)(2,1)S(1)}, bf16[2,256,256]{2,1,0:T(8,128)(2,1)S(1)}, u32[]{:S(2)}, u32[]{:S(2)}) %collective-permute-start.16) | collective-permute-done | bytes 262176 | tf_op jit(solution)/shard_map/ppermute | solution.py:409
  131.3 0.5 collective-permute-start.20
  131.9 0.9 collective-permute-done.20.t3_ref
  132.9 0.6 copy-done.20
  133.5 4.5 %shard_map.172 = (bf16[256,512]{1,0:T(8,128)(2,1)}, bf16[256,512]{1,0:T(8,128)(2,1)}) custom-call(bf16[2,256,256]{2,1,0:T(8,128)(2,1)} %get-tuple-element.63.r0_ref, bf16[2,256,256]{2,1,0:T(8,128)(2,1)} %copy-done.8, bf16[2,256,256]{2,1,0:T(8,128)(2,1)} %copy-done.9, bf16[2,256,256]{2,1,0:T(8,128)(2,1)} %copy-done.10, bf16[256,256]{1,0:T(8,128)(2,1)} %copy-done.17, ...), custom_call_target="tpu_custom_call" | custom-call | flops 2000000000 | bytes 1048576 | tf_op jit(solution)/shard_map/pallas_call | solution.py:38
  137.9 0.4 collective-permute-start.21
  138.4 2.8 %collective-permute-done.21.other_ref = bf16[16,336,128]{2,1,0:T(8,128)(2,1)S(1)} collective-permute-done((bf16[16,336,128]{2,1,0:T(8,128)(2,1)S(1)}, bf16[16,336,128]{2,1,0:T(8,128)(2,1)S(1)}, u32[]{:S(2)}, u32[]{:S(2)}) %collective-permute-start.21) | collective-permute-done | bytes 1376288 | tf_op jit(solution)/shard_map/ppermute | solution.py:413
  141.2 1.1 copy-done.3
  142.3 5.4 %shard_map.173 = (f32[5,512,512]{2,1,0:T(8,128)}, f32[1,512]{1,0:T(1,128)}) custom-call(bf16[16,336,128]{2,1,0:T(8,128)(2,1)} %copy-done, bf16[16,336,128]{2,1,0:T(8,128)(2,1)} %copy-done.3, f32[1,512]{1,0:T(1,128)} %bitcast.15), custom_call_target="tpu_custom_call" | custom-call | tf_op jit(solution)/shard_map/pallas_call | solution.py:515
  (69 shorter events, 0.8 us)
Async XLA Ops:
  4.1 35.4 %all-to-all-start = ((bf16[16,128,512]{2,1,0:T(8,128)(2,1)}), bf16[16,128,512]{2,1,0:T(8,128)(2,1)S(1)}, u32[]{:S(2)}, u32[]{:S(2)}) async-start(bf16[16,128,512]{2,1,0:T(8,128)(2,1)} %get-tuple-element.48), calls=%async_computation | async-start | bytes 4194304 | tf_op jit(solution)/shard_map/all_to_all | solution.py:417
  11.7 14.8 %collective-permute-start.1 = (bf16[528,512]{1,0:T(8,128)(2,1)}, bf16[528,512]{1,0:T(8,128)(2,1)S(1)}, u32[]{:S(2)}, u32[]{:S(2)}) collective-permute-start(bf16[528,512]{1,0:T(8,128)(2,1)} %get-tuple-element.40.p0_ref), channel_id=1, source_target_pairs={{0,6},{1,7},{2,0},{3,1},{4,2},{5,3},{6,4},{7,5},{8,14},{9,15},{10,... | collective-permute-start | bytes 1622024 | tf_op jit(solution)/shard_map/ppermute | solution.py:409
  15.5 13.9 %collective-permute-start = (bf16[528,512]{1,0:T(8,128)(2,1)}, bf16[528,512]{1,0:T(8,128)(2,1)S(1)}, u32[]{:S(2)}, u32[]{:S(2)}) collective-permute-start(bf16[528,512]{1,0:T(8,128)(2,1)} %get-tuple-element.40.p0_ref), channel_id=1, source_target_pairs={{0,2},{1,3},{2,4},{3,5},{4,6},{5,7},{6,0},{7,1},{8,10},{9,11},{10,... | collective-permute-start | bytes 1622024 | tf_op jit(solution)/shard_map/ppermute | solution.py:409
  26.4 21.8 %copy-start.5 = (bf16[528,512]{1,0:T(8,128)(2,1)}, bf16[528,512]{1,0:T(8,128)(2,1)S(1)}, u32[]{:S(2)}) copy-start(bf16[528,512]{1,0:T(8,128)(2,1)S(1)} %collective-permute-done.1.p3_ref) | copy-start | bytes 1622020
  29.4 0.8 copy-start.6
  30.3 18.4 %collective-permute-start.3 = (bf16[272,512]{1,0:T(8,128)(2,1)S(1)}, bf16[272,512]{1,0:T(8,128)(2,1)S(1)}, u32[]{:S(2)}, u32[]{:S(2)}) collective-permute-start(bf16[272,512]{1,0:T(8,128)(2,1)S(1)} %slice.19), channel_id=1, source_target_pairs={{0,6},{1,7},{2,0},{3,1},{4,2},{5,3},{6,4},{7,5},{8,14},{9,15},{10,... | collective-permute-start | bytes 835592 | tf_op jit(solution)/shard_map/ppermute | solution.py:409
  31.7 17.0 %collective-permute-start.2 = (bf16[256,512]{1,0:T(8,128)(2,1)S(1)}, bf16[256,512]{1,0:T(8,128)(2,1)}, u32[]{:S(2)}, u32[]{:S(2)}) collective-permute-start(bf16[256,512]{1,0:T(8,128)(2,1)S(1)} %slice.18), channel_id=1, source_target_pairs={{0,2},{1,3},{2,4},{3,5},{4,6},{5,7},{6,0},{7,1},{8,10},{9,11},{10,... | collective-permute-start | bytes 786440 | tf_op jit(solution)/shard_map/ppermute | solution.py:409
  39.5 1.3 copy-start.2
  40.8 38.1 %all-to-all-start.1 = ((bf16[16,128,512]{2,1,0:T(8,128)(2,1)}), bf16[16,128,512]{2,1,0:T(8,128)(2,1)S(1)}, u32[]{:S(2)}, u32[]{:S(2)}) async-start(bf16[16,128,512]{2,1,0:T(8,128)(2,1)} %get-tuple-element.54), calls=%async_computation.1 | async-start | bytes 4194304 | tf_op jit(solution)/shard_map/all_to_all | solution.py:417
  44.8 8.7 %collective-permute-start.4 = (bf16[528,512]{1,0:T(8,128)(2,1)}, bf16[528,512]{1,0:T(8,128)(2,1)}, u32[]{:S(2)}, u32[]{:S(2)}) collective-permute-start(bf16[528,512]{1,0:T(8,128)(2,1)} %get-tuple-element.40.p0_ref), channel_id=1, source_target_pairs={{0,1},{1,0},{2,3},{3,2},{4,5},{5,4},{6,7},{7,6},{8,9},{9,8},{10,11... | collective-permute-start | bytes 1622024 | tf_op jit(solution)/shard_map/ppermute | solution.py:413
  48.1 5.8 %collective-permute-start.5 = (bf16[528,512]{1,0:T(8,128)(2,1)}, bf16[528,512]{1,0:T(8,128)(2,1)}, u32[]{:S(2)}, u32[]{:S(2)}) collective-permute-start(bf16[528,512]{1,0:T(8,128)(2,1)} %copy-done.6), channel_id=1, source_target_pairs={{0,1},{1,0},{2,3},{3,2},{4,5},{5,4},{6,7},{7,6},{8,9},{9,8},{10,11... | collective-permute-start | bytes 1622024 | tf_op jit(solution)/shard_map/ppermute | solution.py:413
  48.2 5.7 %collective-permute-start.8 = (bf16[528,512]{1,0:T(8,128)(2,1)S(1)}, bf16[528,512]{1,0:T(8,128)(2,1)}, u32[]{:S(2)}, u32[]{:S(2)}) collective-permute-start(bf16[528,512]{1,0:T(8,128)(2,1)S(1)} %collective-permute-done.1.p3_ref), channel_id=1, source_target_pairs={{0,1},{1,0},{2,3},{3,2},{4,5},{5,4},{6,7},{7,6},{8,9},{9,8},{10,11... | collective-permute-start | bytes 1622024 | tf_op jit(solution)/shard_map/ppermute | solution.py:413
  48.6 5.2 %collective-permute-start.6 = (bf16[256,512]{1,0:T(8,128)(2,1)}, bf16[256,512]{1,0:T(8,128)(2,1)S(1)}, u32[]{:S(2)}, u32[]{:S(2)}) collective-permute-start(bf16[256,512]{1,0:T(8,128)(2,1)} %collective-permute-done.2.t2_ref), channel_id=1, source_target_pairs={{0,1},{1,0},{2,3},{3,2},{4,5},{5,4},{6,7},{7,6},{8,9},{9,8},{10,11... | collective-permute-start | bytes 786440 | tf_op jit(solution)/shard_map/ppermute | solution.py:413
  48.7 4.8 %copy-start.11 = (bf16[272,512]{1,0:T(8,128)(2,1)}, bf16[272,512]{1,0:T(8,128)(2,1)S(1)}, u32[]{:S(2)}) copy-start(bf16[272,512]{1,0:T(8,128)(2,1)S(1)} %collective-permute-done.3.b2_ref) | copy-start | bytes 835588
  48.7 5.2 %collective-permute-start.7 = (bf16[272,512]{1,0:T(8,128)(2,1)S(1)}, bf16[272,512]{1,0:T(8,128)(2,1)S(1)}, u32[]{:S(2)}, u32[]{:S(2)}) collective-permute-start(bf16[272,512]{1,0:T(8,128)(2,1)S(1)} %collective-permute-done.3.b2_ref), channel_id=1, source_target_pairs={{0,1},{1,0},{2,3},{3,2},{4,5},{5,4},{6,7},{7,6},{8,9},{9,8},{10,11... | collective-permute-start | bytes 835592 | tf_op jit(solution)/shard_map/ppermute | solution.py:413
  53.5 2.1 %collective-permute-start.9 = (bf16[16,64,128]{2,1,0:T(8,128)(2,1)}, bf16[16,64,128]{2,1,0:T(8,128)(2,1)}, u32[]{:S(2)}, u32[]{:S(2)}) collective-permute-start(bf16[16,64,128]{2,1,0:T(8,128)(2,1)} %get-tuple-element.52), channel_id=1, source_target_pairs={{0,1},{1,0},{2,3},{3,2},{4,5},{5,4},{6,7},{7,6},{8,9},{9,8},{10,11... | collective-permute-start | bytes 786440 | tf_op jit(solution)/shard_map/ppermute | solution.py:413
  53.9 1.8 %copy-start.16 = (bf16[256,512]{1,0:T(8,128)(2,1)}, bf16[256,512]{1,0:T(8,128)(2,1)S(1)}, u32[]{:S(2)}) copy-start(bf16[256,512]{1,0:T(8,128)(2,1)S(1)} %collective-permute-done.6.t6_ref) | copy-start | bytes 786436
  53.9 1.7 %copy-start.12 = (bf16[272,512]{1,0:T(8,128)(2,1)}, bf16[272,512]{1,0:T(8,128)(2,1)S(1)}, u32[]{:S(2)}) copy-start(bf16[272,512]{1,0:T(8,128)(2,1)S(1)} %collective-permute-done.7.b6_ref) | copy-start | bytes 835588
  79.0 6.8 %copy-start.1 = (bf16[16,128,512]{2,1,0:T(8,128)(2,1)}, bf16[16,128,512]{2,1,0:T(8,128)(2,1)S(1)}, u32[]{:S(2)}) copy-start(bf16[16,128,512]{2,1,0:T(8,128)(2,1)S(1)} %all-to-all-done.1.back_ref) | copy-start | bytes 6291460
  79.0 17.0 %all-to-all-start.2 = ((bf16[16,128,128]{2,1,0:T(8,128)(2,1)}), bf16[16,128,128]{2,1,0:T(8,128)(2,1)S(1)}, u32[]{:S(2)}, u32[]{:S(2)}) async-start(bf16[16,128,128]{2,1,0:T(8,128)(2,1)} %get-tuple-element.55), calls=%async_computation.2 | async-start | bytes 1048576 | tf_op jit(solution)/shard_map/all_to_all | solution.py:417
  89.0 1.5 collective-permute-start.10
  90.4 5.6 %copy-start.24 = (f32[8,128]{1,0:T(8,128)}, f32[8,128]{1,0:T(8,128)S(1)}, u32[]{:S(2)}) copy-start(f32[8,128]{1,0:T(8,128)S(1)} %collective-permute-done.10.g1_ref) | copy-start | bytes 12292
  96.0 0.8 copy-start.4
  98.6 5.1 %collective-permute-start.13 = (bf16[144,128]{1,0:T(8,128)(2,1)}, bf16[144,128]{1,0:T(8,128)(2,1)S(1)}, u32[]{:S(2)}, u32[]{:S(2)}) collective-permute-start(bf16[144,128]{1,0:T(8,128)(2,1)} %shard_map.170.c0_ref), channel_id=1, source_target_pairs={{0,6},{1,7},{2,0},{3,1},{4,2},{5,3},{6,4},{7,5},{8,14},{9,15},{10,... | collective-permute-start | bytes 110600 | tf_op jit(solution)/shard_map/ppermute | solution.py:409
  102.4 4.6 %collective-permute-start.12 = (bf16[144,128]{1,0:T(8,128)(2,1)}, bf16[144,128]{1,0:T(8,128)(2,1)S(1)}, u32[]{:S(2)}, u32[]{:S(2)}) collective-permute-start(bf16[144,128]{1,0:T(8,128)(2,1)} %shard_map.170.c0_ref), channel_id=1, source_target_pairs={{0,4},{1,5},{2,6},{3,7},{4,0},{5,1},{6,2},{7,3},{8,12},{9,13},{10,... | collective-permute-start | bytes 110600 | tf_op jit(solution)/shard_map/ppermute | solution.py:409
  102.4 4.6 %collective-permute-start.11 = (bf16[144,128]{1,0:T(8,128)(2,1)}, bf16[144,128]{1,0:T(8,128)(2,1)S(1)}, u32[]{:S(2)}, u32[]{:S(2)}) collective-permute-start(bf16[144,128]{1,0:T(8,128)(2,1)} %shard_map.170.c0_ref), channel_id=1, source_target_pairs={{0,2},{1,3},{2,4},{3,5},{4,6},{5,7},{6,0},{7,1},{8,10},{9,11},{10,... | collective-permute-start | bytes 110600 | tf_op jit(solution)/shard_map/ppermute | solution.py:409
  103.7 3.3 %copy-start.21 = (bf16[144,128]{1,0:T(8,128)(2,1)}, bf16[144,128]{1,0:T(8,128)(2,1)S(1)}, u32[]{:S(2)}) copy-start(bf16[144,128]{1,0:T(8,128)(2,1)S(1)} %collective-permute-done.13.c3_ref) | copy-start | bytes 110596
  110.3 4.3 %copy-start.15 = (bf16[2,256,256]{2,1,0:T(8,128)(2,1)S(1)}, bf16[2,256,256]{2,1,0:T(8,128)(2,1)}, u32[]{:S(2)}) copy-start(bf16[2,256,256]{2,1,0:T(8,128)(2,1)} %get-tuple-element.64) | copy-start | bytes 786436
  110.3 4.4 %copy-start.14 = (bf16[2,256,256]{2,1,0:T(8,128)(2,1)S(1)}, bf16[2,256,256]{2,1,0:T(8,128)(2,1)}, u32[]{:S(2)}) copy-start(bf16[2,256,256]{2,1,0:T(8,128)(2,1)} %get-tuple-element.65) | copy-start | bytes 786436
  110.3 5.6 %copy-start.7 = (bf16[2,256,256]{2,1,0:T(8,128)(2,1)S(1)}, bf16[2,256,256]{2,1,0:T(8,128)(2,1)}, u32[]{:S(2)}) copy-start(bf16[2,256,256]{2,1,0:T(8,128)(2,1)} %get-tuple-element.63.r0_ref) | copy-start | bytes 786436
  110.3 9.2 %copy-start.13 = (bf16[2,256,256]{2,1,0:T(8,128)(2,1)S(1)}, bf16[2,256,256]{2,1,0:T(8,128)(2,1)}, u32[]{:S(2)}) copy-start(bf16[2,256,256]{2,1,0:T(8,128)(2,1)} %get-tuple-element.66) | copy-start | bytes 786436
  110.3 27.6 %all-to-all-start.3 = ((bf16[16,336,128]{2,1,0:T(8,128)(2,1)}), bf16[16,336,128]{2,1,0:T(8,128)(2,1)S(1)}, u32[]{:S(2)}, u32[]{:S(2)}) async-start(bf16[16,336,128]{2,1,0:T(8,128)(2,1)} %shard_map.171), calls=%async_computation.3 | async-start | bytes 2752512 | tf_op jit(solution)/shard_map/all_to_all | solution.py:417
  114.6 5.9 %collective-permute-start.14 = (bf16[2,256,256]{2,1,0:T(8,128)(2,1)S(1)}, bf16[2,256,256]{2,1,0:T(8,128)(2,1)S(1)}, u32[]{:S(2)}, u32[]{:S(2)}) collective-permute-start(bf16[2,256,256]{2,1,0:T(8,128)(2,1)S(1)} %copy-done.15), channel_id=1, source_target_pairs={{0,6},{1,7},{2,0},{3,1},{4,2},{5,3},{6,4},{7,5},{8,14},{9,15},{10,... | collective-permute-start | bytes 786440 | tf_op jit(solution)/shard_map/ppermute | solution.py:409
  114.7 11.6 %collective-permute-start.15 = (bf16[2,256,256]{2,1,0:T(8,128)(2,1)S(1)}, bf16[2,256,256]{2,1,0:T(8,128)(2,1)S(1)}, u32[]{:S(2)}, u32[]{:S(2)}) collective-permute-start(bf16[2,256,256]{2,1,0:T(8,128)(2,1)S(1)} %copy-done.14), channel_id=1, source_target_pairs={{0,4},{1,5},{2,6},{3,7},{4,0},{5,1},{6,2},{7,3},{8,12},{9,13},{10,... | collective-permute-start | bytes 786440 | tf_op jit(solution)/shard_map/ppermute | solution.py:409
  115.9 16.0 %collective-permute-start.17 = (bf16[256,256]{1,0:T(8,128)(2,1)S(1)}, bf16[256,256]{1,0:T(8,128)(2,1)S(1)}, u32[]{:S(2)}, u32[]{:S(2)}) collective-permute-start(bf16[256,256]{1,0:T(8,128)(2,1)S(1)} %slice_bitcast_fusion.3), channel_id=1, source_target_pairs={{0,1},{1,0},{2,3},{3,2},{4,5},{5,4},{6,7},{7,6},{8,9},{9,8},{10,11... | collective-permute-start | bytes 393224 | tf_op jit(solution)/shard_map/ppermute | solution.py:413
  119.5 11.9 %collective-permute-start.16 = (bf16[2,256,256]{2,1,0:T(8,128)(2,1)S(1)}, bf16[2,256,256]{2,1,0:T(8,128)(2,1)S(1)}, u32[]{:S(2)}, u32[]{:S(2)}) collective-permute-start(bf16[2,256,256]{2,1,0:T(8,128)(2,1)S(1)} %copy-done.13), channel_id=1, source_target_pairs={{0,2},{1,3},{2,4},{3,5},{4,6},{5,7},{6,0},{7,1},{8,10},{9,11},{10,... | collective-permute-start | bytes 786440 | tf_op jit(solution)/shard_map/ppermute | solution.py:409
  120.5 12.3 %copy-start.8 = (bf16[2,256,256]{2,1,0:T(8,128)(2,1)}, bf16[2,256,256]{2,1,0:T(8,128)(2,1)S(1)}, u32[]{:S(2)}) copy-start(bf16[2,256,256]{2,1,0:T(8,128)(2,1)S(1)} %collective-permute-done.14.r1_ref) | copy-start | bytes 786436
  120.5 11.3 %collective-permute-start.18 = (bf16[256,256]{1,0:T(8,128)(2,1)S(1)}, bf16[256,256]{1,0:T(8,128)(2,1)S(1)}, u32[]{:S(2)}, u32[]{:S(2)}) collective-permute-start(bf16[256,256]{1,0:T(8,128)(2,1)S(1)} %slice_bitcast_fusion.2), channel_id=1, source_target_pairs={{0,1},{1,0},{2,3},{3,2},{4,5},{5,4},{6,7},{7,6},{8,9},{9,8},{10,11... | collective-permute-start | bytes 393224 | tf_op jit(solution)/shard_map/ppermute | solution.py:413
  126.3 6.5 %copy-start.9 = (bf16[2,256,256]{2,1,0:T(8,128)(2,1)}, bf16[2,256,256]{2,1,0:T(8,128)(2,1)S(1)}, u32[]{:S(2)}) copy-start(bf16[2,256,256]{2,1,0:T(8,128)(2,1)S(1)} %collective-permute-done.15.r2_ref) | copy-start | bytes 786436
  126.4 5.5 %collective-permute-start.19 = (bf16[256,256]{1,0:T(8,128)(2,1)S(1)}, bf16[256,256]{1,0:T(8,128)(2,1)S(1)}, u32[]{:S(2)}, u32[]{:S(2)}) collective-permute-start(bf16[256,256]{1,0:T(8,128)(2,1)S(1)} %slice_bitcast_fusion.1), channel_id=1, source_target_pairs={{0,1},{1,0},{2,3},{3,2},{4,5},{5,4},{6,7},{7,6},{8,9},{9,8},{10,11... | collective-permute-start | bytes 393224 | tf_op jit(solution)/shard_map/ppermute | solution.py:413
  131.3 1.5 %copy-start.10 = (bf16[2,256,256]{2,1,0:T(8,128)(2,1)}, bf16[2,256,256]{2,1,0:T(8,128)(2,1)S(1)}, u32[]{:S(2)}) copy-start(bf16[2,256,256]{2,1,0:T(8,128)(2,1)S(1)} %collective-permute-done.16.r3_ref) | copy-start | bytes 786436
  131.3 1.5 %collective-permute-start.20 = (bf16[256,256]{1,0:T(8,128)(2,1)S(1)}, bf16[256,256]{1,0:T(8,128)(2,1)S(1)}, u32[]{:S(2)}, u32[]{:S(2)}) collective-permute-start(bf16[256,256]{1,0:T(8,128)(2,1)S(1)} %slice_bitcast_fusion), channel_id=1, source_target_pairs={{0,1},{1,0},{2,3},{3,2},{4,5},{5,4},{6,7},{7,6},{8,9},{9,8},{10,11... | collective-permute-start | bytes 393224 | tf_op jit(solution)/shard_map/ppermute | solution.py:413
  131.8 1.0 copy-start.17
  131.8 1.0 copy-start.18
  131.9 1.0 copy-start.19
  137.9 3.2 %copy-start = (bf16[16,336,128]{2,1,0:T(8,128)(2,1)}, bf16[16,336,128]{2,1,0:T(8,128)(2,1)S(1)}, u32[]{:S(2)}) copy-start(bf16[16,336,128]{2,1,0:T(8,128)(2,1)S(1)} %all-to-all-done.3.mine_ref) | copy-start | bytes 4128772
  137.9 3.2 %collective-permute-start.21 = (bf16[16,336,128]{2,1,0:T(8,128)(2,1)S(1)}, bf16[16,336,128]{2,1,0:T(8,128)(2,1)S(1)}, u32[]{:S(2)}, u32[]{:S(2)}) collective-permute-start(bf16[16,336,128]{2,1,0:T(8,128)(2,1)S(1)} %all-to-all-done.3.mine_ref), channel_id=1, source_target_pairs={{0,1},{1,0},{2,3},{3,2},{4,5},{5,4},{6,7},{7,6},{8,9},{9,8},{10,11... | collective-permute-start | bytes 4128776 | tf_op jit(solution)/shard_map/ppermute | solution.py:413
  141.2 1.1 copy-start.3
  (3 other events, 1.9 us)

commit v7 on v6

--- a/solution.py
+++ b/solution.py
@@ -154,23 +154,21 @@
             fill(other_ref)
 
 
-def attention_body(
-    p0_ref, p1_ref, t2_ref, b2_ref, p3_ref, p4_ref, p5_ref, t6_ref, b6_ref, p7_ref, wqkv_ref, wo_ref, mine_ref, other_ref,
-    r0_ref, r1_ref, r2_ref, r3_ref, chunks_ref,
-    y_ref, s_ref, qt_ref, kt_ref, k_ref, v_ref, vt_ref, w_ref, dq_ref, dk_ref, dv_ref, at_ref, ga_ref, sl_ref, qr_ref, gr_ref,
-):
-    pays = (p0_ref, p1_ref, (t2_ref, b2_ref), p3_ref, p4_ref, p5_ref, (t6_ref, b6_ref), p7_ref)
-
-    def normed_of(pay):
-        return pay[0][...] if isinstance(pay, tuple) else pay[0:ROWS, :]
-
-    def grads_of(pay):
-        return pay[1][0:ROWS, :] if isinstance(pay, tuple) else pay[ROWS : 2 * ROWS, :]
-
-    def tail_of(pay):
-        return pay[1][ROWS : PAY - ROWS, 0:ROWS] if isinstance(pay, tuple) else pay[2 * ROWS : PAY, 0:ROWS]
-
-    outs = (r0_ref, r1_ref, r2_ref, r3_ref)
+def unpack(refs):
+    p0, p1, t2, b2, p3, p4, p5, t6, b6, p7 = refs
+
+    def split(pay):
+        return pay.at[0:ROWS], pay.at[ROWS : 2 * ROWS], pay.at[2 * ROWS : PAY]
+
+    def joined(top, bottom):
+        return top, bottom.at[0:ROWS], bottom.at[ROWS : PAY - ROWS]
+
+    return [split(p0), split(p1), joined(t2, b2), split(p3), split(p4), split(p5), joined(t6, b6), split(p7)]
+
+
+def projections_body(*refs):
+    blocks = unpack(refs[0:10])
+    wqkv_ref, wo_ref, y_ref, s_ref, qt_ref, kt_ref, k_ref, v_ref, vt_ref, ga_ref, qr_ref = refs[10:]
     z, core = position()
     row = lax.broadcasted_iota(jnp.int32, (HEAD, ROWS), 0)
     number = row.astype(F32)
@@ -179,8 +177,8 @@
         return lax.rsqrt(jnp.sum(part * part, axis=0, keepdims=True) * (1.0 / HEAD) + EPS)
 
     for r in range(BLK):
-        pay = pays[r]
-        projected = dot(wqkv_ref[...], normed_of(pay), NT)
+        normed_ref, grads_ref, tail_ref = blocks[r]
+        projected = dot(wqkv_ref[...], normed_ref[...], NT)
         query, key, value = projected[0:HEAD], projected[HEAD:128], projected[128:192]
         scale_q, scale_k = head_scale(query), head_scale(key)
         query, key = query * scale_q, key * scale_k
@@ -188,7 +186,7 @@
         y_ref[r, HEAD:128] = key
         s_ref[r, 0:1] = scale_q
         s_ref[r, 1:2] = scale_k
-        tail = tail_of(pay).astype(F32)
+        tail = tail_ref[:, 0:ROWS].astype(F32)
         same = jnp.where(number == tail[0:1], 32.0, 0.0)
         sender = ((z - (r & 3)) & 3) * 2 + (core ^ (r >> 2))
         wanted = jnp.concatenate([jnp.zeros((16, ROWS), F32), tail[1:9] * 32.0, jnp.zeros((40, ROWS), F32)], axis=0)
@@ -200,9 +198,16 @@
         value = jnp.concatenate([value, jnp.where(row < 2, 1.0, 0.0)], axis=0)
         vt_ref[r] = value[0:80].astype(BF16)
         v_ref[r] = jnp.transpose(value).astype(BF16)
-        ga_ref[r] = dot(wo_ref[...], grads_of(pay), NT)
+        ga_ref[r] = dot(wo_ref[...], grads_ref[...], NT)
         qr_ref[r] = jnp.transpose(qt_ref[r].astype(F32)).astype(BF16)
 
+
+def attention_body(*refs):
+    blocks = unpack(refs[0:10])
+    mine_ref, other_ref, y_ref, s_ref, qt_ref, kt_ref, k_ref, v_ref, vt_ref, ga_ref, qr_ref = refs[10:21]
+    *outs, chunks_ref = refs[21:26]
+    w_ref, dq_ref, dk_ref, dv_ref, at_ref, sl_ref, gr_ref = refs[26:]
+    row = lax.broadcasted_iota(jnp.int32, (HEAD, ROWS), 0)
     keys_t = jnp.concatenate([kt_ref[j] for j in range(BLK)], axis=1)
     values_t = jnp.concatenate([vt_ref[j] for j in range(BLK)], axis=1)
 
@@ -243,7 +248,7 @@
     dw = jnp.zeros((192, D), F32)
     dwo = jnp.zeros((HEAD, D), F32)
     for r in range(BLK):
-        pay = pays[r]
+        normed_ref, grads_ref, tail_ref = blocks[r]
 
         def pull(grad, y, scale):
             grad = grad * (8.0 / HEAD)
@@ -256,8 +261,8 @@
         outs[r & 3][r >> 2, :, 0:128] = jnp.transpose(first).astype(BF16)
         outs[r & 3][r >> 2, :, 128:256] = jnp.transpose(second).astype(BF16)
         left = jnp.concatenate([first, second[0:HEAD]], axis=0).astype(BF16)
-        dw = dw + dot(left, normed_of(pay))
-        dwo = dwo + dot(at_ref[r], grads_of(pay))
+        dw = dw + dot(left, normed_ref[...])
+        dwo = dwo + dot(at_ref[r], grads_ref[...])
     dw = jnp.concatenate([dw, dwo], axis=0).astype(BF16)
     for a in range(4):
         for b in range(4):
@@ -444,7 +449,17 @@
     near, far, degree = lax.optimization_barrier((near, far, degree))
     pays = [pay, near, along_chips(near[0:ROWS], 1), along_chips(far[ROWS:PAY], 3), far]
     pays = pays + [other_core(part) for part in pays]
-    incoming, slot_grads = lax.optimization_barrier((incoming, slot_grads))
+    projections = call(
+        projections_body,
+        (
+            shape((BLK, 128, ROWS), F32), shape((BLK, 8, ROWS), F32), shape((BLK, 128, ROWS), BF16),
+            shape((BLK, HEAD, ROWS), BF16), shape((BLK, ROWS, 128), BF16), shape((BLK, ROWS, 128), BF16),
+            shape((BLK, 80, ROWS), BF16), shape((BLK, HEAD, ROWS), F32), shape((BLK, ROWS, 128), BF16),
+        ),
+        (*pays, wqkv, wo_head),
+        micros=3,
+    )
+    incoming, slot_grads, *projections = lax.optimization_barrier((incoming, slot_grads, *projections))
     back = to_dom_peers(slot_grads)
 
     base, mine, other = call(
@@ -457,23 +472,14 @@
     *results, chunks = call(
         attention_body,
         (*[shape((2, ROWS, 256), BF16)] * 4, shape((DOM, 128, 128), BF16)),
-        (*pays, wqkv, wo_head, mine, other_core(other)),
+        (*pays, mine, other_core(other), *projections),
         scratch=[
-            pltpu.VMEM((BLK, 128, ROWS), F32),
-            pltpu.VMEM((BLK, 8, ROWS), F32),
-            pltpu.VMEM((BLK, 128, ROWS), BF16),
-            pltpu.VMEM((BLK, HEAD, ROWS), BF16),
-            pltpu.VMEM((BLK, ROWS, 128), BF16),
-            pltpu.VMEM((BLK, ROWS, 128), BF16),
-            pltpu.VMEM((BLK, 80, ROWS), BF16),
             pltpu.VMEM((BLK, BLK, ROWS, ROWS), BF16),
             pltpu.VMEM((BLK, HEAD, ROWS), F32),
             pltpu.VMEM((BLK, HEAD, ROWS), F32),
             pltpu.VMEM((BLK, HEAD, ROWS), F32),
             pltpu.VMEM((BLK, HEAD, ROWS), BF16),
-            pltpu.VMEM((BLK, HEAD, ROWS), F32),
             pltpu.VMEM((BLK, BLK, ROWS, ROWS), BF16),
-            pltpu.VMEM((BLK, ROWS, 128), BF16),
             pltpu.VMEM((BLK, ROWS, 128), BF16),
         ],
         micros=12,
@@ -487,6 +493,8 @@
         scalars=1,
         micros=3,
     )
+    *results, gain_part = lax.optimization_barrier((*results, gain_part))
+    results = [results[0]] + [along_chips(results[dz], -dz) for dz in (1, 2, 3)]
     chunk = call(
         chunk_sum_body,
         shape((CHUNK, 128), BF16),
@@ -495,12 +503,13 @@
         micros=1,
     )
     chunk_parts = [chunk] + [along_chips(chunk, step) for step in (1, 2, 3)]
+    *chunk_parts, r1, r2, r3 = lax.optimization_barrier((*chunk_parts, *results[1:]))
+    results = [results[0], r1, r2, r3]
     spread = call(
         spread_body, shape((DOM, SPREAD, 128), BF16), chunk_parts, scratch=[pltpu.VMEM((4, 80, 128), F32)], micros=1
     )
     spread, *results = lax.optimization_barrier((spread, *results))
     gathered = to_dom_peers(spread)
-    results = [results[0]] + [along_chips(results[dz], -dz) for dz in (1, 2, 3)]
     swapped = [other_core(part[1]) for part in results]
     layer_out, feature_grad = call(
         rows_body,

time: 148 us -> 157 us (1.061)
  Pallas kernels: 57 us -> 62.4 us
  waiting for transfers between devices: 31.9 us -> 33.9 us
    pallas_call x8 -> x9, Pallas kernels: 51.6 us -> 57.1 us  [call(): pl.pallas_call(body, out_shape=out_shape, in_specs=specs, out_specs=jax.t...]
    all_to_all x4, starting transfers between devices: 22.6 us -> 27.8 us  [to_dom_peers(): return lax.all_to_all(array, 'dom', split_axis=0, concat_axis=0, tiled=True)]
    ppermute x10, starting transfers between devices: 12.2 us -> 9.77 us  [along_chips(): return lax.ppermute(array, 'blk', chip_shift(step, 0))]
    unnamed x50 -> x58, local copies, waits for them, and re-layouts: 5.93 us -> 7.24 us
  transfers between devices with their start and end apart: 26 -> 26, of which waited for: 11 -> 16; matrix products, arithmetic and copies ran while one was open for 1% -> 0% of each run, Pallas kernels for 30% -> 33%
where the time goes in v7:
time: 157 us
  Pallas kernels  62.4 us (40%)
  starting transfers between devices  52.2 us (33%)
  waiting for transfers between devices  33.9 us (22%)
  local copies, waits for them, and re-layouts  7.32 us (5%)
    pallas_call x9, Pallas kernels, call(): pl.pallas_call(body, out_shape=out_shape, in_specs=specs, out_specs=jax.t...  57.1 us
    all_to_all x4, starting transfers between devices, to_dom_peers(): return lax.all_to_all(array, 'dom', split_axis=0, concat_axis=0, tiled=True)  27.8 us
    ppermute x12, starting transfers between devices, other_core(): return lax.ppermute(array, 'blk', chip_shift(0, 1))  14.6 us
    ppermute x10, waiting for transfers between devices, along_chips(): return lax.ppermute(array, 'blk', chip_shift(step, 0))  13.8 us
    all_to_all x4, waiting for transfers between devices, to_dom_peers(): return lax.all_to_all(array, 'dom', split_axis=0, concat_axis=0, tiled=True)  12.5 us
    ppermute x10, starting transfers between devices, along_chips(): return lax.ppermute(array, 'blk', chip_shift(step, 0))  9.77 us
    ppermute x12, waiting for transfers between devices, other_core(): return lax.ppermute(array, 'blk', chip_shift(0, 1))  7.58 us
    unnamed x58, local copies, waits for them, and re-layouts  7.24 us
  transfers between devices with their start and end apart: 26, of which 16 were waited for; matrix products, arithmetic and copies ran while one was open for 0% of the time, Pallas kernels for 33%

profile of v7, /device:TPU:1, one launch (start us, length us, event | category | flops | bytes accessed | tf_op | source)
XLA Modules:
  0.0 156.7 jit_solution(14483183980524130337)
XLA Ops:
  0.6 3.4 %shard_map.165 = (bf16[528,512]{1,0:T(8,128)(2,1)}, bf16[16,128,512]{2,1,0:T(8,128)(2,1)}) custom-call(s32[1,8]{1,0:T(1,128)} %pattern_ref.1, s32[16]{0:T(128)} %counts_ref.3, bf16[256,512]{1,0:T(8,128)(2,1)} %x_ref.7, f32[1,512]{1,0:T(1,128)} %bitcast.13, s32[1,256]{1,0:T(1,128)} %bitcast.19, bf16[256,512]{1,0:T(8,128)(2,1)} %grad_ref.7, s32[16,128]{1,0:T(8,128)} %rows_ref.3), custom_call_target="tpu_custom_call" | custom-call | flops 4000000000 | bytes 1048576 | tf_op jit(solution)/shard_map/pallas_call | solution.py:38
  4.1 7.6 %all-to-all-start = ((bf16[16,128,512]{2,1,0:T(8,128)(2,1)}), bf16[16,128,512]{2,1,0:T(8,128)(2,1)S(1)}, u32[]{:S(2)}, u32[]{:S(2)}) async-start(bf16[16,128,512]{2,1,0:T(8,128)(2,1)} %get-tuple-element.76), calls=%async_computation | async-start | bytes 4194304 | tf_op jit(solution)/shard_map/all_to_all | solution.py:422
  11.7 3.8 %collective-permute-start.1 = (bf16[528,512]{1,0:T(8,128)(2,1)}, bf16[528,512]{1,0:T(8,128)(2,1)S(1)}, u32[]{:S(2)}, u32[]{:S(2)}) collective-permute-start(bf16[528,512]{1,0:T(8,128)(2,1)} %get-tuple-element.70.refs_0_), channel_id=1, source_target_pairs={{0,6},{1,7},{2,0},{3,1},{4,2},{5,3},{6,4},{7,5},{8,14},{9,15},{10,... | collective-permute-start | bytes 1622024 | tf_op jit(solution)/shard_map/ppermute | solution.py:414
  15.5 8.9 %shard_map.166 = (bf16[1024,512]{1,0:T(8,128)(2,1)}, f32[256,128]{1,0:T(8,128)}, bf16[16,128,512]{2,1,0:T(8,128)(2,1)}, bf16[192,512]{1,0:T(8,128)(2,1)}, bf16[64,512]{1,0:T(8,128)(2,1)}) custom-call(s32[32,128]{1,0:T(8,128)} %bitcast.16, s32[32,128]{1,0:T(8,128)} %bitcast.17, bf16[256,512]{1,0:T(8,128)(2,1)} %grad_ref.7, bf16[512,512]{1,0:T(8,128)(2,1)} %w_ref.3, ...), custom_call_target="tpu_custom_call" | custom-call | flops 10000000000 | bytes 1048576 | tf_op jit(solution)/shard_map/pallas_call | solution.py:38
  24.4 2.0 %collective-permute-done.1.refs_4_ = bf16[528,512]{1,0:T(8,128)(2,1)S(1)} collective-permute-done((bf16[528,512]{1,0:T(8,128)(2,1)}, bf16[528,512]{1,0:T(8,128)(2,1)S(1)}, u32[]{:S(2)}, u32[]{:S(2)}) %collective-permute-start.1) | collective-permute-done | bytes 540704 | tf_op jit(solution)/shard_map/ppermute | solution.py:414
  26.4 3.0 %collective-permute-done.refs_1_ = bf16[528,512]{1,0:T(8,128)(2,1)S(1)} collective-permute-done((bf16[528,512]{1,0:T(8,128)(2,1)}, bf16[528,512]{1,0:T(8,128)(2,1)S(1)}, u32[]{:S(2)}, u32[]{:S(2)}) %collective-permute-start) | collective-permute-done | bytes 540704 | tf_op jit(solution)/shard_map/ppermute | solution.py:414
  29.8 2.2 %collective-permute-start.4 = (bf16[528,512]{1,0:T(8,128)(2,1)}, bf16[528,512]{1,0:T(8,128)(2,1)S(1)}, u32[]{:S(2)}, u32[]{:S(2)}) collective-permute-start(bf16[528,512]{1,0:T(8,128)(2,1)} %get-tuple-element.70.refs_0_), channel_id=1, source_target_pairs={{0,1},{1,0},{2,3},{3,2},{4,5},{5,4},{6,7},{7,6},{8,9},{9,8},{10,11... | collective-permute-start | bytes 1622024 | tf_op jit(solution)/shard_map/ppermute | solution.py:418
  32.0 0.5 collective-permute-start.8
  32.5 1.5 collective-permute-start.2
  34.0 1.5 collective-permute-done.3.refs_3_
  35.5 3.1 %collective-permute-start.7 = (bf16[272,512]{1,0:T(8,128)(2,1)S(1)}, bf16[272,512]{1,0:T(8,128)(2,1)S(1)}, u32[]{:S(2)}, u32[]{:S(2)}) collective-permute-start(bf16[272,512]{1,0:T(8,128)(2,1)S(1)} %collective-permute-done.3.refs_3_), channel_id=1, source_target_pairs={{0,1},{1,0},{2,3},{3,2},{4,5},{5,4},{6,7},{7,6},{8,9},{9,8},{10,11... | collective-permute-start | bytes 835592 | tf_op jit(solution)/shard_map/ppermute | solution.py:418
  38.6 3.1 %collective-permute-done.2.refs_2_ = bf16[256,512]{1,0:T(8,128)(2,1)S(1)} collective-permute-done((bf16[256,512]{1,0:T(8,128)(2,1)S(1)}, bf16[256,512]{1,0:T(8,128)(2,1)S(1)}, u32[]{:S(2)}, u32[]{:S(2)}) %collective-permute-start.2) | collective-permute-done | bytes 262176 | tf_op jit(solution)/shard_map/ppermute | solution.py:414
  41.7 0.8 collective-permute-start.6
  42.5 1.2 collective-permute-done.6.refs_7_
  43.7 0.8 copy-done.11
  44.7 0.5 copy-done.14
  45.2 5.7 %shard_map.167 = (f32[8,128,256]{2,1,0:T(8,128)}, f32[8,8,256]{2,1,0:T(8,128)}, bf16[8,128,256]{2,1,0:T(8,128)(2,1)}, bf16[8,64,256]{2,1,0:T(8,128)(2,1)}, bf16[...) custom-call(bf16[528,512]{1,0:T(8,128)(2,1)} %get-tuple-element.70.r, ...), custom_call_target="tpu_custom_call" | custom-call | flops 3000000000 | bytes 1048576 | tf_op jit(solution)/shard_map/pallas_call | solution.py:38
  51.0 1.3 copy-done.1
  52.3 6.6 %all-to-all-start.1 = ((bf16[16,128,512]{2,1,0:T(8,128)(2,1)}), bf16[16,128,512]{2,1,0:T(8,128)(2,1)}, u32[]{:S(2)}, u32[]{:S(2)}) async-start(bf16[16,128,512]{2,1,0:T(8,128)(2,1)} %get-tuple-element.102), calls=%async_computation.1 | async-start | bytes 4194304 | tf_op jit(solution)/shard_map/all_to_all | solution.py:422
  58.9 4.3 %shard_map.168 = (f32[256,512]{1,0:T(8,128)}, bf16[16,64,128]{2,1,0:T(8,128)(2,1)}, bf16[16,64,128]{2,1,0:T(8,128)(2,1)}) custom-call(bf16[1024,512]{1,0:T(8,128)(2,1)} %get-tuple-element.74.counts_t_ref, f32[256,128]{1,0:T(8,128)} %get-tuple-element.75.degree_ref, bf16[16,128,512]{2,1,0:T(8,128)(2,1)} %copy-done.1, bf16[256,512]{1,0:T(8,128)(2,1)} %x_ref.7, ...), custom_call_target="tpu_custom_call" | custom-call | flops 4000000000 | bytes 1048576 | tf_op jit(solution)/shard_map/pallas_call | solution.py:38
  63.3 0.7 collective-permute-start.9
  63.9 1.4 collective-permute-done.9.refs_11_
  65.3 0.7 copy-done.20
  66.0 23.1 %shard_map.169 = (bf16[2,256,256]{2,1,0:T(8,128)(2,1)}, bf16[2,256,256]{2,1,0:T(8,128)(2,1)}, bf16[2,256,256]{2,1,0:T(8,128)(2,1)}, bf16[2,256,256]{2,1,0:T(8,128)(2,1)}, bf16[16,128,128]{2,1,0:T(8,128)(2,1)}) custom-call(bf16[528,512]{1,0:T(8,128)(2,1)} %get-tuple-element.70.refs_0_, bf16[528,512]{1,0:T(8,128)(2,1)} %copy-done.5, ...), custom_call_target="tpu_custom_call" | custom-call | flops 12000000000 | bytes 1048576 | tf_op jit(solution)/shard_map/pallas_call | solution.py:38
  89.1 6.9 %all-to-all-start.2 = ((bf16[16,128,128]{2,1,0:T(8,128)(2,1)}), bf16[16,128,128]{2,1,0:T(8,128)(2,1)S(1)}, u32[]{:S(2)}, u32[]{:S(2)}) async-start(bf16[16,128,128]{2,1,0:T(8,128)(2,1)} %get-tuple-element.103), calls=%async_computation.2 | async-start | bytes 1048576 | tf_op jit(solution)/shard_map/all_to_all | solution.py:422
  96.0 3.2 %shard_map.170 = (f32[256,512]{1,0:T(8,128)}, f32[8,128]{1,0:T(8,128)}) custom-call(s32[16]{0:T(128)} %counts_ref.3, bf16[16,128,512]{2,1,0:T(8,128)(2,1)} %all-to-all-done.1.back_ref, s32[16,128]{1,0:T(8,128)} %rows_ref.3, bf16[256,512]{1,0:T(8,128)(2,1)} %x_ref.7), custom_call_target="tpu_custom_call" | custom-call | flops 3000000000 | bytes 1048576 | tf_op jit(solution)/shard_map/pallas_call | solution.py:38
  99.2 2.0 %collective-permute-start.15 = (bf16[2,256,256]{2,1,0:T(8,128)(2,1)S(1)}, bf16[2,256,256]{2,1,0:T(8,128)(2,1)S(1)}, u32[]{:S(2)}, u32[]{:S(2)}) collective-permute-start(bf16[2,256,256]{2,1,0:T(8,128)(2,1)S(1)} %copy-done.16), channel_id=1, source_target_pairs={{0,4},{1,5},{2,6},{3,7},{4,0},{5,1},{6,2},{7,3},{8,12},{9,13},{10,... | collective-permute-start | bytes 786440 | tf_op jit(solution)/shard_map/ppermute | solution.py:414
  101.2 1.2 collective-permute-start.10
  102.5 1.0 collective-permute-done.10.g1_ref
  103.5 2.8 %all-to-all-done.2.in_ref = bf16[16,128,128]{2,1,0:T(8,128)(2,1)S(1)} async-done(((bf16[16,128,128]{2,1,0:T(8,128)(2,1)}), bf16[16,128,128]{2,1,0:T(8,128)(2,1)S(1)}, u32[]{:S(2)}, u32[]{:S(2)}) %all-to-all-start.2) | async-done | bytes 524320 | tf_op jit(solution)/shard_map/all_to_all | solution.py:422
  106.3 0.8 copy-done.3
  107.1 1.8 %shard_map.171.c0_ref = bf16[144,128]{1,0:T(8,128)(2,1)} custom-call(bf16[16,128,128]{2,1,0:T(8,128)(2,1)} %copy-done.3, f32[8,128]{1,0:T(8,128)} %get-tuple-element.110.g0_ref, f32[8,128]{1,0:T(8,128)} %copy-done.28, bf16[192,512]{1,0:T(8,128)(2,1)} %get-tuple-element.78.refs_10_.wqkv_ref), custom_call_target="tpu_custom_call" | custom-call | flops 1000000000 | bytes 1048576 | tf_op jit(solution)/shard_map/pallas_call | solution.py:38
  109.0 0.7 collective-permute-start.13
  109.7 1.3 collective-permute-start.12
  111.0 4.0 %collective-permute-done.16.r3_ref = bf16[2,256,256]{2,1,0:T(8,128)(2,1)S(1)} collective-permute-done((bf16[2,256,256]{2,1,0:T(8,128)(2,1)S(1)}, bf16[2,256,256]{2,1,0:T(8,128)(2,1)S(1)}, u32[]{:S(2)}, u32[]{:S(2)}) %collective-permute-start.16) | collective-permute-done | bytes 262176 | tf_op jit(solution)/shard_map/ppermute | solution.py:414
  115.2 0.5 copy-done.25
  115.7 0.6 copy-done.27
  116.3 2.1 %shard_map.172 = bf16[16,336,128]{2,1,0:T(8,128)(2,1)} custom-call(bf16[144,128]{1,0:T(8,128)(2,1)} %shard_map.171.c0_ref, bf16[144,128]{1,0:T(8,128)(2,1)} %copy-done.27, bf16[144,128]{1,0:T(8,128)(2,1)} %copy-done.26, bf16[144,128]{1,0:T(8,128)(2,1)} %copy-done.25), custom_call_target="tpu_custom_call" | custom-call | flops 1000000000 | bytes 1048576 | tf_op jit(solution)/shard_map/pallas_call | solution.py:38
  118.4 6.7 %all-to-all-start.3 = ((bf16[16,336,128]{2,1,0:T(8,128)(2,1)}), bf16[16,336,128]{2,1,0:T(8,128)(2,1)S(1)}, u32[]{:S(2)}, u32[]{:S(2)}) async-start(bf16[16,336,128]{2,1,0:T(8,128)(2,1)} %shard_map.172), calls=%async_computation.3 | async-start | bytes 2752512 | tf_op jit(solution)/shard_map/all_to_all | solution.py:422
  125.2 1.7 %collective-permute-start.20 = (bf16[256,256]{1,0:T(8,128)(2,1)S(1)}, bf16[256,256]{1,0:T(8,128)(2,1)S(1)}, u32[]{:S(2)}, u32[]{:S(2)}) collective-permute-start(bf16[256,256]{1,0:T(8,128)(2,1)S(1)} %slice_bitcast_fusion), channel_id=1, source_target_pairs={{0,1},{1,0},{2,3},{3,2},{4,5},{5,4},{6,7},{7,6},{8,9},{9,8},{10,11... | collective-permute-start | bytes 393224 | tf_op jit(solution)/shard_map/ppermute | solution.py:418
  127.1 0.4 collective-permute-start.18
  127.6 0.4 collective-permute-done.20.t3_ref
  129.5 4.5 %shard_map.173 = (bf16[256,512]{1,0:T(8,128)(2,1)}, bf16[256,512]{1,0:T(8,128)(2,1)}) custom-call(bf16[2,256,256]{2,1,0:T(8,128)(2,1)} %get-tuple-element.123.r0_ref, bf16[2,256,256]{2,1,0:T(8,128)(2,1)} %copy-done.7, bf16[2,256,256]{2,1,0:T(8,128)(2,1)} %copy-done.8, bf16[2,256,256]{2,1,0:T(8,128)(2,1)} %copy-done.9, bf16[256,256]{1,0:T(8,128)(2,1)} %copy-done.24, ...), custom_call_target="tpu_custom_call" | custom-call | flops 2000000000 | bytes 1048576 | tf_op jit(solution)/shard_map/pallas_call | solution.py:38
  134.0 9.7 %all-to-all-done.3.mine_ref = bf16[16,336,128]{2,1,0:T(8,128)(2,1)S(1)} async-done(((bf16[16,336,128]{2,1,0:T(8,128)(2,1)}), bf16[16,336,128]{2,1,0:T(8,128)(2,1)S(1)}, u32[]{:S(2)}, u32[]{:S(2)}) %all-to-all-start.3) | async-done | bytes 1376288 | tf_op jit(solution)/shard_map/all_to_all | solution.py:422
  143.7 3.8 %collective-permute-start.21 = (bf16[16,336,128]{2,1,0:T(8,128)(2,1)S(1)}, bf16[16,336,128]{2,1,0:T(8,128)(2,1)S(1)}, u32[]{:S(2)}, u32[]{:S(2)}) collective-permute-start(bf16[16,336,128]{2,1,0:T(8,128)(2,1)S(1)} %all-to-all-done.3.mine_ref), channel_id=1, source_target_pairs={{0,1},{1,0},{2,3},{3,2},{4,5},{5,4},{6,7},{7,6},{8,9},{9,8},{10,11... | collective-permute-start | bytes 4128776 | tf_op jit(solution)/shard_map/ppermute | solution.py:418
  147.5 2.8 %collective-permute-done.21.other_ref = bf16[16,336,128]{2,1,0:T(8,128)(2,1)S(1)} collective-permute-done((bf16[16,336,128]{2,1,0:T(8,128)(2,1)S(1)}, bf16[16,336,128]{2,1,0:T(8,128)(2,1)S(1)}, u32[]{:S(2)}, u32[]{:S(2)}) %collective-permute-start.21) | collective-permute-done | bytes 1376288 | tf_op jit(solution)/shard_map/ppermute | solution.py:418
  150.3 1.1 copy-done.2
  151.4 5.4 %shard_map.174 = (f32[5,512,512]{2,1,0:T(8,128)}, f32[1,512]{1,0:T(1,128)}) custom-call(bf16[16,336,128]{2,1,0:T(8,128)(2,1)} %copy-done, bf16[16,336,128]{2,1,0:T(8,128)(2,1)} %copy-done.2, f32[1,512]{1,0:T(1,128)} %bitcast.15), custom_call_target="tpu_custom_call" | custom-call | tf_op jit(solution)/shard_map/pallas_call | solution.py:524
  (78 shorter events, 2.7 us)
Async XLA Ops:
  4.1 46.9 %all-to-all-start = ((bf16[16,128,512]{2,1,0:T(8,128)(2,1)}), bf16[16,128,512]{2,1,0:T(8,128)(2,1)S(1)}, u32[]{:S(2)}, u32[]{:S(2)}) async-start(bf16[16,128,512]{2,1,0:T(8,128)(2,1)} %get-tuple-element.76), calls=%async_computation | async-start | bytes 4194304 | tf_op jit(solution)/shard_map/all_to_all | solution.py:422
  11.7 14.8 %collective-permute-start.1 = (bf16[528,512]{1,0:T(8,128)(2,1)}, bf16[528,512]{1,0:T(8,128)(2,1)S(1)}, u32[]{:S(2)}, u32[]{:S(2)}) collective-permute-start(bf16[528,512]{1,0:T(8,128)(2,1)} %get-tuple-element.70.refs_0_), channel_id=1, source_target_pairs={{0,6},{1,7},{2,0},{3,1},{4,2},{5,3},{6,4},{7,5},{8,14},{9,15},{10,... | collective-permute-start | bytes 1622024 | tf_op jit(solution)/shard_map/ppermute | solution.py:414
  15.5 13.9 %collective-permute-start = (bf16[528,512]{1,0:T(8,128)(2,1)}, bf16[528,512]{1,0:T(8,128)(2,1)S(1)}, u32[]{:S(2)}, u32[]{:S(2)}) collective-permute-start(bf16[528,512]{1,0:T(8,128)(2,1)} %get-tuple-element.70.refs_0_), channel_id=1, source_target_pairs={{0,2},{1,3},{2,4},{3,5},{4,6},{5,7},{6,0},{7,1},{8,10},{9,11},{10,... | collective-permute-start | bytes 1622024 | tf_op jit(solution)/shard_map/ppermute | solution.py:414
  26.4 18.8 %copy-start.4 = (bf16[528,512]{1,0:T(8,128)(2,1)}, bf16[528,512]{1,0:T(8,128)(2,1)S(1)}, u32[]{:S(2)}) copy-start(bf16[528,512]{1,0:T(8,128)(2,1)S(1)} %collective-permute-done.1.refs_4_) | copy-start | bytes 1622020
  29.4 15.8 %copy-start.5 = (bf16[528,512]{1,0:T(8,128)(2,1)}, bf16[528,512]{1,0:T(8,128)(2,1)S(1)}, u32[]{:S(2)}) copy-start(bf16[528,512]{1,0:T(8,128)(2,1)S(1)} %collective-permute-done.refs_1_) | copy-start | bytes 1622020
  29.5 6.1 %collective-permute-start.3 = (bf16[272,512]{1,0:T(8,128)(2,1)S(1)}, bf16[272,512]{1,0:T(8,128)(2,1)S(1)}, u32[]{:S(2)}, u32[]{:S(2)}) collective-permute-start(bf16[272,512]{1,0:T(8,128)(2,1)S(1)} %slice.19), channel_id=1, source_target_pairs={{0,6},{1,7},{2,0},{3,1},{4,2},{5,3},{6,4},{7,5},{8,14},{9,15},{10,... | collective-permute-start | bytes 835592 | tf_op jit(solution)/shard_map/ppermute | solution.py:414
  29.8 12.7 %collective-permute-start.4 = (bf16[528,512]{1,0:T(8,128)(2,1)}, bf16[528,512]{1,0:T(8,128)(2,1)S(1)}, u32[]{:S(2)}, u32[]{:S(2)}) collective-permute-start(bf16[528,512]{1,0:T(8,128)(2,1)} %get-tuple-element.70.refs_0_), channel_id=1, source_target_pairs={{0,1},{1,0},{2,3},{3,2},{4,5},{5,4},{6,7},{7,6},{8,9},{9,8},{10,11... | collective-permute-start | bytes 1622024 | tf_op jit(solution)/shard_map/ppermute | solution.py:418
  32.0 11.7 %collective-permute-start.5 = (bf16[528,512]{1,0:T(8,128)(2,1)S(1)}, bf16[528,512]{1,0:T(8,128)(2,1)S(1)}, u32[]{:S(2)}, u32[]{:S(2)}) collective-permute-start(bf16[528,512]{1,0:T(8,128)(2,1)S(1)} %collective-permute-done.refs_1_), channel_id=1, source_target_pairs={{0,1},{1,0},{2,3},{3,2},{4,5},{5,4},{6,7},{7,6},{8,9},{9,8},{10,11... | collective-permute-start | bytes 1622024 | tf_op jit(solution)/shard_map/ppermute | solution.py:418
  32.0 11.7 %collective-permute-start.8 = (bf16[528,512]{1,0:T(8,128)(2,1)S(1)}, bf16[528,512]{1,0:T(8,128)(2,1)S(1)}, u32[]{:S(2)}, u32[]{:S(2)}) collective-permute-start(bf16[528,512]{1,0:T(8,128)(2,1)S(1)} %collective-permute-done.1.refs_4_), channel_id=1, source_target_pairs={{0,1},{1,0},{2,3},{3,2},{4,5},{5,4},{6,7},{7,6},{8,9},{9,8},{10,11... | collective-permute-start | bytes 1622024 | tf_op jit(solution)/shard_map/ppermute | solution.py:418
  32.5 9.2 %collective-permute-start.2 = (bf16[256,512]{1,0:T(8,128)(2,1)S(1)}, bf16[256,512]{1,0:T(8,128)(2,1)S(1)}, u32[]{:S(2)}, u32[]{:S(2)}) collective-permute-start(bf16[256,512]{1,0:T(8,128)(2,1)S(1)} %slice.18), channel_id=1, source_target_pairs={{0,2},{1,3},{2,4},{3,5},{4,6},{5,7},{6,0},{7,1},{8,10},{9,11},{10,... | collective-permute-start | bytes 786440 | tf_op jit(solution)/shard_map/ppermute | solution.py:414
  35.5 9.7 %copy-start.13 = (bf16[272,512]{1,0:T(8,128)(2,1)}, bf16[272,512]{1,0:T(8,128)(2,1)S(1)}, u32[]{:S(2)}) copy-start(bf16[272,512]{1,0:T(8,128)(2,1)S(1)} %collective-permute-done.3.refs_3_) | copy-start | bytes 835588
  35.5 8.2 %collective-permute-start.7 = (bf16[272,512]{1,0:T(8,128)(2,1)S(1)}, bf16[272,512]{1,0:T(8,128)(2,1)S(1)}, u32[]{:S(2)}, u32[]{:S(2)}) collective-permute-start(bf16[272,512]{1,0:T(8,128)(2,1)S(1)} %collective-permute-done.3.refs_3_), channel_id=1, source_target_pairs={{0,1},{1,0},{2,3},{3,2},{4,5},{5,4},{6,7},{7,6},{8,9},{9,8},{10,11... | collective-permute-start | bytes 835592 | tf_op jit(solution)/shard_map/ppermute | solution.py:418
  41.7 2.8 %copy-start.17 = (bf16[256,512]{1,0:T(8,128)(2,1)}, bf16[256,512]{1,0:T(8,128)(2,1)S(1)}, u32[]{:S(2)}) copy-start(bf16[256,512]{1,0:T(8,128)(2,1)S(1)} %collective-permute-done.2.refs_2_) | copy-start | bytes 786436
  41.7 1.9 %collective-permute-start.6 = (bf16[256,512]{1,0:T(8,128)(2,1)S(1)}, bf16[256,512]{1,0:T(8,128)(2,1)S(1)}, u32[]{:S(2)}, u32[]{:S(2)}) collective-permute-start(bf16[256,512]{1,0:T(8,128)(2,1)S(1)} %collective-permute-done.2.refs_2_), channel_id=1, source_target_pairs={{0,1},{1,0},{2,3},{3,2},{4,5},{5,4},{6,7},{7,6},{8,9},{9,8},{10,11... | collective-permute-start | bytes 786440 | tf_op jit(solution)/shard_map/ppermute | solution.py:418
  42.5 1.2 copy-start.10
  43.7 0.9 copy-start.19
  43.7 0.8 copy-start.11
  43.7 1.0 copy-start.12
  51.0 1.3 copy-start.1
  52.3 36.8 %all-to-all-start.1 = ((bf16[16,128,512]{2,1,0:T(8,128)(2,1)}), bf16[16,128,512]{2,1,0:T(8,128)(2,1)}, u32[]{:S(2)}, u32[]{:S(2)}) async-start(bf16[16,128,512]{2,1,0:T(8,128)(2,1)} %get-tuple-element.102), calls=%async_computation.1 | async-start | bytes 4194304 | tf_op jit(solution)/shard_map/all_to_all | solution.py:422
  63.3 2.0 %collective-permute-start.9 = (bf16[16,64,128]{2,1,0:T(8,128)(2,1)}, bf16[16,64,128]{2,1,0:T(8,128)(2,1)S(1)}, u32[]{:S(2)}, u32[]{:S(2)}) collective-permute-start(bf16[16,64,128]{2,1,0:T(8,128)(2,1)} %get-tuple-element.91), channel_id=1, source_target_pairs={{0,1},{1,0},{2,3},{3,2},{4,5},{5,4},{6,7},{7,6},{8,9},{9,8},{10,11... | collective-permute-start | bytes 786440 | tf_op jit(solution)/shard_map/ppermute | solution.py:418
  65.3 0.7 copy-start.20
  89.1 17.3 %all-to-all-start.2 = ((bf16[16,128,128]{2,1,0:T(8,128)(2,1)}), bf16[16,128,128]{2,1,0:T(8,128)(2,1)S(1)}, u32[]{:S(2)}, u32[]{:S(2)}) async-start(bf16[16,128,128]{2,1,0:T(8,128)(2,1)} %get-tuple-element.103), calls=%async_computation.2 | async-start | bytes 1048576 | tf_op jit(solution)/shard_map/all_to_all | solution.py:422
  96.0 3.2 %copy-start.18 = (bf16[2,256,256]{2,1,0:T(8,128)(2,1)S(1)}, bf16[2,256,256]{2,1,0:T(8,128)(2,1)}, u32[]{:S(2)}) copy-start(bf16[2,256,256]{2,1,0:T(8,128)(2,1)} %get-tuple-element.111) | copy-start | bytes 786436
  96.0 3.2 %copy-start.16 = (bf16[2,256,256]{2,1,0:T(8,128)(2,1)S(1)}, bf16[2,256,256]{2,1,0:T(8,128)(2,1)}, u32[]{:S(2)}) copy-start(bf16[2,256,256]{2,1,0:T(8,128)(2,1)} %get-tuple-element.112) | copy-start | bytes 786436
  96.0 5.2 %copy-start.15 = (bf16[2,256,256]{2,1,0:T(8,128)(2,1)S(1)}, bf16[2,256,256]{2,1,0:T(8,128)(2,1)}, u32[]{:S(2)}) copy-start(bf16[2,256,256]{2,1,0:T(8,128)(2,1)} %get-tuple-element.113) | copy-start | bytes 786436
  99.2 11.8 %collective-permute-start.14 = (bf16[2,256,256]{2,1,0:T(8,128)(2,1)S(1)}, bf16[2,256,256]{2,1,0:T(8,128)(2,1)S(1)}, u32[]{:S(2)}, u32[]{:S(2)}) collective-permute-start(bf16[2,256,256]{2,1,0:T(8,128)(2,1)S(1)} %copy-done.18), channel_id=1, source_target_pairs={{0,6},{1,7},{2,0},{3,1},{4,2},{5,3},{6,4},{7,5},{8,14},{9,15},{10,... | collective-permute-start | bytes 786440 | tf_op jit(solution)/shard_map/ppermute | solution.py:414
  99.2 11.8 %collective-permute-start.15 = (bf16[2,256,256]{2,1,0:T(8,128)(2,1)S(1)}, bf16[2,256,256]{2,1,0:T(8,128)(2,1)S(1)}, u32[]{:S(2)}, u32[]{:S(2)}) collective-permute-start(bf16[2,256,256]{2,1,0:T(8,128)(2,1)S(1)} %copy-done.16), channel_id=1, source_target_pairs={{0,4},{1,5},{2,6},{3,7},{4,0},{5,1},{6,2},{7,3},{8,12},{9,13},{10,... | collective-permute-start | bytes 786440 | tf_op jit(solution)/shard_map/ppermute | solution.py:414
  101.2 13.8 %collective-permute-start.16 = (bf16[2,256,256]{2,1,0:T(8,128)(2,1)S(1)}, bf16[2,256,256]{2,1,0:T(8,128)(2,1)S(1)}, u32[]{:S(2)}, u32[]{:S(2)}) collective-permute-start(bf16[2,256,256]{2,1,0:T(8,128)(2,1)S(1)} %copy-done.15), channel_id=1, source_target_pairs={{0,2},{1,3},{2,4},{3,5},{4,6},{5,7},{6,0},{7,1},{8,10},{9,11},{10,... | collective-permute-start | bytes 786440 | tf_op jit(solution)/shard_map/ppermute | solution.py:414
  101.2 2.3 %collective-permute-start.10 = (f32[8,128]{1,0:T(8,128)}, f32[8,128]{1,0:T(8,128)S(1)}, u32[]{:S(2)}, u32[]{:S(2)}) collective-permute-start(f32[8,128]{1,0:T(8,128)} %get-tuple-element.110.g0_ref), channel_id=1, source_target_pairs={{0,1},{1,0},{2,3},{3,2},{4,5},{5,4},{6,7},{7,6},{8,9},{9,8},{10,11... | collective-permute-start | bytes 12296 | tf_op jit(solution)/shard_map/ppermute | solution.py:418
  103.5 2.8 %copy-start.28 = (f32[8,128]{1,0:T(8,128)}, f32[8,128]{1,0:T(8,128)S(1)}, u32[]{:S(2)}) copy-start(f32[8,128]{1,0:T(8,128)S(1)} %collective-permute-done.10.g1_ref) | copy-start | bytes 12292
  106.3 0.8 copy-start.3
  109.0 6.1 %collective-permute-start.13 = (bf16[144,128]{1,0:T(8,128)(2,1)}, bf16[144,128]{1,0:T(8,128)(2,1)S(1)}, u32[]{:S(2)}, u32[]{:S(2)}) collective-permute-start(bf16[144,128]{1,0:T(8,128)(2,1)} %shard_map.171.c0_ref), channel_id=1, source_target_pairs={{0,6},{1,7},{2,0},{3,1},{4,2},{5,3},{6,4},{7,5},{8,14},{9,15},{10,... | collective-permute-start | bytes 110600 | tf_op jit(solution)/shard_map/ppermute | solution.py:414
  109.7 5.4 %collective-permute-start.12 = (bf16[144,128]{1,0:T(8,128)(2,1)}, bf16[144,128]{1,0:T(8,128)(2,1)S(1)}, u32[]{:S(2)}, u32[]{:S(2)}) collective-permute-start(bf16[144,128]{1,0:T(8,128)(2,1)} %shard_map.171.c0_ref), channel_id=1, source_target_pairs={{0,4},{1,5},{2,6},{3,7},{4,0},{5,1},{6,2},{7,3},{8,12},{9,13},{10,... | collective-permute-start | bytes 110600 | tf_op jit(solution)/shard_map/ppermute | solution.py:414
  111.0 14.2 %copy-start.7 = (bf16[2,256,256]{2,1,0:T(8,128)(2,1)}, bf16[2,256,256]{2,1,0:T(8,128)(2,1)S(1)}, u32[]{:S(2)}) copy-start(bf16[2,256,256]{2,1,0:T(8,128)(2,1)S(1)} %collective-permute-done.14.r1_ref) | copy-start | bytes 786436
  111.0 4.3 %collective-permute-start.11 = (bf16[144,128]{1,0:T(8,128)(2,1)}, bf16[144,128]{1,0:T(8,128)(2,1)S(1)}, u32[]{:S(2)}, u32[]{:S(2)}) collective-permute-start(bf16[144,128]{1,0:T(8,128)(2,1)} %shard_map.171.c0_ref), channel_id=1, source_target_pairs={{0,2},{1,3},{2,4},{3,5},{4,6},{5,7},{6,0},{7,1},{8,10},{9,11},{10,... | collective-permute-start | bytes 110600 | tf_op jit(solution)/shard_map/ppermute | solution.py:414
  111.0 14.2 %copy-start.8 = (bf16[2,256,256]{2,1,0:T(8,128)(2,1)}, bf16[2,256,256]{2,1,0:T(8,128)(2,1)S(1)}, u32[]{:S(2)}) copy-start(bf16[2,256,256]{2,1,0:T(8,128)(2,1)S(1)} %collective-permute-done.15.r2_ref) | copy-start | bytes 786436
  115.0 10.2 %copy-start.9 = (bf16[2,256,256]{2,1,0:T(8,128)(2,1)}, bf16[2,256,256]{2,1,0:T(8,128)(2,1)S(1)}, u32[]{:S(2)}) copy-start(bf16[2,256,256]{2,1,0:T(8,128)(2,1)S(1)} %collective-permute-done.16.r3_ref) | copy-start | bytes 786436
  118.4 6.7 %copy-start.6 = (bf16[2,256,256]{2,1,0:T(8,128)(2,1)S(1)}, bf16[2,256,256]{2,1,0:T(8,128)(2,1)}, u32[]{:S(2)}) copy-start(bf16[2,256,256]{2,1,0:T(8,128)(2,1)} %get-tuple-element.123.r0_ref) | copy-start | bytes 786436
  118.4 25.2 %all-to-all-start.3 = ((bf16[16,336,128]{2,1,0:T(8,128)(2,1)}), bf16[16,336,128]{2,1,0:T(8,128)(2,1)S(1)}, u32[]{:S(2)}, u32[]{:S(2)}) async-start(bf16[16,336,128]{2,1,0:T(8,128)(2,1)} %shard_map.172), calls=%async_computation.3 | async-start | bytes 2752512 | tf_op jit(solution)/shard_map/all_to_all | solution.py:422
  125.2 2.7 %collective-permute-start.20 = (bf16[256,256]{1,0:T(8,128)(2,1)S(1)}, bf16[256,256]{1,0:T(8,128)(2,1)S(1)}, u32[]{:S(2)}, u32[]{:S(2)}) collective-permute-start(bf16[256,256]{1,0:T(8,128)(2,1)S(1)} %slice_bitcast_fusion), channel_id=1, source_target_pairs={{0,1},{1,0},{2,3},{3,2},{4,5},{5,4},{6,7},{7,6},{8,9},{9,8},{10,11... | collective-permute-start | bytes 393224 | tf_op jit(solution)/shard_map/ppermute | solution.py:418
  127.0 1.3 collective-permute-start.19
  127.1 1.4 collective-permute-start.18
  127.5 1.3 collective-permute-start.17
  128.0 0.9 copy-start.21
  143.7 6.6 %copy-start = (bf16[16,336,128]{2,1,0:T(8,128)(2,1)}, bf16[16,336,128]{2,1,0:T(8,128)(2,1)S(1)}, u32[]{:S(2)}) copy-start(bf16[16,336,128]{2,1,0:T(8,128)(2,1)S(1)} %all-to-all-done.3.mine_ref) | copy-start | bytes 4128772
  143.7 6.6 %collective-permute-start.21 = (bf16[16,336,128]{2,1,0:T(8,128)(2,1)S(1)}, bf16[16,336,128]{2,1,0:T(8,128)(2,1)S(1)}, u32[]{:S(2)}, u32[]{:S(2)}) collective-permute-start(bf16[16,336,128]{2,1,0:T(8,128)(2,1)S(1)} %all-to-all-done.3.mine_ref), channel_id=1, source_target_pairs={{0,1},{1,0},{2,3},{3,2},{4,5},{5,4},{6,7},{7,6},{8,9},{9,8},{10,11... | collective-permute-start | bytes 4128776 | tf_op jit(solution)/shard_map/ppermute | solution.py:418
  150.3 1.1 copy-start.2
  (7 other events, 4.6 us)

commit v8 on v6

--- a/solution.py
+++ b/solution.py
@@ -32,9 +32,11 @@
     return lax.dot_general(a, b, dims, preferred_element_type=F32)
 
 
-def call(body, out_shape, operands, scratch=(), scalars=0, micros=2):
+def call(body, out_shape, operands, scratch=(), scalars=0, micros=2, left=()):
     specs = [pl.BlockSpec(memory_space=pltpu.SMEM)] * scalars
     specs += [pl.BlockSpec(memory_space=pltpu.VMEM)] * (len(operands) - scalars)
+    for at in left:
+        specs[at] = pl.BlockSpec(memory_space=pltpu.HBM)
     return pl.pallas_call(
         body,
         out_shape=out_shape,
@@ -444,7 +446,7 @@
     near, far, degree = lax.optimization_barrier((near, far, degree))
     pays = [pay, near, along_chips(near[0:ROWS], 1), along_chips(far[ROWS:PAY], 3), far]
     pays = pays + [other_core(part) for part in pays]
-    incoming, slot_grads = lax.optimization_barrier((incoming, slot_grads))
+    slot_grads = lax.optimization_barrier((incoming, slot_grads))[1]
     back = to_dom_peers(slot_grads)
 
     base, mine, other = call(
@@ -478,7 +480,7 @@
         ],
         micros=12,
     )
-    chunks, back = lax.optimization_barrier((chunks, back))
+    chunks = lax.optimization_barrier((chunks, back))[0]
     chunks = to_dom_peers(chunks)
     halo, gain_part = call(
         halo_body,
@@ -502,6 +504,8 @@
     gathered = to_dom_peers(spread)
     results = [results[0]] + [along_chips(results[dz], -dz) for dz in (1, 2, 3)]
     swapped = [other_core(part[1]) for part in results]
+    gathered, *swapped = lax.optimization_barrier((gathered, *swapped))
+    gathered_other = other_core(gathered)
     layer_out, feature_grad = call(
         rows_body,
         (shape((ROWS, D), BF16), shape((ROWS, D), BF16)),
@@ -509,7 +513,9 @@
         scratch=[pltpu.VMEM((4, ROWS, 128), BF16)] * 4,
         micros=2,
     )
-    gathered, layer_out, feature_grad = lax.optimization_barrier((gathered, layer_out, feature_grad))
+    gathered, gathered_other, layer_out, feature_grad = lax.optimization_barrier(
+        (gathered, gathered_other, layer_out, feature_grad)
+    )
     whole = pl.BlockSpec((DOM, SPREAD, 128), lambda t: (0, 0, 0))
     row = pl.BlockSpec((1, D), lambda t: (0, 0))
     weight_grads, gain_grad = pl.pallas_call(
@@ -519,7 +525,7 @@
         in_specs=[whole, whole, row],
         out_specs=(pl.BlockSpec((1, D, D), lambda t: (t, 0, 0)), row),
         scratch_shapes=[pltpu.VMEM((2, DOM, SPREAD, 128), BF16)],
-    )(gathered, other_core(gathered), gain_row)
+    )(gathered, gathered_other, gain_row)
     return layer_out, feature_grad, weight_grads, gain_grad.reshape(D)
 
 

time: 148 us -> 148 us (level)
  waiting for transfers between devices: 31.9 us -> 28.2 us
  starting transfers between devices: 50.9 us -> 53.8 us
    ppermute x12, waiting for transfers between devices: 6.48 us -> 2.78 us  [other_core(): return lax.ppermute(array, 'blk', chip_shift(0, 1))]
    ppermute x12, starting transfers between devices: 16.1 us -> 18.9 us  [other_core(): return lax.ppermute(array, 'blk', chip_shift(0, 1))]
  transfers between devices with their start and end apart: 26 -> 26, of which waited for: 11 -> 9; matrix products, arithmetic and copies ran while one was open for 1% -> 1% of each run, Pallas kernels for 30% -> 30%
where the time goes in v8:
time: 148 us; the launch traced here: 147 us
  Pallas kernels  57 us (39%)
  starting transfers between devices  53.8 us (36%)
  waiting for transfers between devices  28.2 us (19%)
  local copies, waits for them, and re-layouts  7.63 us (5%)
    pallas_call x8, Pallas kernels, call(): pl.pallas_call(body, out_shape=out_shape, in_specs=specs, out_specs=jax.t...  51.6 us
    all_to_all x4, starting transfers between devices, to_dom_peers(): return lax.all_to_all(array, 'dom', split_axis=0, concat_axis=0, tiled=True)  22.6 us
    ppermute x12, starting transfers between devices, other_core(): return lax.ppermute(array, 'blk', chip_shift(0, 1))  18.9 us
    ppermute x10, waiting for transfers between devices, along_chips(): return lax.ppermute(array, 'blk', chip_shift(step, 0))  13.2 us
    all_to_all x4, waiting for transfers between devices, to_dom_peers(): return lax.all_to_all(array, 'dom', split_axis=0, concat_axis=0, tiled=True)  12.2 us
    ppermute x10, starting transfers between devices, along_chips(): return lax.ppermute(array, 'blk', chip_shift(step, 0))  12.2 us
    unnamed x50, local copies, waits for them, and re-layouts  6.61 us
    pallas_call x1, Pallas kernels, local(): pl.pallas_call(weights_body, grid=(5,), out_shape=(shape((5, D, D), F32),...  5.37 us
  transfers between devices with their start and end apart: 26, of which 9 were waited for; matrix products, arithmetic and copies ran while one was open for 1% of the time, Pallas kernels for 30%

profile of v8, /device:TPU:1, one launch (start us, length us, event | category | flops | bytes accessed | tf_op | source)
XLA Modules:
  0.0 147.4 jit_solution(5844727504753691279)
XLA Ops:
  0.6 3.4 %shard_map.165 = (bf16[528,512]{1,0:T(8,128)(2,1)}, bf16[16,128,512]{2,1,0:T(8,128)(2,1)}) custom-call(s32[1,8]{1,0:T(1,128)} %pattern_ref.1, s32[16]{0:T(128)} %counts_ref.3, bf16[256,512]{1,0:T(8,128)(2,1)} %x_ref.7, f32[1,512]{1,0:T(1,128)} %bitcast.13, s32[1,256]{1,0:T(1,128)} %bitcast.19, bf16[256,512]{1,0:T(8,128)(2,1)} %grad_ref.7, s32[16,128]{1,0:T(8,128)} %rows_ref.3), custom_call_target="tpu_custom_call" | custom-call | flops 4000000000 | bytes 1048576 | tf_op jit(solution)/shard_map/pallas_call | solution.py:40
  4.1 7.6 %all-to-all-start = ((bf16[16,128,512]{2,1,0:T(8,128)(2,1)}), bf16[16,128,512]{2,1,0:T(8,128)(2,1)S(1)}, u32[]{:S(2)}, u32[]{:S(2)}) async-start(bf16[16,128,512]{2,1,0:T(8,128)(2,1)} %get-tuple-element.52), calls=%async_computation | async-start | bytes 4194304 | tf_op jit(solution)/shard_map/all_to_all | solution.py:419
  11.7 3.8 %collective-permute-start.1 = (bf16[528,512]{1,0:T(8,128)(2,1)}, bf16[528,512]{1,0:T(8,128)(2,1)S(1)}, u32[]{:S(2)}, u32[]{:S(2)}) collective-permute-start(bf16[528,512]{1,0:T(8,128)(2,1)} %get-tuple-element.44.p0_ref), channel_id=1, source_target_pairs={{0,6},{1,7},{2,0},{3,1},{4,2},{5,3},{6,4},{7,5},{8,14},{9,15},{10,... | collective-permute-start | bytes 1622024 | tf_op jit(solution)/shard_map/ppermute | solution.py:411
  15.5 9.0 %shard_map.166 = (bf16[1024,512]{1,0:T(8,128)(2,1)}, f32[256,128]{1,0:T(8,128)}, bf16[16,128,512]{2,1,0:T(8,128)(2,1)}, bf16[192,512]{1,0:T(8,128)(2,1)}, bf16[64,512]{1,0:T(8,128)(2,1)}) custom-call(s32[32,128]{1,0:T(8,128)} %bitcast.16, s32[32,128]{1,0:T(8,128)} %bitcast.17, bf16[256,512]{1,0:T(8,128)(2,1)} %grad_ref.7, bf16[512,512]{1,0:T(8,128)(2,1)} %w_ref.3, ...), custom_call_target="tpu_custom_call" | custom-call | flops 10000000000 | bytes 1048576 | tf_op jit(solution)/shard_map/pallas_call | solution.py:40
  24.5 1.9 %collective-permute-done.1.p3_ref = bf16[528,512]{1,0:T(8,128)(2,1)S(1)} collective-permute-done((bf16[528,512]{1,0:T(8,128)(2,1)}, bf16[528,512]{1,0:T(8,128)(2,1)S(1)}, u32[]{:S(2)}, u32[]{:S(2)}) %collective-permute-start.1) | collective-permute-done | bytes 540704 | tf_op jit(solution)/shard_map/ppermute | solution.py:411
  26.4 3.0 %collective-permute-done.p1_ref = bf16[528,512]{1,0:T(8,128)(2,1)S(1)} collective-permute-done((bf16[528,512]{1,0:T(8,128)(2,1)}, bf16[528,512]{1,0:T(8,128)(2,1)S(1)}, u32[]{:S(2)}, u32[]{:S(2)}) %collective-permute-start) | collective-permute-done | bytes 540704 | tf_op jit(solution)/shard_map/ppermute | solution.py:411
  29.4 0.8 copy-done.6
  30.3 0.4 collective-permute-start.3
  30.7 1.0 slice.18
  31.7 1.2 collective-permute-start.2
  32.9 6.6 %all-to-all-done.table_ref = bf16[16,128,512]{2,1,0:T(8,128)(2,1)S(1)} async-done(((bf16[16,128,512]{2,1,0:T(8,128)(2,1)}), bf16[16,128,512]{2,1,0:T(8,128)(2,1)S(1)}, u32[]{:S(2)}, u32[]{:S(2)}) %all-to-all-start) | async-done | bytes 2097184 | tf_op jit(solution)/shard_map/all_to_all | solution.py:419
  39.5 1.3 copy-done.2
  40.8 3.9 %all-to-all-start.1 = ((bf16[16,128,512]{2,1,0:T(8,128)(2,1)}), bf16[16,128,512]{2,1,0:T(8,128)(2,1)S(1)}, u32[]{:S(2)}, u32[]{:S(2)}) async-start(bf16[16,128,512]{2,1,0:T(8,128)(2,1)} %get-tuple-element.57), calls=%async_computation.1 | async-start | bytes 4194304 | tf_op jit(solution)/shard_map/all_to_all | solution.py:419
  44.8 3.3 %collective-permute-start.4 = (bf16[528,512]{1,0:T(8,128)(2,1)}, bf16[528,512]{1,0:T(8,128)(2,1)}, u32[]{:S(2)}, u32[]{:S(2)}) collective-permute-start(bf16[528,512]{1,0:T(8,128)(2,1)} %get-tuple-element.44.p0_ref), channel_id=1, source_target_pairs={{0,1},{1,0},{2,3},{3,2},{4,5},{5,4},{6,7},{7,6},{8,9},{9,8},{10,11... | collective-permute-start | bytes 1622024 | tf_op jit(solution)/shard_map/ppermute | solution.py:415
  48.2 0.4 collective-permute-start.8
  48.7 0.4 collective-permute-start.7
  49.2 4.3 %shard_map.167 = (f32[256,512]{1,0:T(8,128)}, bf16[16,64,128]{2,1,0:T(8,128)(2,1)}, bf16[16,64,128]{2,1,0:T(8,128)(2,1)}) custom-call(bf16[1024,512]{1,0:T(8,128)(2,1)} %get-tuple-element.50.counts_t_ref, f32[256,128]{1,0:T(8,128)} %get-tuple-element.51.degree_ref, bf16[16,128,512]{2,1,0:T(8,128)(2,1)} %copy-done.2, bf16[256,512]{1,0:T(8,128)(2,1)} %x_ref.7, ...), custom_call_target="tpu_custom_call" | custom-call | flops 4000000000 | bytes 1048576 | tf_op jit(solution)/shard_map/pallas_call | solution.py:40
  53.5 0.4 collective-permute-start.9
  53.9 1.7 %collective-permute-done.9.other_ref = bf16[16,64,128]{2,1,0:T(8,128)(2,1)} collective-permute-done((bf16[16,64,128]{2,1,0:T(8,128)(2,1)}, bf16[16,64,128]{2,1,0:T(8,128)(2,1)}, u32[]{:S(2)}, u32[]{:S(2)}) %collective-permute-start.9) | collective-permute-done | bytes 262176 | tf_op jit(solution)/shard_map/ppermute | solution.py:415
  55.6 23.3 %shard_map.168 = (bf16[2,256,256]{2,1,0:T(8,128)(2,1)}, bf16[2,256,256]{2,1,0:T(8,128)(2,1)}, bf16[2,256,256]{2,1,0:T(8,128)(2,1)}, bf16[2,256,256]{2,1,0:T(8,128)(2,1)}, bf16[16,128,128]{2,1,0:T(8,128)(2,1)}) custom-call(bf16[528,512]{1,0:T(8,128)(2,1)} %get-tuple-element.44.p0_ref, bf16[528,512]{1,0:T(8,128)(2,1)} %copy-done.6, ...), custom_call_target="tpu_custom_call" | custom-call | flops 12000000000 | bytes 1048576 | tf_op jit(solution)/shard_map/pallas_call | solution.py:40
  79.0 6.8 %all-to-all-start.2 = ((bf16[16,128,128]{2,1,0:T(8,128)(2,1)}), bf16[16,128,128]{2,1,0:T(8,128)(2,1)S(1)}, u32[]{:S(2)}, u32[]{:S(2)}) async-start(bf16[16,128,128]{2,1,0:T(8,128)(2,1)} %get-tuple-element.58), calls=%async_computation.2 | async-start | bytes 1048576 | tf_op jit(solution)/shard_map/all_to_all | solution.py:419
  85.8 3.1 %shard_map.169 = (f32[256,512]{1,0:T(8,128)}, f32[8,128]{1,0:T(8,128)}) custom-call(s32[16]{0:T(128)} %counts_ref.3, bf16[16,128,512]{2,1,0:T(8,128)(2,1)} %copy-done.1, s32[16,128]{1,0:T(8,128)} %rows_ref.3, bf16[256,512]{1,0:T(8,128)(2,1)} %x_ref.7), custom_call_target="tpu_custom_call" | custom-call | flops 3000000000 | bytes 1048576 | tf_op jit(solution)/shard_map/pallas_call | solution.py:40
  89.0 0.4 collective-permute-start.10
  89.4 1.0 collective-permute-done.10.g1_ref
  90.4 5.5 %all-to-all-done.2.in_ref = bf16[16,128,128]{2,1,0:T(8,128)(2,1)S(1)} async-done(((bf16[16,128,128]{2,1,0:T(8,128)(2,1)}), bf16[16,128,128]{2,1,0:T(8,128)(2,1)S(1)}, u32[]{:S(2)}, u32[]{:S(2)}) %all-to-all-start.2) | async-done | bytes 524320 | tf_op jit(solution)/shard_map/all_to_all | solution.py:419
  96.0 0.8 copy-done.4
  96.8 1.8 %shard_map.170.c0_ref = bf16[144,128]{1,0:T(8,128)(2,1)} custom-call(bf16[16,128,128]{2,1,0:T(8,128)(2,1)} %copy-done.4, f32[8,128]{1,0:T(8,128)} %get-tuple-element.59.g0_ref, f32[8,128]{1,0:T(8,128)} %copy-done.24, bf16[192,512]{1,0:T(8,128)(2,1)} %get-tuple-element.48.wqkv_ref), custom_call_target="tpu_custom_call" | custom-call | flops 1000000000 | bytes 1048576 | tf_op jit(solution)/shard_map/pallas_call | solution.py:40
  98.6 3.8 %collective-permute-start.13 = (bf16[144,128]{1,0:T(8,128)(2,1)}, bf16[144,128]{1,0:T(8,128)(2,1)S(1)}, u32[]{:S(2)}, u32[]{:S(2)}) collective-permute-start(bf16[144,128]{1,0:T(8,128)(2,1)} %shard_map.170.c0_ref), channel_id=1, source_target_pairs={{0,6},{1,7},{2,0},{3,1},{4,2},{5,3},{6,4},{7,5},{8,14},{9,15},{10,... | collective-permute-start | bytes 110600 | tf_op jit(solution)/shard_map/ppermute | solution.py:411
  102.4 0.7 collective-permute-start.11
  103.1 0.7 collective-permute-done.13.c3_ref
  103.7 3.2 %collective-permute-done.12.c2_ref = bf16[144,128]{1,0:T(8,128)(2,1)S(1)} collective-permute-done((bf16[144,128]{1,0:T(8,128)(2,1)}, bf16[144,128]{1,0:T(8,128)(2,1)S(1)}, u32[]{:S(2)}, u32[]{:S(2)}) %collective-permute-start.12) | collective-permute-done | bytes 36896 | tf_op jit(solution)/shard_map/ppermute | solution.py:411
  107.0 0.6 copy-done.22
  107.6 0.6 copy-done.23
  108.2 2.1 %shard_map.171 = bf16[16,336,128]{2,1,0:T(8,128)(2,1)} custom-call(bf16[144,128]{1,0:T(8,128)(2,1)} %shard_map.170.c0_ref, bf16[144,128]{1,0:T(8,128)(2,1)} %copy-done.23, bf16[144,128]{1,0:T(8,128)(2,1)} %copy-done.22, bf16[144,128]{1,0:T(8,128)(2,1)} %copy-done.21), custom_call_target="tpu_custom_call" | custom-call | flops 1000000000 | bytes 1048576 | tf_op jit(solution)/shard_map/pallas_call | solution.py:40
  110.3 4.3 %all-to-all-start.3 = ((bf16[16,336,128]{2,1,0:T(8,128)(2,1)}), bf16[16,336,128]{2,1,0:T(8,128)(2,1)S(1)}, u32[]{:S(2)}, u32[]{:S(2)}) async-start(bf16[16,336,128]{2,1,0:T(8,128)(2,1)} %shard_map.171), calls=%async_computation.3 | async-start | bytes 2752512 | tf_op jit(solution)/shard_map/all_to_all | solution.py:419
  114.7 1.1 collective-permute-start.17
  115.9 3.6 %collective-permute-start.14 = (bf16[256,256]{1,0:T(8,128)(2,1)S(1)}, bf16[256,256]{1,0:T(8,128)(2,1)S(1)}, u32[]{:S(2)}, u32[]{:S(2)}) collective-permute-start(bf16[256,256]{1,0:T(8,128)(2,1)S(1)} %slice_bitcast_fusion.3), channel_id=1, source_target_pairs={{0,1},{1,0},{2,3},{3,2},{4,5},{5,4},{6,7},{7,6},{8,9},{9,8},{10,11... | collective-permute-start | bytes 393224 | tf_op jit(solution)/shard_map/ppermute | solution.py:415
  119.4 1.1 collective-permute-start.19
  120.5 5.8 %collective-permute-start.16 = (bf16[256,256]{1,0:T(8,128)(2,1)S(1)}, bf16[256,256]{1,0:T(8,128)(2,1)S(1)}, u32[]{:S(2)}, u32[]{:S(2)}) collective-permute-start(bf16[256,256]{1,0:T(8,128)(2,1)S(1)} %slice_bitcast_fusion.2), channel_id=1, source_target_pairs={{0,1},{1,0},{2,3},{3,2},{4,5},{5,4},{6,7},{7,6},{8,9},{9,8},{10,11... | collective-permute-start | bytes 393224 | tf_op jit(solution)/shard_map/ppermute | solution.py:415
  126.4 0.6 collective-permute-start.18
  127.0 4.3 %collective-permute-done.19.r3_ref = bf16[2,256,256]{2,1,0:T(8,128)(2,1)S(1)} collective-permute-done((bf16[2,256,256]{2,1,0:T(8,128)(2,1)S(1)}, bf16[2,256,256]{2,1,0:T(8,128)(2,1)S(1)}, u32[]{:S(2)}, u32[]{:S(2)}) %collective-permute-start.19) | collective-permute-done | bytes 262176 | tf_op jit(solution)/shard_map/ppermute | solution.py:411
  131.3 0.5 collective-permute-start.20
  132.0 0.5 copy-done.17
  132.5 0.6 copy-done.19
  133.2 3.3 %collective-permute-start.21 = (bf16[16,336,128]{2,1,0:T(8,128)(2,1)S(1)}, bf16[16,336,128]{2,1,0:T(8,128)(2,1)S(1)}, u32[]{:S(2)}, u32[]{:S(2)}) collective-permute-start(bf16[16,336,128]{2,1,0:T(8,128)(2,1)S(1)} %all-to-all-done.3.mine_ref), channel_id=1, source_target_pairs={{0,1},{1,0},{2,3},{3,2},{4,5},{5,4},{6,7},{7,6},{8,9},{9,8},{10,11... | collective-permute-start | bytes 4128776 | tf_op jit(solution)/shard_map/ppermute | solution.py:415
  136.5 4.5 %shard_map.172 = (bf16[256,512]{1,0:T(8,128)(2,1)}, bf16[256,512]{1,0:T(8,128)(2,1)}) custom-call(bf16[2,256,256]{2,1,0:T(8,128)(2,1)} %get-tuple-element.65.r0_ref, bf16[2,256,256]{2,1,0:T(8,128)(2,1)} %copy-done.8, bf16[2,256,256]{2,1,0:T(8,128)(2,1)} %copy-done.9, bf16[2,256,256]{2,1,0:T(8,128)(2,1)} %copy-done.10, bf16[256,256]{1,0:T(8,128)(2,1)} %copy-done.17, ...), custom_call_target="tpu_custom_call" | custom-call | flops 2000000000 | bytes 1048576 | tf_op jit(solution)/shard_map/pallas_call | solution.py:40
  141.0 1.1 copy-done.3
  142.0 5.4 %shard_map.173 = (f32[5,512,512]{2,1,0:T(8,128)}, f32[1,512]{1,0:T(1,128)}) custom-call(bf16[16,336,128]{2,1,0:T(8,128)(2,1)} %copy-done, bf16[16,336,128]{2,1,0:T(8,128)(2,1)} %copy-done.3, f32[1,512]{1,0:T(1,128)} %bitcast.15), custom_call_target="tpu_custom_call" | custom-call | tf_op jit(solution)/shard_map/pallas_call | solution.py:521
  (69 shorter events, 0.7 us)
Async XLA Ops:
  4.1 35.4 %all-to-all-start = ((bf16[16,128,512]{2,1,0:T(8,128)(2,1)}), bf16[16,128,512]{2,1,0:T(8,128)(2,1)S(1)}, u32[]{:S(2)}, u32[]{:S(2)}) async-start(bf16[16,128,512]{2,1,0:T(8,128)(2,1)} %get-tuple-element.52), calls=%async_computation | async-start | bytes 4194304 | tf_op jit(solution)/shard_map/all_to_all | solution.py:419
  11.7 14.8 %collective-permute-start.1 = (bf16[528,512]{1,0:T(8,128)(2,1)}, bf16[528,512]{1,0:T(8,128)(2,1)S(1)}, u32[]{:S(2)}, u32[]{:S(2)}) collective-permute-start(bf16[528,512]{1,0:T(8,128)(2,1)} %get-tuple-element.44.p0_ref), channel_id=1, source_target_pairs={{0,6},{1,7},{2,0},{3,1},{4,2},{5,3},{6,4},{7,5},{8,14},{9,15},{10,... | collective-permute-start | bytes 1622024 | tf_op jit(solution)/shard_map/ppermute | solution.py:411
  15.5 13.9 %collective-permute-start = (bf16[528,512]{1,0:T(8,128)(2,1)}, bf16[528,512]{1,0:T(8,128)(2,1)S(1)}, u32[]{:S(2)}, u32[]{:S(2)}) collective-permute-start(bf16[528,512]{1,0:T(8,128)(2,1)} %get-tuple-element.44.p0_ref), channel_id=1, source_target_pairs={{0,2},{1,3},{2,4},{3,5},{4,6},{5,7},{6,0},{7,1},{8,10},{9,11},{10,... | collective-permute-start | bytes 1622024 | tf_op jit(solution)/shard_map/ppermute | solution.py:411
  26.4 21.8 %copy-start.5 = (bf16[528,512]{1,0:T(8,128)(2,1)}, bf16[528,512]{1,0:T(8,128)(2,1)S(1)}, u32[]{:S(2)}) copy-start(bf16[528,512]{1,0:T(8,128)(2,1)S(1)} %collective-permute-done.1.p3_ref) | copy-start | bytes 1622020
  29.4 0.8 copy-start.6
  30.3 18.4 %collective-permute-start.3 = (bf16[272,512]{1,0:T(8,128)(2,1)S(1)}, bf16[272,512]{1,0:T(8,128)(2,1)S(1)}, u32[]{:S(2)}, u32[]{:S(2)}) collective-permute-start(bf16[272,512]{1,0:T(8,128)(2,1)S(1)} %slice.19), channel_id=1, source_target_pairs={{0,6},{1,7},{2,0},{3,1},{4,2},{5,3},{6,4},{7,5},{8,14},{9,15},{10,... | collective-permute-start | bytes 835592 | tf_op jit(solution)/shard_map/ppermute | solution.py:411
  31.7 17.0 %collective-permute-start.2 = (bf16[256,512]{1,0:T(8,128)(2,1)S(1)}, bf16[256,512]{1,0:T(8,128)(2,1)}, u32[]{:S(2)}, u32[]{:S(2)}) collective-permute-start(bf16[256,512]{1,0:T(8,128)(2,1)S(1)} %slice.18), channel_id=1, source_target_pairs={{0,2},{1,3},{2,4},{3,5},{4,6},{5,7},{6,0},{7,1},{8,10},{9,11},{10,... | collective-permute-start | bytes 786440 | tf_op jit(solution)/shard_map/ppermute | solution.py:411
  39.5 1.3 copy-start.2
  40.8 38.1 %all-to-all-start.1 = ((bf16[16,128,512]{2,1,0:T(8,128)(2,1)}), bf16[16,128,512]{2,1,0:T(8,128)(2,1)S(1)}, u32[]{:S(2)}, u32[]{:S(2)}) async-start(bf16[16,128,512]{2,1,0:T(8,128)(2,1)} %get-tuple-element.57), calls=%async_computation.1 | async-start | bytes 4194304 | tf_op jit(solution)/shard_map/all_to_all | solution.py:419
  44.8 8.7 %collective-permute-start.4 = (bf16[528,512]{1,0:T(8,128)(2,1)}, bf16[528,512]{1,0:T(8,128)(2,1)}, u32[]{:S(2)}, u32[]{:S(2)}) collective-permute-start(bf16[528,512]{1,0:T(8,128)(2,1)} %get-tuple-element.44.p0_ref), channel_id=1, source_target_pairs={{0,1},{1,0},{2,3},{3,2},{4,5},{5,4},{6,7},{7,6},{8,9},{9,8},{10,11... | collective-permute-start | bytes 1622024 | tf_op jit(solution)/shard_map/ppermute | solution.py:415
  48.1 5.8 %collective-permute-start.5 = (bf16[528,512]{1,0:T(8,128)(2,1)}, bf16[528,512]{1,0:T(8,128)(2,1)}, u32[]{:S(2)}, u32[]{:S(2)}) collective-permute-start(bf16[528,512]{1,0:T(8,128)(2,1)} %copy-done.6), channel_id=1, source_target_pairs={{0,1},{1,0},{2,3},{3,2},{4,5},{5,4},{6,7},{7,6},{8,9},{9,8},{10,11... | collective-permute-start | bytes 1622024 | tf_op jit(solution)/shard_map/ppermute | solution.py:415
  48.2 5.7 %collective-permute-start.8 = (bf16[528,512]{1,0:T(8,128)(2,1)S(1)}, bf16[528,512]{1,0:T(8,128)(2,1)}, u32[]{:S(2)}, u32[]{:S(2)}) collective-permute-start(bf16[528,512]{1,0:T(8,128)(2,1)S(1)} %collective-permute-done.1.p3_ref), channel_id=1, source_target_pairs={{0,1},{1,0},{2,3},{3,2},{4,5},{5,4},{6,7},{7,6},{8,9},{9,8},{10,11... | collective-permute-start | bytes 1622024 | tf_op jit(solution)/shard_map/ppermute | solution.py:415
  48.6 5.2 %collective-permute-start.6 = (bf16[256,512]{1,0:T(8,128)(2,1)}, bf16[256,512]{1,0:T(8,128)(2,1)S(1)}, u32[]{:S(2)}, u32[]{:S(2)}) collective-permute-start(bf16[256,512]{1,0:T(8,128)(2,1)} %collective-permute-done.2.t2_ref), channel_id=1, source_target_pairs={{0,1},{1,0},{2,3},{3,2},{4,5},{5,4},{6,7},{7,6},{8,9},{9,8},{10,11... | collective-permute-start | bytes 786440 | tf_op jit(solution)/shard_map/ppermute | solution.py:415
  48.7 4.8 %copy-start.11 = (bf16[272,512]{1,0:T(8,128)(2,1)}, bf16[272,512]{1,0:T(8,128)(2,1)S(1)}, u32[]{:S(2)}) copy-start(bf16[272,512]{1,0:T(8,128)(2,1)S(1)} %collective-permute-done.3.b2_ref) | copy-start | bytes 835588
  48.7 5.2 %collective-permute-start.7 = (bf16[272,512]{1,0:T(8,128)(2,1)S(1)}, bf16[272,512]{1,0:T(8,128)(2,1)S(1)}, u32[]{:S(2)}, u32[]{:S(2)}) collective-permute-start(bf16[272,512]{1,0:T(8,128)(2,1)S(1)} %collective-permute-done.3.b2_ref), channel_id=1, source_target_pairs={{0,1},{1,0},{2,3},{3,2},{4,5},{5,4},{6,7},{7,6},{8,9},{9,8},{10,11... | collective-permute-start | bytes 835592 | tf_op jit(solution)/shard_map/ppermute | solution.py:415
  53.5 2.1 %collective-permute-start.9 = (bf16[16,64,128]{2,1,0:T(8,128)(2,1)}, bf16[16,64,128]{2,1,0:T(8,128)(2,1)}, u32[]{:S(2)}, u32[]{:S(2)}) collective-permute-start(bf16[16,64,128]{2,1,0:T(8,128)(2,1)} %get-tuple-element.54), channel_id=1, source_target_pairs={{0,1},{1,0},{2,3},{3,2},{4,5},{5,4},{6,7},{7,6},{8,9},{9,8},{10,11... | collective-permute-start | bytes 786440 | tf_op jit(solution)/shard_map/ppermute | solution.py:415
  53.9 1.8 %copy-start.16 = (bf16[256,512]{1,0:T(8,128)(2,1)}, bf16[256,512]{1,0:T(8,128)(2,1)S(1)}, u32[]{:S(2)}) copy-start(bf16[256,512]{1,0:T(8,128)(2,1)S(1)} %collective-permute-done.6.t6_ref) | copy-start | bytes 786436
  53.9 1.7 %copy-start.12 = (bf16[272,512]{1,0:T(8,128)(2,1)}, bf16[272,512]{1,0:T(8,128)(2,1)S(1)}, u32[]{:S(2)}) copy-start(bf16[272,512]{1,0:T(8,128)(2,1)S(1)} %collective-permute-done.7.b6_ref) | copy-start | bytes 835588
  79.0 6.8 %copy-start.1 = (bf16[16,128,512]{2,1,0:T(8,128)(2,1)}, bf16[16,128,512]{2,1,0:T(8,128)(2,1)S(1)}, u32[]{:S(2)}) copy-start(bf16[16,128,512]{2,1,0:T(8,128)(2,1)S(1)} %all-to-all-done.1.back_ref) | copy-start | bytes 6291460
  79.0 17.0 %all-to-all-start.2 = ((bf16[16,128,128]{2,1,0:T(8,128)(2,1)}), bf16[16,128,128]{2,1,0:T(8,128)(2,1)S(1)}, u32[]{:S(2)}, u32[]{:S(2)}) async-start(bf16[16,128,128]{2,1,0:T(8,128)(2,1)} %get-tuple-element.58), calls=%async_computation.2 | async-start | bytes 1048576 | tf_op jit(solution)/shard_map/all_to_all | solution.py:419
  89.0 1.5 collective-permute-start.10
  90.4 5.6 %copy-start.24 = (f32[8,128]{1,0:T(8,128)}, f32[8,128]{1,0:T(8,128)S(1)}, u32[]{:S(2)}) copy-start(f32[8,128]{1,0:T(8,128)S(1)} %collective-permute-done.10.g1_ref) | copy-start | bytes 12292
  96.0 0.8 copy-start.4
  98.6 5.1 %collective-permute-start.13 = (bf16[144,128]{1,0:T(8,128)(2,1)}, bf16[144,128]{1,0:T(8,128)(2,1)S(1)}, u32[]{:S(2)}, u32[]{:S(2)}) collective-permute-start(bf16[144,128]{1,0:T(8,128)(2,1)} %shard_map.170.c0_ref), channel_id=1, source_target_pairs={{0,6},{1,7},{2,0},{3,1},{4,2},{5,3},{6,4},{7,5},{8,14},{9,15},{10,... | collective-permute-start | bytes 110600 | tf_op jit(solution)/shard_map/ppermute | solution.py:411
  102.4 4.6 %collective-permute-start.12 = (bf16[144,128]{1,0:T(8,128)(2,1)}, bf16[144,128]{1,0:T(8,128)(2,1)S(1)}, u32[]{:S(2)}, u32[]{:S(2)}) collective-permute-start(bf16[144,128]{1,0:T(8,128)(2,1)} %shard_map.170.c0_ref), channel_id=1, source_target_pairs={{0,4},{1,5},{2,6},{3,7},{4,0},{5,1},{6,2},{7,3},{8,12},{9,13},{10,... | collective-permute-start | bytes 110600 | tf_op jit(solution)/shard_map/ppermute | solution.py:411
  102.4 4.6 %collective-permute-start.11 = (bf16[144,128]{1,0:T(8,128)(2,1)}, bf16[144,128]{1,0:T(8,128)(2,1)S(1)}, u32[]{:S(2)}, u32[]{:S(2)}) collective-permute-start(bf16[144,128]{1,0:T(8,128)(2,1)} %shard_map.170.c0_ref), channel_id=1, source_target_pairs={{0,2},{1,3},{2,4},{3,5},{4,6},{5,7},{6,0},{7,1},{8,10},{9,11},{10,... | collective-permute-start | bytes 110600 | tf_op jit(solution)/shard_map/ppermute | solution.py:411
  103.7 3.3 %copy-start.21 = (bf16[144,128]{1,0:T(8,128)(2,1)}, bf16[144,128]{1,0:T(8,128)(2,1)S(1)}, u32[]{:S(2)}) copy-start(bf16[144,128]{1,0:T(8,128)(2,1)S(1)} %collective-permute-done.13.c3_ref) | copy-start | bytes 110596
  110.3 4.3 %copy-start.15 = (bf16[2,256,256]{2,1,0:T(8,128)(2,1)S(1)}, bf16[2,256,256]{2,1,0:T(8,128)(2,1)}, u32[]{:S(2)}) copy-start(bf16[2,256,256]{2,1,0:T(8,128)(2,1)} %get-tuple-element.66) | copy-start | bytes 786436
  110.3 4.4 %copy-start.14 = (bf16[2,256,256]{2,1,0:T(8,128)(2,1)S(1)}, bf16[2,256,256]{2,1,0:T(8,128)(2,1)}, u32[]{:S(2)}) copy-start(bf16[2,256,256]{2,1,0:T(8,128)(2,1)} %get-tuple-element.67) | copy-start | bytes 786436
  110.3 5.6 %copy-start.7 = (bf16[2,256,256]{2,1,0:T(8,128)(2,1)S(1)}, bf16[2,256,256]{2,1,0:T(8,128)(2,1)}, u32[]{:S(2)}) copy-start(bf16[2,256,256]{2,1,0:T(8,128)(2,1)} %get-tuple-element.65.r0_ref) | copy-start | bytes 786436
  110.3 9.2 %copy-start.13 = (bf16[2,256,256]{2,1,0:T(8,128)(2,1)S(1)}, bf16[2,256,256]{2,1,0:T(8,128)(2,1)}, u32[]{:S(2)}) copy-start(bf16[2,256,256]{2,1,0:T(8,128)(2,1)} %get-tuple-element.68) | copy-start | bytes 786436
  110.3 22.9 %all-to-all-start.3 = ((bf16[16,336,128]{2,1,0:T(8,128)(2,1)}), bf16[16,336,128]{2,1,0:T(8,128)(2,1)S(1)}, u32[]{:S(2)}, u32[]{:S(2)}) async-start(bf16[16,336,128]{2,1,0:T(8,128)(2,1)} %shard_map.171), calls=%async_computation.3 | async-start | bytes 2752512 | tf_op jit(solution)/shard_map/all_to_all | solution.py:419
  114.6 5.9 %collective-permute-start.15 = (bf16[2,256,256]{2,1,0:T(8,128)(2,1)S(1)}, bf16[2,256,256]{2,1,0:T(8,128)(2,1)S(1)}, u32[]{:S(2)}, u32[]{:S(2)}) collective-permute-start(bf16[2,256,256]{2,1,0:T(8,128)(2,1)S(1)} %copy-done.15), channel_id=1, source_target_pairs={{0,6},{1,7},{2,0},{3,1},{4,2},{5,3},{6,4},{7,5},{8,14},{9,15},{10,... | collective-permute-start | bytes 786440 | tf_op jit(solution)/shard_map/ppermute | solution.py:411
  114.7 11.6 %collective-permute-start.17 = (bf16[2,256,256]{2,1,0:T(8,128)(2,1)S(1)}, bf16[2,256,256]{2,1,0:T(8,128)(2,1)S(1)}, u32[]{:S(2)}, u32[]{:S(2)}) collective-permute-start(bf16[2,256,256]{2,1,0:T(8,128)(2,1)S(1)} %copy-done.14), channel_id=1, source_target_pairs={{0,4},{1,5},{2,6},{3,7},{4,0},{5,1},{6,2},{7,3},{8,12},{9,13},{10,... | collective-permute-start | bytes 786440 | tf_op jit(solution)/shard_map/ppermute | solution.py:411
  115.9 16.0 %collective-permute-start.14 = (bf16[256,256]{1,0:T(8,128)(2,1)S(1)}, bf16[256,256]{1,0:T(8,128)(2,1)S(1)}, u32[]{:S(2)}, u32[]{:S(2)}) collective-permute-start(bf16[256,256]{1,0:T(8,128)(2,1)S(1)} %slice_bitcast_fusion.3), channel_id=1, source_target_pairs={{0,1},{1,0},{2,3},{3,2},{4,5},{5,4},{6,7},{7,6},{8,9},{9,8},{10,11... | collective-permute-start | bytes 393224 | tf_op jit(solution)/shard_map/ppermute | solution.py:415
  119.4 11.9 %collective-permute-start.19 = (bf16[2,256,256]{2,1,0:T(8,128)(2,1)S(1)}, bf16[2,256,256]{2,1,0:T(8,128)(2,1)S(1)}, u32[]{:S(2)}, u32[]{:S(2)}) collective-permute-start(bf16[2,256,256]{2,1,0:T(8,128)(2,1)S(1)} %copy-done.13), channel_id=1, source_target_pairs={{0,2},{1,3},{2,4},{3,5},{4,6},{5,7},{6,0},{7,1},{8,10},{9,11},{10,... | collective-permute-start | bytes 786440 | tf_op jit(solution)/shard_map/ppermute | solution.py:411
  120.5 6.5 %copy-start.8 = (bf16[2,256,256]{2,1,0:T(8,128)(2,1)}, bf16[2,256,256]{2,1,0:T(8,128)(2,1)S(1)}, u32[]{:S(2)}) copy-start(bf16[2,256,256]{2,1,0:T(8,128)(2,1)S(1)} %collective-permute-done.15.r1_ref) | copy-start | bytes 786436
  120.5 11.3 %collective-permute-start.16 = (bf16[256,256]{1,0:T(8,128)(2,1)S(1)}, bf16[256,256]{1,0:T(8,128)(2,1)S(1)}, u32[]{:S(2)}, u32[]{:S(2)}) collective-permute-start(bf16[256,256]{1,0:T(8,128)(2,1)S(1)} %slice_bitcast_fusion.2), channel_id=1, source_target_pairs={{0,1},{1,0},{2,3},{3,2},{4,5},{5,4},{6,7},{7,6},{8,9},{9,8},{10,11... | collective-permute-start | bytes 393224 | tf_op jit(solution)/shard_map/ppermute | solution.py:415
  126.3 5.5 %copy-start.9 = (bf16[2,256,256]{2,1,0:T(8,128)(2,1)}, bf16[2,256,256]{2,1,0:T(8,128)(2,1)S(1)}, u32[]{:S(2)}) copy-start(bf16[2,256,256]{2,1,0:T(8,128)(2,1)S(1)} %collective-permute-done.17.r2_ref) | copy-start | bytes 786436
  126.4 5.5 %collective-permute-start.18 = (bf16[256,256]{1,0:T(8,128)(2,1)S(1)}, bf16[256,256]{1,0:T(8,128)(2,1)S(1)}, u32[]{:S(2)}, u32[]{:S(2)}) collective-permute-start(bf16[256,256]{1,0:T(8,128)(2,1)S(1)} %slice_bitcast_fusion.1), channel_id=1, source_target_pairs={{0,1},{1,0},{2,3},{3,2},{4,5},{5,4},{6,7},{7,6},{8,9},{9,8},{10,11... | collective-permute-start | bytes 393224 | tf_op jit(solution)/shard_map/ppermute | solution.py:415
  131.3 0.7 copy-start.10
  131.3 1.8 %collective-permute-start.20 = (bf16[256,256]{1,0:T(8,128)(2,1)S(1)}, bf16[256,256]{1,0:T(8,128)(2,1)S(1)}, u32[]{:S(2)}, u32[]{:S(2)}) collective-permute-start(bf16[256,256]{1,0:T(8,128)(2,1)S(1)} %slice_bitcast_fusion), channel_id=1, source_target_pairs={{0,1},{1,0},{2,3},{3,2},{4,5},{5,4},{6,7},{7,6},{8,9},{9,8},{10,11... | collective-permute-start | bytes 393224 | tf_op jit(solution)/shard_map/ppermute | solution.py:415
  131.8 0.7 copy-start.17
  131.8 0.7 copy-start.18
  133.2 3.3 %copy-start.20 = (bf16[256,256]{1,0:T(8,128)(2,1)}, bf16[256,256]{1,0:T(8,128)(2,1)S(1)}, u32[]{:S(2)}) copy-start(bf16[256,256]{1,0:T(8,128)(2,1)S(1)} %collective-permute-done.20.t3_ref) | copy-start | bytes 393220
  133.2 7.8 %copy-start = (bf16[16,336,128]{2,1,0:T(8,128)(2,1)}, bf16[16,336,128]{2,1,0:T(8,128)(2,1)S(1)}, u32[]{:S(2)}) copy-start(bf16[16,336,128]{2,1,0:T(8,128)(2,1)S(1)} %all-to-all-done.3.mine_ref) | copy-start | bytes 4128772
  133.2 7.7 %collective-permute-start.21 = (bf16[16,336,128]{2,1,0:T(8,128)(2,1)S(1)}, bf16[16,336,128]{2,1,0:T(8,128)(2,1)S(1)}, u32[]{:S(2)}, u32[]{:S(2)}) collective-permute-start(bf16[16,336,128]{2,1,0:T(8,128)(2,1)S(1)} %all-to-all-done.3.mine_ref), channel_id=1, source_target_pairs={{0,1},{1,0},{2,3},{3,2},{4,5},{5,4},{6,7},{7,6},{8,9},{9,8},{10,11... | collective-permute-start | bytes 4128776 | tf_op jit(solution)/shard_map/ppermute | solution.py:415
  140.9 1.1 copy-start.3
  (3 other events, 1.9 us)

commit v9 on v8

--- a/solution.py
+++ b/solution.py
@@ -91,15 +91,16 @@
     counts_t_ref, degree_ref, slots_ref, wqkv_ref, wo_head_ref, acc_ref,
 ):
     z, core = position()
+    head = core * 4 + z
     for m in range(4):
-        @pl.when(z == m)
+        @pl.when(head >> 1 == m)
         def _():
             for k, ref in enumerate((wq_ref, wk_ref, wv_ref)):
                 pair = jnp.transpose(ref[:, m * 128 : (m + 1) * 128].astype(F32))
-                picked = jnp.where(core == 0, pair[0:HEAD], pair[HEAD:128])
+                picked = jnp.where(head & 1 == 0, pair[0:HEAD], pair[HEAD:128])
                 wqkv_ref[k * HEAD : (k + 1) * HEAD, :] = picked.astype(BF16)
             for c in range(2):
-                @pl.when(core == c)
+                @pl.when(head & 1 == c)
                 def _():
                     wo_head_ref[...] = wo_ref[m * 128 + c * HEAD : m * 128 + (c + 1) * HEAD, :]
 
@@ -326,21 +327,22 @@
 def rows_body(
     r0_ref, r1_ref, r2_ref, r3_ref, t0_ref, t1_ref, t2_ref, t3_ref, halo_ref, base_ref, x_ref,
     gain_ref, grad_ref, wq_ref, wk_ref, wv_ref, wo_ref,
-    out_ref, feature_ref, dq_ref, dk_ref, dv_ref, at_ref,
+    out_ref, feature_ref, dq_ref, dk_ref, dv_ref, at_ref, heads_ref,
 ):
     left = lax.broadcasted_iota(jnp.int32, (ROWS, 128), 1) < HEAD
     z, core = position()
-    even = core == 0
     for dz, (r_ref, t_ref) in enumerate(zip((r0_ref, r1_ref, r2_ref, r3_ref), (t0_ref, t1_ref, t2_ref, t3_ref))):
         chip = (z + dz) & 3
-        one, two = r_ref[0].astype(F32), t_ref[...].astype(F32)
-        low, high = jnp.where(even, one, two), jnp.where(even, two, one)
+        heads_ref[core * 4 + chip] = r_ref[0]
+        heads_ref[(1 - core) * 4 + chip] = t_ref[...]
+    for m in range(4):
+        low, high = heads_ref[2 * m].astype(F32), heads_ref[2 * m + 1].astype(F32)
         low0, low1 = low[:, 0:128], low[:, 128:256]
         high0, high1 = high[:, 0:128], high[:, 128:256]
-        dq_ref[chip] = jnp.where(left, low0, pltpu.roll(high0, HEAD, 1)).astype(BF16)
-        dk_ref[chip] = jnp.where(left, pltpu.roll(low0, HEAD, 1), high0).astype(BF16)
-        dv_ref[chip] = jnp.where(left, low1, pltpu.roll(high1, HEAD, 1)).astype(BF16)
-        at_ref[chip] = jnp.where(left, pltpu.roll(low1, HEAD, 1), high1).astype(BF16)
+        dq_ref[m] = jnp.where(left, low0, pltpu.roll(high0, HEAD, 1)).astype(BF16)
+        dk_ref[m] = jnp.where(left, pltpu.roll(low0, HEAD, 1), high0).astype(BF16)
+        dv_ref[m] = jnp.where(left, low1, pltpu.roll(high1, HEAD, 1)).astype(BF16)
+        at_ref[m] = jnp.where(left, pltpu.roll(low1, HEAD, 1), high1).astype(BF16)
 
     def whole(ref):
         return jnp.concatenate([ref[m] for m in range(4)], axis=1)
@@ -356,51 +358,74 @@
     feature_ref[...] = (grad_ref[...].astype(F32) + dx).astype(BF16)
 
 
-def weights_body(mine_ref, other_ref, gain_in_ref, out_ref, gain_ref, all_ref):
-    which = pl.program_id(0)
-
-    @pl.when(which == 0)
-    def _():
-        z, core = position()
-        all_ref[core] = mine_ref[...]
-        all_ref[1 - core] = other_ref[...]
-        gain = jnp.zeros((8, 128), F32)
-        through = []
-        for p in range(DOM):
-            tails = [ref[p, 320:SPREAD, :].astype(F32) for ref in (mine_ref, other_ref)]
-            tails = [tail[0:8] + tail[8:16] for tail in tails]
-            gain = gain + tails[0]
-            through.append(tails[0] + tails[1])
+def half_body(core, in_ref, out_hbm, tall_ref, wide_ref, sems):
+    z, _ = position()
+    first = pl.multiple_of(core * 256, 256)
+    copies = [
+        pltpu.make_async_copy(tall_ref.at[t], out_hbm.at[t, :, pl.ds(first, 256)], sems.at[t]) for t in range(3)
+    ] + [
+        pltpu.make_async_copy(wide_ref.at[t], out_hbm.at[3 + t, pl.ds(first, 256), :], sems.at[3 + t]) for t in range(2)
+    ]
+
+    def piece(chip, p):
+        start = pl.multiple_of(((z - chip) & 3) * 64, 64)
+        return in_ref[p, pl.ds(start, 64), :].astype(F32)
+
+    for t in range(3):
         for b in range(4):
-            part = (through[b] + through[4 + b] + through[8 + b])[4:5]
-            lanes = slice(b * 128, (b + 1) * 128)
-            gain_ref[:, lanes] = gain[b : b + 1] + part / gain_in_ref[:, lanes]
-
-    def piece(h, p):
-        z, core = position()
-        start = pl.multiple_of(((z - (h >> 1)) & 3) * 64, 64)
-        return all_ref[h & 1, p, pl.ds(start, 64), :].astype(F32)
-
-    @pl.when(which < 3)
-    def _():
+            part = jnp.concatenate([piece(chip, t * 4 + b) for chip in range(4)], axis=0)
+            tall_ref[t, b * 128 : (b + 1) * 128, :] = jnp.transpose(part)
+        copies[t].start()
+    for b in range(4):
+        for chip in range(4):
+            wide_ref[0, chip * 64 : (chip + 1) * 64, b * 128 : (b + 1) * 128] = piece(chip, 12 + b)
+    copies[3].start()
+    for p in range(DOM):
         for b in range(4):
-            part = jnp.concatenate([piece(h, which * 4 + b) for h in range(BLK)], axis=0)
-            out_ref[0, b * 128 : (b + 1) * 128, :] = jnp.transpose(part)
-
-    @pl.when(which == 3)
-    def _():
-        for h in range(BLK):
-            for b in range(4):
-                out_ref[0, h * 64 : (h + 1) * 64, b * 128 : (b + 1) * 128] = piece(h, 12 + b)
-
-    @pl.when(which == 4)
-    def _():
-        for half in range(2):
-            for p in range(DOM):
-                top = half * 256 + p * 16
-                for b in range(4):
-                    part = all_ref[half, p, 256 + b * 16 : 272 + b * 16, :]
-                    out_ref[0, top : top + 16, b * 128 : (b + 1) * 128] = part.astype(F32)
+            part = in_ref[p, 256 + b * 16 : 272 + b * 16, :]
+            wide_ref[1, p * 16 : (p + 1) * 16, b * 128 : (b + 1) * 128] = part.astype(F32)
+    copies[4].start()
+    for copy in copies:
+        copy.wait()
+
+
+def tails_of(ref):
+    tails = [ref[p, 320:SPREAD, :].astype(F32) for p in range(DOM)]
+    return [tail[0:8] + tail[8:16] for tail in tails]
+
+
+def first_half_body(mine_ref, out_hbm, tall_ref, wide_ref, sems):
+    half_body(position()[1], mine_ref, out_hbm, tall_ref, wide_ref, sems)
+
+
+def second_half_body(before_hbm, mine_ref, other_ref, gain_in_ref, out_hbm, gain_ref, tall_ref, wide_ref, sems):
+    gain = jnp.zeros((8, 128), F32)
+    mine, through = tails_of(mine_ref), tails_of(other_ref)
+    for p in range(DOM):
+        gain = gain + mine[p]
+        through[p] = through[p] + mine[p]
+    for b in range(4):
+        part = (through[b] + through[4 + b] + through[8 + b])[4:5]
+        lanes = slice(b * 128, (b + 1) * 128)
+        gain_ref[:, lanes] = gain[b : b + 1] + part / gain_in_ref[:, lanes]
+    half_body(1 - position()[1], other_ref, out_hbm, tall_ref, wide_ref, sems)
+
+
+def in_halves(mine, other, gain_row):
+    vmem, hbm = pl.BlockSpec(memory_space=pltpu.VMEM), pl.BlockSpec(memory_space=pltpu.HBM)
+    scratch = [pltpu.VMEM((3, D, 256), F32), pltpu.VMEM((2, 256, D), F32), pltpu.SemaphoreType.DMA((5,))]
+    half = pl.pallas_call(
+        first_half_body, out_shape=shape((5, D, D), F32), in_specs=[vmem], out_specs=hbm, scratch_shapes=scratch,
+        cost_estimate=pl.CostEstimate(flops=int(3e9), transcendentals=0, bytes_accessed=1 << 20),
+    )(mine)
+    return pl.pallas_call(
+        second_half_body,
+        out_shape=(shape((5, D, D), F32), shape((1, D), F32)),
+        in_specs=[hbm, vmem, vmem, vmem],
+        out_specs=(hbm, vmem),
+        input_output_aliases={0: 0},
+        scratch_shapes=scratch,
+    )(half, mine, other, gain_row)
 
 
 def chip_shift(step, swap):
@@ -489,6 +514,8 @@
         scalars=1,
         micros=3,
     )
+    *results, gain_part = lax.optimization_barrier((*results, gain_part))
+    results = [results[0]] + [along_chips(results[dz], -dz) for dz in (1, 2, 3)]
     chunk = call(
         chunk_sum_body,
         shape((CHUNK, 128), BF16),
@@ -497,35 +524,24 @@
         micros=1,
     )
     chunk_parts = [chunk] + [along_chips(chunk, step) for step in (1, 2, 3)]
+    *chunk_parts, r1, r2, r3 = lax.optimization_barrier((*chunk_parts, *results[1:]))
+    results = [results[0], r1, r2, r3]
     spread = call(
         spread_body, shape((DOM, SPREAD, 128), BF16), chunk_parts, scratch=[pltpu.VMEM((4, 80, 128), F32)], micros=1
     )
     spread, *results = lax.optimization_barrier((spread, *results))
     gathered = to_dom_peers(spread)
-    results = [results[0]] + [along_chips(results[dz], -dz) for dz in (1, 2, 3)]
     swapped = [other_core(part[1]) for part in results]
-    gathered, *swapped = lax.optimization_barrier((gathered, *swapped))
-    gathered_other = other_core(gathered)
     layer_out, feature_grad = call(
         rows_body,
         (shape((ROWS, D), BF16), shape((ROWS, D), BF16)),
         (*results, *swapped, halo, base, x, gain_row, out_grad, wq, wk, wv, wo),
-        scratch=[pltpu.VMEM((4, ROWS, 128), BF16)] * 4,
+        scratch=[pltpu.VMEM((4, ROWS, 128), BF16)] * 4 + [pltpu.VMEM((BLK, ROWS, 256), BF16)],
         micros=2,
     )
-    gathered, gathered_other, layer_out, feature_grad = lax.optimization_barrier(
-        (gathered, gathered_other, layer_out, feature_grad)
-    )
-    whole = pl.BlockSpec((DOM, SPREAD, 128), lambda t: (0, 0, 0))
-    row = pl.BlockSpec((1, D), lambda t: (0, 0))
-    weight_grads, gain_grad = pl.pallas_call(
-        weights_body,
-        grid=(5,),
-        out_shape=(shape((5, D, D), F32), shape((1, D), F32)),
-        in_specs=[whole, whole, row],
-        out_specs=(pl.BlockSpec((1, D, D), lambda t: (t, 0, 0)), row),
-        scratch_shapes=[pltpu.VMEM((2, DOM, SPREAD, 128), BF16)],
-    )(gathered, gathered_other, gain_row)
+    gathered, layer_out, feature_grad = lax.optimization_barrier((gathered, layer_out, feature_grad))
+    gathered_other = other_core(gathered)
+    weight_grads, gain_grad = in_halves(gathered, gathered_other, gain_row)
     return layer_out, feature_grad, weight_grads, gain_grad.reshape(D)
 
 

time: 148 us -> 150 us (1.014)
  waiting for transfers between devices: 28.2 us -> 29.7 us
    ppermute x12, starting transfers between devices: 18.9 us -> 14.3 us  [other_core(): return lax.ppermute(array, 'blk', chip_shift(0, 1))]
    all_to_all x4, starting transfers between devices: 22.6 us -> 25.3 us  [to_dom_peers(): return lax.all_to_all(array, 'dom', split_axis=0, concat_axis=0, tiled=True)]
    all_to_all x4, waiting for transfers between devices: 12.2 us -> 14.2 us  [to_dom_peers(): return lax.all_to_all(array, 'dom', split_axis=0, concat_axis=0, tiled=True)]
    ppermute x10, waiting for transfers between devices: 13.2 us -> 11.5 us  [along_chips(): return lax.ppermute(array, 'blk', chip_shift(step, 0))]
    pallas_call x1 -> x2, Pallas kernels: 5.37 us -> 7.01 us  [the longest x1 4.01 us: in_halves(): pl.pallas_call(second_half_body, out_shape=(shape((5, D, D), F32), shape(...]
    unnamed x50 -> x44, local copies, waits for them, and re-layouts: 6.61 us -> 5.66 us
  transfers between devices with their start and end apart: 26 -> 26, of which waited for: 9 -> 14; matrix products, arithmetic and copies ran while one was open for 1% -> 1% of each run, Pallas kernels for 30% -> 33%
where the time goes in v9:
time: 150 us; the launch traced here: 149 us
  Pallas kernels  58.3 us (39%)
  starting transfers between devices  53.2 us (35%)
  waiting for transfers between devices  29.7 us (20%)
  local copies, waits for them, and re-layouts  6.69 us (4%)
    pallas_call x8, Pallas kernels, call(): pl.pallas_call(body, out_shape=out_shape, in_specs=specs, out_specs=jax.t...  51.3 us
    all_to_all x4, starting transfers between devices, to_dom_peers(): return lax.all_to_all(array, 'dom', split_axis=0, concat_axis=0, tiled=True)  25.3 us
    ppermute x12, starting transfers between devices, other_core(): return lax.ppermute(array, 'blk', chip_shift(0, 1))  14.3 us
    all_to_all x4, waiting for transfers between devices, to_dom_peers(): return lax.all_to_all(array, 'dom', split_axis=0, concat_axis=0, tiled=True)  14.2 us
    ppermute x10, starting transfers between devices, along_chips(): return lax.ppermute(array, 'blk', chip_shift(step, 0))  13.6 us
    ppermute x10, waiting for transfers between devices, along_chips(): return lax.ppermute(array, 'blk', chip_shift(step, 0))  11.5 us
    unnamed x44, local copies, waits for them, and re-layouts  5.66 us
    ppermute x12, waiting for transfers between devices, other_core(): return lax.ppermute(array, 'blk', chip_shift(0, 1))  4.02 us
  transfers between devices with their start and end apart: 26, of which 14 were waited for; matrix products, arithmetic and copies ran while one was open for 1% of the time, Pallas kernels for 33%

profile of v9, /device:TPU:1, one launch (start us, length us, event | category | flops | bytes accessed | tf_op | source)
XLA Modules:
  0.0 148.9 jit_solution(12244222871689468713)
XLA Ops:
  0.6 3.4 %shard_map.165 = (bf16[528,512]{1,0:T(8,128)(2,1)}, bf16[16,128,512]{2,1,0:T(8,128)(2,1)}) custom-call(s32[1,8]{1,0:T(1,128)} %pattern_ref.1, s32[16]{0:T(128)} %counts_ref.3, bf16[256,512]{1,0:T(8,128)(2,1)} %x_ref.7, f32[1,512]{1,0:T(1,128)} %bitcast.13, s32[1,256]{1,0:T(1,128)} %bitcast.19, bf16[256,512]{1,0:T(8,128)(2,1)} %grad_ref.7, s32[16,128]{1,0:T(8,128)} %rows_ref.3), custom_call_target="tpu_custom_call" | custom-call | flops 4000000000 | bytes 1048576 | tf_op jit(solution)/shard_map/pallas_call | solution.py:40
  4.1 7.6 %all-to-all-start = ((bf16[16,128,512]{2,1,0:T(8,128)(2,1)}), bf16[16,128,512]{2,1,0:T(8,128)(2,1)S(1)}, u32[]{:S(2)}, u32[]{:S(2)}) async-start(bf16[16,128,512]{2,1,0:T(8,128)(2,1)} %get-tuple-element.58), calls=%async_computation | async-start | bytes 4194304 | tf_op jit(solution)/shard_map/all_to_all | solution.py:444
  11.7 3.8 %collective-permute-start.1 = (bf16[528,512]{1,0:T(8,128)(2,1)}, bf16[528,512]{1,0:T(8,128)(2,1)S(1)}, u32[]{:S(2)}, u32[]{:S(2)}) collective-permute-start(bf16[528,512]{1,0:T(8,128)(2,1)} %get-tuple-element.50.p0_ref), channel_id=1, source_target_pairs={{0,6},{1,7},{2,0},{3,1},{4,2},{5,3},{6,4},{7,5},{8,14},{9,15},{10,... | collective-permute-start | bytes 1622024 | tf_op jit(solution)/shard_map/ppermute | solution.py:436
  15.5 8.9 %shard_map.166 = (bf16[1024,512]{1,0:T(8,128)(2,1)}, f32[256,128]{1,0:T(8,128)}, bf16[16,128,512]{2,1,0:T(8,128)(2,1)}, bf16[192,512]{1,0:T(8,128)(2,1)}, bf16[64,512]{1,0:T(8,128)(2,1)}) custom-call(s32[32,128]{1,0:T(8,128)} %bitcast.16, s32[32,128]{1,0:T(8,128)} %bitcast.17, bf16[256,512]{1,0:T(8,128)(2,1)} %grad_ref.7, bf16[512,512]{1,0:T(8,128)(2,1)} %w_ref.3, ...), custom_call_target="tpu_custom_call" | custom-call | flops 10000000000 | bytes 1048576 | tf_op jit(solution)/shard_map/pallas_call | solution.py:40
  24.4 2.0 %collective-permute-done.1.p3_ref = bf16[528,512]{1,0:T(8,128)(2,1)S(1)} collective-permute-done((bf16[528,512]{1,0:T(8,128)(2,1)}, bf16[528,512]{1,0:T(8,128)(2,1)S(1)}, u32[]{:S(2)}, u32[]{:S(2)}) %collective-permute-start.1) | collective-permute-done | bytes 540704 | tf_op jit(solution)/shard_map/ppermute | solution.py:436
  26.4 3.0 %collective-permute-done.p1_ref = bf16[528,512]{1,0:T(8,128)(2,1)S(1)} collective-permute-done((bf16[528,512]{1,0:T(8,128)(2,1)}, bf16[528,512]{1,0:T(8,128)(2,1)S(1)}, u32[]{:S(2)}, u32[]{:S(2)}) %collective-permute-start) | collective-permute-done | bytes 540704 | tf_op jit(solution)/shard_map/ppermute | solution.py:436
  29.4 0.8 copy-done.6
  30.3 0.4 collective-permute-start.3
  30.7 1.0 slice.18
  31.7 1.2 collective-permute-start.2
  32.9 6.7 %all-to-all-done.table_ref = bf16[16,128,512]{2,1,0:T(8,128)(2,1)S(1)} async-done(((bf16[16,128,512]{2,1,0:T(8,128)(2,1)}), bf16[16,128,512]{2,1,0:T(8,128)(2,1)S(1)}, u32[]{:S(2)}, u32[]{:S(2)}) %all-to-all-start) | async-done | bytes 2097184 | tf_op jit(solution)/shard_map/all_to_all | solution.py:444
  39.5 1.3 copy-done.2
  40.8 3.9 %all-to-all-start.1 = ((bf16[16,128,512]{2,1,0:T(8,128)(2,1)}), bf16[16,128,512]{2,1,0:T(8,128)(2,1)S(1)}, u32[]{:S(2)}, u32[]{:S(2)}) async-start(bf16[16,128,512]{2,1,0:T(8,128)(2,1)} %get-tuple-element.63), calls=%async_computation.1 | async-start | bytes 4194304 | tf_op jit(solution)/shard_map/all_to_all | solution.py:444
  44.8 3.3 %collective-permute-start.4 = (bf16[528,512]{1,0:T(8,128)(2,1)}, bf16[528,512]{1,0:T(8,128)(2,1)}, u32[]{:S(2)}, u32[]{:S(2)}) collective-permute-start(bf16[528,512]{1,0:T(8,128)(2,1)} %get-tuple-element.50.p0_ref), channel_id=1, source_target_pairs={{0,1},{1,0},{2,3},{3,2},{4,5},{5,4},{6,7},{7,6},{8,9},{9,8},{10,11... | collective-permute-start | bytes 1622024 | tf_op jit(solution)/shard_map/ppermute | solution.py:440
  48.2 0.4 collective-permute-start.8
  48.7 0.4 collective-permute-start.7
  49.2 4.3 %shard_map.167 = (f32[256,512]{1,0:T(8,128)}, bf16[16,64,128]{2,1,0:T(8,128)(2,1)}, bf16[16,64,128]{2,1,0:T(8,128)(2,1)}) custom-call(bf16[1024,512]{1,0:T(8,128)(2,1)} %get-tuple-element.56.counts_t_ref, f32[256,128]{1,0:T(8,128)} %get-tuple-element.57.degree_ref, bf16[16,128,512]{2,1,0:T(8,128)(2,1)} %copy-done.2, bf16[256,512]{1,0:T(8,128)(2,1)} %x_ref.7, ...), custom_call_target="tpu_custom_call" | custom-call | flops 4000000000 | bytes 1048576 | tf_op jit(solution)/shard_map/pallas_call | solution.py:40
  53.5 0.4 collective-permute-start.9
  53.9 1.7 %collective-permute-done.9.other_ref = bf16[16,64,128]{2,1,0:T(8,128)(2,1)} collective-permute-done((bf16[16,64,128]{2,1,0:T(8,128)(2,1)}, bf16[16,64,128]{2,1,0:T(8,128)(2,1)}, u32[]{:S(2)}, u32[]{:S(2)}) %collective-permute-start.9) | collective-permute-done | bytes 262176 | tf_op jit(solution)/shard_map/ppermute | solution.py:440
  55.6 23.3 %shard_map.168 = (bf16[2,256,256]{2,1,0:T(8,128)(2,1)}, bf16[2,256,256]{2,1,0:T(8,128)(2,1)}, bf16[2,256,256]{2,1,0:T(8,128)(2,1)}, bf16[2,256,256]{2,1,0:T(8,128)(2,1)}, bf16[16,128,128]{2,1,0:T(8,128)(2,1)}) custom-call(bf16[528,512]{1,0:T(8,128)(2,1)} %get-tuple-element.50.p0_ref, bf16[528,512]{1,0:T(8,128)(2,1)} %copy-done.6, ...), custom_call_target="tpu_custom_call" | custom-call | flops 12000000000 | bytes 1048576 | tf_op jit(solution)/shard_map/pallas_call | solution.py:40
  79.0 6.8 %all-to-all-start.2 = ((bf16[16,128,128]{2,1,0:T(8,128)(2,1)}), bf16[16,128,128]{2,1,0:T(8,128)(2,1)S(1)}, u32[]{:S(2)}, u32[]{:S(2)}) async-start(bf16[16,128,128]{2,1,0:T(8,128)(2,1)} %get-tuple-element.64), calls=%async_computation.2 | async-start | bytes 1048576 | tf_op jit(solution)/shard_map/all_to_all | solution.py:444
  85.8 3.1 %shard_map.169 = (f32[256,512]{1,0:T(8,128)}, f32[8,128]{1,0:T(8,128)}) custom-call(s32[16]{0:T(128)} %counts_ref.3, bf16[16,128,512]{2,1,0:T(8,128)(2,1)} %copy-done.1, s32[16,128]{1,0:T(8,128)} %rows_ref.3, bf16[256,512]{1,0:T(8,128)(2,1)} %x_ref.7), custom_call_target="tpu_custom_call" | custom-call | flops 3000000000 | bytes 1048576 | tf_op jit(solution)/shard_map/pallas_call | solution.py:40
  88.9 3.8 %collective-permute-start.14 = (bf16[2,256,256]{2,1,0:T(8,128)(2,1)}, bf16[2,256,256]{2,1,0:T(8,128)(2,1)S(1)}, u32[]{:S(2)}, u32[]{:S(2)}) collective-permute-start(bf16[2,256,256]{2,1,0:T(8,128)(2,1)} %get-tuple-element.71), channel_id=1, source_target_pairs={{0,6},{1,7},{2,0},{3,1},{4,2},{5,3},{6,4},{7,5},{8,14},{9,15},{10,... | collective-permute-start | bytes 786440 | tf_op jit(solution)/shard_map/ppermute | solution.py:436
  92.7 0.7 collective-permute-start.16
  93.4 1.3 collective-permute-start.10
  94.7 1.0 collective-permute-done.10.g1_ref
  96.0 0.3 copy-done.21
  96.3 0.8 copy-done.4
  97.1 1.8 %shard_map.170.c0_ref = bf16[144,128]{1,0:T(8,128)(2,1)} custom-call(bf16[16,128,128]{2,1,0:T(8,128)(2,1)} %copy-done.4, f32[8,128]{1,0:T(8,128)} %get-tuple-element.70.g0_ref, f32[8,128]{1,0:T(8,128)} %copy-done.21, bf16[192,512]{1,0:T(8,128)(2,1)} %get-tuple-element.54.wqkv_ref), custom_call_target="tpu_custom_call" | custom-call | flops 1000000000 | bytes 1048576 | tf_op jit(solution)/shard_map/pallas_call | solution.py:40
  98.9 3.4 %collective-permute-start.13 = (bf16[144,128]{1,0:T(8,128)(2,1)}, bf16[144,128]{1,0:T(8,128)(2,1)S(1)}, u32[]{:S(2)}, u32[]{:S(2)}) collective-permute-start(bf16[144,128]{1,0:T(8,128)(2,1)} %shard_map.170.c0_ref), channel_id=1, source_target_pairs={{0,6},{1,7},{2,0},{3,1},{4,2},{5,3},{6,4},{7,5},{8,14},{9,15},{10,... | collective-permute-start | bytes 110600 | tf_op jit(solution)/shard_map/ppermute | solution.py:436
  102.7 1.1 collective-permute-done.14.r1_ref
  103.8 4.3 %collective-permute-done.16.r3_ref = bf16[2,256,256]{2,1,0:T(8,128)(2,1)S(1)} collective-permute-done((bf16[2,256,256]{2,1,0:T(8,128)(2,1)}, bf16[2,256,256]{2,1,0:T(8,128)(2,1)S(1)}, u32[]{:S(2)}, u32[]{:S(2)}) %collective-permute-start.16) | collective-permute-done | bytes 262176 | tf_op jit(solution)/shard_map/ppermute | solution.py:436
  108.1 1.1 collective-permute-done.11.c1_ref
  109.2 0.6 copy-done.20
  109.8 2.1 %shard_map.171 = bf16[16,336,128]{2,1,0:T(8,128)(2,1)} custom-call(bf16[144,128]{1,0:T(8,128)(2,1)} %shard_map.170.c0_ref, bf16[144,128]{1,0:T(8,128)(2,1)} %copy-done.20, bf16[144,128]{1,0:T(8,128)(2,1)} %copy-done.19, bf16[144,128]{1,0:T(8,128)(2,1)} %copy-done.18), custom_call_target="tpu_custom_call" | custom-call | flops 1000000000 | bytes 1048576 | tf_op jit(solution)/shard_map/pallas_call | solution.py:40
  111.8 6.9 %all-to-all-start.3 = ((bf16[16,336,128]{2,1,0:T(8,128)(2,1)}), bf16[16,336,128]{2,1,0:T(8,128)(2,1)S(1)}, u32[]{:S(2)}, u32[]{:S(2)}) async-start(bf16[16,336,128]{2,1,0:T(8,128)(2,1)} %shard_map.171), calls=%async_computation.3 | async-start | bytes 2752512 | tf_op jit(solution)/shard_map/all_to_all | solution.py:444
  118.9 3.1 %collective-permute-start.20 = (bf16[256,256]{1,0:T(8,128)(2,1)S(1)}, bf16[256,256]{1,0:T(8,128)(2,1)S(1)}, u32[]{:S(2)}, u32[]{:S(2)}) collective-permute-start(bf16[256,256]{1,0:T(8,128)(2,1)S(1)} %slice_bitcast_fusion), channel_id=1, source_target_pairs={{0,1},{1,0},{2,3},{3,2},{4,5},{5,4},{6,7},{7,6},{8,9},{9,8},{10,11... | collective-permute-start | bytes 393224 | tf_op jit(solution)/shard_map/ppermute | solution.py:440
  122.1 0.4 collective-permute-start.18
  122.7 0.4 collective-permute-done.20.t3_ref
  123.0 0.4 collective-permute-done.19.t2_ref
  123.6 0.3 collective-permute-done.17.t0_ref
  124.3 0.3 copy-done.17
  124.6 4.2 %shard_map.172 = (bf16[256,512]{1,0:T(8,128)(2,1)}, bf16[256,512]{1,0:T(8,128)(2,1)}) custom-call(bf16[2,256,256]{2,1,0:T(8,128)(2,1)} %get-tuple-element.83.r0_ref, bf16[2,256,256]{2,1,0:T(8,128)(2,1)} %copy-done.8, bf16[2,256,256]{2,1,0:T(8,128)(2,1)} %copy-done.9, bf16[2,256,256]{2,1,0:T(8,128)(2,1)} %copy-done.10, bf16[256,256]{1,0:T(8,128)(2,1)} %copy-done.17, ...), custom_call_target="tpu_custom_call" | custom-call | flops 2000000000 | bytes 1048576 | tf_op jit(solution)/shard_map/pallas_call | solution.py:40
  128.8 7.3 %all-to-all-done.3.mine_ref = bf16[16,336,128]{2,1,0:T(8,128)(2,1)S(1)} async-done(((bf16[16,336,128]{2,1,0:T(8,128)(2,1)}), bf16[16,336,128]{2,1,0:T(8,128)(2,1)S(1)}, u32[]{:S(2)}, u32[]{:S(2)}) %all-to-all-start.3) | async-done | bytes 1376288 | tf_op jit(solution)/shard_map/all_to_all | solution.py:444
  136.1 4.6 %collective-permute-start.21 = (bf16[16,336,128]{2,1,0:T(8,128)(2,1)S(1)}, bf16[16,336,128]{2,1,0:T(8,128)(2,1)S(1)}, u32[]{:S(2)}, u32[]{:S(2)}) collective-permute-start(bf16[16,336,128]{2,1,0:T(8,128)(2,1)S(1)} %all-to-all-done.3.mine_ref), channel_id=1, source_target_pairs={{0,1},{1,0},{2,3},{3,2},{4,5},{5,4},{6,7},{7,6},{8,9},{9,8},{10,11... | collective-permute-start | bytes 4128776 | tf_op jit(solution)/shard_map/ppermute | solution.py:440
  140.7 3.0 %shard_map.173.before_hbm = f32[5,512,512]{2,1,0:T(8,128)} custom-call(bf16[16,336,128]{2,1,0:T(8,128)(2,1)} %copy-done), custom_call_target="tpu_custom_call" | custom-call | flops 3000000000 | bytes 1048576 | tf_op jit(solution)/shard_map/pallas_call | solution.py:417
  143.7 1.1 copy-done.3
  144.8 4.0 %shard_map.174 = (f32[5,512,512]{2,1,0:T(8,128)}, f32[1,512]{1,0:T(1,128)}) custom-call(f32[5,512,512]{2,1,0:T(8,128)} %shard_map.173.before_hbm, bf16[16,336,128]{2,1,0:T(8,128)(2,1)} %copy-done, bf16[16,336,128]{2,1,0:T(8,128)(2,1)} %copy-done.3, f32[1,512]{1,0:T(1,128)} %bitcast.15), custom_call_target="tpu_custom_call", output_to_operand_aliasing={{0}: (0, {})} | custom-call | tf_op jit(solution)/shard_map/pallas_call | solution.py:421
  (64 shorter events, 1.6 us)
Async XLA Ops:
  4.1 35.4 %all-to-all-start = ((bf16[16,128,512]{2,1,0:T(8,128)(2,1)}), bf16[16,128,512]{2,1,0:T(8,128)(2,1)S(1)}, u32[]{:S(2)}, u32[]{:S(2)}) async-start(bf16[16,128,512]{2,1,0:T(8,128)(2,1)} %get-tuple-element.58), calls=%async_computation | async-start | bytes 4194304 | tf_op jit(solution)/shard_map/all_to_all | solution.py:444
  11.7 14.8 %collective-permute-start.1 = (bf16[528,512]{1,0:T(8,128)(2,1)}, bf16[528,512]{1,0:T(8,128)(2,1)S(1)}, u32[]{:S(2)}, u32[]{:S(2)}) collective-permute-start(bf16[528,512]{1,0:T(8,128)(2,1)} %get-tuple-element.50.p0_ref), channel_id=1, source_target_pairs={{0,6},{1,7},{2,0},{3,1},{4,2},{5,3},{6,4},{7,5},{8,14},{9,15},{10,... | collective-permute-start | bytes 1622024 | tf_op jit(solution)/shard_map/ppermute | solution.py:436
  15.5 13.9 %collective-permute-start = (bf16[528,512]{1,0:T(8,128)(2,1)}, bf16[528,512]{1,0:T(8,128)(2,1)S(1)}, u32[]{:S(2)}, u32[]{:S(2)}) collective-permute-start(bf16[528,512]{1,0:T(8,128)(2,1)} %get-tuple-element.50.p0_ref), channel_id=1, source_target_pairs={{0,2},{1,3},{2,4},{3,5},{4,6},{5,7},{6,0},{7,1},{8,10},{9,11},{10,... | collective-permute-start | bytes 1622024 | tf_op jit(solution)/shard_map/ppermute | solution.py:436
  26.4 21.8 %copy-start.5 = (bf16[528,512]{1,0:T(8,128)(2,1)}, bf16[528,512]{1,0:T(8,128)(2,1)S(1)}, u32[]{:S(2)}) copy-start(bf16[528,512]{1,0:T(8,128)(2,1)S(1)} %collective-permute-done.1.p3_ref) | copy-start | bytes 1622020
  29.4 0.8 copy-start.6
  30.3 18.5 %collective-permute-start.3 = (bf16[272,512]{1,0:T(8,128)(2,1)S(1)}, bf16[272,512]{1,0:T(8,128)(2,1)S(1)}, u32[]{:S(2)}, u32[]{:S(2)}) collective-permute-start(bf16[272,512]{1,0:T(8,128)(2,1)S(1)} %slice.19), channel_id=1, source_target_pairs={{0,6},{1,7},{2,0},{3,1},{4,2},{5,3},{6,4},{7,5},{8,14},{9,15},{10,... | collective-permute-start | bytes 835592 | tf_op jit(solution)/shard_map/ppermute | solution.py:436
  31.7 17.0 %collective-permute-start.2 = (bf16[256,512]{1,0:T(8,128)(2,1)S(1)}, bf16[256,512]{1,0:T(8,128)(2,1)}, u32[]{:S(2)}, u32[]{:S(2)}) collective-permute-start(bf16[256,512]{1,0:T(8,128)(2,1)S(1)} %slice.18), channel_id=1, source_target_pairs={{0,2},{1,3},{2,4},{3,5},{4,6},{5,7},{6,0},{7,1},{8,10},{9,11},{10,... | collective-permute-start | bytes 786440 | tf_op jit(solution)/shard_map/ppermute | solution.py:436
  39.5 1.3 copy-start.2
  40.8 38.1 %all-to-all-start.1 = ((bf16[16,128,512]{2,1,0:T(8,128)(2,1)}), bf16[16,128,512]{2,1,0:T(8,128)(2,1)S(1)}, u32[]{:S(2)}, u32[]{:S(2)}) async-start(bf16[16,128,512]{2,1,0:T(8,128)(2,1)} %get-tuple-element.63), calls=%async_computation.1 | async-start | bytes 4194304 | tf_op jit(solution)/shard_map/all_to_all | solution.py:444
  44.8 8.7 %collective-permute-start.4 = (bf16[528,512]{1,0:T(8,128)(2,1)}, bf16[528,512]{1,0:T(8,128)(2,1)}, u32[]{:S(2)}, u32[]{:S(2)}) collective-permute-start(bf16[528,512]{1,0:T(8,128)(2,1)} %get-tuple-element.50.p0_ref), channel_id=1, source_target_pairs={{0,1},{1,0},{2,3},{3,2},{4,5},{5,4},{6,7},{7,6},{8,9},{9,8},{10,11... | collective-permute-start | bytes 1622024 | tf_op jit(solution)/shard_map/ppermute | solution.py:440
  48.1 5.7 %collective-permute-start.5 = (bf16[528,512]{1,0:T(8,128)(2,1)}, bf16[528,512]{1,0:T(8,128)(2,1)}, u32[]{:S(2)}, u32[]{:S(2)}) collective-permute-start(bf16[528,512]{1,0:T(8,128)(2,1)} %copy-done.6), channel_id=1, source_target_pairs={{0,1},{1,0},{2,3},{3,2},{4,5},{5,4},{6,7},{7,6},{8,9},{9,8},{10,11... | collective-permute-start | bytes 1622024 | tf_op jit(solution)/shard_map/ppermute | solution.py:440
  48.2 5.6 %collective-permute-start.8 = (bf16[528,512]{1,0:T(8,128)(2,1)S(1)}, bf16[528,512]{1,0:T(8,128)(2,1)}, u32[]{:S(2)}, u32[]{:S(2)}) collective-permute-start(bf16[528,512]{1,0:T(8,128)(2,1)S(1)} %collective-permute-done.1.p3_ref), channel_id=1, source_target_pairs={{0,1},{1,0},{2,3},{3,2},{4,5},{5,4},{6,7},{7,6},{8,9},{9,8},{10,11... | collective-permute-start | bytes 1622024 | tf_op jit(solution)/shard_map/ppermute | solution.py:440
  48.6 5.2 %collective-permute-start.6 = (bf16[256,512]{1,0:T(8,128)(2,1)}, bf16[256,512]{1,0:T(8,128)(2,1)S(1)}, u32[]{:S(2)}, u32[]{:S(2)}) collective-permute-start(bf16[256,512]{1,0:T(8,128)(2,1)} %collective-permute-done.2.t2_ref), channel_id=1, source_target_pairs={{0,1},{1,0},{2,3},{3,2},{4,5},{5,4},{6,7},{7,6},{8,9},{9,8},{10,11... | collective-permute-start | bytes 786440 | tf_op jit(solution)/shard_map/ppermute | solution.py:440
  48.7 4.7 %copy-start.11 = (bf16[272,512]{1,0:T(8,128)(2,1)}, bf16[272,512]{1,0:T(8,128)(2,1)S(1)}, u32[]{:S(2)}) copy-start(bf16[272,512]{1,0:T(8,128)(2,1)S(1)} %collective-permute-done.3.b2_ref) | copy-start | bytes 835588
  48.7 5.1 %collective-permute-start.7 = (bf16[272,512]{1,0:T(8,128)(2,1)S(1)}, bf16[272,512]{1,0:T(8,128)(2,1)S(1)}, u32[]{:S(2)}, u32[]{:S(2)}) collective-permute-start(bf16[272,512]{1,0:T(8,128)(2,1)S(1)} %collective-permute-done.3.b2_ref), channel_id=1, source_target_pairs={{0,1},{1,0},{2,3},{3,2},{4,5},{5,4},{6,7},{7,6},{8,9},{9,8},{10,11... | collective-permute-start | bytes 835592 | tf_op jit(solution)/shard_map/ppermute | solution.py:440
  53.5 2.1 %collective-permute-start.9 = (bf16[16,64,128]{2,1,0:T(8,128)(2,1)}, bf16[16,64,128]{2,1,0:T(8,128)(2,1)}, u32[]{:S(2)}, u32[]{:S(2)}) collective-permute-start(bf16[16,64,128]{2,1,0:T(8,128)(2,1)} %get-tuple-element.60), channel_id=1, source_target_pairs={{0,1},{1,0},{2,3},{3,2},{4,5},{5,4},{6,7},{7,6},{8,9},{9,8},{10,11... | collective-permute-start | bytes 786440 | tf_op jit(solution)/shard_map/ppermute | solution.py:440
  53.9 1.8 %copy-start.13 = (bf16[256,512]{1,0:T(8,128)(2,1)}, bf16[256,512]{1,0:T(8,128)(2,1)S(1)}, u32[]{:S(2)}) copy-start(bf16[256,512]{1,0:T(8,128)(2,1)S(1)} %collective-permute-done.6.t6_ref) | copy-start | bytes 786436
  53.9 1.7 %copy-start.12 = (bf16[272,512]{1,0:T(8,128)(2,1)}, bf16[272,512]{1,0:T(8,128)(2,1)S(1)}, u32[]{:S(2)}) copy-start(bf16[272,512]{1,0:T(8,128)(2,1)S(1)} %collective-permute-done.7.b6_ref) | copy-start | bytes 835588
  79.0 6.8 %copy-start.1 = (bf16[16,128,512]{2,1,0:T(8,128)(2,1)}, bf16[16,128,512]{2,1,0:T(8,128)(2,1)S(1)}, u32[]{:S(2)}) copy-start(bf16[16,128,512]{2,1,0:T(8,128)(2,1)S(1)} %all-to-all-done.1.back_ref) | copy-start | bytes 6291460
  79.0 17.0 %all-to-all-start.2 = ((bf16[16,128,128]{2,1,0:T(8,128)(2,1)}), bf16[16,128,128]{2,1,0:T(8,128)(2,1)S(1)}, u32[]{:S(2)}, u32[]{:S(2)}) async-start(bf16[16,128,128]{2,1,0:T(8,128)(2,1)} %get-tuple-element.64), calls=%async_computation.2 | async-start | bytes 1048576 | tf_op jit(solution)/shard_map/all_to_all | solution.py:444
  88.9 14.8 %collective-permute-start.14 = (bf16[2,256,256]{2,1,0:T(8,128)(2,1)}, bf16[2,256,256]{2,1,0:T(8,128)(2,1)S(1)}, u32[]{:S(2)}, u32[]{:S(2)}) collective-permute-start(bf16[2,256,256]{2,1,0:T(8,128)(2,1)} %get-tuple-element.71), channel_id=1, source_target_pairs={{0,6},{1,7},{2,0},{3,1},{4,2},{5,3},{6,4},{7,5},{8,14},{9,15},{10,... | collective-permute-start | bytes 786440 | tf_op jit(solution)/shard_map/ppermute | solution.py:436
  92.7 11.0 %collective-permute-start.15 = (bf16[2,256,256]{2,1,0:T(8,128)(2,1)}, bf16[2,256,256]{2,1,0:T(8,128)(2,1)S(1)}, u32[]{:S(2)}, u32[]{:S(2)}) collective-permute-start(bf16[2,256,256]{2,1,0:T(8,128)(2,1)} %get-tuple-element.72), channel_id=1, source_target_pairs={{0,4},{1,5},{2,6},{3,7},{4,0},{5,1},{6,2},{7,3},{8,12},{9,13},{10,... | collective-permute-start | bytes 786440 | tf_op jit(solution)/shard_map/ppermute | solution.py:436
  92.7 15.3 %collective-permute-start.16 = (bf16[2,256,256]{2,1,0:T(8,128)(2,1)}, bf16[2,256,256]{2,1,0:T(8,128)(2,1)S(1)}, u32[]{:S(2)}, u32[]{:S(2)}) collective-permute-start(bf16[2,256,256]{2,1,0:T(8,128)(2,1)} %get-tuple-element.73), channel_id=1, source_target_pairs={{0,2},{1,3},{2,4},{3,5},{4,6},{5,7},{6,0},{7,1},{8,10},{9,11},{10,... | collective-permute-start | bytes 786440 | tf_op jit(solution)/shard_map/ppermute | solution.py:436
  93.4 2.3 %collective-permute-start.10 = (f32[8,128]{1,0:T(8,128)}, f32[8,128]{1,0:T(8,128)S(1)}, u32[]{:S(2)}, u32[]{:S(2)}) collective-permute-start(f32[8,128]{1,0:T(8,128)} %get-tuple-element.70.g0_ref), channel_id=1, source_target_pairs={{0,1},{1,0},{2,3},{3,2},{4,5},{5,4},{6,7},{7,6},{8,9},{9,8},{10,11... | collective-permute-start | bytes 12296 | tf_op jit(solution)/shard_map/ppermute | solution.py:440
  95.7 0.6 copy-start.21
  96.3 0.8 copy-start.4
  98.9 9.1 %collective-permute-start.13 = (bf16[144,128]{1,0:T(8,128)(2,1)}, bf16[144,128]{1,0:T(8,128)(2,1)S(1)}, u32[]{:S(2)}, u32[]{:S(2)}) collective-permute-start(bf16[144,128]{1,0:T(8,128)(2,1)} %shard_map.170.c0_ref), channel_id=1, source_target_pairs={{0,6},{1,7},{2,0},{3,1},{4,2},{5,3},{6,4},{7,5},{8,14},{9,15},{10,... | collective-permute-start | bytes 110600 | tf_op jit(solution)/shard_map/ppermute | solution.py:436
  102.4 5.7 %collective-permute-start.12 = (bf16[144,128]{1,0:T(8,128)(2,1)}, bf16[144,128]{1,0:T(8,128)(2,1)S(1)}, u32[]{:S(2)}, u32[]{:S(2)}) collective-permute-start(bf16[144,128]{1,0:T(8,128)(2,1)} %shard_map.170.c0_ref), channel_id=1, source_target_pairs={{0,4},{1,5},{2,6},{3,7},{4,0},{5,1},{6,2},{7,3},{8,12},{9,13},{10,... | collective-permute-start | bytes 110600 | tf_op jit(solution)/shard_map/ppermute | solution.py:436
  103.7 15.1 %copy-start.8 = (bf16[2,256,256]{2,1,0:T(8,128)(2,1)}, bf16[2,256,256]{2,1,0:T(8,128)(2,1)S(1)}, u32[]{:S(2)}) copy-start(bf16[2,256,256]{2,1,0:T(8,128)(2,1)S(1)} %collective-permute-done.14.r1_ref) | copy-start | bytes 786436
  103.7 5.4 %collective-permute-start.11 = (bf16[144,128]{1,0:T(8,128)(2,1)}, bf16[144,128]{1,0:T(8,128)(2,1)S(1)}, u32[]{:S(2)}, u32[]{:S(2)}) collective-permute-start(bf16[144,128]{1,0:T(8,128)(2,1)} %shard_map.170.c0_ref), channel_id=1, source_target_pairs={{0,2},{1,3},{2,4},{3,5},{4,6},{5,7},{6,0},{7,1},{8,10},{9,11},{10,... | collective-permute-start | bytes 110600 | tf_op jit(solution)/shard_map/ppermute | solution.py:436
  103.8 15.1 %copy-start.9 = (bf16[2,256,256]{2,1,0:T(8,128)(2,1)}, bf16[2,256,256]{2,1,0:T(8,128)(2,1)S(1)}, u32[]{:S(2)}) copy-start(bf16[2,256,256]{2,1,0:T(8,128)(2,1)S(1)} %collective-permute-done.15.r2_ref) | copy-start | bytes 786436
  108.1 10.8 %copy-start.10 = (bf16[2,256,256]{2,1,0:T(8,128)(2,1)}, bf16[2,256,256]{2,1,0:T(8,128)(2,1)S(1)}, u32[]{:S(2)}) copy-start(bf16[2,256,256]{2,1,0:T(8,128)(2,1)S(1)} %collective-permute-done.16.r3_ref) | copy-start | bytes 786436
  108.1 1.1 copy-start.18
  108.1 1.1 copy-start.19
  109.2 0.6 copy-start.20
  111.8 6.9 %copy-start.7 = (bf16[2,256,256]{2,1,0:T(8,128)(2,1)S(1)}, bf16[2,256,256]{2,1,0:T(8,128)(2,1)}, u32[]{:S(2)}) copy-start(bf16[2,256,256]{2,1,0:T(8,128)(2,1)} %get-tuple-element.83.r0_ref) | copy-start | bytes 786436
  111.8 24.2 %all-to-all-start.3 = ((bf16[16,336,128]{2,1,0:T(8,128)(2,1)}), bf16[16,336,128]{2,1,0:T(8,128)(2,1)S(1)}, u32[]{:S(2)}, u32[]{:S(2)}) async-start(bf16[16,336,128]{2,1,0:T(8,128)(2,1)} %shard_map.171), calls=%async_computation.3 | async-start | bytes 2752512 | tf_op jit(solution)/shard_map/all_to_all | solution.py:444
  118.9 4.1 %collective-permute-start.20 = (bf16[256,256]{1,0:T(8,128)(2,1)S(1)}, bf16[256,256]{1,0:T(8,128)(2,1)S(1)}, u32[]{:S(2)}, u32[]{:S(2)}) collective-permute-start(bf16[256,256]{1,0:T(8,128)(2,1)S(1)} %slice_bitcast_fusion), channel_id=1, source_target_pairs={{0,1},{1,0},{2,3},{3,2},{4,5},{5,4},{6,7},{7,6},{8,9},{9,8},{10,11... | collective-permute-start | bytes 393224 | tf_op jit(solution)/shard_map/ppermute | solution.py:440
  122.0 1.3 collective-permute-start.19
  122.1 1.4 collective-permute-start.18
  122.6 1.3 collective-permute-start.17
  123.0 0.9 copy-start.14
  123.4 0.7 copy-start.15
  123.6 0.7 copy-start.16
  123.9 0.6 copy-start.17
  136.1 4.6 %copy-start = (bf16[16,336,128]{2,1,0:T(8,128)(2,1)}, bf16[16,336,128]{2,1,0:T(8,128)(2,1)S(1)}, u32[]{:S(2)}) copy-start(bf16[16,336,128]{2,1,0:T(8,128)(2,1)S(1)} %all-to-all-done.3.mine_ref) | copy-start | bytes 4128772
  136.1 7.6 %collective-permute-start.21 = (bf16[16,336,128]{2,1,0:T(8,128)(2,1)S(1)}, bf16[16,336,128]{2,1,0:T(8,128)(2,1)S(1)}, u32[]{:S(2)}, u32[]{:S(2)}) collective-permute-start(bf16[16,336,128]{2,1,0:T(8,128)(2,1)S(1)} %all-to-all-done.3.mine_ref), channel_id=1, source_target_pairs={{0,1},{1,0},{2,3},{3,2},{4,5},{5,4},{6,7},{7,6},{8,9},{9,8},{10,11... | collective-permute-start | bytes 4128776 | tf_op jit(solution)/shard_map/ppermute | solution.py:440
  143.7 1.1 copy-start.3

commit v10 on v9

--- a/solution.py
+++ b/solution.py
@@ -159,7 +159,7 @@
 
 def attention_body(
     p0_ref, p1_ref, t2_ref, b2_ref, p3_ref, p4_ref, p5_ref, t6_ref, b6_ref, p7_ref, wqkv_ref, wo_ref, mine_ref, other_ref,
-    r0_ref, r1_ref, r2_ref, r3_ref, chunks_ref,
+    paya_ref, payb_ref, chunks_ref,
     y_ref, s_ref, qt_ref, kt_ref, k_ref, v_ref, vt_ref, w_ref, dq_ref, dk_ref, dv_ref, at_ref, ga_ref, sl_ref, qr_ref, gr_ref,
 ):
     pays = (p0_ref, p1_ref, (t2_ref, b2_ref), p3_ref, p4_ref, p5_ref, (t6_ref, b6_ref), p7_ref)
@@ -173,7 +173,7 @@
     def tail_of(pay):
         return pay[1][ROWS : PAY - ROWS, 0:ROWS] if isinstance(pay, tuple) else pay[2 * ROWS : PAY, 0:ROWS]
 
-    outs = (r0_ref, r1_ref, r2_ref, r3_ref)
+    outs = (paya_ref, payb_ref)
     z, core = position()
     row = lax.broadcasted_iota(jnp.int32, (HEAD, ROWS), 0)
     number = row.astype(F32)
@@ -256,8 +256,8 @@
         dkey = pull(dk_ref[r], y_ref[r, HEAD:128], s_ref[r, 1:2])
         first = jnp.concatenate([dquery, dkey], axis=0)
         second = jnp.concatenate([dv_ref[r], at_ref[r].astype(F32)], axis=0)
-        outs[r & 3][r >> 2, :, 0:128] = jnp.transpose(first).astype(BF16)
-        outs[r & 3][r >> 2, :, 128:256] = jnp.transpose(second).astype(BF16)
+        outs[r >> 2][r & 3, :, 0:128] = jnp.transpose(first).astype(BF16)
+        outs[r >> 2][r & 3, :, 128:256] = jnp.transpose(second).astype(BF16)
         left = jnp.concatenate([first, second[0:HEAD]], axis=0).astype(BF16)
         dw = dw + dot(left, normed_of(pay))
         dwo = dwo + dot(at_ref[r], grads_of(pay))
@@ -304,7 +304,13 @@
         out_ref[p] = whole
 
 
-def halo_body(counts_ref, back_ref, rows_ref, x_ref, out_ref, gain_grad_ref):
+def halo_body(
+    counts_ref, back_ref, rows_ref, x_ref, paya_ref, payb_ref,
+    out_ref, gain_grad_ref, r0_ref, r1_ref, r2_ref, r3_ref,
+):
+    for dz, r_ref in enumerate((r0_ref, r1_ref, r2_ref, r3_ref)):
+        r_ref[0] = paya_ref[dz]
+        r_ref[1] = payb_ref[dz]
     row = lax.broadcasted_iota(jnp.int32, (ROWS, CAP), 0)
     slot = lax.broadcasted_iota(jnp.int32, (ROWS, CAP), 1)
     total = jnp.zeros((ROWS, D), F32)
@@ -325,16 +331,16 @@
 
 
 def rows_body(
-    r0_ref, r1_ref, r2_ref, r3_ref, t0_ref, t1_ref, t2_ref, t3_ref, halo_ref, base_ref, x_ref,
+    r0_ref, r1_ref, r2_ref, r3_ref, halo_ref, base_ref, x_ref,
     gain_ref, grad_ref, wq_ref, wk_ref, wv_ref, wo_ref,
     out_ref, feature_ref, dq_ref, dk_ref, dv_ref, at_ref, heads_ref,
 ):
     left = lax.broadcasted_iota(jnp.int32, (ROWS, 128), 1) < HEAD
     z, core = position()
-    for dz, (r_ref, t_ref) in enumerate(zip((r0_ref, r1_ref, r2_ref, r3_ref), (t0_ref, t1_ref, t2_ref, t3_ref))):
+    for dz, r_ref in enumerate((r0_ref, r1_ref, r2_ref, r3_ref)):
         chip = (z + dz) & 3
         heads_ref[core * 4 + chip] = r_ref[0]
-        heads_ref[(1 - core) * 4 + chip] = t_ref[...]
+        heads_ref[(1 - core) * 4 + chip] = r_ref[1]
     for m in range(4):
         low, high = heads_ref[2 * m].astype(F32), heads_ref[2 * m + 1].astype(F32)
         low0, low1 = low[:, 0:128], low[:, 128:256]
@@ -481,9 +487,9 @@
         micros=4,
     )
 
-    *results, chunks = call(
+    pay_a, pay_b, chunks = call(
         attention_body,
-        (*[shape((2, ROWS, 256), BF16)] * 4, shape((DOM, 128, 128), BF16)),
+        (*[shape((4, ROWS, 256), BF16)] * 2, shape((DOM, 128, 128), BF16)),
         (*pays, wqkv, wo_head, mine, other_core(other)),
         scratch=[
             pltpu.VMEM((BLK, 128, ROWS), F32),
@@ -507,15 +513,13 @@
     )
     chunks = lax.optimization_barrier((chunks, back))[0]
     chunks = to_dom_peers(chunks)
-    halo, gain_part = call(
+    halo, gain_part, *results = call(
         halo_body,
-        (shape((ROWS, D), F32), shape((8, 128), F32)),
-        (send_counts, back, send_rows, x),
+        (shape((ROWS, D), F32), shape((8, 128), F32), *[shape((2, ROWS, 256), BF16)] * 4),
+        (send_counts, back, send_rows, x, pay_a, other_core(pay_b)),
         scalars=1,
         micros=3,
     )
-    *results, gain_part = lax.optimization_barrier((*results, gain_part))
-    results = [results[0]] + [along_chips(results[dz], -dz) for dz in (1, 2, 3)]
     chunk = call(
         chunk_sum_body,
         shape((CHUNK, 128), BF16),
@@ -524,18 +528,16 @@
         micros=1,
     )
     chunk_parts = [chunk] + [along_chips(chunk, step) for step in (1, 2, 3)]
-    *chunk_parts, r1, r2, r3 = lax.optimization_barrier((*chunk_parts, *results[1:]))
-    results = [results[0], r1, r2, r3]
     spread = call(
         spread_body, shape((DOM, SPREAD, 128), BF16), chunk_parts, scratch=[pltpu.VMEM((4, 80, 128), F32)], micros=1
     )
     spread, *results = lax.optimization_barrier((spread, *results))
     gathered = to_dom_peers(spread)
-    swapped = [other_core(part[1]) for part in results]
+    results = [results[0]] + [along_chips(results[dz], -dz) for dz in (1, 2, 3)]
     layer_out, feature_grad = call(
         rows_body,
         (shape((ROWS, D), BF16), shape((ROWS, D), BF16)),
-        (*results, *swapped, halo, base, x, gain_row, out_grad, wq, wk, wv, wo),
+        (*results, halo, base, x, gain_row, out_grad, wq, wk, wv, wo),
         scratch=[pltpu.VMEM((4, ROWS, 128), BF16)] * 4 + [pltpu.VMEM((BLK, ROWS, 256), BF16)],
         micros=2,
     )

time: 150 us -> 144 us (0.960)
  starting transfers between devices: 53.2 us -> 47.9 us
    ppermute x10, waiting for transfers between devices: 11.5 us -> 23.5 us  [along_chips(): return lax.ppermute(array, 'blk', chip_shift(step, 0))]
    all_to_all x4, waiting for transfers between devices: 14.2 us -> 4.14 us  [to_dom_peers(): return lax.all_to_all(array, 'dom', split_axis=0, concat_axis=0, tiled=True)]
    ppermute x12 -> x9, starting transfers between devices: 14.3 us -> 11.3 us  [other_core(): return lax.ppermute(array, 'blk', chip_shift(0, 1))]
    ppermute x10, starting transfers between devices: 13.6 us -> 11.4 us  [along_chips(): return lax.ppermute(array, 'blk', chip_shift(step, 0))]
    ppermute x12 -> x9, waiting for transfers between devices: 4.02 us -> 2.53 us  [other_core(): return lax.ppermute(array, 'blk', chip_shift(0, 1))]
    unnamed x44 -> x38, local copies, waits for them, and re-layouts: 5.66 us -> 5.94 us
  transfers between devices with their start and end apart: 26 -> 23, of which waited for: 14 -> 11; matrix products, arithmetic and copies ran while one was open for 1% -> 0% of each run, Pallas kernels for 33% -> 33%
where the time goes in v10:
time: 144 us
  Pallas kernels  58.7 us (41%)
  starting transfers between devices  47.9 us (33%)
  waiting for transfers between devices  30.1 us (21%)
  local copies, waits for them, and re-layouts  5.98 us (4%)
    pallas_call x8, Pallas kernels, call(): pl.pallas_call(body, out_shape=out_shape, in_specs=specs, out_specs=jax.t...  51.7 us
    all_to_all x4, starting transfers between devices, to_dom_peers(): return lax.all_to_all(array, 'dom', split_axis=0, concat_axis=0, tiled=True)  25.2 us
    ppermute x10, waiting for transfers between devices, along_chips(): return lax.ppermute(array, 'blk', chip_shift(step, 0))  23.5 us
    ppermute x10, starting transfers between devices, along_chips(): return lax.ppermute(array, 'blk', chip_shift(step, 0))  11.4 us
    ppermute x9, starting transfers between devices, other_core(): return lax.ppermute(array, 'blk', chip_shift(0, 1))  11.3 us
    unnamed x38, local copies, waits for them, and re-layouts  5.94 us
    all_to_all x4, waiting for transfers between devices, to_dom_peers(): return lax.all_to_all(array, 'dom', split_axis=0, concat_axis=0, tiled=True)  4.14 us
    pallas_call x1, Pallas kernels, in_halves(): pl.pallas_call(second_half_body, out_shape=(shape((5, D, D), F32), shape(...  4.01 us
  transfers between devices with their start and end apart: 23, of which 11 were waited for; matrix products, arithmetic and copies ran while one was open for 0% of the time, Pallas kernels for 33%

profile of v10, /device:TPU:1, one launch (start us, length us, event | category | flops | bytes accessed | tf_op | source)
XLA Modules:
  0.0 143.7 jit_solution(1056681718693853057)
XLA Ops:
  0.6 3.5 %shard_map.165 = (bf16[528,512]{1,0:T(8,128)(2,1)}, bf16[16,128,512]{2,1,0:T(8,128)(2,1)}) custom-call(s32[1,8]{1,0:T(1,128)} %pattern_ref.1, s32[16]{0:T(128)} %counts_ref.3, bf16[256,512]{1,0:T(8,128)(2,1)} %x_ref.7, f32[1,512]{1,0:T(1,128)} %bitcast.5, s32[1,256]{1,0:T(1,128)} %bitcast.11, bf16[256,512]{1,0:T(8,128)(2,1)} %grad_ref.7, s32[16,128]{1,0:T(8,128)} %rows_ref.3), custom_call_target="tpu_custom_call" | custom-call | flops 4000000000 | bytes 1048576 | tf_op jit(solution)/shard_map/pallas_call | solution.py:40
  4.1 7.6 %all-to-all-start = ((bf16[16,128,512]{2,1,0:T(8,128)(2,1)}), bf16[16,128,512]{2,1,0:T(8,128)(2,1)S(1)}, u32[]{:S(2)}, u32[]{:S(2)}) async-start(bf16[16,128,512]{2,1,0:T(8,128)(2,1)} %get-tuple-element.48), calls=%async_computation | async-start | bytes 4194304 | tf_op jit(solution)/shard_map/all_to_all | solution.py:450
  11.7 3.8 %collective-permute-start.1 = (bf16[528,512]{1,0:T(8,128)(2,1)}, bf16[528,512]{1,0:T(8,128)(2,1)S(1)}, u32[]{:S(2)}, u32[]{:S(2)}) collective-permute-start(bf16[528,512]{1,0:T(8,128)(2,1)} %get-tuple-element.40.p0_ref), channel_id=1, source_target_pairs={{0,6},{1,7},{2,0},{3,1},{4,2},{5,3},{6,4},{7,5},{8,14},{9,15},{10,... | collective-permute-start | bytes 1622024 | tf_op jit(solution)/shard_map/ppermute | solution.py:442
  15.5 8.9 %shard_map.166 = (bf16[1024,512]{1,0:T(8,128)(2,1)}, f32[256,128]{1,0:T(8,128)}, bf16[16,128,512]{2,1,0:T(8,128)(2,1)}, bf16[192,512]{1,0:T(8,128)(2,1)}, bf16[64,512]{1,0:T(8,128)(2,1)}) custom-call(s32[32,128]{1,0:T(8,128)} %bitcast.8, s32[32,128]{1,0:T(8,128)} %bitcast.9, bf16[256,512]{1,0:T(8,128)(2,1)} %grad_ref.7, bf16[512,512]{1,0:T(8,128)(2,1)} %w_ref.3, ...), custom_call_target="tpu_custom_call" | custom-call | flops 10000000000 | bytes 1048576 | tf_op jit(solution)/shard_map/pallas_call | solution.py:40
  24.5 2.0 %collective-permute-done.1.p3_ref = bf16[528,512]{1,0:T(8,128)(2,1)S(1)} collective-permute-done((bf16[528,512]{1,0:T(8,128)(2,1)}, bf16[528,512]{1,0:T(8,128)(2,1)S(1)}, u32[]{:S(2)}, u32[]{:S(2)}) %collective-permute-start.1) | collective-permute-done | bytes 540704 | tf_op jit(solution)/shard_map/ppermute | solution.py:442
  26.4 3.0 %collective-permute-done.p1_ref = bf16[528,512]{1,0:T(8,128)(2,1)S(1)} collective-permute-done((bf16[528,512]{1,0:T(8,128)(2,1)}, bf16[528,512]{1,0:T(8,128)(2,1)S(1)}, u32[]{:S(2)}, u32[]{:S(2)}) %collective-permute-start) | collective-permute-done | bytes 540704 | tf_op jit(solution)/shard_map/ppermute | solution.py:442
  29.5 0.4 collective-permute-start.3
  29.9 1.2 collective-permute-start.2
  31.1 2.7 %collective-permute-start.4 = (bf16[528,512]{1,0:T(8,128)(2,1)}, bf16[528,512]{1,0:T(8,128)(2,1)}, u32[]{:S(2)}, u32[]{:S(2)}) collective-permute-start(bf16[528,512]{1,0:T(8,128)(2,1)} %get-tuple-element.40.p0_ref), channel_id=1, source_target_pairs={{0,1},{1,0},{2,3},{3,2},{4,5},{5,4},{6,7},{7,6},{8,9},{9,8},{10,11... | collective-permute-start | bytes 1622024 | tf_op jit(solution)/shard_map/ppermute | solution.py:446
  33.8 0.5 collective-permute-start.8
  34.3 2.6 %collective-permute-done.2.t2_ref = bf16[256,512]{1,0:T(8,128)(2,1)} collective-permute-done((bf16[256,512]{1,0:T(8,128)(2,1)S(1)}, bf16[256,512]{1,0:T(8,128)(2,1)}, u32[]{:S(2)}, u32[]{:S(2)}) %collective-permute-start.2) | collective-permute-done | bytes 262176 | tf_op jit(solution)/shard_map/ppermute | solution.py:442
  36.9 3.1 %collective-permute-start.6 = (bf16[256,512]{1,0:T(8,128)(2,1)}, bf16[256,512]{1,0:T(8,128)(2,1)}, u32[]{:S(2)}, u32[]{:S(2)}) collective-permute-start(bf16[256,512]{1,0:T(8,128)(2,1)} %collective-permute-done.2.t2_ref), channel_id=1, source_target_pairs={{0,1},{1,0},{2,3},{3,2},{4,5},{5,4},{6,7},{7,6},{8,9},{9,8},{10,11... | collective-permute-start | bytes 786440 | tf_op jit(solution)/shard_map/ppermute | solution.py:446
  40.0 0.1 collective-permute-start.7
  40.1 1.3 copy-done.2
  41.4 6.4 %all-to-all-start.1 = ((bf16[16,128,512]{2,1,0:T(8,128)(2,1)}), bf16[16,128,512]{2,1,0:T(8,128)(2,1)S(1)}, u32[]{:S(2)}, u32[]{:S(2)}) async-start(bf16[16,128,512]{2,1,0:T(8,128)(2,1)} %get-tuple-element.53), calls=%async_computation.1 | async-start | bytes 4194304 | tf_op jit(solution)/shard_map/all_to_all | solution.py:450
  47.8 4.3 %shard_map.167 = (f32[256,512]{1,0:T(8,128)}, bf16[16,64,128]{2,1,0:T(8,128)(2,1)}, bf16[16,64,128]{2,1,0:T(8,128)(2,1)}) custom-call(bf16[1024,512]{1,0:T(8,128)(2,1)} %get-tuple-element.46.counts_t_ref, f32[256,128]{1,0:T(8,128)} %get-tuple-element.47.degree_ref, bf16[16,128,512]{2,1,0:T(8,128)(2,1)} %copy-done.2, bf16[256,512]{1,0:T(8,128)(2,1)} %x_ref.7, ...), custom_call_target="tpu_custom_call" | custom-call | flops 4000000000 | bytes 1048576 | tf_op jit(solution)/shard_map/pallas_call | solution.py:40
  52.1 1.0 collective-permute-start.9
  53.1 1.5 %collective-permute-done.9.other_ref = bf16[16,64,128]{2,1,0:T(8,128)(2,1)} collective-permute-done((bf16[16,64,128]{2,1,0:T(8,128)(2,1)}, bf16[16,64,128]{2,1,0:T(8,128)(2,1)}, u32[]{:S(2)}, u32[]{:S(2)}) %collective-permute-start.9) | collective-permute-done | bytes 262176 | tf_op jit(solution)/shard_map/ppermute | solution.py:446
  54.6 23.3 %shard_map.168 = (bf16[4,256,256]{2,1,0:T(8,128)(2,1)}, bf16[4,256,256]{2,1,0:T(8,128)(2,1)}, bf16[16,128,128]{2,1,0:T(8,128)(2,1)}) custom-call(bf16[528,512]{1,0:T(8,128)(2,1)} %get-tuple-element.40.p0_ref, bf16[528,512]{1,0:T(8,128)(2,1)} %copy-done.6, bf16[256,512]{1,0:T(8,128)(2,1)} %collective-permute-done.2.t2_ref, bf16[272,512]{1,0:T(8,128)(2,1)} %copy-done.8, ...), custom_call_target="tpu_custom_call" | custom-call | flops 12000000000 | bytes 1048576 | tf_op jit(solution)/shard_map/pallas_call | solution.py:40
  77.9 0.4 collective-permute-start.10
  78.3 6.9 %all-to-all-start.2 = ((bf16[16,128,128]{2,1,0:T(8,128)(2,1)}), bf16[16,128,128]{2,1,0:T(8,128)(2,1)S(1)}, u32[]{:S(2)}, u32[]{:S(2)}) async-start(bf16[16,128,128]{2,1,0:T(8,128)(2,1)} %get-tuple-element.54), calls=%async_computation.2 | async-start | bytes 1048576 | tf_op jit(solution)/shard_map/all_to_all | solution.py:450
  85.3 0.8 copy-done.7
  86.0 3.8 %shard_map.169 = (f32[256,512]{1,0:T(8,128)}, f32[8,128]{1,0:T(8,128)}, bf16[2,256,256]{2,1,0:T(8,128)(2,1)}, bf16[2,256,256]{2,1,0:T(8,128)(2,1)}, bf16[2,256,2...) custom-call(s32[16]{0:T(128)} %counts_ref.3, bf16[16,128,512]{2,1,0:T(8,128)(2,1)} %copy-done.1, s32[16,128]{1,0:T(8,128)} %rows_ref.3, ...), custom_call_target="tpu_custom_call" | custom-call | flops 3000000000 | bytes 1048576 | tf_op jit(solution)/shard_map/pallas_call | solution.py:40
  89.8 0.4 collective-permute-start.11
  90.2 1.0 collective-permute-done.11.g1_ref
  91.3 4.1 %all-to-all-done.2.in_ref = bf16[16,128,128]{2,1,0:T(8,128)(2,1)S(1)} async-done(((bf16[16,128,128]{2,1,0:T(8,128)(2,1)}), bf16[16,128,128]{2,1,0:T(8,128)(2,1)S(1)}, u32[]{:S(2)}, u32[]{:S(2)}) %all-to-all-start.2) | async-done | bytes 524320 | tf_op jit(solution)/shard_map/all_to_all | solution.py:450
  95.4 0.8 copy-done.4
  96.2 1.8 %shard_map.170.c0_ref = bf16[144,128]{1,0:T(8,128)(2,1)} custom-call(bf16[16,128,128]{2,1,0:T(8,128)(2,1)} %copy-done.4, f32[8,128]{1,0:T(8,128)} %get-tuple-element.57.g0_ref, f32[8,128]{1,0:T(8,128)} %copy-done.18, bf16[192,512]{1,0:T(8,128)(2,1)} %get-tuple-element.44.wqkv_ref), custom_call_target="tpu_custom_call" | custom-call | flops 1000000000 | bytes 1048576 | tf_op jit(solution)/shard_map/pallas_call | solution.py:40
  98.0 3.3 %collective-permute-start.14 = (bf16[144,128]{1,0:T(8,128)(2,1)}, bf16[144,128]{1,0:T(8,128)(2,1)S(1)}, u32[]{:S(2)}, u32[]{:S(2)}) collective-permute-start(bf16[144,128]{1,0:T(8,128)(2,1)} %shard_map.170.c0_ref), channel_id=1, source_target_pairs={{0,6},{1,7},{2,0},{3,1},{4,2},{5,3},{6,4},{7,5},{8,14},{9,15},{10,... | collective-permute-start | bytes 110600 | tf_op jit(solution)/shard_map/ppermute | solution.py:442
  101.3 0.7 collective-permute-start.12
  102.0 0.7 collective-permute-done.14.c3_ref
  102.6 3.2 %collective-permute-done.13.c2_ref = bf16[144,128]{1,0:T(8,128)(2,1)S(1)} collective-permute-done((bf16[144,128]{1,0:T(8,128)(2,1)}, bf16[144,128]{1,0:T(8,128)(2,1)S(1)}, u32[]{:S(2)}, u32[]{:S(2)}) %collective-permute-start.13) | collective-permute-done | bytes 36896 | tf_op jit(solution)/shard_map/ppermute | solution.py:442
  105.9 0.6 copy-done.16
  106.5 0.6 copy-done.17
  107.1 2.1 %shard_map.171 = bf16[16,336,128]{2,1,0:T(8,128)(2,1)} custom-call(bf16[144,128]{1,0:T(8,128)(2,1)} %shard_map.170.c0_ref, bf16[144,128]{1,0:T(8,128)(2,1)} %copy-done.17, bf16[144,128]{1,0:T(8,128)(2,1)} %copy-done.16, bf16[144,128]{1,0:T(8,128)(2,1)} %copy-done.15), custom_call_target="tpu_custom_call" | custom-call | flops 1000000000 | bytes 1048576 | tf_op jit(solution)/shard_map/pallas_call | solution.py:40
  109.2 4.3 %all-to-all-start.3 = ((bf16[16,336,128]{2,1,0:T(8,128)(2,1)}), bf16[16,336,128]{2,1,0:T(8,128)(2,1)S(1)}, u32[]{:S(2)}, u32[]{:S(2)}) async-start(bf16[16,336,128]{2,1,0:T(8,128)(2,1)} %shard_map.171), calls=%async_computation.3 | async-start | bytes 2752512 | tf_op jit(solution)/shard_map/all_to_all | solution.py:450
  113.5 0.1 collective-permute-start.15
  113.6 1.1 collective-permute-start.16
  114.8 0.8 collective-permute-start.17
  115.5 3.3 %collective-permute-done.15.r1_ref = bf16[2,256,256]{2,1,0:T(8,128)(2,1)S(1)} collective-permute-done((bf16[2,256,256]{2,1,0:T(8,128)(2,1)S(1)}, bf16[2,256,256]{2,1,0:T(8,128)(2,1)S(1)}, u32[]{:S(2)}, u32[]{:S(2)}) %collective-permute-start.15) | collective-permute-done | bytes 262176 | tf_op jit(solution)/shard_map/ppermute | solution.py:442
  118.8 1.7 %collective-permute-done.16.r2_ref = bf16[2,256,256]{2,1,0:T(8,128)(2,1)S(1)} collective-permute-done((bf16[2,256,256]{2,1,0:T(8,128)(2,1)S(1)}, bf16[2,256,256]{2,1,0:T(8,128)(2,1)S(1)}, u32[]{:S(2)}, u32[]{:S(2)}) %collective-permute-start.16) | collective-permute-done | bytes 262176 | tf_op jit(solution)/shard_map/ppermute | solution.py:442
  120.5 7.0 %collective-permute-done.17.r3_ref = bf16[2,256,256]{2,1,0:T(8,128)(2,1)S(1)} collective-permute-done((bf16[2,256,256]{2,1,0:T(8,128)(2,1)S(1)}, bf16[2,256,256]{2,1,0:T(8,128)(2,1)S(1)}, u32[]{:S(2)}, u32[]{:S(2)}) %collective-permute-start.17) | collective-permute-done | bytes 262176 | tf_op jit(solution)/shard_map/ppermute | solution.py:442
  127.5 0.7 copy-done.14
  128.2 4.0 %shard_map.172 = (bf16[256,512]{1,0:T(8,128)(2,1)}, bf16[256,512]{1,0:T(8,128)(2,1)}) custom-call(bf16[2,256,256]{2,1,0:T(8,128)(2,1)} %get-tuple-element.63.r0_ref, bf16[2,256,256]{2,1,0:T(8,128)(2,1)} %copy-done.12, bf16[2,256,256]{2,1,0:T(8,128)(2,1)} %copy-done.13, bf16[2,256,256]{2,1,0:T(8,128)(2,1)} %copy-done.14, ...), custom_call_target="tpu_custom_call" | custom-call | flops 2000000000 | bytes 1048576 | tf_op jit(solution)/shard_map/pallas_call | solution.py:40
  132.2 3.1 %collective-permute-start.18 = (bf16[16,336,128]{2,1,0:T(8,128)(2,1)S(1)}, bf16[16,336,128]{2,1,0:T(8,128)(2,1)S(1)}, u32[]{:S(2)}, u32[]{:S(2)}) collective-permute-start(bf16[16,336,128]{2,1,0:T(8,128)(2,1)S(1)} %all-to-all-done.3.mine_ref), channel_id=1, source_target_pairs={{0,1},{1,0},{2,3},{3,2},{4,5},{5,4},{6,7},{7,6},{8,9},{9,8},{10,11... | collective-permute-start | bytes 4128776 | tf_op jit(solution)/shard_map/ppermute | solution.py:446
  135.4 3.0 %shard_map.173.before_hbm = f32[5,512,512]{2,1,0:T(8,128)} custom-call(bf16[16,336,128]{2,1,0:T(8,128)(2,1)} %copy-done), custom_call_target="tpu_custom_call" | custom-call | flops 3000000000 | bytes 1048576 | tf_op jit(solution)/shard_map/pallas_call | solution.py:423
  138.4 1.1 copy-done.3
  139.5 4.0 %shard_map.174 = (f32[5,512,512]{2,1,0:T(8,128)}, f32[1,512]{1,0:T(1,128)}) custom-call(f32[5,512,512]{2,1,0:T(8,128)} %shard_map.173.before_hbm, bf16[16,336,128]{2,1,0:T(8,128)(2,1)} %copy-done, bf16[16,336,128]{2,1,0:T(8,128)(2,1)} %copy-done.3, f32[1,512]{1,0:T(1,128)} %bitcast.7), custom_call_target="tpu_custom_call", output_to_operand_aliasing={{0}: (0, {})} | custom-call | tf_op jit(solution)/shard_map/pallas_call | solution.py:427
  (48 shorter events, 0.1 us)
Async XLA Ops:
  4.1 36.0 %all-to-all-start = ((bf16[16,128,512]{2,1,0:T(8,128)(2,1)}), bf16[16,128,512]{2,1,0:T(8,128)(2,1)S(1)}, u32[]{:S(2)}, u32[]{:S(2)}) async-start(bf16[16,128,512]{2,1,0:T(8,128)(2,1)} %get-tuple-element.48), calls=%async_computation | async-start | bytes 4194304 | tf_op jit(solution)/shard_map/all_to_all | solution.py:450
  11.7 14.8 %collective-permute-start.1 = (bf16[528,512]{1,0:T(8,128)(2,1)}, bf16[528,512]{1,0:T(8,128)(2,1)S(1)}, u32[]{:S(2)}, u32[]{:S(2)}) collective-permute-start(bf16[528,512]{1,0:T(8,128)(2,1)} %get-tuple-element.40.p0_ref), channel_id=1, source_target_pairs={{0,6},{1,7},{2,0},{3,1},{4,2},{5,3},{6,4},{7,5},{8,14},{9,15},{10,... | collective-permute-start | bytes 1622024 | tf_op jit(solution)/shard_map/ppermute | solution.py:442
  15.5 13.9 %collective-permute-start = (bf16[528,512]{1,0:T(8,128)(2,1)}, bf16[528,512]{1,0:T(8,128)(2,1)S(1)}, u32[]{:S(2)}, u32[]{:S(2)}) collective-permute-start(bf16[528,512]{1,0:T(8,128)(2,1)} %get-tuple-element.40.p0_ref), channel_id=1, source_target_pairs={{0,2},{1,3},{2,4},{3,5},{4,6},{5,7},{6,0},{7,1},{8,10},{9,11},{10,... | collective-permute-start | bytes 1622024 | tf_op jit(solution)/shard_map/ppermute | solution.py:442
  26.4 15.0 %copy-start.5 = (bf16[528,512]{1,0:T(8,128)(2,1)}, bf16[528,512]{1,0:T(8,128)(2,1)S(1)}, u32[]{:S(2)}) copy-start(bf16[528,512]{1,0:T(8,128)(2,1)S(1)} %collective-permute-done.1.p3_ref) | copy-start | bytes 1622020
  29.5 12.0 %copy-start.6 = (bf16[528,512]{1,0:T(8,128)(2,1)}, bf16[528,512]{1,0:T(8,128)(2,1)S(1)}, u32[]{:S(2)}) copy-start(bf16[528,512]{1,0:T(8,128)(2,1)S(1)} %collective-permute-done.p1_ref) | copy-start | bytes 1622020
  29.5 10.5 %collective-permute-start.3 = (bf16[272,512]{1,0:T(8,128)(2,1)S(1)}, bf16[272,512]{1,0:T(8,128)(2,1)S(1)}, u32[]{:S(2)}, u32[]{:S(2)}) collective-permute-start(bf16[272,512]{1,0:T(8,128)(2,1)S(1)} %slice.7), channel_id=1, source_target_pairs={{0,6},{1,7},{2,0},{3,1},{4,2},{5,3},{6,4},{7,5},{8,14},{9,15},{10,... | collective-permute-start | bytes 835592 | tf_op jit(solution)/shard_map/ppermute | solution.py:442
  29.9 7.0 %collective-permute-start.2 = (bf16[256,512]{1,0:T(8,128)(2,1)S(1)}, bf16[256,512]{1,0:T(8,128)(2,1)}, u32[]{:S(2)}, u32[]{:S(2)}) collective-permute-start(bf16[256,512]{1,0:T(8,128)(2,1)S(1)} %slice.6), channel_id=1, source_target_pairs={{0,2},{1,3},{2,4},{3,5},{4,6},{5,7},{6,0},{7,1},{8,10},{9,11},{10,... | collective-permute-start | bytes 786440 | tf_op jit(solution)/shard_map/ppermute | solution.py:442
  31.1 21.0 %collective-permute-start.4 = (bf16[528,512]{1,0:T(8,128)(2,1)}, bf16[528,512]{1,0:T(8,128)(2,1)}, u32[]{:S(2)}, u32[]{:S(2)}) collective-permute-start(bf16[528,512]{1,0:T(8,128)(2,1)} %get-tuple-element.40.p0_ref), channel_id=1, source_target_pairs={{0,1},{1,0},{2,3},{3,2},{4,5},{5,4},{6,7},{7,6},{8,9},{9,8},{10,11... | collective-permute-start | bytes 1622024 | tf_op jit(solution)/shard_map/ppermute | solution.py:446
  33.8 19.3 %collective-permute-start.5 = (bf16[528,512]{1,0:T(8,128)(2,1)S(1)}, bf16[528,512]{1,0:T(8,128)(2,1)}, u32[]{:S(2)}, u32[]{:S(2)}) collective-permute-start(bf16[528,512]{1,0:T(8,128)(2,1)S(1)} %collective-permute-done.p1_ref), channel_id=1, source_target_pairs={{0,1},{1,0},{2,3},{3,2},{4,5},{5,4},{6,7},{7,6},{8,9},{9,8},{10,11... | collective-permute-start | bytes 1622024 | tf_op jit(solution)/shard_map/ppermute | solution.py:446
  33.8 19.3 %collective-permute-start.8 = (bf16[528,512]{1,0:T(8,128)(2,1)S(1)}, bf16[528,512]{1,0:T(8,128)(2,1)}, u32[]{:S(2)}, u32[]{:S(2)}) collective-permute-start(bf16[528,512]{1,0:T(8,128)(2,1)S(1)} %collective-permute-done.1.p3_ref), channel_id=1, source_target_pairs={{0,1},{1,0},{2,3},{3,2},{4,5},{5,4},{6,7},{7,6},{8,9},{9,8},{10,11... | collective-permute-start | bytes 1622024 | tf_op jit(solution)/shard_map/ppermute | solution.py:446
  36.9 16.2 %collective-permute-start.6 = (bf16[256,512]{1,0:T(8,128)(2,1)}, bf16[256,512]{1,0:T(8,128)(2,1)}, u32[]{:S(2)}, u32[]{:S(2)}) collective-permute-start(bf16[256,512]{1,0:T(8,128)(2,1)} %collective-permute-done.2.t2_ref), channel_id=1, source_target_pairs={{0,1},{1,0},{2,3},{3,2},{4,5},{5,4},{6,7},{7,6},{8,9},{9,8},{10,11... | collective-permute-start | bytes 786440 | tf_op jit(solution)/shard_map/ppermute | solution.py:446
  40.0 12.1 %copy-start.8 = (bf16[272,512]{1,0:T(8,128)(2,1)}, bf16[272,512]{1,0:T(8,128)(2,1)S(1)}, u32[]{:S(2)}) copy-start(bf16[272,512]{1,0:T(8,128)(2,1)S(1)} %collective-permute-done.3.b2_ref) | copy-start | bytes 835588
  40.0 13.1 %collective-permute-start.7 = (bf16[272,512]{1,0:T(8,128)(2,1)S(1)}, bf16[272,512]{1,0:T(8,128)(2,1)}, u32[]{:S(2)}, u32[]{:S(2)}) collective-permute-start(bf16[272,512]{1,0:T(8,128)(2,1)S(1)} %collective-permute-done.3.b2_ref), channel_id=1, source_target_pairs={{0,1},{1,0},{2,3},{3,2},{4,5},{5,4},{6,7},{7,6},{8,9},{9,8},{10,11... | collective-permute-start | bytes 835592 | tf_op jit(solution)/shard_map/ppermute | solution.py:446
  40.1 1.3 copy-start.2
  41.4 36.9 %all-to-all-start.1 = ((bf16[16,128,512]{2,1,0:T(8,128)(2,1)}), bf16[16,128,512]{2,1,0:T(8,128)(2,1)S(1)}, u32[]{:S(2)}, u32[]{:S(2)}) async-start(bf16[16,128,512]{2,1,0:T(8,128)(2,1)} %get-tuple-element.53), calls=%async_computation.1 | async-start | bytes 4194304 | tf_op jit(solution)/shard_map/all_to_all | solution.py:450
  52.1 2.5 %collective-permute-start.9 = (bf16[16,64,128]{2,1,0:T(8,128)(2,1)}, bf16[16,64,128]{2,1,0:T(8,128)(2,1)}, u32[]{:S(2)}, u32[]{:S(2)}) collective-permute-start(bf16[16,64,128]{2,1,0:T(8,128)(2,1)} %get-tuple-element.50), channel_id=1, source_target_pairs={{0,1},{1,0},{2,3},{3,2},{4,5},{5,4},{6,7},{7,6},{8,9},{9,8},{10,11... | collective-permute-start | bytes 786440 | tf_op jit(solution)/shard_map/ppermute | solution.py:446
  77.9 7.3 %collective-permute-start.10 = (bf16[4,256,256]{2,1,0:T(8,128)(2,1)}, bf16[4,256,256]{2,1,0:T(8,128)(2,1)S(1)}, u32[]{:S(2)}, u32[]{:S(2)}) collective-permute-start(bf16[4,256,256]{2,1,0:T(8,128)(2,1)} %get-tuple-element.56), channel_id=1, source_target_pairs={{0,1},{1,0},{2,3},{3,2},{4,5},{5,4},{6,7},{7,6},{8,9},{9,8},{10,11... | collective-permute-start | bytes 1572872 | tf_op jit(solution)/shard_map/ppermute | solution.py:446
  78.3 7.0 %copy-start.1 = (bf16[16,128,512]{2,1,0:T(8,128)(2,1)}, bf16[16,128,512]{2,1,0:T(8,128)(2,1)S(1)}, u32[]{:S(2)}) copy-start(bf16[16,128,512]{2,1,0:T(8,128)(2,1)S(1)} %all-to-all-done.1.back_ref) | copy-start | bytes 6291460
  78.3 17.1 %all-to-all-start.2 = ((bf16[16,128,128]{2,1,0:T(8,128)(2,1)}), bf16[16,128,128]{2,1,0:T(8,128)(2,1)S(1)}, u32[]{:S(2)}, u32[]{:S(2)}) async-start(bf16[16,128,128]{2,1,0:T(8,128)(2,1)} %get-tuple-element.54), calls=%async_computation.2 | async-start | bytes 1048576 | tf_op jit(solution)/shard_map/all_to_all | solution.py:450
  85.2 0.8 copy-start.7
  89.8 1.5 %collective-permute-start.11 = (f32[8,128]{1,0:T(8,128)}, f32[8,128]{1,0:T(8,128)S(1)}, u32[]{:S(2)}, u32[]{:S(2)}) collective-permute-start(f32[8,128]{1,0:T(8,128)} %get-tuple-element.57.g0_ref), channel_id=1, source_target_pairs={{0,1},{1,0},{2,3},{3,2},{4,5},{5,4},{6,7},{7,6},{8,9},{9,8},{10,11... | collective-permute-start | bytes 12296 | tf_op jit(solution)/shard_map/ppermute | solution.py:446
  91.3 4.1 %copy-start.18 = (f32[8,128]{1,0:T(8,128)}, f32[8,128]{1,0:T(8,128)S(1)}, u32[]{:S(2)}) copy-start(f32[8,128]{1,0:T(8,128)S(1)} %collective-permute-done.11.g1_ref) | copy-start | bytes 12292
  95.4 0.8 copy-start.4
  98.0 4.6 %collective-permute-start.14 = (bf16[144,128]{1,0:T(8,128)(2,1)}, bf16[144,128]{1,0:T(8,128)(2,1)S(1)}, u32[]{:S(2)}, u32[]{:S(2)}) collective-permute-start(bf16[144,128]{1,0:T(8,128)(2,1)} %shard_map.170.c0_ref), channel_id=1, source_target_pairs={{0,6},{1,7},{2,0},{3,1},{4,2},{5,3},{6,4},{7,5},{8,14},{9,15},{10,... | collective-permute-start | bytes 110600 | tf_op jit(solution)/shard_map/ppermute | solution.py:442
  101.3 4.6 %collective-permute-start.13 = (bf16[144,128]{1,0:T(8,128)(2,1)}, bf16[144,128]{1,0:T(8,128)(2,1)S(1)}, u32[]{:S(2)}, u32[]{:S(2)}) collective-permute-start(bf16[144,128]{1,0:T(8,128)(2,1)} %shard_map.170.c0_ref), channel_id=1, source_target_pairs={{0,4},{1,5},{2,6},{3,7},{4,0},{5,1},{6,2},{7,3},{8,12},{9,13},{10,... | collective-permute-start | bytes 110600 | tf_op jit(solution)/shard_map/ppermute | solution.py:442
  101.3 4.6 %collective-permute-start.12 = (bf16[144,128]{1,0:T(8,128)(2,1)}, bf16[144,128]{1,0:T(8,128)(2,1)S(1)}, u32[]{:S(2)}, u32[]{:S(2)}) collective-permute-start(bf16[144,128]{1,0:T(8,128)(2,1)} %shard_map.170.c0_ref), channel_id=1, source_target_pairs={{0,2},{1,3},{2,4},{3,5},{4,6},{5,7},{6,0},{7,1},{8,10},{9,11},{10,... | collective-permute-start | bytes 110600 | tf_op jit(solution)/shard_map/ppermute | solution.py:442
  102.6 3.3 %copy-start.15 = (bf16[144,128]{1,0:T(8,128)(2,1)}, bf16[144,128]{1,0:T(8,128)(2,1)S(1)}, u32[]{:S(2)}) copy-start(bf16[144,128]{1,0:T(8,128)(2,1)S(1)} %collective-permute-done.14.c3_ref) | copy-start | bytes 110596
  105.9 0.6 copy-start.16
  106.5 0.6 copy-start.17
  109.2 4.3 %copy-start.11 = (bf16[2,256,256]{2,1,0:T(8,128)(2,1)S(1)}, bf16[2,256,256]{2,1,0:T(8,128)(2,1)}, u32[]{:S(2)}) copy-start(bf16[2,256,256]{2,1,0:T(8,128)(2,1)} %get-tuple-element.64) | copy-start | bytes 786436
  109.2 4.4 %copy-start.10 = (bf16[2,256,256]{2,1,0:T(8,128)(2,1)S(1)}, bf16[2,256,256]{2,1,0:T(8,128)(2,1)}, u32[]{:S(2)}) copy-start(bf16[2,256,256]{2,1,0:T(8,128)(2,1)} %get-tuple-element.65) | copy-start | bytes 786436
  109.2 5.6 %copy-start.9 = (bf16[2,256,256]{2,1,0:T(8,128)(2,1)S(1)}, bf16[2,256,256]{2,1,0:T(8,128)(2,1)}, u32[]{:S(2)}) copy-start(bf16[2,256,256]{2,1,0:T(8,128)(2,1)} %get-tuple-element.66) | copy-start | bytes 786436
  109.2 23.0 %all-to-all-start.3 = ((bf16[16,336,128]{2,1,0:T(8,128)(2,1)}), bf16[16,336,128]{2,1,0:T(8,128)(2,1)S(1)}, u32[]{:S(2)}, u32[]{:S(2)}) async-start(bf16[16,336,128]{2,1,0:T(8,128)(2,1)} %shard_map.171), calls=%async_computation.3 | async-start | bytes 2752512 | tf_op jit(solution)/shard_map/all_to_all | solution.py:450
  113.5 5.3 %collective-permute-start.15 = (bf16[2,256,256]{2,1,0:T(8,128)(2,1)S(1)}, bf16[2,256,256]{2,1,0:T(8,128)(2,1)S(1)}, u32[]{:S(2)}, u32[]{:S(2)}) collective-permute-start(bf16[2,256,256]{2,1,0:T(8,128)(2,1)S(1)} %copy-done.11), channel_id=1, source_target_pairs={{0,6},{1,7},{2,0},{3,1},{4,2},{5,3},{6,4},{7,5},{8,14},{9,15},{10,... | collective-permute-start | bytes 786440 | tf_op jit(solution)/shard_map/ppermute | solution.py:442
  113.6 6.9 %collective-permute-start.16 = (bf16[2,256,256]{2,1,0:T(8,128)(2,1)S(1)}, bf16[2,256,256]{2,1,0:T(8,128)(2,1)S(1)}, u32[]{:S(2)}, u32[]{:S(2)}) collective-permute-start(bf16[2,256,256]{2,1,0:T(8,128)(2,1)S(1)} %copy-done.10), channel_id=1, source_target_pairs={{0,4},{1,5},{2,6},{3,7},{4,0},{5,1},{6,2},{7,3},{8,12},{9,13},{10,... | collective-permute-start | bytes 786440 | tf_op jit(solution)/shard_map/ppermute | solution.py:442
  114.8 12.8 %collective-permute-start.17 = (bf16[2,256,256]{2,1,0:T(8,128)(2,1)S(1)}, bf16[2,256,256]{2,1,0:T(8,128)(2,1)S(1)}, u32[]{:S(2)}, u32[]{:S(2)}) collective-permute-start(bf16[2,256,256]{2,1,0:T(8,128)(2,1)S(1)} %copy-done.9), channel_id=1, source_target_pairs={{0,2},{1,3},{2,4},{3,5},{4,6},{5,7},{6,0},{7,1},{8,10},{9,11},{10,... | collective-permute-start | bytes 786440 | tf_op jit(solution)/shard_map/ppermute | solution.py:442
  118.8 8.7 %copy-start.12 = (bf16[2,256,256]{2,1,0:T(8,128)(2,1)}, bf16[2,256,256]{2,1,0:T(8,128)(2,1)S(1)}, u32[]{:S(2)}) copy-start(bf16[2,256,256]{2,1,0:T(8,128)(2,1)S(1)} %collective-permute-done.15.r1_ref) | copy-start | bytes 786436
  120.5 7.0 %copy-start.13 = (bf16[2,256,256]{2,1,0:T(8,128)(2,1)}, bf16[2,256,256]{2,1,0:T(8,128)(2,1)S(1)}, u32[]{:S(2)}) copy-start(bf16[2,256,256]{2,1,0:T(8,128)(2,1)S(1)} %collective-permute-done.16.r2_ref) | copy-start | bytes 786436
  127.5 0.7 copy-start.14
  132.2 3.1 %copy-start = (bf16[16,336,128]{2,1,0:T(8,128)(2,1)}, bf16[16,336,128]{2,1,0:T(8,128)(2,1)S(1)}, u32[]{:S(2)}) copy-start(bf16[16,336,128]{2,1,0:T(8,128)(2,1)S(1)} %all-to-all-done.3.mine_ref) | copy-start | bytes 4128772
  132.2 6.1 %collective-permute-start.18 = (bf16[16,336,128]{2,1,0:T(8,128)(2,1)S(1)}, bf16[16,336,128]{2,1,0:T(8,128)(2,1)S(1)}, u32[]{:S(2)}, u32[]{:S(2)}) collective-permute-start(bf16[16,336,128]{2,1,0:T(8,128)(2,1)S(1)} %all-to-all-done.3.mine_ref), channel_id=1, source_target_pairs={{0,1},{1,0},{2,3},{3,2},{4,5},{5,4},{6,7},{7,6},{8,9},{9,8},{10,11... | collective-permute-start | bytes 4128776 | tf_op jit(solution)/shard_map/ppermute | solution.py:446
  138.4 1.1 copy-start.3

commit v11 on v10

--- a/solution.py
+++ b/solution.py
@@ -400,28 +400,38 @@
     return [tail[0:8] + tail[8:16] for tail in tails]
 
 
-def first_half_body(mine_ref, out_hbm, tall_ref, wide_ref, sems):
+def through_of(tails):
+    return [(tails[b] + tails[4 + b] + tails[8 + b])[4:5] for b in range(4)]
+
+
+def first_half_body(mine_ref, out_hbm, gain_ref, tall_ref, wide_ref, sems):
+    tails = tails_of(mine_ref)
+    total = tails[0]
+    for p in range(1, DOM):
+        total = total + tails[p]
+    gain_ref[0:4, :] = total[0:4]
+    for b, part in enumerate(through_of(tails)):
+        gain_ref[4 + b : 5 + b, :] = part
     half_body(position()[1], mine_ref, out_hbm, tall_ref, wide_ref, sems)
 
 
-def second_half_body(before_hbm, mine_ref, other_ref, gain_in_ref, out_hbm, gain_ref, tall_ref, wide_ref, sems):
-    gain = jnp.zeros((8, 128), F32)
-    mine, through = tails_of(mine_ref), tails_of(other_ref)
-    for p in range(DOM):
-        gain = gain + mine[p]
-        through[p] = through[p] + mine[p]
-    for b in range(4):
-        part = (through[b] + through[4 + b] + through[8 + b])[4:5]
+def second_half_body(before_hbm, mine_gain_ref, other_ref, gain_in_ref, out_hbm, gain_ref, tall_ref, wide_ref, sems):
+    for b, part in enumerate(through_of(tails_of(other_ref))):
         lanes = slice(b * 128, (b + 1) * 128)
-        gain_ref[:, lanes] = gain[b : b + 1] + part / gain_in_ref[:, lanes]
+        part = (part + mine_gain_ref[4 + b : 5 + b, :]) / gain_in_ref[:, lanes]
+        gain_ref[:, lanes] = mine_gain_ref[b : b + 1, :] + part
     half_body(1 - position()[1], other_ref, out_hbm, tall_ref, wide_ref, sems)
 
 
 def in_halves(mine, other, gain_row):
     vmem, hbm = pl.BlockSpec(memory_space=pltpu.VMEM), pl.BlockSpec(memory_space=pltpu.HBM)
     scratch = [pltpu.VMEM((3, D, 256), F32), pltpu.VMEM((2, 256, D), F32), pltpu.SemaphoreType.DMA((5,))]
-    half = pl.pallas_call(
-        first_half_body, out_shape=shape((5, D, D), F32), in_specs=[vmem], out_specs=hbm, scratch_shapes=scratch,
+    half, mine_gain = pl.pallas_call(
+        first_half_body,
+        out_shape=(shape((5, D, D), F32), shape((8, 128), F32)),
+        in_specs=[vmem],
+        out_specs=(hbm, vmem),
+        scratch_shapes=scratch,
         cost_estimate=pl.CostEstimate(flops=int(3e9), transcendentals=0, bytes_accessed=1 << 20),
     )(mine)
     return pl.pallas_call(
@@ -431,7 +441,7 @@
         out_specs=(hbm, vmem),
         input_output_aliases={0: 0},
         scratch_shapes=scratch,
-    )(half, mine, other, gain_row)
+    )(half, mine_gain, other, gain_row)
 
 
 def chip_shift(step, swap):

time: 144 us -> 145 us (level)
  no operation moved by 1% of the time
where the time goes in v11:
time: 145 us; the launch traced here: 144 us
  Pallas kernels  58.8 us (41%)
  starting transfers between devices  47.9 us (33%)
  waiting for transfers between devices  30.2 us (21%)
  local copies, waits for them, and re-layouts  6.01 us (4%)
    pallas_call x8, Pallas kernels, call(): pl.pallas_call(body, out_shape=out_shape, in_specs=specs, out_specs=jax.t...  51.6 us
    all_to_all x4, starting transfers between devices, to_dom_peers(): return lax.all_to_all(array, 'dom', split_axis=0, concat_axis=0, tiled=True)  25.2 us
    ppermute x10, waiting for transfers between devices, along_chips(): return lax.ppermute(array, 'blk', chip_shift(step, 0))  23.5 us
    ppermute x10, starting transfers between devices, along_chips(): return lax.ppermute(array, 'blk', chip_shift(step, 0))  11.4 us
    ppermute x9, starting transfers between devices, other_core(): return lax.ppermute(array, 'blk', chip_shift(0, 1))  11.3 us
    unnamed x38, local copies, waits for them, and re-layouts  5.98 us
    all_to_all x4, waiting for transfers between devices, to_dom_peers(): return lax.all_to_all(array, 'dom', split_axis=0, concat_axis=0, tiled=True)  4.16 us
    pallas_call x1, Pallas kernels, in_halves(): pl.pallas_call(first_half_body, out_shape=(shape((5, D, D), F32), shape((...  3.6 us
  transfers between devices with their start and end apart: 23, of which 11 were waited for; matrix products, arithmetic and copies ran while one was open for 0% of the time, Pallas kernels for 33%

profile of v11, /device:TPU:1, one launch (start us, length us, event | category | flops | bytes accessed | tf_op | source)
XLA Modules:
  0.0 143.9 jit_solution(16110357805047601114)
XLA Ops:
  0.6 3.5 %shard_map.165 = (bf16[528,512]{1,0:T(8,128)(2,1)}, bf16[16,128,512]{2,1,0:T(8,128)(2,1)}) custom-call(s32[1,8]{1,0:T(1,128)} %pattern_ref.1, s32[16]{0:T(128)} %counts_ref.3, bf16[256,512]{1,0:T(8,128)(2,1)} %x_ref.7, f32[1,512]{1,0:T(1,128)} %bitcast.5, s32[1,256]{1,0:T(1,128)} %bitcast.11, bf16[256,512]{1,0:T(8,128)(2,1)} %grad_ref.7, s32[16,128]{1,0:T(8,128)} %rows_ref.3), custom_call_target="tpu_custom_call" | custom-call | flops 4000000000 | bytes 1048576 | tf_op jit(solution)/shard_map/pallas_call | solution.py:40
  4.1 7.6 %all-to-all-start = ((bf16[16,128,512]{2,1,0:T(8,128)(2,1)}), bf16[16,128,512]{2,1,0:T(8,128)(2,1)S(1)}, u32[]{:S(2)}, u32[]{:S(2)}) async-start(bf16[16,128,512]{2,1,0:T(8,128)(2,1)} %get-tuple-element.50), calls=%async_computation | async-start | bytes 4194304 | tf_op jit(solution)/shard_map/all_to_all | solution.py:460
  11.7 3.8 %collective-permute-start.1 = (bf16[528,512]{1,0:T(8,128)(2,1)}, bf16[528,512]{1,0:T(8,128)(2,1)S(1)}, u32[]{:S(2)}, u32[]{:S(2)}) collective-permute-start(bf16[528,512]{1,0:T(8,128)(2,1)} %get-tuple-element.42.p0_ref), channel_id=1, source_target_pairs={{0,6},{1,7},{2,0},{3,1},{4,2},{5,3},{6,4},{7,5},{8,14},{9,15},{10,... | collective-permute-start | bytes 1622024 | tf_op jit(solution)/shard_map/ppermute | solution.py:452
  15.5 8.9 %shard_map.166 = (bf16[1024,512]{1,0:T(8,128)(2,1)}, f32[256,128]{1,0:T(8,128)}, bf16[16,128,512]{2,1,0:T(8,128)(2,1)}, bf16[192,512]{1,0:T(8,128)(2,1)}, bf16[64,512]{1,0:T(8,128)(2,1)}) custom-call(s32[32,128]{1,0:T(8,128)} %bitcast.8, s32[32,128]{1,0:T(8,128)} %bitcast.9, bf16[256,512]{1,0:T(8,128)(2,1)} %grad_ref.7, bf16[512,512]{1,0:T(8,128)(2,1)} %w_ref.3, ...), custom_call_target="tpu_custom_call" | custom-call | flops 10000000000 | bytes 1048576 | tf_op jit(solution)/shard_map/pallas_call | solution.py:40
  24.5 2.0 %collective-permute-done.1.p3_ref = bf16[528,512]{1,0:T(8,128)(2,1)S(1)} collective-permute-done((bf16[528,512]{1,0:T(8,128)(2,1)}, bf16[528,512]{1,0:T(8,128)(2,1)S(1)}, u32[]{:S(2)}, u32[]{:S(2)}) %collective-permute-start.1) | collective-permute-done | bytes 540704 | tf_op jit(solution)/shard_map/ppermute | solution.py:452
  26.5 3.0 %collective-permute-done.p1_ref = bf16[528,512]{1,0:T(8,128)(2,1)S(1)} collective-permute-done((bf16[528,512]{1,0:T(8,128)(2,1)}, bf16[528,512]{1,0:T(8,128)(2,1)S(1)}, u32[]{:S(2)}, u32[]{:S(2)}) %collective-permute-start) | collective-permute-done | bytes 540704 | tf_op jit(solution)/shard_map/ppermute | solution.py:452
  29.5 0.4 collective-permute-start.3
  29.9 1.2 collective-permute-start.2
  31.1 2.7 %collective-permute-start.4 = (bf16[528,512]{1,0:T(8,128)(2,1)}, bf16[528,512]{1,0:T(8,128)(2,1)}, u32[]{:S(2)}, u32[]{:S(2)}) collective-permute-start(bf16[528,512]{1,0:T(8,128)(2,1)} %get-tuple-element.42.p0_ref), channel_id=1, source_target_pairs={{0,1},{1,0},{2,3},{3,2},{4,5},{5,4},{6,7},{7,6},{8,9},{9,8},{10,11... | collective-permute-start | bytes 1622024 | tf_op jit(solution)/shard_map/ppermute | solution.py:456
  33.9 0.5 collective-permute-start.8
  34.4 2.6 %collective-permute-done.2.t2_ref = bf16[256,512]{1,0:T(8,128)(2,1)} collective-permute-done((bf16[256,512]{1,0:T(8,128)(2,1)S(1)}, bf16[256,512]{1,0:T(8,128)(2,1)}, u32[]{:S(2)}, u32[]{:S(2)}) %collective-permute-start.2) | collective-permute-done | bytes 262176 | tf_op jit(solution)/shard_map/ppermute | solution.py:452
  36.9 3.1 %collective-permute-start.6 = (bf16[256,512]{1,0:T(8,128)(2,1)}, bf16[256,512]{1,0:T(8,128)(2,1)}, u32[]{:S(2)}, u32[]{:S(2)}) collective-permute-start(bf16[256,512]{1,0:T(8,128)(2,1)} %collective-permute-done.2.t2_ref), channel_id=1, source_target_pairs={{0,1},{1,0},{2,3},{3,2},{4,5},{5,4},{6,7},{7,6},{8,9},{9,8},{10,11... | collective-permute-start | bytes 786440 | tf_op jit(solution)/shard_map/ppermute | solution.py:456
  40.0 0.1 collective-permute-start.7
  40.1 1.3 copy-done.1
  41.4 6.4 %all-to-all-start.1 = ((bf16[16,128,512]{2,1,0:T(8,128)(2,1)}), bf16[16,128,512]{2,1,0:T(8,128)(2,1)S(1)}, u32[]{:S(2)}, u32[]{:S(2)}) async-start(bf16[16,128,512]{2,1,0:T(8,128)(2,1)} %get-tuple-element.55), calls=%async_computation.1 | async-start | bytes 4194304 | tf_op jit(solution)/shard_map/all_to_all | solution.py:460
  47.8 4.3 %shard_map.167 = (f32[256,512]{1,0:T(8,128)}, bf16[16,64,128]{2,1,0:T(8,128)(2,1)}, bf16[16,64,128]{2,1,0:T(8,128)(2,1)}) custom-call(bf16[1024,512]{1,0:T(8,128)(2,1)} %get-tuple-element.48.counts_t_ref, f32[256,128]{1,0:T(8,128)} %get-tuple-element.49.degree_ref, bf16[16,128,512]{2,1,0:T(8,128)(2,1)} %copy-done.1, bf16[256,512]{1,0:T(8,128)(2,1)} %x_ref.7, ...), custom_call_target="tpu_custom_call" | custom-call | flops 4000000000 | bytes 1048576 | tf_op jit(solution)/shard_map/pallas_call | solution.py:40
  52.1 1.0 collective-permute-start.9
  53.1 1.5 %collective-permute-done.9.other_ref = bf16[16,64,128]{2,1,0:T(8,128)(2,1)} collective-permute-done((bf16[16,64,128]{2,1,0:T(8,128)(2,1)}, bf16[16,64,128]{2,1,0:T(8,128)(2,1)}, u32[]{:S(2)}, u32[]{:S(2)}) %collective-permute-start.9) | collective-permute-done | bytes 262176 | tf_op jit(solution)/shard_map/ppermute | solution.py:456
  54.6 23.3 %shard_map.168 = (bf16[4,256,256]{2,1,0:T(8,128)(2,1)}, bf16[4,256,256]{2,1,0:T(8,128)(2,1)}, bf16[16,128,128]{2,1,0:T(8,128)(2,1)}) custom-call(bf16[528,512]{1,0:T(8,128)(2,1)} %get-tuple-element.42.p0_ref, bf16[528,512]{1,0:T(8,128)(2,1)} %copy-done.6, bf16[256,512]{1,0:T(8,128)(2,1)} %collective-permute-done.2.t2_ref, bf16[272,512]{1,0:T(8,128)(2,1)} %copy-done.8, ...), custom_call_target="tpu_custom_call" | custom-call | flops 12000000000 | bytes 1048576 | tf_op jit(solution)/shard_map/pallas_call | solution.py:40
  77.9 0.4 collective-permute-start.10
  78.3 6.9 %all-to-all-start.2 = ((bf16[16,128,128]{2,1,0:T(8,128)(2,1)}), bf16[16,128,128]{2,1,0:T(8,128)(2,1)S(1)}, u32[]{:S(2)}, u32[]{:S(2)}) async-start(bf16[16,128,128]{2,1,0:T(8,128)(2,1)} %get-tuple-element.56), calls=%async_computation.2 | async-start | bytes 1048576 | tf_op jit(solution)/shard_map/all_to_all | solution.py:460
  85.2 0.8 copy-done.7
  86.0 3.7 %shard_map.169 = (f32[256,512]{1,0:T(8,128)}, f32[8,128]{1,0:T(8,128)}, bf16[2,256,256]{2,1,0:T(8,128)(2,1)}, bf16[2,256,256]{2,1,0:T(8,128)(2,1)}, bf16[2,256,2...) custom-call(s32[16]{0:T(128)} %counts_ref.3, bf16[16,128,512]{2,1,0:T(8,128)(2,1)} %copy-done, s32[16,128]{1,0:T(8,128)} %rows_ref.3, ...), custom_call_target="tpu_custom_call" | custom-call | flops 3000000000 | bytes 1048576 | tf_op jit(solution)/shard_map/pallas_call | solution.py:40
  89.8 0.4 collective-permute-start.11
  90.2 1.0 collective-permute-done.11.g1_ref
  91.2 4.1 %all-to-all-done.2.in_ref = bf16[16,128,128]{2,1,0:T(8,128)(2,1)S(1)} async-done(((bf16[16,128,128]{2,1,0:T(8,128)(2,1)}), bf16[16,128,128]{2,1,0:T(8,128)(2,1)S(1)}, u32[]{:S(2)}, u32[]{:S(2)}) %all-to-all-start.2) | async-done | bytes 524320 | tf_op jit(solution)/shard_map/all_to_all | solution.py:460
  95.4 0.8 copy-done.4
  96.2 1.8 %shard_map.170.c0_ref = bf16[144,128]{1,0:T(8,128)(2,1)} custom-call(bf16[16,128,128]{2,1,0:T(8,128)(2,1)} %copy-done.4, f32[8,128]{1,0:T(8,128)} %get-tuple-element.59.g0_ref, f32[8,128]{1,0:T(8,128)} %copy-done.18, bf16[192,512]{1,0:T(8,128)(2,1)} %get-tuple-element.46.wqkv_ref), custom_call_target="tpu_custom_call" | custom-call | flops 1000000000 | bytes 1048576 | tf_op jit(solution)/shard_map/pallas_call | solution.py:40
  98.0 3.3 %collective-permute-start.14 = (bf16[144,128]{1,0:T(8,128)(2,1)}, bf16[144,128]{1,0:T(8,128)(2,1)S(1)}, u32[]{:S(2)}, u32[]{:S(2)}) collective-permute-start(bf16[144,128]{1,0:T(8,128)(2,1)} %shard_map.170.c0_ref), channel_id=1, source_target_pairs={{0,6},{1,7},{2,0},{3,1},{4,2},{5,3},{6,4},{7,5},{8,14},{9,15},{10,... | collective-permute-start | bytes 110600 | tf_op jit(solution)/shard_map/ppermute | solution.py:452
  101.2 0.7 collective-permute-start.12
  101.9 0.7 collective-permute-done.14.c3_ref
  102.6 3.2 %collective-permute-done.13.c2_ref = bf16[144,128]{1,0:T(8,128)(2,1)S(1)} collective-permute-done((bf16[144,128]{1,0:T(8,128)(2,1)}, bf16[144,128]{1,0:T(8,128)(2,1)S(1)}, u32[]{:S(2)}, u32[]{:S(2)}) %collective-permute-start.13) | collective-permute-done | bytes 36896 | tf_op jit(solution)/shard_map/ppermute | solution.py:452
  105.9 0.6 copy-done.16
  106.5 0.6 copy-done.17
  107.1 2.1 %shard_map.171 = bf16[16,336,128]{2,1,0:T(8,128)(2,1)} custom-call(bf16[144,128]{1,0:T(8,128)(2,1)} %shard_map.170.c0_ref, bf16[144,128]{1,0:T(8,128)(2,1)} %copy-done.17, bf16[144,128]{1,0:T(8,128)(2,1)} %copy-done.16, bf16[144,128]{1,0:T(8,128)(2,1)} %copy-done.15), custom_call_target="tpu_custom_call" | custom-call | flops 1000000000 | bytes 1048576 | tf_op jit(solution)/shard_map/pallas_call | solution.py:40
  109.2 4.3 %all-to-all-start.3 = ((bf16[16,336,128]{2,1,0:T(8,128)(2,1)}), bf16[16,336,128]{2,1,0:T(8,128)(2,1)S(1)}, u32[]{:S(2)}, u32[]{:S(2)}) async-start(bf16[16,336,128]{2,1,0:T(8,128)(2,1)} %shard_map.171), calls=%async_computation.3 | async-start | bytes 2752512 | tf_op jit(solution)/shard_map/all_to_all | solution.py:460
  113.5 0.1 collective-permute-start.15
  113.6 1.1 collective-permute-start.16
  114.8 0.8 collective-permute-start.17
  115.5 3.3 %collective-permute-done.15.r1_ref = bf16[2,256,256]{2,1,0:T(8,128)(2,1)S(1)} collective-permute-done((bf16[2,256,256]{2,1,0:T(8,128)(2,1)S(1)}, bf16[2,256,256]{2,1,0:T(8,128)(2,1)S(1)}, u32[]{:S(2)}, u32[]{:S(2)}) %collective-permute-start.15) | collective-permute-done | bytes 262176 | tf_op jit(solution)/shard_map/ppermute | solution.py:452
  118.8 1.7 %collective-permute-done.16.r2_ref = bf16[2,256,256]{2,1,0:T(8,128)(2,1)S(1)} collective-permute-done((bf16[2,256,256]{2,1,0:T(8,128)(2,1)S(1)}, bf16[2,256,256]{2,1,0:T(8,128)(2,1)S(1)}, u32[]{:S(2)}, u32[]{:S(2)}) %collective-permute-start.16) | collective-permute-done | bytes 262176 | tf_op jit(solution)/shard_map/ppermute | solution.py:452
  120.5 7.0 %collective-permute-done.17.r3_ref = bf16[2,256,256]{2,1,0:T(8,128)(2,1)S(1)} collective-permute-done((bf16[2,256,256]{2,1,0:T(8,128)(2,1)S(1)}, bf16[2,256,256]{2,1,0:T(8,128)(2,1)S(1)}, u32[]{:S(2)}, u32[]{:S(2)}) %collective-permute-start.17) | collective-permute-done | bytes 262176 | tf_op jit(solution)/shard_map/ppermute | solution.py:452
  127.5 0.7 copy-done.14
  128.2 4.0 %shard_map.172 = (bf16[256,512]{1,0:T(8,128)(2,1)}, bf16[256,512]{1,0:T(8,128)(2,1)}) custom-call(bf16[2,256,256]{2,1,0:T(8,128)(2,1)} %get-tuple-element.65.r0_ref, bf16[2,256,256]{2,1,0:T(8,128)(2,1)} %copy-done.12, bf16[2,256,256]{2,1,0:T(8,128)(2,1)} %copy-done.13, bf16[2,256,256]{2,1,0:T(8,128)(2,1)} %copy-done.14, ...), custom_call_target="tpu_custom_call" | custom-call | flops 2000000000 | bytes 1048576 | tf_op jit(solution)/shard_map/pallas_call | solution.py:40
  132.2 3.1 %collective-permute-start.18 = (bf16[16,336,128]{2,1,0:T(8,128)(2,1)S(1)}, bf16[16,336,128]{2,1,0:T(8,128)(2,1)S(1)}, u32[]{:S(2)}, u32[]{:S(2)}) collective-permute-start(bf16[16,336,128]{2,1,0:T(8,128)(2,1)S(1)} %all-to-all-done.3.mine_ref), channel_id=1, source_target_pairs={{0,1},{1,0},{2,3},{3,2},{4,5},{5,4},{6,7},{7,6},{8,9},{9,8},{10,11... | collective-permute-start | bytes 4128776 | tf_op jit(solution)/shard_map/ppermute | solution.py:456
  135.4 3.6 %shard_map.173 = (f32[5,512,512]{2,1,0:T(8,128)}, f32[8,128]{1,0:T(8,128)}) custom-call(bf16[16,336,128]{2,1,0:T(8,128)(2,1)} %copy-done.2), custom_call_target="tpu_custom_call" | custom-call | flops 3000000000 | bytes 1048576 | tf_op jit(solution)/shard_map/pallas_call | solution.py:429
  139.0 1.1 copy-done.3
  140.1 3.6 %shard_map.174 = (f32[5,512,512]{2,1,0:T(8,128)}, f32[1,512]{1,0:T(1,128)}) custom-call(f32[5,512,512]{2,1,0:T(8,128)} %get-tuple-element.76.before_hbm, f32[8,128]{1,0:T(8,128)} %get-tuple-element.77.mine_gain_ref, bf16[16,336,128]{2,1,0:T(8,128)(2,1)} %copy-done.3, f32[1,512]{1,0:T(1,128)} %bitcast.7), custom_call_target="tpu_custom_call", output_to_operand_aliasing={{0}: (0, {})} | custom-call | tf_op jit(solution)/shard_map/pallas_call | solution.py:437
  (48 shorter events, 0.1 us)
Async XLA Ops:
  4.1 36.0 %all-to-all-start = ((bf16[16,128,512]{2,1,0:T(8,128)(2,1)}), bf16[16,128,512]{2,1,0:T(8,128)(2,1)S(1)}, u32[]{:S(2)}, u32[]{:S(2)}) async-start(bf16[16,128,512]{2,1,0:T(8,128)(2,1)} %get-tuple-element.50), calls=%async_computation | async-start | bytes 4194304 | tf_op jit(solution)/shard_map/all_to_all | solution.py:460
  11.7 14.8 %collective-permute-start.1 = (bf16[528,512]{1,0:T(8,128)(2,1)}, bf16[528,512]{1,0:T(8,128)(2,1)S(1)}, u32[]{:S(2)}, u32[]{:S(2)}) collective-permute-start(bf16[528,512]{1,0:T(8,128)(2,1)} %get-tuple-element.42.p0_ref), channel_id=1, source_target_pairs={{0,6},{1,7},{2,0},{3,1},{4,2},{5,3},{6,4},{7,5},{8,14},{9,15},{10,... | collective-permute-start | bytes 1622024 | tf_op jit(solution)/shard_map/ppermute | solution.py:452
  15.5 13.9 %collective-permute-start = (bf16[528,512]{1,0:T(8,128)(2,1)}, bf16[528,512]{1,0:T(8,128)(2,1)S(1)}, u32[]{:S(2)}, u32[]{:S(2)}) collective-permute-start(bf16[528,512]{1,0:T(8,128)(2,1)} %get-tuple-element.42.p0_ref), channel_id=1, source_target_pairs={{0,2},{1,3},{2,4},{3,5},{4,6},{5,7},{6,0},{7,1},{8,10},{9,11},{10,... | collective-permute-start | bytes 1622024 | tf_op jit(solution)/shard_map/ppermute | solution.py:452
  26.5 15.0 %copy-start.5 = (bf16[528,512]{1,0:T(8,128)(2,1)}, bf16[528,512]{1,0:T(8,128)(2,1)S(1)}, u32[]{:S(2)}) copy-start(bf16[528,512]{1,0:T(8,128)(2,1)S(1)} %collective-permute-done.1.p3_ref) | copy-start | bytes 1622020
  29.5 12.0 %copy-start.6 = (bf16[528,512]{1,0:T(8,128)(2,1)}, bf16[528,512]{1,0:T(8,128)(2,1)S(1)}, u32[]{:S(2)}) copy-start(bf16[528,512]{1,0:T(8,128)(2,1)S(1)} %collective-permute-done.p1_ref) | copy-start | bytes 1622020
  29.5 10.5 %collective-permute-start.3 = (bf16[272,512]{1,0:T(8,128)(2,1)S(1)}, bf16[272,512]{1,0:T(8,128)(2,1)S(1)}, u32[]{:S(2)}, u32[]{:S(2)}) collective-permute-start(bf16[272,512]{1,0:T(8,128)(2,1)S(1)} %slice.7), channel_id=1, source_target_pairs={{0,6},{1,7},{2,0},{3,1},{4,2},{5,3},{6,4},{7,5},{8,14},{9,15},{10,... | collective-permute-start | bytes 835592 | tf_op jit(solution)/shard_map/ppermute | solution.py:452
  29.9 7.0 %collective-permute-start.2 = (bf16[256,512]{1,0:T(8,128)(2,1)S(1)}, bf16[256,512]{1,0:T(8,128)(2,1)}, u32[]{:S(2)}, u32[]{:S(2)}) collective-permute-start(bf16[256,512]{1,0:T(8,128)(2,1)S(1)} %slice.6), channel_id=1, source_target_pairs={{0,2},{1,3},{2,4},{3,5},{4,6},{5,7},{6,0},{7,1},{8,10},{9,11},{10,... | collective-permute-start | bytes 786440 | tf_op jit(solution)/shard_map/ppermute | solution.py:452
  31.1 21.0 %collective-permute-start.4 = (bf16[528,512]{1,0:T(8,128)(2,1)}, bf16[528,512]{1,0:T(8,128)(2,1)}, u32[]{:S(2)}, u32[]{:S(2)}) collective-permute-start(bf16[528,512]{1,0:T(8,128)(2,1)} %get-tuple-element.42.p0_ref), channel_id=1, source_target_pairs={{0,1},{1,0},{2,3},{3,2},{4,5},{5,4},{6,7},{7,6},{8,9},{9,8},{10,11... | collective-permute-start | bytes 1622024 | tf_op jit(solution)/shard_map/ppermute | solution.py:456
  33.8 19.3 %collective-permute-start.5 = (bf16[528,512]{1,0:T(8,128)(2,1)S(1)}, bf16[528,512]{1,0:T(8,128)(2,1)}, u32[]{:S(2)}, u32[]{:S(2)}) collective-permute-start(bf16[528,512]{1,0:T(8,128)(2,1)S(1)} %collective-permute-done.p1_ref), channel_id=1, source_target_pairs={{0,1},{1,0},{2,3},{3,2},{4,5},{5,4},{6,7},{7,6},{8,9},{9,8},{10,11... | collective-permute-start | bytes 1622024 | tf_op jit(solution)/shard_map/ppermute | solution.py:456
  33.9 19.3 %collective-permute-start.8 = (bf16[528,512]{1,0:T(8,128)(2,1)S(1)}, bf16[528,512]{1,0:T(8,128)(2,1)}, u32[]{:S(2)}, u32[]{:S(2)}) collective-permute-start(bf16[528,512]{1,0:T(8,128)(2,1)S(1)} %collective-permute-done.1.p3_ref), channel_id=1, source_target_pairs={{0,1},{1,0},{2,3},{3,2},{4,5},{5,4},{6,7},{7,6},{8,9},{9,8},{10,11... | collective-permute-start | bytes 1622024 | tf_op jit(solution)/shard_map/ppermute | solution.py:456
  36.9 16.2 %collective-permute-start.6 = (bf16[256,512]{1,0:T(8,128)(2,1)}, bf16[256,512]{1,0:T(8,128)(2,1)}, u32[]{:S(2)}, u32[]{:S(2)}) collective-permute-start(bf16[256,512]{1,0:T(8,128)(2,1)} %collective-permute-done.2.t2_ref), channel_id=1, source_target_pairs={{0,1},{1,0},{2,3},{3,2},{4,5},{5,4},{6,7},{7,6},{8,9},{9,8},{10,11... | collective-permute-start | bytes 786440 | tf_op jit(solution)/shard_map/ppermute | solution.py:456
  40.0 12.1 %copy-start.8 = (bf16[272,512]{1,0:T(8,128)(2,1)}, bf16[272,512]{1,0:T(8,128)(2,1)S(1)}, u32[]{:S(2)}) copy-start(bf16[272,512]{1,0:T(8,128)(2,1)S(1)} %collective-permute-done.3.b2_ref) | copy-start | bytes 835588
  40.0 13.1 %collective-permute-start.7 = (bf16[272,512]{1,0:T(8,128)(2,1)S(1)}, bf16[272,512]{1,0:T(8,128)(2,1)}, u32[]{:S(2)}, u32[]{:S(2)}) collective-permute-start(bf16[272,512]{1,0:T(8,128)(2,1)S(1)} %collective-permute-done.3.b2_ref), channel_id=1, source_target_pairs={{0,1},{1,0},{2,3},{3,2},{4,5},{5,4},{6,7},{7,6},{8,9},{9,8},{10,11... | collective-permute-start | bytes 835592 | tf_op jit(solution)/shard_map/ppermute | solution.py:456
  40.1 1.3 copy-start.1
  41.4 36.8 %all-to-all-start.1 = ((bf16[16,128,512]{2,1,0:T(8,128)(2,1)}), bf16[16,128,512]{2,1,0:T(8,128)(2,1)S(1)}, u32[]{:S(2)}, u32[]{:S(2)}) async-start(bf16[16,128,512]{2,1,0:T(8,128)(2,1)} %get-tuple-element.55), calls=%async_computation.1 | async-start | bytes 4194304 | tf_op jit(solution)/shard_map/all_to_all | solution.py:460
  52.1 2.5 %collective-permute-start.9 = (bf16[16,64,128]{2,1,0:T(8,128)(2,1)}, bf16[16,64,128]{2,1,0:T(8,128)(2,1)}, u32[]{:S(2)}, u32[]{:S(2)}) collective-permute-start(bf16[16,64,128]{2,1,0:T(8,128)(2,1)} %get-tuple-element.52), channel_id=1, source_target_pairs={{0,1},{1,0},{2,3},{3,2},{4,5},{5,4},{6,7},{7,6},{8,9},{9,8},{10,11... | collective-permute-start | bytes 786440 | tf_op jit(solution)/shard_map/ppermute | solution.py:456
  77.9 7.3 %collective-permute-start.10 = (bf16[4,256,256]{2,1,0:T(8,128)(2,1)}, bf16[4,256,256]{2,1,0:T(8,128)(2,1)S(1)}, u32[]{:S(2)}, u32[]{:S(2)}) collective-permute-start(bf16[4,256,256]{2,1,0:T(8,128)(2,1)} %get-tuple-element.58), channel_id=1, source_target_pairs={{0,1},{1,0},{2,3},{3,2},{4,5},{5,4},{6,7},{7,6},{8,9},{9,8},{10,11... | collective-permute-start | bytes 1572872 | tf_op jit(solution)/shard_map/ppermute | solution.py:456
  78.3 7.0 %copy-start = (bf16[16,128,512]{2,1,0:T(8,128)(2,1)}, bf16[16,128,512]{2,1,0:T(8,128)(2,1)S(1)}, u32[]{:S(2)}) copy-start(bf16[16,128,512]{2,1,0:T(8,128)(2,1)S(1)} %all-to-all-done.1.back_ref) | copy-start | bytes 6291460
  78.3 17.1 %all-to-all-start.2 = ((bf16[16,128,128]{2,1,0:T(8,128)(2,1)}), bf16[16,128,128]{2,1,0:T(8,128)(2,1)S(1)}, u32[]{:S(2)}, u32[]{:S(2)}) async-start(bf16[16,128,128]{2,1,0:T(8,128)(2,1)} %get-tuple-element.56), calls=%async_computation.2 | async-start | bytes 1048576 | tf_op jit(solution)/shard_map/all_to_all | solution.py:460
  85.2 0.8 copy-start.7
  89.8 1.5 %collective-permute-start.11 = (f32[8,128]{1,0:T(8,128)}, f32[8,128]{1,0:T(8,128)S(1)}, u32[]{:S(2)}, u32[]{:S(2)}) collective-permute-start(f32[8,128]{1,0:T(8,128)} %get-tuple-element.59.g0_ref), channel_id=1, source_target_pairs={{0,1},{1,0},{2,3},{3,2},{4,5},{5,4},{6,7},{7,6},{8,9},{9,8},{10,11... | collective-permute-start | bytes 12296 | tf_op jit(solution)/shard_map/ppermute | solution.py:456
  91.2 4.2 %copy-start.18 = (f32[8,128]{1,0:T(8,128)}, f32[8,128]{1,0:T(8,128)S(1)}, u32[]{:S(2)}) copy-start(f32[8,128]{1,0:T(8,128)S(1)} %collective-permute-done.11.g1_ref) | copy-start | bytes 12292
  95.4 0.8 copy-start.4
  98.0 4.6 %collective-permute-start.14 = (bf16[144,128]{1,0:T(8,128)(2,1)}, bf16[144,128]{1,0:T(8,128)(2,1)S(1)}, u32[]{:S(2)}, u32[]{:S(2)}) collective-permute-start(bf16[144,128]{1,0:T(8,128)(2,1)} %shard_map.170.c0_ref), channel_id=1, source_target_pairs={{0,6},{1,7},{2,0},{3,1},{4,2},{5,3},{6,4},{7,5},{8,14},{9,15},{10,... | collective-permute-start | bytes 110600 | tf_op jit(solution)/shard_map/ppermute | solution.py:452
  101.2 4.6 %collective-permute-start.13 = (bf16[144,128]{1,0:T(8,128)(2,1)}, bf16[144,128]{1,0:T(8,128)(2,1)S(1)}, u32[]{:S(2)}, u32[]{:S(2)}) collective-permute-start(bf16[144,128]{1,0:T(8,128)(2,1)} %shard_map.170.c0_ref), channel_id=1, source_target_pairs={{0,4},{1,5},{2,6},{3,7},{4,0},{5,1},{6,2},{7,3},{8,12},{9,13},{10,... | collective-permute-start | bytes 110600 | tf_op jit(solution)/shard_map/ppermute | solution.py:452
  101.2 4.6 %collective-permute-start.12 = (bf16[144,128]{1,0:T(8,128)(2,1)}, bf16[144,128]{1,0:T(8,128)(2,1)S(1)}, u32[]{:S(2)}, u32[]{:S(2)}) collective-permute-start(bf16[144,128]{1,0:T(8,128)(2,1)} %shard_map.170.c0_ref), channel_id=1, source_target_pairs={{0,2},{1,3},{2,4},{3,5},{4,6},{5,7},{6,0},{7,1},{8,10},{9,11},{10,... | collective-permute-start | bytes 110600 | tf_op jit(solution)/shard_map/ppermute | solution.py:452
  102.6 3.3 %copy-start.15 = (bf16[144,128]{1,0:T(8,128)(2,1)}, bf16[144,128]{1,0:T(8,128)(2,1)S(1)}, u32[]{:S(2)}) copy-start(bf16[144,128]{1,0:T(8,128)(2,1)S(1)} %collective-permute-done.14.c3_ref) | copy-start | bytes 110596
  105.9 0.6 copy-start.16
  106.5 0.6 copy-start.17
  109.2 4.3 %copy-start.11 = (bf16[2,256,256]{2,1,0:T(8,128)(2,1)S(1)}, bf16[2,256,256]{2,1,0:T(8,128)(2,1)}, u32[]{:S(2)}) copy-start(bf16[2,256,256]{2,1,0:T(8,128)(2,1)} %get-tuple-element.66) | copy-start | bytes 786436
  109.2 4.4 %copy-start.10 = (bf16[2,256,256]{2,1,0:T(8,128)(2,1)S(1)}, bf16[2,256,256]{2,1,0:T(8,128)(2,1)}, u32[]{:S(2)}) copy-start(bf16[2,256,256]{2,1,0:T(8,128)(2,1)} %get-tuple-element.67) | copy-start | bytes 786436
  109.2 5.6 %copy-start.9 = (bf16[2,256,256]{2,1,0:T(8,128)(2,1)S(1)}, bf16[2,256,256]{2,1,0:T(8,128)(2,1)}, u32[]{:S(2)}) copy-start(bf16[2,256,256]{2,1,0:T(8,128)(2,1)} %get-tuple-element.68) | copy-start | bytes 786436
  109.2 23.1 %all-to-all-start.3 = ((bf16[16,336,128]{2,1,0:T(8,128)(2,1)}), bf16[16,336,128]{2,1,0:T(8,128)(2,1)S(1)}, u32[]{:S(2)}, u32[]{:S(2)}) async-start(bf16[16,336,128]{2,1,0:T(8,128)(2,1)} %shard_map.171), calls=%async_computation.3 | async-start | bytes 2752512 | tf_op jit(solution)/shard_map/all_to_all | solution.py:460
  113.5 5.3 %collective-permute-start.15 = (bf16[2,256,256]{2,1,0:T(8,128)(2,1)S(1)}, bf16[2,256,256]{2,1,0:T(8,128)(2,1)S(1)}, u32[]{:S(2)}, u32[]{:S(2)}) collective-permute-start(bf16[2,256,256]{2,1,0:T(8,128)(2,1)S(1)} %copy-done.11), channel_id=1, source_target_pairs={{0,6},{1,7},{2,0},{3,1},{4,2},{5,3},{6,4},{7,5},{8,14},{9,15},{10,... | collective-permute-start | bytes 786440 | tf_op jit(solution)/shard_map/ppermute | solution.py:452
  113.6 6.9 %collective-permute-start.16 = (bf16[2,256,256]{2,1,0:T(8,128)(2,1)S(1)}, bf16[2,256,256]{2,1,0:T(8,128)(2,1)S(1)}, u32[]{:S(2)}, u32[]{:S(2)}) collective-permute-start(bf16[2,256,256]{2,1,0:T(8,128)(2,1)S(1)} %copy-done.10), channel_id=1, source_target_pairs={{0,4},{1,5},{2,6},{3,7},{4,0},{5,1},{6,2},{7,3},{8,12},{9,13},{10,... | collective-permute-start | bytes 786440 | tf_op jit(solution)/shard_map/ppermute | solution.py:452
  114.8 12.8 %collective-permute-start.17 = (bf16[2,256,256]{2,1,0:T(8,128)(2,1)S(1)}, bf16[2,256,256]{2,1,0:T(8,128)(2,1)S(1)}, u32[]{:S(2)}, u32[]{:S(2)}) collective-permute-start(bf16[2,256,256]{2,1,0:T(8,128)(2,1)S(1)} %copy-done.9), channel_id=1, source_target_pairs={{0,2},{1,3},{2,4},{3,5},{4,6},{5,7},{6,0},{7,1},{8,10},{9,11},{10,... | collective-permute-start | bytes 786440 | tf_op jit(solution)/shard_map/ppermute | solution.py:452
  118.8 8.7 %copy-start.12 = (bf16[2,256,256]{2,1,0:T(8,128)(2,1)}, bf16[2,256,256]{2,1,0:T(8,128)(2,1)S(1)}, u32[]{:S(2)}) copy-start(bf16[2,256,256]{2,1,0:T(8,128)(2,1)S(1)} %collective-permute-done.15.r1_ref) | copy-start | bytes 786436
  120.5 7.0 %copy-start.13 = (bf16[2,256,256]{2,1,0:T(8,128)(2,1)}, bf16[2,256,256]{2,1,0:T(8,128)(2,1)S(1)}, u32[]{:S(2)}) copy-start(bf16[2,256,256]{2,1,0:T(8,128)(2,1)S(1)} %collective-permute-done.16.r2_ref) | copy-start | bytes 786436
  127.5 0.7 copy-start.14
  132.2 3.1 %copy-start.2 = (bf16[16,336,128]{2,1,0:T(8,128)(2,1)}, bf16[16,336,128]{2,1,0:T(8,128)(2,1)S(1)}, u32[]{:S(2)}) copy-start(bf16[16,336,128]{2,1,0:T(8,128)(2,1)S(1)} %all-to-all-done.3.mine_ref) | copy-start | bytes 4128772
  132.2 6.7 %collective-permute-start.18 = (bf16[16,336,128]{2,1,0:T(8,128)(2,1)S(1)}, bf16[16,336,128]{2,1,0:T(8,128)(2,1)S(1)}, u32[]{:S(2)}, u32[]{:S(2)}) collective-permute-start(bf16[16,336,128]{2,1,0:T(8,128)(2,1)S(1)} %all-to-all-done.3.mine_ref), channel_id=1, source_target_pairs={{0,1},{1,0},{2,3},{3,2},{4,5},{5,4},{6,7},{7,6},{8,9},{9,8},{10,11... | collective-permute-start | bytes 4128776 | tf_op jit(solution)/shard_map/ppermute | solution.py:456
  139.0 1.1 copy-start.3

commit v12 on v10

--- a/solution.py
+++ b/solution.py
@@ -509,7 +509,7 @@
             pltpu.VMEM((BLK, ROWS, 128), BF16),
             pltpu.VMEM((BLK, ROWS, 128), BF16),
         ],
-        micros=12,
+        micros=8,
     )
     chunks = lax.optimization_barrier((chunks, back))[0]
     chunks = to_dom_peers(chunks)

time: 144 us -> 145 us (level)
  starting transfers between devices: 47.9 us -> 42.8 us
  waiting for transfers between devices: 30.1 us -> 34.6 us
  local copies, waits for them, and re-layouts: 5.98 us -> 7.72 us
    all_to_all x4, waiting for transfers between devices: 4.14 us -> 10.8 us  [to_dom_peers(): return lax.all_to_all(array, 'dom', split_axis=0, concat_axis=0, tiled=True)]
    all_to_all x4, starting transfers between devices: 25.2 us -> 22.2 us  [to_dom_peers(): return lax.all_to_all(array, 'dom', split_axis=0, concat_axis=0, tiled=True)]
    ppermute x10, waiting for transfers between devices: 23.5 us -> 21 us  [along_chips(): return lax.ppermute(array, 'blk', chip_shift(step, 0))]
    ppermute x9, starting transfers between devices: 11.3 us -> 9.05 us  [other_core(): return lax.ppermute(array, 'blk', chip_shift(0, 1))]
    unnamed x38 -> x42, local copies, waits for them, and re-layouts: 5.94 us -> 6.74 us
  transfers between devices with their start and end apart: 23 -> 23, of which waited for: 11 -> 11; matrix products, arithmetic and copies ran while one was open for 0% -> 1% of each run, Pallas kernels for 33% -> 33%
where the time goes in v12:
time: 145 us
  Pallas kernels  58.7 us (40%)
  starting transfers between devices  42.8 us (30%)
  waiting for transfers between devices  34.6 us (24%)
  local copies, waits for them, and re-layouts  7.72 us (5%)
    pallas_call x8, Pallas kernels, call(): pl.pallas_call(body, out_shape=out_shape, in_specs=specs, out_specs=jax.t...  51.7 us
    all_to_all x4, starting transfers between devices, to_dom_peers(): return lax.all_to_all(array, 'dom', split_axis=0, concat_axis=0, tiled=True)  22.2 us
    ppermute x10, waiting for transfers between devices, along_chips(): return lax.ppermute(array, 'blk', chip_shift(step, 0))  21 us
    ppermute x10, starting transfers between devices, along_chips(): return lax.ppermute(array, 'blk', chip_shift(step, 0))  11.6 us
    all_to_all x4, waiting for transfers between devices, to_dom_peers(): return lax.all_to_all(array, 'dom', split_axis=0, concat_axis=0, tiled=True)  10.8 us
    ppermute x9, starting transfers between devices, other_core(): return lax.ppermute(array, 'blk', chip_shift(0, 1))  9.05 us
    unnamed x42, local copies, waits for them, and re-layouts  6.74 us
    pallas_call x1, Pallas kernels, in_halves(): pl.pallas_call(second_half_body, out_shape=(shape((5, D, D), F32), shape(...  4.01 us
  transfers between devices with their start and end apart: 23, of which 11 were waited for; matrix products, arithmetic and copies ran while one was open for 1% of the time, Pallas kernels for 33%

profile of v12, /device:TPU:1, one launch (start us, length us, event | category | flops | bytes accessed | tf_op | source)
XLA Modules:
  0.0 144.7 jit_solution(3177100160730343149)
XLA Ops:
  0.6 3.5 %shard_map.165 = (bf16[528,512]{1,0:T(8,128)(2,1)}, bf16[16,128,512]{2,1,0:T(8,128)(2,1)}) custom-call(s32[1,8]{1,0:T(1,128)} %pattern_ref.1, s32[16]{0:T(128)} %counts_ref.3, bf16[256,512]{1,0:T(8,128)(2,1)} %x_ref.7, f32[1,512]{1,0:T(1,128)} %bitcast.5, s32[1,256]{1,0:T(1,128)} %bitcast.11, bf16[256,512]{1,0:T(8,128)(2,1)} %grad_ref.7, s32[16,128]{1,0:T(8,128)} %rows_ref.3), custom_call_target="tpu_custom_call" | custom-call | flops 4000000000 | bytes 1048576 | tf_op jit(solution)/shard_map/pallas_call | solution.py:40
  4.1 7.6 %all-to-all-start = ((bf16[16,128,512]{2,1,0:T(8,128)(2,1)}), bf16[16,128,512]{2,1,0:T(8,128)(2,1)S(1)}, u32[]{:S(2)}, u32[]{:S(2)}) async-start(bf16[16,128,512]{2,1,0:T(8,128)(2,1)} %get-tuple-element.48), calls=%async_computation | async-start | bytes 4194304 | tf_op jit(solution)/shard_map/all_to_all | solution.py:450
  11.7 3.8 %collective-permute-start.1 = (bf16[528,512]{1,0:T(8,128)(2,1)}, bf16[528,512]{1,0:T(8,128)(2,1)S(1)}, u32[]{:S(2)}, u32[]{:S(2)}) collective-permute-start(bf16[528,512]{1,0:T(8,128)(2,1)} %get-tuple-element.40.p0_ref), channel_id=1, source_target_pairs={{0,6},{1,7},{2,0},{3,1},{4,2},{5,3},{6,4},{7,5},{8,14},{9,15},{10,... | collective-permute-start | bytes 1622024 | tf_op jit(solution)/shard_map/ppermute | solution.py:442
  15.5 8.9 %shard_map.166 = (bf16[1024,512]{1,0:T(8,128)(2,1)}, f32[256,128]{1,0:T(8,128)}, bf16[16,128,512]{2,1,0:T(8,128)(2,1)}, bf16[192,512]{1,0:T(8,128)(2,1)}, bf16[64,512]{1,0:T(8,128)(2,1)}) custom-call(s32[32,128]{1,0:T(8,128)} %bitcast.8, s32[32,128]{1,0:T(8,128)} %bitcast.9, bf16[256,512]{1,0:T(8,128)(2,1)} %grad_ref.7, bf16[512,512]{1,0:T(8,128)(2,1)} %w_ref.3, ...), custom_call_target="tpu_custom_call" | custom-call | flops 10000000000 | bytes 1048576 | tf_op jit(solution)/shard_map/pallas_call | solution.py:40
  24.5 2.0 %collective-permute-done.1.p3_ref = bf16[528,512]{1,0:T(8,128)(2,1)S(1)} collective-permute-done((bf16[528,512]{1,0:T(8,128)(2,1)}, bf16[528,512]{1,0:T(8,128)(2,1)S(1)}, u32[]{:S(2)}, u32[]{:S(2)}) %collective-permute-start.1) | collective-permute-done | bytes 540704 | tf_op jit(solution)/shard_map/ppermute | solution.py:442
  26.5 3.0 %collective-permute-done.p1_ref = bf16[528,512]{1,0:T(8,128)(2,1)S(1)} collective-permute-done((bf16[528,512]{1,0:T(8,128)(2,1)}, bf16[528,512]{1,0:T(8,128)(2,1)S(1)}, u32[]{:S(2)}, u32[]{:S(2)}) %collective-permute-start) | collective-permute-done | bytes 540704 | tf_op jit(solution)/shard_map/ppermute | solution.py:442
  29.5 0.8 copy-done.6
  30.3 0.4 collective-permute-start.3
  30.7 1.0 slice.6
  31.7 1.2 collective-permute-start.2
  32.9 6.7 %all-to-all-done.table_ref = bf16[16,128,512]{2,1,0:T(8,128)(2,1)S(1)} async-done(((bf16[16,128,512]{2,1,0:T(8,128)(2,1)}), bf16[16,128,512]{2,1,0:T(8,128)(2,1)S(1)}, u32[]{:S(2)}, u32[]{:S(2)}) %all-to-all-start) | async-done | bytes 2097184 | tf_op jit(solution)/shard_map/all_to_all | solution.py:450
  39.6 1.3 copy-done.2
  40.9 3.9 %all-to-all-start.1 = ((bf16[16,128,512]{2,1,0:T(8,128)(2,1)}), bf16[16,128,512]{2,1,0:T(8,128)(2,1)S(1)}, u32[]{:S(2)}, u32[]{:S(2)}) async-start(bf16[16,128,512]{2,1,0:T(8,128)(2,1)} %get-tuple-element.53), calls=%async_computation.1 | async-start | bytes 4194304 | tf_op jit(solution)/shard_map/all_to_all | solution.py:450
  44.8 3.3 %collective-permute-start.4 = (bf16[528,512]{1,0:T(8,128)(2,1)}, bf16[528,512]{1,0:T(8,128)(2,1)}, u32[]{:S(2)}, u32[]{:S(2)}) collective-permute-start(bf16[528,512]{1,0:T(8,128)(2,1)} %get-tuple-element.40.p0_ref), channel_id=1, source_target_pairs={{0,1},{1,0},{2,3},{3,2},{4,5},{5,4},{6,7},{7,6},{8,9},{9,8},{10,11... | collective-permute-start | bytes 1622024 | tf_op jit(solution)/shard_map/ppermute | solution.py:446
  48.3 0.4 collective-permute-start.8
  48.8 0.4 collective-permute-start.7
  49.2 4.3 %shard_map.167 = (f32[256,512]{1,0:T(8,128)}, bf16[16,64,128]{2,1,0:T(8,128)(2,1)}, bf16[16,64,128]{2,1,0:T(8,128)(2,1)}) custom-call(bf16[1024,512]{1,0:T(8,128)(2,1)} %get-tuple-element.46.counts_t_ref, f32[256,128]{1,0:T(8,128)} %get-tuple-element.47.degree_ref, bf16[16,128,512]{2,1,0:T(8,128)(2,1)} %copy-done.2, bf16[256,512]{1,0:T(8,128)(2,1)} %x_ref.7, ...), custom_call_target="tpu_custom_call" | custom-call | flops 4000000000 | bytes 1048576 | tf_op jit(solution)/shard_map/pallas_call | solution.py:40
  53.5 0.4 collective-permute-start.9
  54.0 1.7 %collective-permute-done.9.other_ref = bf16[16,64,128]{2,1,0:T(8,128)(2,1)} collective-permute-done((bf16[16,64,128]{2,1,0:T(8,128)(2,1)}, bf16[16,64,128]{2,1,0:T(8,128)(2,1)}, u32[]{:S(2)}, u32[]{:S(2)}) %collective-permute-start.9) | collective-permute-done | bytes 262176 | tf_op jit(solution)/shard_map/ppermute | solution.py:446
  55.7 23.3 %shard_map.168 = (bf16[4,256,256]{2,1,0:T(8,128)(2,1)}, bf16[4,256,256]{2,1,0:T(8,128)(2,1)}, bf16[16,128,128]{2,1,0:T(8,128)(2,1)}) custom-call(bf16[528,512]{1,0:T(8,128)(2,1)} %get-tuple-element.40.p0_ref, bf16[528,512]{1,0:T(8,128)(2,1)} %copy-done.6, bf16[256,512]{1,0:T(8,128)(2,1)} %collective-permute-done.2.t2_ref, bf16[272,512]{1,0:T(8,128)(2,1)} %copy-done.8, ...), custom_call_target="tpu_custom_call" | custom-call | flops 8000000000 | bytes 1048576 | tf_op jit(solution)/shard_map/pallas_call | solution.py:40
  79.0 0.1 collective-permute-start.10
  79.1 6.8 %all-to-all-start.2 = ((bf16[16,128,128]{2,1,0:T(8,128)(2,1)}), bf16[16,128,128]{2,1,0:T(8,128)(2,1)S(1)}, u32[]{:S(2)}, u32[]{:S(2)}) async-start(bf16[16,128,128]{2,1,0:T(8,128)(2,1)} %get-tuple-element.54), calls=%async_computation.2 | async-start | bytes 1048576 | tf_op jit(solution)/shard_map/all_to_all | solution.py:450
  85.9 0.8 copy-done.7
  86.7 3.8 %shard_map.169 = (f32[256,512]{1,0:T(8,128)}, f32[8,128]{1,0:T(8,128)}, bf16[2,256,256]{2,1,0:T(8,128)(2,1)}, bf16[2,256,256]{2,1,0:T(8,128)(2,1)}, bf16[2,256,2...) custom-call(s32[16]{0:T(128)} %counts_ref.3, bf16[16,128,512]{2,1,0:T(8,128)(2,1)} %copy-done.1, s32[16,128]{1,0:T(8,128)} %rows_ref.3, ...), custom_call_target="tpu_custom_call" | custom-call | flops 3000000000 | bytes 1048576 | tf_op jit(solution)/shard_map/pallas_call | solution.py:40
  90.5 0.7 collective-permute-start.11
  91.1 1.0 collective-permute-done.11.g1_ref
  92.2 4.1 %all-to-all-done.2.in_ref = bf16[16,128,128]{2,1,0:T(8,128)(2,1)S(1)} async-done(((bf16[16,128,128]{2,1,0:T(8,128)(2,1)}), bf16[16,128,128]{2,1,0:T(8,128)(2,1)S(1)}, u32[]{:S(2)}, u32[]{:S(2)}) %all-to-all-start.2) | async-done | bytes 524320 | tf_op jit(solution)/shard_map/all_to_all | solution.py:450
  96.3 0.8 copy-done.4
  97.1 1.8 %shard_map.170.c0_ref = bf16[144,128]{1,0:T(8,128)(2,1)} custom-call(bf16[16,128,128]{2,1,0:T(8,128)(2,1)} %copy-done.4, f32[8,128]{1,0:T(8,128)} %get-tuple-element.57.g0_ref, f32[8,128]{1,0:T(8,128)} %copy-done.20, bf16[192,512]{1,0:T(8,128)(2,1)} %get-tuple-element.44.wqkv_ref), custom_call_target="tpu_custom_call" | custom-call | flops 1000000000 | bytes 1048576 | tf_op jit(solution)/shard_map/pallas_call | solution.py:40
  98.9 3.8 %collective-permute-start.14 = (bf16[144,128]{1,0:T(8,128)(2,1)}, bf16[144,128]{1,0:T(8,128)(2,1)S(1)}, u32[]{:S(2)}, u32[]{:S(2)}) collective-permute-start(bf16[144,128]{1,0:T(8,128)(2,1)} %shard_map.170.c0_ref), channel_id=1, source_target_pairs={{0,6},{1,7},{2,0},{3,1},{4,2},{5,3},{6,4},{7,5},{8,14},{9,15},{10,... | collective-permute-start | bytes 110600 | tf_op jit(solution)/shard_map/ppermute | solution.py:442
  102.6 0.7 collective-permute-start.12
  103.3 0.7 collective-permute-done.14.c3_ref
  104.0 3.2 %collective-permute-done.13.c2_ref = bf16[144,128]{1,0:T(8,128)(2,1)S(1)} collective-permute-done((bf16[144,128]{1,0:T(8,128)(2,1)}, bf16[144,128]{1,0:T(8,128)(2,1)S(1)}, u32[]{:S(2)}, u32[]{:S(2)}) %collective-permute-start.13) | collective-permute-done | bytes 36896 | tf_op jit(solution)/shard_map/ppermute | solution.py:442
  107.3 0.6 copy-done.18
  107.9 0.6 copy-done.19
  108.5 2.1 %shard_map.171 = bf16[16,336,128]{2,1,0:T(8,128)(2,1)} custom-call(bf16[144,128]{1,0:T(8,128)(2,1)} %shard_map.170.c0_ref, bf16[144,128]{1,0:T(8,128)(2,1)} %copy-done.19, bf16[144,128]{1,0:T(8,128)(2,1)} %copy-done.18, bf16[144,128]{1,0:T(8,128)(2,1)} %copy-done.17), custom_call_target="tpu_custom_call" | custom-call | flops 1000000000 | bytes 1048576 | tf_op jit(solution)/shard_map/pallas_call | solution.py:40
  110.6 3.9 %all-to-all-start.3 = ((bf16[16,336,128]{2,1,0:T(8,128)(2,1)}), bf16[16,336,128]{2,1,0:T(8,128)(2,1)S(1)}, u32[]{:S(2)}, u32[]{:S(2)}) async-start(bf16[16,336,128]{2,1,0:T(8,128)(2,1)} %shard_map.171), calls=%async_computation.3 | async-start | bytes 2752512 | tf_op jit(solution)/shard_map/all_to_all | solution.py:450
  114.5 0.8 collective-permute-start.16
  115.4 0.8 collective-permute-start.17
  116.1 3.6 %collective-permute-done.15.r1_ref = bf16[2,256,256]{2,1,0:T(8,128)(2,1)S(1)} collective-permute-done((bf16[2,256,256]{2,1,0:T(8,128)(2,1)S(1)}, bf16[2,256,256]{2,1,0:T(8,128)(2,1)S(1)}, u32[]{:S(2)}, u32[]{:S(2)}) %collective-permute-start.15) | collective-permute-done | bytes 262176 | tf_op jit(solution)/shard_map/ppermute | solution.py:442
  119.7 1.7 %collective-permute-done.16.r2_ref = bf16[2,256,256]{2,1,0:T(8,128)(2,1)S(1)} collective-permute-done((bf16[2,256,256]{2,1,0:T(8,128)(2,1)S(1)}, bf16[2,256,256]{2,1,0:T(8,128)(2,1)S(1)}, u32[]{:S(2)}, u32[]{:S(2)}) %collective-permute-start.16) | collective-permute-done | bytes 262176 | tf_op jit(solution)/shard_map/ppermute | solution.py:442
  121.5 6.7 %collective-permute-done.17.r3_ref = bf16[2,256,256]{2,1,0:T(8,128)(2,1)S(1)} collective-permute-done((bf16[2,256,256]{2,1,0:T(8,128)(2,1)S(1)}, bf16[2,256,256]{2,1,0:T(8,128)(2,1)S(1)}, u32[]{:S(2)}, u32[]{:S(2)}) %collective-permute-start.17) | collective-permute-done | bytes 262176 | tf_op jit(solution)/shard_map/ppermute | solution.py:442
  128.2 0.7 copy-done.16
  128.9 4.0 %shard_map.172 = (bf16[256,512]{1,0:T(8,128)(2,1)}, bf16[256,512]{1,0:T(8,128)(2,1)}) custom-call(bf16[2,256,256]{2,1,0:T(8,128)(2,1)} %get-tuple-element.63.r0_ref, bf16[2,256,256]{2,1,0:T(8,128)(2,1)} %copy-done.14, bf16[2,256,256]{2,1,0:T(8,128)(2,1)} %copy-done.15, bf16[2,256,256]{2,1,0:T(8,128)(2,1)} %copy-done.16, ...), custom_call_target="tpu_custom_call" | custom-call | flops 2000000000 | bytes 1048576 | tf_op jit(solution)/shard_map/pallas_call | solution.py:40
  132.9 3.5 %collective-permute-start.18 = (bf16[16,336,128]{2,1,0:T(8,128)(2,1)S(1)}, bf16[16,336,128]{2,1,0:T(8,128)(2,1)S(1)}, u32[]{:S(2)}, u32[]{:S(2)}) collective-permute-start(bf16[16,336,128]{2,1,0:T(8,128)(2,1)S(1)} %all-to-all-done.3.mine_ref), channel_id=1, source_target_pairs={{0,1},{1,0},{2,3},{3,2},{4,5},{5,4},{6,7},{7,6},{8,9},{9,8},{10,11... | collective-permute-start | bytes 4128776 | tf_op jit(solution)/shard_map/ppermute | solution.py:446
  136.4 3.0 %shard_map.173.before_hbm = f32[5,512,512]{2,1,0:T(8,128)} custom-call(bf16[16,336,128]{2,1,0:T(8,128)(2,1)} %copy-done), custom_call_target="tpu_custom_call" | custom-call | flops 3000000000 | bytes 1048576 | tf_op jit(solution)/shard_map/pallas_call | solution.py:423
  139.5 1.1 copy-done.3
  140.5 4.0 %shard_map.174 = (f32[5,512,512]{2,1,0:T(8,128)}, f32[1,512]{1,0:T(1,128)}) custom-call(f32[5,512,512]{2,1,0:T(8,128)} %shard_map.173.before_hbm, bf16[16,336,128]{2,1,0:T(8,128)(2,1)} %copy-done, bf16[16,336,128]{2,1,0:T(8,128)(2,1)} %copy-done.3, f32[1,512]{1,0:T(1,128)} %bitcast.7), custom_call_target="tpu_custom_call", output_to_operand_aliasing={{0}: (0, {})} | custom-call | tf_op jit(solution)/shard_map/pallas_call | solution.py:427
  (52 shorter events, 0.4 us)
Async XLA Ops:
  4.1 35.5 %all-to-all-start = ((bf16[16,128,512]{2,1,0:T(8,128)(2,1)}), bf16[16,128,512]{2,1,0:T(8,128)(2,1)S(1)}, u32[]{:S(2)}, u32[]{:S(2)}) async-start(bf16[16,128,512]{2,1,0:T(8,128)(2,1)} %get-tuple-element.48), calls=%async_computation | async-start | bytes 4194304 | tf_op jit(solution)/shard_map/all_to_all | solution.py:450
  11.7 14.8 %collective-permute-start.1 = (bf16[528,512]{1,0:T(8,128)(2,1)}, bf16[528,512]{1,0:T(8,128)(2,1)S(1)}, u32[]{:S(2)}, u32[]{:S(2)}) collective-permute-start(bf16[528,512]{1,0:T(8,128)(2,1)} %get-tuple-element.40.p0_ref), channel_id=1, source_target_pairs={{0,6},{1,7},{2,0},{3,1},{4,2},{5,3},{6,4},{7,5},{8,14},{9,15},{10,... | collective-permute-start | bytes 1622024 | tf_op jit(solution)/shard_map/ppermute | solution.py:442
  15.5 13.9 %collective-permute-start = (bf16[528,512]{1,0:T(8,128)(2,1)}, bf16[528,512]{1,0:T(8,128)(2,1)S(1)}, u32[]{:S(2)}, u32[]{:S(2)}) collective-permute-start(bf16[528,512]{1,0:T(8,128)(2,1)} %get-tuple-element.40.p0_ref), channel_id=1, source_target_pairs={{0,2},{1,3},{2,4},{3,5},{4,6},{5,7},{6,0},{7,1},{8,10},{9,11},{10,... | collective-permute-start | bytes 1622024 | tf_op jit(solution)/shard_map/ppermute | solution.py:442
  26.5 21.8 %copy-start.5 = (bf16[528,512]{1,0:T(8,128)(2,1)}, bf16[528,512]{1,0:T(8,128)(2,1)S(1)}, u32[]{:S(2)}) copy-start(bf16[528,512]{1,0:T(8,128)(2,1)S(1)} %collective-permute-done.1.p3_ref) | copy-start | bytes 1622020
  29.5 0.8 copy-start.6
  30.3 18.5 %collective-permute-start.3 = (bf16[272,512]{1,0:T(8,128)(2,1)S(1)}, bf16[272,512]{1,0:T(8,128)(2,1)S(1)}, u32[]{:S(2)}, u32[]{:S(2)}) collective-permute-start(bf16[272,512]{1,0:T(8,128)(2,1)S(1)} %slice.7), channel_id=1, source_target_pairs={{0,6},{1,7},{2,0},{3,1},{4,2},{5,3},{6,4},{7,5},{8,14},{9,15},{10,... | collective-permute-start | bytes 835592 | tf_op jit(solution)/shard_map/ppermute | solution.py:442
  31.7 17.0 %collective-permute-start.2 = (bf16[256,512]{1,0:T(8,128)(2,1)S(1)}, bf16[256,512]{1,0:T(8,128)(2,1)}, u32[]{:S(2)}, u32[]{:S(2)}) collective-permute-start(bf16[256,512]{1,0:T(8,128)(2,1)S(1)} %slice.6), channel_id=1, source_target_pairs={{0,2},{1,3},{2,4},{3,5},{4,6},{5,7},{6,0},{7,1},{8,10},{9,11},{10,... | collective-permute-start | bytes 786440 | tf_op jit(solution)/shard_map/ppermute | solution.py:442
  39.6 1.3 copy-start.2
  40.9 38.2 %all-to-all-start.1 = ((bf16[16,128,512]{2,1,0:T(8,128)(2,1)}), bf16[16,128,512]{2,1,0:T(8,128)(2,1)S(1)}, u32[]{:S(2)}, u32[]{:S(2)}) async-start(bf16[16,128,512]{2,1,0:T(8,128)(2,1)} %get-tuple-element.53), calls=%async_computation.1 | async-start | bytes 4194304 | tf_op jit(solution)/shard_map/all_to_all | solution.py:450
  44.8 8.7 %collective-permute-start.4 = (bf16[528,512]{1,0:T(8,128)(2,1)}, bf16[528,512]{1,0:T(8,128)(2,1)}, u32[]{:S(2)}, u32[]{:S(2)}) collective-permute-start(bf16[528,512]{1,0:T(8,128)(2,1)} %get-tuple-element.40.p0_ref), channel_id=1, source_target_pairs={{0,1},{1,0},{2,3},{3,2},{4,5},{5,4},{6,7},{7,6},{8,9},{9,8},{10,11... | collective-permute-start | bytes 1622024 | tf_op jit(solution)/shard_map/ppermute | solution.py:446
  48.2 5.7 %collective-permute-start.5 = (bf16[528,512]{1,0:T(8,128)(2,1)}, bf16[528,512]{1,0:T(8,128)(2,1)}, u32[]{:S(2)}, u32[]{:S(2)}) collective-permute-start(bf16[528,512]{1,0:T(8,128)(2,1)} %copy-done.6), channel_id=1, source_target_pairs={{0,1},{1,0},{2,3},{3,2},{4,5},{5,4},{6,7},{7,6},{8,9},{9,8},{10,11... | collective-permute-start | bytes 1622024 | tf_op jit(solution)/shard_map/ppermute | solution.py:446
  48.3 5.6 %collective-permute-start.8 = (bf16[528,512]{1,0:T(8,128)(2,1)S(1)}, bf16[528,512]{1,0:T(8,128)(2,1)}, u32[]{:S(2)}, u32[]{:S(2)}) collective-permute-start(bf16[528,512]{1,0:T(8,128)(2,1)S(1)} %collective-permute-done.1.p3_ref), channel_id=1, source_target_pairs={{0,1},{1,0},{2,3},{3,2},{4,5},{5,4},{6,7},{7,6},{8,9},{9,8},{10,11... | collective-permute-start | bytes 1622024 | tf_op jit(solution)/shard_map/ppermute | solution.py:446
  48.7 5.2 %collective-permute-start.6 = (bf16[256,512]{1,0:T(8,128)(2,1)}, bf16[256,512]{1,0:T(8,128)(2,1)S(1)}, u32[]{:S(2)}, u32[]{:S(2)}) collective-permute-start(bf16[256,512]{1,0:T(8,128)(2,1)} %collective-permute-done.2.t2_ref), channel_id=1, source_target_pairs={{0,1},{1,0},{2,3},{3,2},{4,5},{5,4},{6,7},{7,6},{8,9},{9,8},{10,11... | collective-permute-start | bytes 786440 | tf_op jit(solution)/shard_map/ppermute | solution.py:446
  48.8 4.7 %copy-start.8 = (bf16[272,512]{1,0:T(8,128)(2,1)}, bf16[272,512]{1,0:T(8,128)(2,1)S(1)}, u32[]{:S(2)}) copy-start(bf16[272,512]{1,0:T(8,128)(2,1)S(1)} %collective-permute-done.3.b2_ref) | copy-start | bytes 835588
  48.8 5.1 %collective-permute-start.7 = (bf16[272,512]{1,0:T(8,128)(2,1)S(1)}, bf16[272,512]{1,0:T(8,128)(2,1)S(1)}, u32[]{:S(2)}, u32[]{:S(2)}) collective-permute-start(bf16[272,512]{1,0:T(8,128)(2,1)S(1)} %collective-permute-done.3.b2_ref), channel_id=1, source_target_pairs={{0,1},{1,0},{2,3},{3,2},{4,5},{5,4},{6,7},{7,6},{8,9},{9,8},{10,11... | collective-permute-start | bytes 835592 | tf_op jit(solution)/shard_map/ppermute | solution.py:446
  53.5 2.1 %collective-permute-start.9 = (bf16[16,64,128]{2,1,0:T(8,128)(2,1)}, bf16[16,64,128]{2,1,0:T(8,128)(2,1)}, u32[]{:S(2)}, u32[]{:S(2)}) collective-permute-start(bf16[16,64,128]{2,1,0:T(8,128)(2,1)} %get-tuple-element.50), channel_id=1, source_target_pairs={{0,1},{1,0},{2,3},{3,2},{4,5},{5,4},{6,7},{7,6},{8,9},{9,8},{10,11... | collective-permute-start | bytes 786440 | tf_op jit(solution)/shard_map/ppermute | solution.py:446
  53.9 1.8 %copy-start.13 = (bf16[256,512]{1,0:T(8,128)(2,1)}, bf16[256,512]{1,0:T(8,128)(2,1)S(1)}, u32[]{:S(2)}) copy-start(bf16[256,512]{1,0:T(8,128)(2,1)S(1)} %collective-permute-done.6.t6_ref) | copy-start | bytes 786436
  53.9 1.7 %copy-start.9 = (bf16[272,512]{1,0:T(8,128)(2,1)}, bf16[272,512]{1,0:T(8,128)(2,1)S(1)}, u32[]{:S(2)}) copy-start(bf16[272,512]{1,0:T(8,128)(2,1)S(1)} %collective-permute-done.7.b6_ref) | copy-start | bytes 835588
  79.0 6.9 %collective-permute-start.10 = (bf16[4,256,256]{2,1,0:T(8,128)(2,1)}, bf16[4,256,256]{2,1,0:T(8,128)(2,1)S(1)}, u32[]{:S(2)}, u32[]{:S(2)}) collective-permute-start(bf16[4,256,256]{2,1,0:T(8,128)(2,1)} %get-tuple-element.56), channel_id=1, source_target_pairs={{0,1},{1,0},{2,3},{3,2},{4,5},{5,4},{6,7},{7,6},{8,9},{9,8},{10,11... | collective-permute-start | bytes 1572872 | tf_op jit(solution)/shard_map/ppermute | solution.py:446
  79.1 6.8 %copy-start.1 = (bf16[16,128,512]{2,1,0:T(8,128)(2,1)}, bf16[16,128,512]{2,1,0:T(8,128)(2,1)S(1)}, u32[]{:S(2)}) copy-start(bf16[16,128,512]{2,1,0:T(8,128)(2,1)S(1)} %all-to-all-done.1.back_ref) | copy-start | bytes 6291460
  79.1 17.1 %all-to-all-start.2 = ((bf16[16,128,128]{2,1,0:T(8,128)(2,1)}), bf16[16,128,128]{2,1,0:T(8,128)(2,1)S(1)}, u32[]{:S(2)}, u32[]{:S(2)}) async-start(bf16[16,128,128]{2,1,0:T(8,128)(2,1)} %get-tuple-element.54), calls=%async_computation.2 | async-start | bytes 1048576 | tf_op jit(solution)/shard_map/all_to_all | solution.py:450
  85.9 0.8 copy-start.7
  90.5 1.7 %collective-permute-start.11 = (f32[8,128]{1,0:T(8,128)}, f32[8,128]{1,0:T(8,128)S(1)}, u32[]{:S(2)}, u32[]{:S(2)}) collective-permute-start(f32[8,128]{1,0:T(8,128)} %get-tuple-element.57.g0_ref), channel_id=1, source_target_pairs={{0,1},{1,0},{2,3},{3,2},{4,5},{5,4},{6,7},{7,6},{8,9},{9,8},{10,11... | collective-permute-start | bytes 12296 | tf_op jit(solution)/shard_map/ppermute | solution.py:446
  92.2 4.1 %copy-start.20 = (f32[8,128]{1,0:T(8,128)}, f32[8,128]{1,0:T(8,128)S(1)}, u32[]{:S(2)}) copy-start(f32[8,128]{1,0:T(8,128)S(1)} %collective-permute-done.11.g1_ref) | copy-start | bytes 12292
  96.3 0.8 copy-start.4
  98.9 5.1 %collective-permute-start.14 = (bf16[144,128]{1,0:T(8,128)(2,1)}, bf16[144,128]{1,0:T(8,128)(2,1)S(1)}, u32[]{:S(2)}, u32[]{:S(2)}) collective-permute-start(bf16[144,128]{1,0:T(8,128)(2,1)} %shard_map.170.c0_ref), channel_id=1, source_target_pairs={{0,6},{1,7},{2,0},{3,1},{4,2},{5,3},{6,4},{7,5},{8,14},{9,15},{10,... | collective-permute-start | bytes 110600 | tf_op jit(solution)/shard_map/ppermute | solution.py:442
  102.6 4.6 %collective-permute-start.13 = (bf16[144,128]{1,0:T(8,128)(2,1)}, bf16[144,128]{1,0:T(8,128)(2,1)S(1)}, u32[]{:S(2)}, u32[]{:S(2)}) collective-permute-start(bf16[144,128]{1,0:T(8,128)(2,1)} %shard_map.170.c0_ref), channel_id=1, source_target_pairs={{0,4},{1,5},{2,6},{3,7},{4,0},{5,1},{6,2},{7,3},{8,12},{9,13},{10,... | collective-permute-start | bytes 110600 | tf_op jit(solution)/shard_map/ppermute | solution.py:442
  102.6 4.6 %collective-permute-start.12 = (bf16[144,128]{1,0:T(8,128)(2,1)}, bf16[144,128]{1,0:T(8,128)(2,1)S(1)}, u32[]{:S(2)}, u32[]{:S(2)}) collective-permute-start(bf16[144,128]{1,0:T(8,128)(2,1)} %shard_map.170.c0_ref), channel_id=1, source_target_pairs={{0,2},{1,3},{2,4},{3,5},{4,6},{5,7},{6,0},{7,1},{8,10},{9,11},{10,... | collective-permute-start | bytes 110600 | tf_op jit(solution)/shard_map/ppermute | solution.py:442
  104.0 3.3 %copy-start.17 = (bf16[144,128]{1,0:T(8,128)(2,1)}, bf16[144,128]{1,0:T(8,128)(2,1)S(1)}, u32[]{:S(2)}) copy-start(bf16[144,128]{1,0:T(8,128)(2,1)S(1)} %collective-permute-done.14.c3_ref) | copy-start | bytes 110596
  107.3 0.6 copy-start.18
  107.9 0.6 copy-start.19
  110.5 3.9 %copy-start.12 = (bf16[2,256,256]{2,1,0:T(8,128)(2,1)S(1)}, bf16[2,256,256]{2,1,0:T(8,128)(2,1)}, u32[]{:S(2)}) copy-start(bf16[2,256,256]{2,1,0:T(8,128)(2,1)} %get-tuple-element.64) | copy-start | bytes 786436
  110.6 4.0 %copy-start.11 = (bf16[2,256,256]{2,1,0:T(8,128)(2,1)S(1)}, bf16[2,256,256]{2,1,0:T(8,128)(2,1)}, u32[]{:S(2)}) copy-start(bf16[2,256,256]{2,1,0:T(8,128)(2,1)} %get-tuple-element.65) | copy-start | bytes 786436
  110.6 4.8 %copy-start.10 = (bf16[2,256,256]{2,1,0:T(8,128)(2,1)S(1)}, bf16[2,256,256]{2,1,0:T(8,128)(2,1)}, u32[]{:S(2)}) copy-start(bf16[2,256,256]{2,1,0:T(8,128)(2,1)} %get-tuple-element.66) | copy-start | bytes 786436
  110.6 22.4 %all-to-all-start.3 = ((bf16[16,336,128]{2,1,0:T(8,128)(2,1)}), bf16[16,336,128]{2,1,0:T(8,128)(2,1)S(1)}, u32[]{:S(2)}, u32[]{:S(2)}) async-start(bf16[16,336,128]{2,1,0:T(8,128)(2,1)} %shard_map.171), calls=%async_computation.3 | async-start | bytes 2752512 | tf_op jit(solution)/shard_map/all_to_all | solution.py:450
  114.5 5.3 %collective-permute-start.15 = (bf16[2,256,256]{2,1,0:T(8,128)(2,1)S(1)}, bf16[2,256,256]{2,1,0:T(8,128)(2,1)S(1)}, u32[]{:S(2)}, u32[]{:S(2)}) collective-permute-start(bf16[2,256,256]{2,1,0:T(8,128)(2,1)S(1)} %copy-done.12), channel_id=1, source_target_pairs={{0,6},{1,7},{2,0},{3,1},{4,2},{5,3},{6,4},{7,5},{8,14},{9,15},{10,... | collective-permute-start | bytes 786440 | tf_op jit(solution)/shard_map/ppermute | solution.py:442
  114.5 6.9 %collective-permute-start.16 = (bf16[2,256,256]{2,1,0:T(8,128)(2,1)S(1)}, bf16[2,256,256]{2,1,0:T(8,128)(2,1)S(1)}, u32[]{:S(2)}, u32[]{:S(2)}) collective-permute-start(bf16[2,256,256]{2,1,0:T(8,128)(2,1)S(1)} %copy-done.11), channel_id=1, source_target_pairs={{0,4},{1,5},{2,6},{3,7},{4,0},{5,1},{6,2},{7,3},{8,12},{9,13},{10,... | collective-permute-start | bytes 786440 | tf_op jit(solution)/shard_map/ppermute | solution.py:442
  115.4 12.8 %collective-permute-start.17 = (bf16[2,256,256]{2,1,0:T(8,128)(2,1)S(1)}, bf16[2,256,256]{2,1,0:T(8,128)(2,1)S(1)}, u32[]{:S(2)}, u32[]{:S(2)}) collective-permute-start(bf16[2,256,256]{2,1,0:T(8,128)(2,1)S(1)} %copy-done.10), channel_id=1, source_target_pairs={{0,2},{1,3},{2,4},{3,5},{4,6},{5,7},{6,0},{7,1},{8,10},{9,11},{10,... | collective-permute-start | bytes 786440 | tf_op jit(solution)/shard_map/ppermute | solution.py:442
  119.7 8.5 %copy-start.14 = (bf16[2,256,256]{2,1,0:T(8,128)(2,1)}, bf16[2,256,256]{2,1,0:T(8,128)(2,1)S(1)}, u32[]{:S(2)}) copy-start(bf16[2,256,256]{2,1,0:T(8,128)(2,1)S(1)} %collective-permute-done.15.r1_ref) | copy-start | bytes 786436
  121.5 6.7 %copy-start.15 = (bf16[2,256,256]{2,1,0:T(8,128)(2,1)}, bf16[2,256,256]{2,1,0:T(8,128)(2,1)S(1)}, u32[]{:S(2)}) copy-start(bf16[2,256,256]{2,1,0:T(8,128)(2,1)S(1)} %collective-permute-done.16.r2_ref) | copy-start | bytes 786436
  128.2 0.7 copy-start.16
  132.9 3.5 %copy-start = (bf16[16,336,128]{2,1,0:T(8,128)(2,1)}, bf16[16,336,128]{2,1,0:T(8,128)(2,1)S(1)}, u32[]{:S(2)}) copy-start(bf16[16,336,128]{2,1,0:T(8,128)(2,1)S(1)} %all-to-all-done.3.mine_ref) | copy-start | bytes 4128772
  132.9 6.5 %collective-permute-start.18 = (bf16[16,336,128]{2,1,0:T(8,128)(2,1)S(1)}, bf16[16,336,128]{2,1,0:T(8,128)(2,1)S(1)}, u32[]{:S(2)}, u32[]{:S(2)}) collective-permute-start(bf16[16,336,128]{2,1,0:T(8,128)(2,1)S(1)} %all-to-all-done.3.mine_ref), channel_id=1, source_target_pairs={{0,1},{1,0},{2,3},{3,2},{4,5},{5,4},{6,7},{7,6},{8,9},{9,8},{10,11... | collective-permute-start | bytes 4128776 | tf_op jit(solution)/shard_map/ppermute | solution.py:446
  139.5 1.1 copy-start.3
